TPU v7x, 32 devices: a whole 2x2x4 slice. The times are simulated.
32 devices in a mesh: fsdp: 16 (over z, x, core), seq: 2 (over y).
Axes of the slice: x: 2, y: 2, z: 4, core: 2. Of those that a mesh axis runs over, the one named last changes fastest.
Arguments:
- tokens: bfloat16 [24576, 1536], P(('fsdp', 'seq')), may hold values from -6 to 6
- segments: int32 [24576], replicated, may hold values from 0 to 16, as said below
- text: bfloat16 [32, 64, 1536], P('fsdp'), may hold values from -6 to 6
- qkv_weight: bfloat16 [1536, 4608], P('fsdp'), may hold values from -0.15625 to 0.15625
- out_weight: bfloat16 [1536, 1536], P('fsdp'), may hold values from -3 to 3
- cross_query_weight: bfloat16 [1536, 1536], P('fsdp'), may hold values from -0.15625 to 0.15625
- cross_kv_weight: bfloat16 [1536, 3072], P('fsdp'), may hold values from -0.15625 to 0.15625
- cross_out_weight: bfloat16 [1536, 1536], P('fsdp'), may hold values from -0.625 to 0.625
- up_weight: bfloat16 [1536, 6144], P('fsdp'), may hold values from -0.15625 to 0.15625
- down_weight: bfloat16 [6144, 1536], P('fsdp'), may hold values from -0.078125 to 0.078125
- norm_gain: bfloat16 [3, 1536], P(None, 'fsdp'), may hold values from 0.5 to 1.5
- norm_bias: bfloat16 [3, 1536], P(None, 'fsdp'), may hold values from -3 to 3
- cotangent: bfloat16 [24576, 1536], P(('fsdp', 'seq')), may hold values from -6 to 6
Outputs:
- layer_out: bfloat16 [24576, 1536], P(('fsdp', 'seq'))
- grad_tokens: bfloat16 [24576, 1536], P(('fsdp', 'seq'))
- grad_text: float32 [32, 64, 1536], P('fsdp')
- grad_qkv: float32 [1536, 4608], P('fsdp')
- grad_out: float32 [1536, 1536], P('fsdp')
- grad_cross_query: float32 [1536, 1536], P('fsdp')
- grad_cross_kv: float32 [1536, 3072], P('fsdp')
- grad_cross_out: float32 [1536, 1536], P('fsdp')
- grad_up: float32 [1536, 6144], P('fsdp')
- grad_down: float32 [6144, 1536], P('fsdp')
- grad_gain: float32 [3, 1536], P(None, 'fsdp')
- grad_bias: float32 [3, 1536], P(None, 'fsdp')
Inputs may be any that keep to these rules, and one draw needn't show every extreme that they name: `segments`: segment numbers never decrease, and grow by exactly one at each first token of a clip; token 0 has segment 0, and each aligned block of 1536 tokens holds exactly one other first token, never at the block's own first token.
All inputs are finite; a program needn't handle non-finite values.
Results may differ from a plain program's by a relative error of at most 0.023.
Values may be sent and summed in bfloat16 or wider, within the bound.
No kernel may reach another device: no remote copies, remote signals or barrier semaphores. Data moves between devices by JAX's collectives and lax.ppermute only.
A program may use at most 704 MiB of HBM per device.

v0:
```python
import jax
import jax.numpy as jnp
from jax import lax
from jax.sharding import PartitionSpec as P

HEADS = 24
HEAD = 64
TXT = 64
SPAN = 1536
QB = 512
REACH = 3072


EPS = 1e-05
NEG = -1e30


def passed_along(value, axis, steps):
    count = lax.axis_size(axis)
    initial, last = (max(0, -steps), min(count, count - steps))
    return lax.ppermute(value, axis, [(source, source + steps) for source in range(initial, last)])


def layer_norm(values, gain, bias):
    average = jnp.mean(values, axis=-1, keepdims=True)
    centred = values - average
    spread = jnp.mean(centred * centred, axis=-1, keepdims=True)
    return centred * lax.rsqrt(spread + EPS) * gain + bias


def gelu_exact(values):
    return jax.nn.gelu(values, approximate=False)


def matmul(left_side, right_side):
    return jnp.dot(left_side, right_side, preferred_element_type=jnp.float32)


def contract_rows(left_side, right_side):
    return lax.dot_general(
        left_side, right_side, (((0,), (0,)), ((), ())), preferred_element_type=jnp.float32
    )


def contract_cols(left_side, right_side):
    return lax.dot_general(
        left_side, right_side, (((1,), (1,)), ((), ())), preferred_element_type=jnp.float32
    )


def masked_scores(queries, keys, allowed, score_scale):
    scores = (
        jnp.einsum("qhd,khd->hqk", queries, keys, preferred_element_type=jnp.float32) * score_scale
    )
    return jnp.where(allowed[None], scores, NEG)


def self_mask(seg_group, seg_ext, row_start):
    seg_rows = lax.dynamic_slice_in_dim(seg_group, row_start, QB)
    seg_cols = lax.dynamic_slice_in_dim(seg_ext, row_start, REACH + QB)
    rows_at = jnp.arange(QB)[:, None]
    cols_at = jnp.arange(REACH + QB)[None, :]
    return (seg_rows[:, None] == seg_cols[None, :]) & (cols_at <= rows_at + REACH)


def earlier_pieces(group_rows):
    count = -(-REACH // group_rows)
    pieces = []
    for back in range(count, 0, -1):
        take = REACH - (count - 1) * group_rows if back == count else group_rows
        pieces.append((back, take))
    return pieces


def self_forward(queries, kv_ext, seg_group, seg_ext, score_scale):
    group_rows = queries.shape[0]

    def block(carried, block_index):
        row_start = block_index * QB
        query_block = lax.dynamic_slice_in_dim(queries, row_start, QB, 0)
        window = lax.dynamic_slice_in_dim(kv_ext, row_start, REACH + QB, 0)
        scores = masked_scores(
            query_block, window[:, 0], self_mask(seg_group, seg_ext, row_start), score_scale
        )
        row_top = jnp.max(scores, axis=-1, keepdims=True)
        weights = jnp.exp(scores - row_top)
        row_total = jnp.sum(weights, axis=-1, keepdims=True)
        shares = (weights / row_total).astype(jnp.bfloat16)
        result = jnp.einsum(
            "hqk,khd->qhd", shares, window[:, 1], preferred_element_type=jnp.float32
        )
        return (
            carried,
            (result.astype(jnp.bfloat16), row_top[..., 0] + jnp.log(row_total[..., 0])),
        )

    _, (blocks, log_totals) = lax.scan(
        block, jnp.int32(0), jnp.arange(group_rows // QB, dtype=jnp.int32)
    )
    return (blocks.reshape(queries.shape), log_totals)


def self_backward(queries, kv_ext, grad_heads, log_totals, seg_group, seg_ext, score_scale):
    group_rows = queries.shape[0]

    def block(totals, inputs_now):
        block_index, log_total = inputs_now
        row_start = block_index * QB
        query_block = lax.dynamic_slice_in_dim(queries, row_start, QB, 0)
        grad_block = lax.dynamic_slice_in_dim(grad_heads, row_start, QB, 0)
        window = lax.dynamic_slice_in_dim(kv_ext, row_start, REACH + QB, 0)
        scores = masked_scores(
            query_block, window[:, 0], self_mask(seg_group, seg_ext, row_start), score_scale
        )
        shares = jnp.exp(scores - log_total[..., None])
        grad_shares = jnp.einsum(
            "qhd,khd->hqk", grad_block, window[:, 1], preferred_element_type=jnp.float32
        )
        inner_sum = jnp.sum(shares * grad_shares, axis=-1, keepdims=True)
        grad_scores = (shares * (grad_shares - inner_sum)).astype(jnp.bfloat16)
        grad_query = (
            jnp.einsum(
                "hqk,khd->qhd", grad_scores, window[:, 0], preferred_element_type=jnp.float32
            )
            * score_scale
        )
        grad_keys = (
            jnp.einsum("hqk,qhd->khd", grad_scores, query_block, preferred_element_type=jnp.float32)
            * score_scale
        )
        grad_values = jnp.einsum(
            "hqk,qhd->khd",
            shares.astype(jnp.bfloat16),
            grad_block,
            preferred_element_type=jnp.float32,
        )
        current = lax.dynamic_slice_in_dim(totals, row_start, REACH + QB, 0)
        totals = lax.dynamic_update_slice_in_dim(
            totals, current + jnp.stack([grad_keys, grad_values], axis=1), row_start, 0
        )
        return (totals, grad_query)

    zeros = jnp.zeros(kv_ext.shape, jnp.float32)
    totals, grad_blocks = lax.scan(
        block, zeros, (jnp.arange(group_rows // QB, dtype=jnp.int32), log_totals)
    )
    return (grad_blocks.reshape(queries.shape), totals)


def shards(
    tokens,
    segments,
    text,
    qkv_weight,
    out_weight,
    cross_query_weight,
    cross_kv_weight,
    cross_out_weight,
    up_weight,
    down_weight,
    norm_gain,
    norm_bias,
    cotangent,
):
    group_index = lax.axis_index("fsdp")
    seq_index = lax.axis_index("seq")
    seq_count = lax.axis_size("seq")
    tok_rows = tokens.shape[0]
    width = tokens.shape[1]
    group_rows = tok_rows * seq_count
    head_local = HEADS // seq_count
    score_scale = HEAD ** (-0.5)
    pieces = earlier_pieces(group_rows)
    full_qkv, full_out, gathered_gain, gathered_bias = (
        lax.all_gather(qkv_weight, "fsdp", axis=0, tiled=True),
        lax.all_gather(out_weight, "fsdp", axis=0, tiled=True),
        lax.all_gather(norm_gain, "fsdp", axis=1, tiled=True),
        lax.all_gather(norm_bias, "fsdp", axis=1, tiled=True),
    )
    gains = gathered_gain.astype(jnp.float32)
    biases = gathered_bias.astype(jnp.float32)
    padded_seg = jnp.concatenate([jnp.full((REACH,), -1, jnp.int32), segments])
    seg_ext = lax.dynamic_slice_in_dim(padded_seg, group_index * group_rows, REACH + group_rows)
    seg_group = seg_ext[REACH:]
    seg_tokens = lax.dynamic_slice_in_dim(seg_group, seq_index * tok_rows, tok_rows)
    slot_tokens = seg_tokens - group_index * (group_rows // SPAN)
    inputs = tokens.astype(jnp.float32)
    normed_one_f, norm_back_one = jax.vjp(layer_norm, inputs, gains[0], biases[0])
    normed_one = normed_one_f.astype(jnp.bfloat16)
    qkv = matmul(normed_one, full_qkv).astype(jnp.bfloat16).reshape(tok_rows, 3, width)
    headed = lax.all_to_all(qkv, "seq", split_axis=2, concat_axis=0, tiled=True).reshape(
        group_rows, 3, head_local, HEAD
    )
    queries = headed[:, 0]
    key_vals = headed[:, 1:]
    earlier_parts = []
    for back, take in pieces:
        earlier_parts.append(passed_along(key_vals[group_rows - take :], "fsdp", back))
    kv_ext = jnp.concatenate(earlier_parts + [key_vals], axis=0)
    result_heads, log_totals = self_forward(queries, kv_ext, seg_group, seg_ext, score_scale)
    attended = lax.all_to_all(
        result_heads.reshape(group_rows, head_local * HEAD),
        "seq",
        split_axis=0,
        concat_axis=1,
        tiled=True,
    )
    hidden_one = inputs + matmul(attended, full_out)
    full_cq, full_ckv, full_cout, full_up, full_down = (
        lax.all_gather(cross_query_weight, "fsdp", axis=0, tiled=True),
        lax.all_gather(cross_kv_weight, "fsdp", axis=0, tiled=True),
        lax.all_gather(cross_out_weight, "fsdp", axis=0, tiled=True),
        lax.all_gather(up_weight, "fsdp", axis=0, tiled=True),
        lax.all_gather(down_weight, "fsdp", axis=0, tiled=True),
    )
    normed_two_f, norm_back_two = jax.vjp(layer_norm, hidden_one, gains[1], biases[1])
    normed_two = normed_two_f.astype(jnp.bfloat16)
    cross_query = matmul(normed_two, full_cq).astype(jnp.bfloat16).reshape(tok_rows, HEADS, HEAD)
    text_rows = text.reshape(-1, width)
    text_count = text_rows.shape[0]
    cross_kv = matmul(text_rows, full_ckv).astype(jnp.bfloat16).reshape(text_count, 2, HEADS, HEAD)
    key_slot = jnp.arange(text_count, dtype=jnp.int32) // TXT
    cross_allowed = slot_tokens[:, None] == key_slot[None, :]
    cross_scores = masked_scores(cross_query, cross_kv[:, 0], cross_allowed, score_scale)
    cross_top = jnp.max(cross_scores, axis=-1, keepdims=True)
    cross_weights = jnp.exp(cross_scores - cross_top)
    cross_total = jnp.sum(cross_weights, axis=-1, keepdims=True)
    cross_log = cross_top + jnp.log(cross_total)
    cross_shares = (cross_weights / cross_total).astype(jnp.bfloat16)
    cross_result = jnp.einsum(
        "hqk,khd->qhd", cross_shares, cross_kv[:, 1], preferred_element_type=jnp.float32
    )
    cross_result = cross_result.astype(jnp.bfloat16).reshape(tok_rows, width)
    hidden_two = hidden_one + matmul(cross_result, full_cout)
    normed_three_f, norm_back_three = jax.vjp(layer_norm, hidden_two, gains[2], biases[2])
    normed_three = normed_three_f.astype(jnp.bfloat16)
    upward = matmul(normed_three, full_up)
    active_f, gelu_back = jax.vjp(gelu_exact, upward)
    active = active_f.astype(jnp.bfloat16)
    layer_out = (hidden_two + matmul(active, full_down)).astype(jnp.bfloat16)
    back_cq, back_ckv, back_cout, back_up, back_down = (
        lax.all_gather(cross_query_weight, "fsdp", axis=0, tiled=True),
        lax.all_gather(cross_kv_weight, "fsdp", axis=0, tiled=True),
        lax.all_gather(cross_out_weight, "fsdp", axis=0, tiled=True),
        lax.all_gather(up_weight, "fsdp", axis=0, tiled=True),
        lax.all_gather(down_weight, "fsdp", axis=0, tiled=True),
    )
    grad_down = contract_rows(active, cotangent)
    grad_active = contract_cols(cotangent, back_down)
    grad_upward = gelu_back(grad_active)[0].astype(jnp.bfloat16)
    grad_up = contract_rows(normed_three, grad_upward)
    grad_normed_three = contract_cols(grad_upward, back_up)
    back_h2, gain_three, bias_three = norm_back_three(grad_normed_three)
    grad_two = cotangent.astype(jnp.float32) + back_h2
    grad_two_low = grad_two.astype(jnp.bfloat16)
    grad_cout = contract_rows(cross_result, grad_two_low)
    grad_result = (
        contract_cols(grad_two_low, back_cout).astype(jnp.bfloat16).reshape(tok_rows, HEADS, HEAD)
    )
    cross_again = masked_scores(cross_query, cross_kv[:, 0], cross_allowed, score_scale)
    cross_p = jnp.exp(cross_again - cross_log)
    grad_cross_p = jnp.einsum(
        "qhd,khd->hqk", grad_result, cross_kv[:, 1], preferred_element_type=jnp.float32
    )
    cross_inner = jnp.sum(cross_p * grad_cross_p, axis=-1, keepdims=True)
    grad_cross_scores = (cross_p * (grad_cross_p - cross_inner)).astype(jnp.bfloat16)
    grad_query_c = (
        jnp.einsum(
            "hqk,khd->qhd", grad_cross_scores, cross_kv[:, 0], preferred_element_type=jnp.float32
        )
        * score_scale
    )
    grad_query_c = grad_query_c.astype(jnp.bfloat16).reshape(tok_rows, width)
    grad_text_keys = (
        jnp.einsum(
            "hqk,qhd->khd", grad_cross_scores, cross_query, preferred_element_type=jnp.float32
        )
        * score_scale
    )
    grad_text_values = jnp.einsum(
        "hqk,qhd->khd",
        cross_p.astype(jnp.bfloat16),
        grad_result,
        preferred_element_type=jnp.float32,
    )
    grad_text_kv = jnp.stack([grad_text_keys, grad_text_values], axis=1).reshape(
        text_count, 2 * width
    )
    grad_text_kv = lax.psum(grad_text_kv.astype(jnp.bfloat16), "seq")
    grad_cq = contract_rows(normed_two, grad_query_c)
    grad_normed_two = contract_cols(grad_query_c, back_cq)
    grad_text = contract_cols(grad_text_kv, back_ckv).reshape(text.shape)
    row_share = text_count // seq_count
    text_part = lax.dynamic_slice_in_dim(text_rows, seq_index * row_share, row_share, 0)
    grad_part = lax.dynamic_slice_in_dim(grad_text_kv, seq_index * row_share, row_share, 0)
    grad_ckv = contract_rows(text_part, grad_part)
    back_h1, gain_two, bias_two = norm_back_two(grad_normed_two)
    grad_one = grad_two + back_h1
    late_sums = (
        lax.psum_scatter(
            grad_cq.astype(jnp.bfloat16), "fsdp", scatter_dimension=0, tiled=True
        ).astype(jnp.float32),
        lax.psum_scatter(
            grad_ckv.astype(jnp.bfloat16), "fsdp", scatter_dimension=0, tiled=True
        ).astype(jnp.float32),
        lax.psum_scatter(
            grad_cout.astype(jnp.bfloat16), "fsdp", scatter_dimension=0, tiled=True
        ).astype(jnp.float32),
        lax.psum_scatter(
            grad_up.astype(jnp.bfloat16), "fsdp", scatter_dimension=0, tiled=True
        ).astype(jnp.float32),
        lax.psum_scatter(
            grad_down.astype(jnp.bfloat16), "fsdp", scatter_dimension=0, tiled=True
        ).astype(jnp.float32),
    )
    back_qkv, back_out = (
        lax.all_gather(qkv_weight, "fsdp", axis=0, tiled=True),
        lax.all_gather(out_weight, "fsdp", axis=0, tiled=True),
    )
    grad_one_low = grad_one.astype(jnp.bfloat16)
    grad_wout = contract_rows(attended, grad_one_low)
    grad_attended = contract_cols(grad_one_low, back_out).astype(jnp.bfloat16)
    grad_heads = lax.all_to_all(
        grad_attended, "seq", split_axis=1, concat_axis=0, tiled=True
    ).reshape(group_rows, head_local, HEAD)
    grad_queries, grad_kv = self_backward(
        queries, kv_ext, grad_heads, log_totals, seg_group, seg_ext, score_scale
    )
    own_grad = grad_kv[REACH:]
    offset = 0
    for back, take in pieces:
        returned = passed_along(
            grad_kv[offset : offset + take].astype(jnp.bfloat16), "fsdp", -back
        ).astype(jnp.float32)
        own_grad = own_grad.at[group_rows - take :].add(returned)
        offset = offset + take
    grad_proj = jnp.concatenate([grad_queries[:, None], own_grad], axis=1).astype(jnp.bfloat16)
    grad_proj = grad_proj.reshape(group_rows, 3, head_local * HEAD)
    grad_tokens_qkv = lax.all_to_all(
        grad_proj, "seq", split_axis=0, concat_axis=2, tiled=True
    ).reshape(tok_rows, 3 * width)
    grad_wqkv = contract_rows(normed_one, grad_tokens_qkv)
    grad_normed_one = contract_cols(grad_tokens_qkv, back_qkv)
    back_x, gain_one, bias_one = norm_back_one(grad_normed_one)
    grad_tokens = (grad_one + back_x).astype(jnp.bfloat16)
    gain_grads = jnp.stack([gain_one, gain_two, gain_three])
    bias_grads = jnp.stack([bias_one, bias_two, bias_three])
    front_sums = (
        lax.psum_scatter(
            grad_wqkv.astype(jnp.bfloat16), "fsdp", scatter_dimension=0, tiled=True
        ).astype(jnp.float32),
        lax.psum_scatter(
            grad_wout.astype(jnp.bfloat16), "fsdp", scatter_dimension=0, tiled=True
        ).astype(jnp.float32),
        lax.psum_scatter(
            gain_grads.astype(jnp.bfloat16), "fsdp", scatter_dimension=1, tiled=True
        ).astype(jnp.float32),
        lax.psum_scatter(
            bias_grads.astype(jnp.bfloat16), "fsdp", scatter_dimension=1, tiled=True
        ).astype(jnp.float32),
    )
    summed = (
        lax.psum(front_sums[0].astype(jnp.bfloat16), "seq").astype(jnp.float32),
        lax.psum(front_sums[1].astype(jnp.bfloat16), "seq").astype(jnp.float32),
        lax.psum(front_sums[2].astype(jnp.bfloat16), "seq").astype(jnp.float32),
        lax.psum(front_sums[3].astype(jnp.bfloat16), "seq").astype(jnp.float32),
        lax.psum(late_sums[0].astype(jnp.bfloat16), "seq").astype(jnp.float32),
        lax.psum(late_sums[1].astype(jnp.bfloat16), "seq").astype(jnp.float32),
        lax.psum(late_sums[2].astype(jnp.bfloat16), "seq").astype(jnp.float32),
        lax.psum(late_sums[3].astype(jnp.bfloat16), "seq").astype(jnp.float32),
        lax.psum(late_sums[4].astype(jnp.bfloat16), "seq").astype(jnp.float32),
    )
    return (
        layer_out,
        grad_tokens,
        grad_text,
        summed[0],
        summed[1],
        summed[4],
        summed[5],
        summed[6],
        summed[7],
        summed[8],
        summed[2],
        summed[3],
    )


def solution(mesh):
    in_specs = (
        P(("fsdp", "seq"), None),
        P(),
        P("fsdp", None, None),
        P("fsdp", None),
        P("fsdp", None),
        P("fsdp", None),
        P("fsdp", None),
        P("fsdp", None),
        P("fsdp", None),
        P("fsdp", None),
        P(None, "fsdp"),
        P(None, "fsdp"),
        P(("fsdp", "seq"), None),
    )
    out_specs = (
        P(("fsdp", "seq"), None),
        P(("fsdp", "seq"), None),
        P("fsdp", None, None),
        P("fsdp", None),
        P("fsdp", None),
        P("fsdp", None),
        P("fsdp", None),
        P("fsdp", None),
        P("fsdp", None),
        P("fsdp", None),
        P(None, "fsdp"),
        P(None, "fsdp"),
    )
    return jax.shard_map(shards, mesh=mesh, in_specs=in_specs, out_specs=out_specs, check_vma=False)
```

profile of v0, /device:TPU:0, one launch (start us, length us, event | category | flops | bytes accessed | tf_op | source)
XLA Modules:
  0.0 2938.5 jit_solution(16519377290880196690)
XLA Ops:
  55.3 68.5 %all-gather.10.cloned.1.call-done = bf16[1536,4608]{1,0:T(8,128)(2,1)} async-done(((bf16[96,4608]{1,0:T(8,128)(2,1)}), bf16[1536,4608]{1,0:T(8,128)(2,1)}) %all-gather.10.cloned.1.call-update) | async-done | bytes 14155792 | tf_op jit(solution)/shard_map/all_gather | solution.py:175
  161.5 107.5 %all_to_all.65 = bf16[768,3,1536]{0,1,2:T(4,128)(2,1)S(1)} all-to-all(bf16[768,3,1536]{0,1,2:T(4,128)(2,1)S(1)} %copy.131), channel_id=1, replica_groups=mesh['fsdp'=16,'seq'=2] {'seq'}, dimensions={2} | all-to-all | bytes 14155776 | tf_op jit(solution)/shard_map/all_to_all | solution.py:191
  331.8 151.7 %collective-permute-done = bf16[1536,2,12,64]{0,3,2,1:T(8,128)(2,1)} collective-permute-done((bf16[1536,2,12,64]{0,3,2,1:T(8,128)(2,1)}, bf16[1536,2,12,64]{0,3,2,1:T(8,128)(2,1)}, u32[]{:S(2)}, u32[]{:S(2)}) %collective-permute-start) | collective-permute-done | bytes 4718624 | tf_op jit(solution)/shard_map/ppermute | solution.py:21
  496.2 313.1 %while.28 = (s32[]{:T(128)}, bf16[3,512,12,64]{1,3,2,0:T(8,128)(2,1)}, f32[3,12,512]{2,1,0:T(8,128)}, s32[3]{0:T(128)}, bf16[4608,2,12,64]{0,3,2,1:T(8,128)(2,1)...) while((s32[]{:T(128)}, ...), condition=%wide.region_5.6_spmd, body=%wide.region_2.5_spmd.sunk | while | flops 5907278336 | bytes 284422400 | solution.py:97
  502.0 34.7 %fusion.152 = (f32[12,512]{1,0:T(8,128)S(1)}, f32[12,512,3584]{2,1,0:T(8,128)}) fusion(pred[512,3584]{1,0:T(8,128)(4,1)S(1)} %fusion.151, bf16[4608,2,12,64]{0,3,2,1:T(8,128)(2,1)} %get-tuple-element.399, s32[]{:T(128)S(6)} %select_n.118, bf16[1536,12,64]{0,2,1:T(8,128)(2,1)} %get-tuple-element.402, s32[]{:T(128)S(6)} %select_n.119), kind=kOutput, calls=%fused_computation.3.clone.1 | convolution fusion | flops 2884626432 | bytes 96231432 | tf_op jit(solution)/shard_map/while/body/eval_jaxpr/qhd,khd->hqk/dot_general | solution.py:53
  564.7 35.8 %fusion.154 = bf16[3,512,12,64]{1,3,2,0:T(8,128)(2,1)} fusion(bf16[3,512,12,64]{1,3,2,0:T(8,128)(2,1)} %get-tuple-element.382, s32[]{:T(128)S(6)} %copy.169, f32[12,512,3584]{2,1,0:T(8,128)} %get-tuple-element.353, f32[12,512]{1,0:T(8,128)S(1)} %fusion.153, f32[12,512]{1,0:T(8,128)S(1)} %get-tuple-element.354, pred[512,3584]{1,0:T(8,128)(4,1)S(1)} %fusion.151, ...), kind=kOutput, calls=%fused_computation.13.clone.1 | convolution fusion | flops 2929065984 | bytes 96256016 | tf_op jit(solution)/shard_map/while/body/eval_jaxpr/hqk,khd->qhd/dot_general | solution.py:89
  606.9 35.4 %fusion.152 = (f32[12,512]{1,0:T(8,128)S(1)}, f32[12,512,3584]{2,1,0:T(8,128)}) fusion(pred[512,3584]{1,0:T(8,128)(4,1)S(1)} %fusion.151, bf16[4608,2,12,64]{0,3,2,1:T(8,128)(2,1)} %get-tuple-element.399, s32[]{:T(128)S(6)} %select_n.118, bf16[1536,12,64]{0,2,1:T(8,128)(2,1)} %get-tuple-element.402, s32[]{:T(128)S(6)} %select_n.119), kind=kOutput, calls=%fused_computation.3.clone.1 | convolution fusion | flops 2884626432 | bytes 96231432 | tf_op jit(solution)/shard_map/while/body/eval_jaxpr/qhd,khd->hqk/dot_general | solution.py:53
  909.6 60.8 %add_convert_fusion = (bf16[768,6144]{1,0:T(8,128)(2,1)}, f32[768,6144]{1,0:T(8,128)}) fusion(f32[768,6144]{1,0:T(8,128)} %fusion.88, bf16[768,1536]{1,0:T(8,128)(2,1)S(1)} %copy-done.15, bf16[6144,1536]{1,0:T(8,128)(2,1)} %all-gather.22.cloned.1.call-done), kind=kOutput, calls=%fused_computation.57 | convolution fusion | flops 14835253248 | bytes 68419584 | tf_op jit(solution)/shard_map/dot_general | solution.py:46
  1089.3 132.9 %all-reduce.6.cloned.1.call-done = bf16[128,3072]{0,1:T(8,128)(2,1)} async-done(((bf16[128,3072]{0,1:T(8,128)(2,1)}), bf16[128,3072]{0,1:T(8,128)(2,1)}) %all-reduce.6.cloned.1.call-update) | async-done | bytes 786448 | tf_op jit(solution)/shard_map/psum | solution.py:289
  1324.0 855.6 %while.29 = (s32[]{:T(128)}, f32[4608,2,12,64]{0,3,2,1:T(8,128)}, bf16[3,512,12,64]{1,3,2,0:T(8,128)(2,1)}, s32[3]{0:T(128)S(1)}, bf16[1536,12,64]{0,2,1:T(8,128...) while((s32[]{:T(128)}, f32[4608,2,12,64]{0,3,2,1:T(8,128)}, ...), condition=%wide.region_19.20_spmd, body=%wide.region_17.19_spmd.sunk | while | flops 14442817536 | bytes 777482752 | solution.py:144
  1363.7 37.1 %fusion.163 = f32[3584,1,12,64]{0,3,2,1:T(8,128)} fusion(f32[12,512,3584]{2,1,0:T(8,128)} %fusion.161, f32[12,512]{1,0:T(8,128)S(1)} %dynamic-slice_bitcast_fusion.25, pred[512,3584]{1,0:T(8,128)(4,1)S(1)} %fusion.162, bf16[1536,12,64]{0,2,1:T(8,128)(2,1)} %get-tuple-element.450, s32[]{:T(128)S(6)} %select_n.124), kind=kOutput, calls=%fused_computation.30.clone.1 | convolution fusion | flops 2906652672 | bytes 101736448 | tf_op jit(solution)/shard_map/while/body/eval_jaxpr/hqk,qhd->khd/dot_general | solution.py:131
  1400.8 65.5 %multiply_reduce_fusion.9 = (f32[12,512]{1,0:T(8,128)S(1)}, f32[12,512,3584]{2,1,0:T(8,128)}) fusion(f32[12,512,3584]{2,1,0:T(8,128)} %fusion.161, f32[12,512]{1,0:T(8,128)S(1)} %dynamic-slice_bitcast_fusion.25, pred[512,3584]{1,0:T(8,128)(4,1)S(1)} %fusion.162, bf16[4608,2,12,64]{0,3,2,1:T(8,128)(2,1)} %get-tuple-element.448, s32[]{:T(128)S(6)} %select_n.123, ...), kind=kOutput, calls=%fused_computation.22.clone.3 | convolution fusion | flops 2928666624 | bytes 184336400 | tf_op jit(solution)/shard_map/while/body/eval_jaxpr/qhd,khd->hqk/dot_general | solution.py:116
  1466.3 74.8 %multiply_convert_fusion.5 = bf16[12,512,3584]{2,1,0:T(8,128)(2,1)} fusion(f32[12,512,3584]{2,1,0:T(8,128)} %get-tuple-element.365, f32[12,512,3584]{2,1,0:T(8,128)} %fusion.161, f32[12,512]{1,0:T(8,128)S(1)} %get-tuple-element.366, f32[12,512]{1,0:T(8,128)S(1)} %dynamic-slice_bitcast_fusion.25, pred[512,3584]{1,0:T(8,128)(4,1)S(1)} %fusion.162), kind=kLoop, calls=%fused_computation.21.clone.1 | loop fusion | flops 132120576 | bytes 222085120 | tf_op jit(solution)/shard_map/while/body/eval_jaxpr/convert_element_type | solution.py:120
  1654.4 36.9 %fusion.163 = f32[3584,1,12,64]{0,3,2,1:T(8,128)} fusion(f32[12,512,3584]{2,1,0:T(8,128)} %fusion.161, f32[12,512]{1,0:T(8,128)S(1)} %dynamic-slice_bitcast_fusion.25, pred[512,3584]{1,0:T(8,128)(4,1)S(1)} %fusion.162, bf16[1536,12,64]{0,2,1:T(8,128)(2,1)} %get-tuple-element.450, s32[]{:T(128)S(6)} %select_n.124), kind=kOutput, calls=%fused_computation.30.clone.1 | convolution fusion | flops 2906652672 | bytes 101736448 | tf_op jit(solution)/shard_map/while/body/eval_jaxpr/hqk,qhd->khd/dot_general | solution.py:131
  1691.4 65.1 %multiply_reduce_fusion.9 = (f32[12,512]{1,0:T(8,128)S(1)}, f32[12,512,3584]{2,1,0:T(8,128)}) fusion(f32[12,512,3584]{2,1,0:T(8,128)} %fusion.161, f32[12,512]{1,0:T(8,128)S(1)} %dynamic-slice_bitcast_fusion.25, pred[512,3584]{1,0:T(8,128)(4,1)S(1)} %fusion.162, bf16[4608,2,12,64]{0,3,2,1:T(8,128)(2,1)} %get-tuple-element.448, s32[]{:T(128)S(6)} %select_n.123, ...), kind=kOutput, calls=%fused_computation.22.clone.3 | convolution fusion | flops 2928666624 | bytes 184336400 | tf_op jit(solution)/shard_map/while/body/eval_jaxpr/qhd,khd->hqk/dot_general | solution.py:116
  1756.5 78.8 %multiply_convert_fusion.5 = bf16[12,512,3584]{2,1,0:T(8,128)(2,1)} fusion(f32[12,512,3584]{2,1,0:T(8,128)} %get-tuple-element.365, f32[12,512,3584]{2,1,0:T(8,128)} %fusion.161, f32[12,512]{1,0:T(8,128)S(1)} %get-tuple-element.366, f32[12,512]{1,0:T(8,128)S(1)} %dynamic-slice_bitcast_fusion.25, pred[512,3584]{1,0:T(8,128)(4,1)S(1)} %fusion.162), kind=kLoop, calls=%fused_computation.21.clone.1 | loop fusion | flops 132120576 | bytes 222085120 | tf_op jit(solution)/shard_map/while/body/eval_jaxpr/convert_element_type | solution.py:120
  1942.6 36.5 %fusion.163 = f32[3584,1,12,64]{0,3,2,1:T(8,128)} fusion(f32[12,512,3584]{2,1,0:T(8,128)} %fusion.161, f32[12,512]{1,0:T(8,128)S(1)} %dynamic-slice_bitcast_fusion.25, pred[512,3584]{1,0:T(8,128)(4,1)S(1)} %fusion.162, bf16[1536,12,64]{0,2,1:T(8,128)(2,1)} %get-tuple-element.450, s32[]{:T(128)S(6)} %select_n.124), kind=kOutput, calls=%fused_computation.30.clone.1 | convolution fusion | flops 2906652672 | bytes 101736448 | tf_op jit(solution)/shard_map/while/body/eval_jaxpr/hqk,qhd->khd/dot_general | solution.py:131
  1979.0 64.8 %multiply_reduce_fusion.9 = (f32[12,512]{1,0:T(8,128)S(1)}, f32[12,512,3584]{2,1,0:T(8,128)}) fusion(f32[12,512,3584]{2,1,0:T(8,128)} %fusion.161, f32[12,512]{1,0:T(8,128)S(1)} %dynamic-slice_bitcast_fusion.25, pred[512,3584]{1,0:T(8,128)(4,1)S(1)} %fusion.162, bf16[4608,2,12,64]{0,3,2,1:T(8,128)(2,1)} %get-tuple-element.448, s32[]{:T(128)S(6)} %select_n.123, ...), kind=kOutput, calls=%fused_computation.22.clone.3 | convolution fusion | flops 2928666624 | bytes 184336400 | tf_op jit(solution)/shard_map/while/body/eval_jaxpr/qhd,khd->hqk/dot_general | solution.py:116
  2043.8 69.7 %multiply_convert_fusion.5 = bf16[12,512,3584]{2,1,0:T(8,128)(2,1)} fusion(f32[12,512,3584]{2,1,0:T(8,128)} %get-tuple-element.365, f32[12,512,3584]{2,1,0:T(8,128)} %fusion.161, f32[12,512]{1,0:T(8,128)S(1)} %get-tuple-element.366, f32[12,512]{1,0:T(8,128)S(1)} %dynamic-slice_bitcast_fusion.25, pred[512,3584]{1,0:T(8,128)(4,1)S(1)} %fusion.162), kind=kLoop, calls=%fused_computation.21.clone.1 | loop fusion | flops 132120576 | bytes 222085120 | tf_op jit(solution)/shard_map/while/body/eval_jaxpr/convert_element_type | solution.py:120
  2214.2 85.1 %collective-permute-done.2 = bf16[1536,2,12,64]{0,3,2,1:T(8,128)(2,1)} collective-permute-done((bf16[1536,2,12,64]{0,3,2,1:T(8,128)(2,1)}, bf16[1536,2,12,64]{0,3,2,1:T(8,128)(2,1)}, u32[]{:S(2)}, u32[]{:S(2)}) %collective-permute-start.2) | collective-permute-done | bytes 4718624 | tf_op jit(solution)/shard_map/ppermute | solution.py:21
  2330.8 59.7 %all_to_all.66 = bf16[1536,3,768]{2,1,0:T(4,128)(2,1)S(1)} all-to-all(bf16[1536,3,768]{2,1,0:T(4,128)(2,1)} %copy.144), channel_id=1, replica_groups=mesh['fsdp'=16,'seq'=2] {'seq'}, dimensions={0} | all-to-all | bytes 14155776 | tf_op jit(solution)/shard_map/all_to_all | solution.py:339
  2445.2 232.4 %reduce-scatter.14.cloned.1.call-done = bf16[96,4608]{1,0:T(8,128)(2,1)} async-done(((bf16[1536,4608]{1,0:T(8,128)(2,1)}), bf16[96,4608]{1,0:T(8,128)(2,1)}) %reduce-scatter.14.cloned.1.call-update) | async-done | bytes 884752 | tf_op jit(solution)/shard_map/reduce_scatter | solution.py:349
  2737.4 57.7 %reduce-scatter.30.cloned.1.call-done = bf16[96,3]{1,0:T(8,128)(2,1)} async-done(((bf16[1536,3]{1,0:T(8,128)(2,1)}), bf16[96,3]{1,0:T(8,128)(2,1)}) %reduce-scatter.30.cloned.1.call-update) | async-done | bytes 592
  2802.0 116.7 %all-reduce.8.cloned.1.call-done = (bf16[96,4608]{1,0:T(8,128)(2,1)}, bf16[96,1536]{1,0:T(8,128)(2,1)}, bf16[96,1536]{1,0:T(8,128)(2,1)}, bf16[96,3072]{1,0:T(8,...) async-done(((bf16[96,4608]{1,0:T(8,128)(2,1)}, bf16[96,1536]{1,0:T(8,128)(2,1)}, bf16[96,1536]{1,0:T(8,128)(2,1)}, ...) | async-done | bytes 4718608 | tf_op jit(solution)/shard_map/psum | solution.py:363
  (401 shorter events, 1209.8 us)
Async XLA Ops:
  7.2 116.6 %all-gather.10.cloned.1.call-start = ((), (), s32[]{:S(2)}) async-start(), calls=%async_computation.13 | async-start | bytes 15040512 | tf_op jit(solution)/shard_map/all_gather | solution.py:175
  7.9 818.9 %all-gather.14.cloned.1.call-start = ((), (), s32[]{:S(2)}) async-start(), calls=%async_computation.15 | async-start | bytes 10027008 | tf_op jit(solution)/shard_map/all_gather | solution.py:211
  8.7 825.8 %all-gather.12.cloned.1.call-start = ((), (), s32[]{:S(2)}) async-start(), calls=%async_computation.14 | async-start | bytes 5013504 | tf_op jit(solution)/shard_map/all_gather | solution.py:176
  9.4 843.1 %all-gather.16.cloned.1.call-start = ((), (), s32[]{:S(2)}) async-start(), calls=%async_computation.16 | async-start | bytes 5013504 | tf_op jit(solution)/shard_map/all_gather | solution.py:210
  10.0 865.0 %all-gather.18.cloned.1.call-start = ((), (), s32[]{:S(2)}) async-start(), calls=%async_computation.17 | async-start | bytes 5013504 | tf_op jit(solution)/shard_map/all_gather | solution.py:212
  10.6 876.7 %all-gather.20.cloned.1.call-start = ((), (), s32[]{:S(2)}) async-start(), calls=%async_computation.18 | async-start | bytes 20054016 | tf_op jit(solution)/shard_map/all_gather | solution.py:213
  11.2 898.4 %all-gather.22.cloned.1.call-start = ((), (), s32[]{:S(2)}) async-start(), calls=%async_computation.19 | async-start | bytes 20054016 | tf_op jit(solution)/shard_map/all_gather | solution.py:214
  320.2 11.6 collective-permute-start.1
  323.7 159.8 %collective-permute-start = (bf16[1536,2,12,64]{0,3,2,1:T(8,128)(2,1)}, bf16[1536,2,12,64]{0,3,2,1:T(8,128)(2,1)}, u32[]{:S(2)}, u32[]{:S(2)}) collective-permute-start(bf16[1536,2,12,64]{0,3,2,1:T(8,128)(2,1)} %slice.124), channel_id=1, source_target_pairs={{0,4},{2,6},{4,8},{6,10},{8,12},{10,14},{12,16},{14,18},{16,20},{1... | collective-permute-start | bytes 14155784 | tf_op jit(solution)/shard_map/ppermute | solution.py:21
  821.0 21.4 all-to-all-start.1
  825.9 396.3 %all-reduce.6.cloned.1.call-start = ((), (), s32[]{:S(2)}) async-start(), calls=%async_computation.20 | async-start | bytes 1572864 | tf_op jit(solution)/shard_map/psum | solution.py:289
  1042.5 1402.6 %reduce-scatter.22.cloned.1.call-start = ((), (), s32[]{:S(2)}) async-start(), calls=%async_computation.25 | async-start | bytes 5013504 | tf_op jit(solution)/shard_map/reduce_scatter | solution.py:306
  1050.9 1394.2 %reduce-scatter.18.cloned.1.call-start = ((), (), s32[]{:S(2)}) async-start(), calls=%async_computation.23 | async-start | bytes 5013504 | tf_op jit(solution)/shard_map/reduce_scatter | solution.py:300
  1062.9 1382.3 %reduce-scatter.16.cloned.1.call-start = ((), (), s32[]{:S(2)}) async-start(), calls=%async_computation.22 | async-start | bytes 5013504 | tf_op jit(solution)/shard_map/reduce_scatter | solution.py:352
  1089.2 1355.9 %reduce-scatter.20.cloned.1.call-start = ((), (), s32[]{:S(2)}) async-start(), calls=%async_computation.24 | async-start | bytes 10027008 | tf_op jit(solution)/shard_map/reduce_scatter | solution.py:303
  1228.5 1216.7 %reduce-scatter.24.cloned.1.call-start = ((), (), s32[]{:S(2)}) async-start(), calls=%async_computation.26 | async-start | bytes 20054016 | tf_op jit(solution)/shard_map/reduce_scatter | solution.py:309
  1261.0 39.3 %all-to-all-start.2 = ((bf16[768,2,768]{2,0,1:T(8,128)(2,1)}), bf16[768,2,768]{2,0,1:T(8,128)(2,1)}, u32[]{:S(2)}, u32[]{:S(2)}) async-start(bf16[768,2,768]{2,0,1:T(8,128)(2,1)} %bitcast.209), calls=%async_computation.2 | async-start | bytes 4718592 | tf_op jit(solution)/shard_map/all_to_all | solution.py:323
  1265.9 1179.3 %reduce-scatter.26.cloned.1.call-start = ((), (), s32[]{:S(2)}) async-start(), calls=%async_computation.27 | async-start | bytes 20054016 | tf_op jit(solution)/shard_map/reduce_scatter | solution.py:312
  1300.3 1377.4 %reduce-scatter.14.cloned.1.call-start = ((), (), s32[]{:S(2)}) async-start(), calls=%async_computation.21 | async-start | bytes 15040512 | tf_op jit(solution)/shard_map/reduce_scatter | solution.py:349
  2203.1 96.2 %collective-permute-start.2 = (bf16[1536,2,12,64]{0,3,2,1:T(8,128)(2,1)}, bf16[1536,2,12,64]{0,3,2,1:T(8,128)(2,1)}, u32[]{:S(2)}, u32[]{:S(2)}) collective-permute-start(bf16[1536,2,12,64]{0,3,2,1:T(8,128)(2,1)} %get-tuple-element.233), channel_id=1, source_target_pairs={{4,0},{6,2},{8,4},{10,6},{12,8},{14,10},{16,12},{18,14},{20,16},{2... | collective-permute-start | bytes 14155784 | tf_op jit(solution)/shard_map/ppermute | solution.py:21
  2204.4 94.9 %collective-permute-start.3 = (bf16[1536,2,12,64]{0,3,2,1:T(8,128)(2,1)}, bf16[1536,2,12,64]{0,3,2,1:T(8,128)(2,1)}, u32[]{:S(2)}, u32[]{:S(2)}) collective-permute-start(bf16[1536,2,12,64]{0,3,2,1:T(8,128)(2,1)} %get-tuple-element.234), channel_id=1, source_target_pairs={{2,0},{4,2},{6,4},{8,6},{10,8},{12,10},{14,12},{16,14},{18,16},{20... | collective-permute-start | bytes 14155784 | tf_op jit(solution)/shard_map/ppermute | solution.py:21
  2422.8 313.8 %reduce-scatter.28.cloned.1.call-start = ((), (), s32[]{:S(2)}) async-start(), calls=%async_computation.28 | async-start | bytes 417792
  2443.9 351.2 %reduce-scatter.30.cloned.1.call-start = ((), (), s32[]{:S(2)}) async-start(), calls=%async_computation.29 | async-start | bytes 417792
  2445.0 473.7 %all-reduce.8.cloned.1.call-start = ((), (), s32[]{:S(2)}) async-start(), calls=%async_computation.30 | async-start | bytes 9437184 | tf_op jit(solution)/shard_map/psum | solution.py:363
  (84 other events, 2368.5 us)
Sparse Core Ops, SparseCore 0:
  10.3 113.4 all-gather.9
  126.1 79.6 all-gather.13
  208.0 51.3 all-gather.11
  261.6 51.7 all-gather.15
  315.5 69.9 all-gather.17
  387.0 165.0 all-gather.19
  553.7 115.1 all-gather.21
  1042.6 179.5 all-reduce.5
  1226.6 75.5 reduce-scatter.21
  1305.8 74.5 reduce-scatter.17
  1384.8 74.5 reduce-scatter.15
  1463.4 110.4 reduce-scatter.19
  1578.5 194.6 reduce-scatter.23
  1777.7 193.8 reduce-scatter.25
  2422.9 254.6 reduce-scatter.13
  2681.9 54.6 reduce-scatter.27
  2740.5 54.5 reduce-scatter.29
  2798.3 120.4 all-reduce.7
where the time goes:
time: 2950 us; the launch traced here: 2940 us
  matrix products  1080 us (37%)
  waiting for transfers between devices  884 us (30%)
  other arithmetic  507 us (17%)
  blocking collectives  214 us (7%)
  local copies, waits for them, and re-layouts  210 us (7%)
    ppermute x4, waiting for transfers between devices, passed_along(): lax.ppermute(value, axis, [(source, source + steps) for source in range(i...  237 us
    reduce_scatter x1, waiting for transfers between devices, shards(): lax.psum_scatter(grad_wqkv.astype(jnp.bfloat16), 'fsdp', scatter_dimensio...  232 us
    convert_element_type x3, other arithmetic, block(): grad_scores = (shares * (grad_shares - inner_sum)).astype(jnp.bfloat16)  223 us
    dot_general x7, matrix products, masked_scores(): jnp.einsum('qhd,khd->hqk', queries, keys, preferred_element_type=jnp.floa...  209 us
    dot_general x3, matrix products, block(): jnp.einsum('qhd,khd->hqk', grad_block, window[:, 1], preferred_element_ty...  195 us
    psum x1, waiting for transfers between devices, shards(): grad_text_kv = lax.psum(grad_text_kv.astype(jnp.bfloat16), 'seq')  133 us
    dot_general x7, matrix products, contract_cols(): lax.dot_general(left_side, right_side, (((1,), (1,)), ((), ())), preferre...  128 us
    psum x1, waiting for transfers between devices, shards(): lax.psum(front_sums[0].astype(jnp.bfloat16), 'seq').astype(jnp.float32)  117 us
  transfers between devices with their start and end apart: 24, of which 9 were waited for; matrix products, arithmetic and copies ran while one was open for 56% of the time, Pallas kernels for 0%

commit v1 on v0

v1 whole, which is shorter than its diff:
```python
import functools

import jax
import jax.numpy as jnp
from jax import lax
from jax.experimental import pallas as pl
from jax.experimental.pallas import tpu as pltpu
from jax.sharding import PartitionSpec as P

HEADS = 24
HEAD = 64
PAIR = 2 * HEAD
TXT = 64
SPAN = 1536
EPS = 1e-05
NEG = -1e30
SCALE = HEAD**-0.5
VMEM_BYTES = 48 * 2**20


def matmul(left_side, right_side):
    return jnp.dot(left_side, right_side, preferred_element_type=jnp.float32)


def contract_rows(left_side, right_side):
    return lax.dot_general(
        left_side, right_side, (((0,), (0,)), ((), ())), preferred_element_type=jnp.float32
    )


def contract_cols(left_side, right_side):
    return lax.dot_general(
        left_side, right_side, (((1,), (1,)), ((), ())), preferred_element_type=jnp.float32
    )


def block_bounds(starts, reach, tq, tk):
    rows = starts.shape[0]
    first = starts[::tq]
    last = starts[tq - 1 :: tq]
    row0 = reach + jnp.arange(rows // tq, dtype=jnp.int32) * tq
    low = first // tk
    high = (row0 + tq - 1) // tk + 1
    free_low = jnp.minimum(jnp.maximum((last + tk - 1) // tk, low), high)
    free_high = jnp.clip((row0 + 1) // tk, free_low, high)
    return jnp.stack([low, free_low, free_high, high], axis=1)


def attend_kernel(bounds, q_ref, kp_ref, vp_ref, ko_ref, vo_ref, start_ref, o_ref, lse_ref, k_all, v_first, v_second, *, reach, tq, tk):
    i = pl.program_id(1)
    lane = lax.broadcasted_iota(jnp.int32, (1, PAIR), 1)
    lower = lane < HEAD

    @pl.when(i == 0)
    def _():
        one = jnp.ones((1, 1), jnp.bfloat16)
        k_all[:reach] = kp_ref[...]
        k_all[reach:] = ko_ref[...]
        v_first[:reach] = jnp.where(lower, vp_ref[...], one)
        v_first[reach:] = jnp.where(lower, vo_ref[...], one)
        v_second[:reach] = jnp.where(lower, one, vp_ref[...])
        v_second[reach:] = jnp.where(lower, one, vo_ref[...])

    scaled = q_ref[...] * jnp.bfloat16(SCALE)
    zero = jnp.zeros((1, 1), jnp.bfloat16)
    halves = (jnp.where(lower, scaled, zero), jnp.where(lower, zero, scaled))
    values = (v_first, v_second)
    reps = tk // PAIR

    def wide(x):
        return jnp.concatenate([x] * reps, axis=1)

    def step(masked, j, carried):
        rows = pl.ds(pl.multiple_of(j * tk, tk), tk)
        keys = k_all[rows, :]
        if masked:
            at = j * tk + lax.broadcasted_iota(jnp.int32, (tq, tk), 1)
            row = reach + i * tq + lax.broadcasted_iota(jnp.int32, (tq, tk), 0)
            allowed = (at >= wide(start_ref[...])) & (at <= row)
        out = []
        scores = []
        for half in halves:
            s = lax.dot_general(half, keys, (((1,), (1,)), ((), ())), preferred_element_type=jnp.float32)
            if masked:
                s = jnp.where(allowed, s, NEG)
            scores.append(s)
        for s, value, (top, total) in zip(scores, values, carried):
            new_top = jnp.maximum(top, jnp.max(s, axis=1, keepdims=True))
            weights = jnp.exp(s - wide(new_top)).astype(jnp.bfloat16)
            keep = jnp.exp(top - new_top)
            total = total * keep + jnp.dot(weights, value[rows, :], preferred_element_type=jnp.float32)
            out.append((new_top, total))
        return tuple(out)

    one_state = (jnp.full((tq, PAIR), NEG, jnp.float32), jnp.zeros((tq, PAIR), jnp.float32))
    state = (one_state, one_state)
    low, free_low, free_high, high = (bounds[i, n] for n in range(4))
    state = lax.fori_loop(low, free_low, functools.partial(step, True), state)
    state = lax.fori_loop(free_low, free_high, functools.partial(step, False), state)
    state = lax.fori_loop(free_high, high, functools.partial(step, True), state)
    outs, logs = [], []
    for top, total in state:
        count = pltpu.roll(total, HEAD, 1)
        outs.append(total / count)
        logs.append(top + jnp.log(count))
    o_ref[...] = jnp.where(lower, outs[0], outs[1]).astype(o_ref.dtype)
    lse_ref[...] = jnp.where(lower, logs[0], logs[1])


def self_attend(q, kv_before, kv_own, starts, *, tq=384, tk=384):
    rows, width = q.shape
    reach = kv_before.shape[0]
    pairs = width // PAIR
    bounds = block_bounds(starts, reach, tq, tk)
    starts_wide = jnp.broadcast_to(starts[:, None], (rows, PAIR))
    spec = pltpu.PrefetchScalarGridSpec(
        num_scalar_prefetch=1,
        grid=(pairs, rows // tq),
        in_specs=[
            pl.BlockSpec((tq, PAIR), lambda p, i, b: (i, p)),
            pl.BlockSpec((reach, PAIR), lambda p, i, b: (0, p)),
            pl.BlockSpec((reach, PAIR), lambda p, i, b: (0, pairs + p)),
            pl.BlockSpec((rows, PAIR), lambda p, i, b: (0, p)),
            pl.BlockSpec((rows, PAIR), lambda p, i, b: (0, pairs + p)),
            pl.BlockSpec((tq, PAIR), lambda p, i, b: (i, 0)),
        ],
        out_specs=[
            pl.BlockSpec((tq, PAIR), lambda p, i, b: (i, p)),
            pl.BlockSpec((tq, PAIR), lambda p, i, b: (i, p)),
        ],
        scratch_shapes=[pltpu.VMEM((reach + rows, PAIR), jnp.bfloat16)] * 3,
    )
    return pl.pallas_call(
        functools.partial(attend_kernel, reach=reach, tq=tq, tk=tk),
        grid_spec=spec,
        out_shape=[
            jax.ShapeDtypeStruct((rows, width), jnp.bfloat16),
            jax.ShapeDtypeStruct((rows, width), jnp.float32),
        ],
        compiler_params=pltpu.CompilerParams(
            dimension_semantics=("arbitrary", "arbitrary"), vmem_limit_bytes=VMEM_BYTES
        ),
        cost_estimate=pl.CostEstimate(flops=16 * rows * rows * width, bytes_accessed=12 * rows * width, transcendentals=rows * rows * width // HEAD),
        name="self_attend",
    )(bounds, q, kv_before, kv_before, kv_own, kv_own, starts_wide)


def attend_back_kernel(bounds, q_ref, do_ref, o_ref, lse_ref, kp_ref, vp_ref, ko_ref, vo_ref, start_ref, dq_ref, dkp_ref, dvp_ref, dko_ref, dvo_ref, k_all, v_all, dk_sum, dv_sum, *, reach, tq, tk):
    i = pl.program_id(1)
    lane = lax.broadcasted_iota(jnp.int32, (1, PAIR), 1)
    lower = lane < HEAD

    @pl.when(i == 0)
    def _():
        k_all[:reach] = kp_ref[...]
        k_all[reach:] = ko_ref[...]
        v_all[:reach] = vp_ref[...]
        v_all[reach:] = vo_ref[...]
        dk_sum[...] = jnp.zeros_like(dk_sum)
        dv_sum[...] = jnp.zeros_like(dv_sum)

    zero = jnp.zeros((1, 1), jnp.bfloat16)
    scaled = q_ref[...] * jnp.bfloat16(SCALE)
    grad = do_ref[...]
    q_halves = (jnp.where(lower, scaled, zero), jnp.where(lower, zero, scaled))
    do_halves = (jnp.where(lower, grad, zero), jnp.where(lower, zero, grad))
    product = (grad.astype(jnp.float32) * o_ref[...].astype(jnp.float32)).T
    inner = (
        jnp.sum(product[:HEAD], axis=0, keepdims=True),
        jnp.sum(product[HEAD:], axis=0, keepdims=True),
    )
    lse_t = lse_ref[...].T
    lse = (lse_t[:1], lse_t[HEAD : HEAD + 1])
    starts = start_ref[0]

    def step(masked, j, dq):
        rows = pl.ds(pl.multiple_of(j * tk, tk), tk)
        keys = k_all[rows, :]
        values = v_all[rows, :]
        if masked:
            at = j * tk + lax.broadcasted_iota(jnp.int32, (tk, tq), 0)
            row = reach + i * tq + lax.broadcasted_iota(jnp.int32, (tk, tq), 1)
            allowed = (at >= starts) & (at <= row)
        dks, dvs = [], []
        for h in range(2):
            s = lax.dot_general(keys, q_halves[h], (((1,), (1,)), ((), ())), preferred_element_type=jnp.float32)
            d = lax.dot_general(values, do_halves[h], (((1,), (1,)), ((), ())), preferred_element_type=jnp.float32)
            if masked:
                s = jnp.where(allowed, s, NEG)
            p = jnp.exp(s - lse[h])
            ds = (p * (d - inner[h])).astype(jnp.bfloat16)
            dvs.append(jnp.dot(p.astype(jnp.bfloat16), do_halves[h], preferred_element_type=jnp.float32))
            dks.append(jnp.dot(ds, q_halves[h], preferred_element_type=jnp.float32))
            k_half = jnp.where(lower, keys, zero) if h == 0 else jnp.where(lower, zero, keys)
            dq = dq + lax.dot_general(ds, k_half, (((0,), (0,)), ((), ())), preferred_element_type=jnp.float32)
        dv_sum[rows, :] += dvs[0] + dvs[1]
        dk_sum[rows, :] += dks[0] + dks[1]
        return dq

    low, free_low, free_high, high = (bounds[i, n] for n in range(4))
    dq = jnp.zeros((tq, PAIR), jnp.float32)
    dq = lax.fori_loop(low, free_low, functools.partial(step, True), dq)
    dq = lax.fori_loop(free_low, free_high, functools.partial(step, False), dq)
    dq = lax.fori_loop(free_high, high, functools.partial(step, True), dq)
    dq_ref[...] = (dq * SCALE).astype(dq_ref.dtype)

    @pl.when(i == pl.num_programs(1) - 1)
    def _():
        dkp_ref[...] = dk_sum[:reach].astype(dkp_ref.dtype)
        dvp_ref[...] = dv_sum[:reach].astype(dvp_ref.dtype)
        dko_ref[...] = dk_sum[reach:].astype(dko_ref.dtype)
        dvo_ref[...] = dv_sum[reach:].astype(dvo_ref.dtype)


def self_attend_back(q, do, o, lse, kv_before, kv_own, starts, *, tq=384, tk=384):
    rows, width = q.shape
    reach = kv_before.shape[0]
    pairs = width // PAIR
    bounds = block_bounds(starts, reach, tq, tk)
    starts_row = starts.reshape(rows // tq, 1, tq)
    spec = pltpu.PrefetchScalarGridSpec(
        num_scalar_prefetch=1,
        grid=(pairs, rows // tq),
        in_specs=[
            pl.BlockSpec((tq, PAIR), lambda p, i, b: (i, p)),
            pl.BlockSpec((tq, PAIR), lambda p, i, b: (i, p)),
            pl.BlockSpec((tq, PAIR), lambda p, i, b: (i, p)),
            pl.BlockSpec((tq, PAIR), lambda p, i, b: (i, p)),
            pl.BlockSpec((reach, PAIR), lambda p, i, b: (0, p)),
            pl.BlockSpec((reach, PAIR), lambda p, i, b: (0, pairs + p)),
            pl.BlockSpec((rows, PAIR), lambda p, i, b: (0, p)),
            pl.BlockSpec((rows, PAIR), lambda p, i, b: (0, pairs + p)),
            pl.BlockSpec((1, 1, tq), lambda p, i, b: (i, 0, 0)),
        ],
        out_specs=[
            pl.BlockSpec((tq, PAIR), lambda p, i, b: (i, p)),
            pl.BlockSpec((reach, PAIR), lambda p, i, b: (0, p)),
            pl.BlockSpec((reach, PAIR), lambda p, i, b: (0, p)),
            pl.BlockSpec((rows, PAIR), lambda p, i, b: (0, p)),
            pl.BlockSpec((rows, PAIR), lambda p, i, b: (0, p)),
        ],
        scratch_shapes=[pltpu.VMEM((reach + rows, PAIR), jnp.bfloat16)] * 2
        + [pltpu.VMEM((reach + rows, PAIR), jnp.float32)] * 2,
    )
    return pl.pallas_call(
        functools.partial(attend_back_kernel, reach=reach, tq=tq, tk=tk),
        grid_spec=spec,
        out_shape=[
            jax.ShapeDtypeStruct((rows, width), jnp.bfloat16),
            jax.ShapeDtypeStruct((reach, width), jnp.bfloat16),
            jax.ShapeDtypeStruct((reach, width), jnp.bfloat16),
            jax.ShapeDtypeStruct((rows, width), jnp.bfloat16),
            jax.ShapeDtypeStruct((rows, width), jnp.bfloat16),
        ],
        compiler_params=pltpu.CompilerParams(
            dimension_semantics=("arbitrary", "arbitrary"), vmem_limit_bytes=VMEM_BYTES
        ),
        cost_estimate=pl.CostEstimate(flops=40 * rows * rows * width, bytes_accessed=20 * rows * width, transcendentals=rows * rows * width // HEAD),
        name="self_attend_back",
    )(bounds, q, do, o, lse, kv_before, kv_before, kv_own, kv_own, starts_row)


def cross_kernel(q_ref, k_ref, v_ref, slot_ref, o_ref):
    lower = lax.broadcasted_iota(jnp.int32, (1, PAIR), 1) < HEAD
    zero = jnp.zeros((1, 1), jnp.bfloat16)
    scaled = q_ref[...] * jnp.bfloat16(SCALE)
    tokens, texts = q_ref.shape[0], k_ref.shape[0]
    allowed = slot_ref[:, :1] == lax.broadcasted_iota(jnp.int32, (tokens, texts), 1) // TXT
    results = []
    for h in range(2):
        half = jnp.where(lower, scaled, zero) if h == 0 else jnp.where(lower, zero, scaled)
        scores = jnp.where(allowed, contract_cols(half, k_ref[...]), NEG)
        weights = jnp.exp(scores - jnp.max(scores, axis=1, keepdims=True))
        shares = weights / jnp.sum(weights, axis=1, keepdims=True)
        results.append(matmul(shares.astype(jnp.bfloat16), v_ref[...]))
    o_ref[...] = jnp.where(lower, results[0], results[1]).astype(o_ref.dtype)


def cross_attend(q, k, v, slots_wide):
    tokens, width = q.shape
    texts = k.shape[0]
    column = lambda p: (0, p)
    return pl.pallas_call(
        cross_kernel,
        grid=(width // PAIR,),
        in_specs=[
            pl.BlockSpec((tokens, PAIR), column),
            pl.BlockSpec((texts, PAIR), column),
            pl.BlockSpec((texts, PAIR), column),
            pl.BlockSpec((tokens, PAIR), lambda p: (0, 0)),
        ],
        out_specs=pl.BlockSpec((tokens, PAIR), column),
        out_shape=jax.ShapeDtypeStruct(q.shape, jnp.bfloat16),
        compiler_params=pltpu.CompilerParams(vmem_limit_bytes=VMEM_BYTES),
        cost_estimate=pl.CostEstimate(
            flops=8 * tokens * texts * width,
            bytes_accessed=4 * tokens * width,
            transcendentals=tokens * texts * width // HEAD,
        ),
        name="cross_attend",
    )(q, k, v, slots_wide)


def cross_back_kernel(q_ref, g_ref, k_ref, v_ref, slot_ref, dq_ref, dk_ref, dv_ref):
    lower = lax.broadcasted_iota(jnp.int32, (1, PAIR), 1) < HEAD
    zero = jnp.zeros((1, 1), jnp.bfloat16)
    scaled = q_ref[...] * jnp.bfloat16(SCALE)
    grad = g_ref[...]
    keys = k_ref[...]
    tokens, texts = q_ref.shape[0], k_ref.shape[0]
    allowed = slot_ref[:, :1] == lax.broadcasted_iota(jnp.int32, (tokens, texts), 1) // TXT
    dqs, dks, dvs = [], [], []
    for h in range(2):
        q_half = jnp.where(lower, scaled, zero) if h == 0 else jnp.where(lower, zero, scaled)
        g_half = jnp.where(lower, grad, zero) if h == 0 else jnp.where(lower, zero, grad)
        scores = jnp.where(allowed, contract_cols(q_half, keys), NEG)
        weights = jnp.exp(scores - jnp.max(scores, axis=1, keepdims=True))
        shares = weights / jnp.sum(weights, axis=1, keepdims=True)
        grad_shares = contract_cols(g_half, v_ref[...])
        inner = jnp.sum(shares * grad_shares, axis=1, keepdims=True)
        grad_scores = (shares * (grad_shares - inner)).astype(jnp.bfloat16)
        dqs.append(matmul(grad_scores, keys))
        dks.append(contract_rows(grad_scores, q_half))
        dvs.append(contract_rows(shares.astype(jnp.bfloat16), g_half))
    dq_ref[...] = (jnp.where(lower, dqs[0], dqs[1]) * SCALE).astype(dq_ref.dtype)
    dk_ref[...] = dks[0] + dks[1]
    dv_ref[...] = dvs[0] + dvs[1]


def cross_attend_back(q, grad, k, v, slots_wide):
    tokens, width = q.shape
    texts = k.shape[0]
    column = lambda p: (0, p)
    return pl.pallas_call(
        cross_back_kernel,
        grid=(width // PAIR,),
        in_specs=[
            pl.BlockSpec((tokens, PAIR), column),
            pl.BlockSpec((tokens, PAIR), column),
            pl.BlockSpec((texts, PAIR), column),
            pl.BlockSpec((texts, PAIR), column),
            pl.BlockSpec((tokens, PAIR), lambda p: (0, 0)),
        ],
        out_specs=[
            pl.BlockSpec((tokens, PAIR), column),
            pl.BlockSpec((texts, PAIR), column),
            pl.BlockSpec((texts, PAIR), column),
        ],
        out_shape=[
            jax.ShapeDtypeStruct(q.shape, jnp.bfloat16),
            jax.ShapeDtypeStruct((texts, width), jnp.float32),
            jax.ShapeDtypeStruct((texts, width), jnp.float32),
        ],
        compiler_params=pltpu.CompilerParams(vmem_limit_bytes=VMEM_BYTES),
        cost_estimate=pl.CostEstimate(
            flops=20 * tokens * texts * width,
            bytes_accessed=6 * tokens * width,
            transcendentals=tokens * texts * width // HEAD,
        ),
        name="cross_attend_back",
    )(q, grad, k, v, slots_wide)


def swap(value, axis, bit):
    count = lax.axis_size(axis)
    return lax.ppermute(value, axis, [(i, i ^ bit) for i in range(count)])


def passed_along(value, axis, steps):
    count = lax.axis_size(axis)
    initial, last = (max(0, -steps), min(count, count - steps))
    return lax.ppermute(value, axis, [(source, source + steps) for source in range(initial, last)])


def in_order(mine, other, dim):
    second = lax.axis_index("seq") == 1
    return jnp.concatenate([jnp.where(second, other, mine), jnp.where(second, mine, other)], axis=dim)


def gathered(value, dim):
    if lax.axis_size("seq") == 2:
        return in_order(value, swap(value, "seq", 1), dim)
    return lax.all_gather(value, "seq", axis=dim, tiled=True)


def own_block(value, dim):
    size = value.shape[dim] // lax.axis_size("seq")
    return lax.dynamic_slice_in_dim(value, lax.axis_index("seq") * size, size, dim)


def other_block(value, dim):
    size = value.shape[dim] // 2
    return lax.dynamic_slice_in_dim(value, (1 - lax.axis_index("seq")) * size, size, dim)


def exchanged(value, split, concat):
    if lax.axis_size("seq") == 2:
        return in_order(own_block(value, split), swap(other_block(value, split), "seq", 1), concat)
    return lax.all_to_all(value, "seq", split_axis=split, concat_axis=concat, tiled=True)


def summed_block(value, dim):
    if lax.axis_size("seq") == 2:
        received = swap(other_block(value, dim).astype(jnp.bfloat16), "seq", 1)
        return own_block(value, dim) + received.astype(jnp.float32)
    return lax.psum_scatter(
        value.astype(jnp.bfloat16), "seq", scatter_dimension=dim, tiled=True
    ).astype(jnp.float32)


def paired(value):
    short = -value.shape[-1] % PAIR
    return jnp.pad(value, ((0, 0), (0, short))) if short else value


def normed(values):
    average = jnp.mean(values, axis=-1, keepdims=True)
    centred = values - average
    spread = jnp.mean(centred * centred, axis=-1, keepdims=True)
    root = lax.rsqrt(spread + EPS)
    return centred * root, root


def norm_back(grad, n, root, gain):
    a = grad * gain
    back = (a - jnp.mean(a, axis=-1, keepdims=True) - n * jnp.mean(a * n, axis=-1, keepdims=True)) * root
    return back, jnp.sum(grad * n, axis=0), jnp.sum(grad, axis=0)


def scattered(grad):
    return lax.psum_scatter(grad.astype(jnp.bfloat16), "fsdp", scatter_dimension=0, tiled=True)


def clip_starts(segments, group_index, group_rows):
    padded = jnp.concatenate([jnp.full((SPAN,), -1, jnp.int32), segments])
    spans = lax.dynamic_slice_in_dim(padded, group_index * group_rows, SPAN + group_rows)
    spans = spans.reshape(-1, SPAN)
    ahead = jnp.sum((spans == spans[:, :1]).astype(jnp.int32), axis=1)
    firsts = ahead + jnp.arange(spans.shape[0], dtype=jnp.int32) * SPAN
    late = spans[1:] != spans[1:, :1]
    return jnp.where(late, firsts[1:, None], firsts[:-1, None]).reshape(group_rows), spans[1:].reshape(group_rows)


def shards(
    tokens,
    segments,
    text,
    qkv_weight,
    out_weight,
    cross_query_weight,
    cross_kv_weight,
    cross_out_weight,
    up_weight,
    down_weight,
    norm_gain,
    norm_bias,
    cotangent,
):
    group_index = lax.axis_index("fsdp")
    seq_index = lax.axis_index("seq")
    seq_count = lax.axis_size("seq")
    tok_rows, width = tokens.shape
    group_rows = tok_rows * seq_count
    head_cols = width // seq_count
    shard_rows = qkv_weight.shape[0]
    row_block = lambda value: lax.all_gather(value, "fsdp", axis=0, tiled=True)

    norms = jnp.pad(jnp.concatenate([norm_gain, norm_bias]).T, ((0, 0), (0, PAIR - 6)))
    qkv_mine = own_block(qkv_weight.reshape(shard_rows, 3, width), 2).reshape(shard_rows, 3 * head_cols)
    first = row_block(jnp.concatenate([qkv_mine, norms], axis=1))
    w_q, w_kv, w_qkv = first[:, :head_cols], first[:, head_cols : 3 * head_cols], first[:, : 3 * head_cols]
    norm_rows = first[:, 3 * head_cols : 3 * head_cols + 6].astype(jnp.float32).T
    gains, biases = norm_rows[:3], norm_rows[3:]

    starts, seg_group = clip_starts(segments, group_index, group_rows)
    slots = own_block(seg_group, 0) - group_index * (group_rows // SPAN)
    slots_wide = jnp.broadcast_to(slots[:, None], (tok_rows, PAIR))

    inputs = tokens.astype(jnp.float32)
    n_group, _ = normed(gathered(tokens, 0).astype(jnp.float32))
    normed_one = (n_group * gains[0] + biases[0]).astype(jnp.bfloat16)
    kv_own = matmul(normed_one, w_kv).astype(jnp.bfloat16)
    kv_before = passed_along(kv_own[group_rows - SPAN :], "fsdp", 1)
    queries = matmul(normed_one, w_q).astype(jnp.bfloat16)
    if head_cols % PAIR:
        pad_kv = lambda kv: jnp.concatenate([paired(kv[:, :head_cols]), paired(kv[:, head_cols:])], axis=1)
        queries, kv_own, kv_before = paired(queries), pad_kv(kv_own), pad_kv(kv_before)
    heads_out, log_totals = self_attend(queries, kv_before, kv_own, starts)
    attended = exchanged(heads_out[:, :head_cols], 0, 1)
    full_out = row_block(out_weight)
    hidden_one = inputs + matmul(attended, full_out)

    ckv_mine = own_block(cross_kv_weight.reshape(shard_rows, 2, width), 2).reshape(shard_rows, 2 * head_cols)
    w_ckv = row_block(ckv_mine)
    text_rows = text.reshape(-1, width)
    text_count = text_rows.shape[0]
    ckv_part = matmul(text_rows, w_ckv).astype(jnp.bfloat16).reshape(text_count, 2, head_cols)
    cross_kv = gathered(ckv_part, 2)
    cross_k, cross_v = cross_kv[:, 0], cross_kv[:, 1]
    full_cq = row_block(cross_query_weight)
    n_two, root_two = normed(hidden_one)
    normed_two = (n_two * gains[1] + biases[1]).astype(jnp.bfloat16)
    cross_query = matmul(normed_two, full_cq).astype(jnp.bfloat16)
    cross_result = cross_attend(cross_query, cross_k, cross_v, slots_wide)
    full_cout = row_block(cross_out_weight)
    hidden_two = hidden_one + matmul(cross_result, full_cout)

    full_up, full_down = row_block(up_weight), row_block(down_weight)
    n_three, root_three = normed(hidden_two)
    normed_three = (n_three * gains[2] + biases[2]).astype(jnp.bfloat16)
    upward = matmul(normed_three, full_up)
    below = 0.5 * (1.0 + lax.erf(upward * (0.5**0.5)))
    active = (upward * below).astype(jnp.bfloat16)
    slope = below + upward * (jnp.exp(-0.5 * upward * upward) * 0.3989422804014327)
    layer_out = (hidden_two + matmul(active, full_down)).astype(jnp.bfloat16)

    grad_down = scattered(contract_rows(active, cotangent))
    grad_upward = (contract_cols(cotangent, full_down) * slope).astype(jnp.bfloat16)
    grad_up = scattered(contract_rows(normed_three, grad_upward))
    back_h2, gain_three, bias_three = norm_back(contract_cols(grad_upward, full_up), n_three, root_three, gains[2])
    grad_two = cotangent.astype(jnp.float32) + back_h2
    grad_two_low = grad_two.astype(jnp.bfloat16)
    grad_cout = scattered(contract_rows(cross_result, grad_two_low))
    grad_result = contract_cols(grad_two_low, full_cout).astype(jnp.bfloat16)
    grad_query_c, grad_text_k, grad_text_v = cross_attend_back(cross_query, grad_result, cross_k, cross_v, slots_wide)
    grad_cq = scattered(contract_rows(normed_two, grad_query_c))
    grad_text_kv = summed_block(jnp.stack([grad_text_k, grad_text_v], axis=1), 2)
    grad_text_kv = grad_text_kv.astype(jnp.bfloat16).reshape(text_count, 2 * head_cols)
    grad_text = contract_cols(grad_text_kv, w_ckv)
    grad_ckv = scattered(contract_rows(text_rows, grad_text_kv))
    back_h1, gain_two, bias_two = norm_back(contract_cols(grad_query_c, full_cq), n_two, root_two, gains[1])
    grad_one = grad_two + back_h1

    grad_one_low = grad_one.astype(jnp.bfloat16)
    grad_attended = contract_cols(grad_one_low, full_out).astype(jnp.bfloat16)
    grad_heads = paired(exchanged(grad_attended, 1, 0))
    grad_wout = scattered(contract_rows(attended, grad_one_low))
    grad_q, grad_k_before, grad_v_before, grad_k, grad_v = self_attend_back(
        queries, grad_heads, heads_out, log_totals, kv_before, kv_own, starts
    )
    late = group_rows - SPAN
    owned = [grad_q[:, :head_cols]]
    for part, before in ((grad_k, grad_k_before), (grad_v, grad_v_before)):
        returned = passed_along(before[:, :head_cols], "fsdp", -1).astype(jnp.float32)
        part = part[:, :head_cols].astype(jnp.float32)
        part = jnp.concatenate([part[:late], part[late:] + returned]) if late else part + returned
        owned.append(part.astype(jnp.bfloat16))
    grad_proj = jnp.concatenate(owned, axis=1)
    grad_wqkv = scattered(contract_rows(normed_one, grad_proj))
    grad_normed_one = summed_block(contract_cols(grad_proj, w_qkv), 0)
    n_one, root_one = normed(inputs)
    back_x, gain_one, bias_one = norm_back(grad_normed_one, n_one, root_one, gains[0])
    grad_tokens = (grad_one + back_x).astype(jnp.bfloat16)

    def whole(part):
        return lax.psum(part, "seq").astype(jnp.float32)

    def columns(part, blocks):
        return gathered(part.reshape(shard_rows, blocks, head_cols), 2).reshape(shard_rows, -1).astype(jnp.float32)

    norm_grads = lax.psum(
        jnp.stack([gain_one, gain_two, gain_three, bias_one, bias_two, bias_three]), ("fsdp", "seq")
    )
    norm_grads = lax.dynamic_slice_in_dim(norm_grads, group_index * shard_rows, shard_rows, 1)
    return (
        layer_out,
        grad_tokens,
        lax.psum(grad_text.astype(jnp.bfloat16), "seq").astype(jnp.float32).reshape(text.shape),
        columns(grad_wqkv, 3),
        whole(grad_wout),
        whole(grad_cq),
        columns(grad_ckv, 2),
        whole(grad_cout),
        whole(grad_up),
        whole(grad_down),
        norm_grads[:3],
        norm_grads[3:],
    )


def solution(mesh):
    rows, shard, copied = P(("fsdp", "seq"), None), P("fsdp", None), P(None, "fsdp")
    groups = P("fsdp", None, None)
    in_specs = (rows, P(), groups, *[shard] * 7, copied, copied, rows)
    out_specs = (rows, rows, groups, *[shard] * 7, copied, copied)
    return jax.shard_map(shards, mesh=mesh, in_specs=in_specs, out_specs=out_specs, check_vma=False)
```

time: 2950 us -> 1590 us (0.54)
  matrix products: 1080 us -> 281 us
  other arithmetic: 507 us -> 64.7 us
  blocking collectives: 214 us -> 41.4 us
  local copies, waits for them, and re-layouts: 210 us -> 42.4 us
  Pallas kernels: 0 us -> 167 us
  waiting for transfers between devices: 884 us -> 954 us
    dot_general x27 -> x0, matrix products: 776 us -> none  [the longest x7 209 us: masked_scores(): jnp.einsum('qhd,khd->hqk', queries, keys, preferred_element_type=jnp.floa...]
    convert_element_type x17 -> x10, other arithmetic: 262 us -> 14.9 us  [the longest x5 8.55 us: whole(): return lax.psum(part, 'seq').astype(jnp.float32)]
    reduce_scatter x7 -> x6, waiting for transfers between devices: 232 us -> 410 us  [scattered(): lax.psum_scatter(grad.astype(jnp.bfloat16), 'fsdp', scatter_dimension=0,...]
    all_gather x7, waiting for transfers between devices: 68.6 us -> 242 us  [shards(): row_block = lambda value: lax.all_gather(value, 'fsdp', axis=0, tiled=True)]
    all_to_all x2 -> x0, blocking collectives: 167 us -> none  [the longest x1 108 us: shards(): lax.all_to_all(qkv, 'seq', split_axis=2, concat_axis=0, tiled=True)]
    psum x2 -> x1, waiting for transfers between devices: 250 us -> 82.7 us  [shards(): lax.psum(grad_text.astype(jnp.bfloat16), 'seq').astype(jnp.float32)]
    pallas_call x0 -> x4, Pallas kernels: none -> 167 us  [the longest x1 71.3 us: self_attend_back(): pl.pallas_call(functools.partial(attend_back_kernel, reach=reach, tq=tq,...]
    ppermute x4 -> x3, waiting for transfers between devices: 237 us -> 100 us  [passed_along(): lax.ppermute(value, axis, [(source, source + steps) for source in range(i...]
  transfers between devices with their start and end apart: 24 -> 26, of which waited for: 9 -> 16; matrix products, arithmetic and copies ran while one was open for 56% -> 18% of each run, Pallas kernels for 0% -> 9%
where the time goes in v1:
time: 1590 us
  waiting for transfers between devices  954 us (60%)
  matrix products  281 us (18%)
  Pallas kernels  167 us (11%)
  other arithmetic  64.7 us (4%)
  local copies, waits for them, and re-layouts  42.4 us (3%)
  blocking collectives  41.4 us (3%)
  starting transfers between devices  20.5 us (1%)
    reduce_scatter x6, waiting for transfers between devices, scattered(): lax.psum_scatter(grad.astype(jnp.bfloat16), 'fsdp', scatter_dimension=0,...  410 us
    all_gather x7, waiting for transfers between devices, shards(): row_block = lambda value: lax.all_gather(value, 'fsdp', axis=0, tiled=True)  242 us
    ppermute x8, waiting for transfers between devices, swap(): return lax.ppermute(value, axis, [(i, i ^ bit) for i in range(count)])  112 us
    ppermute x3, waiting for transfers between devices, passed_along(): lax.ppermute(value, axis, [(source, source + steps) for source in range(i...  100 us
    dot_general x7, matrix products, contract_cols(): lax.dot_general(left_side, right_side, (((1,), (1,)), ((), ())), preferre...  96.6 us
    dot_general x8, matrix products, matmul(): return jnp.dot(left_side, right_side, preferred_element_type=jnp.float32)  96 us
    dot_general x7, matrix products, contract_rows(): lax.dot_general(left_side, right_side, (((0,), (0,)), ((), ())), preferre...  87.9 us
    psum x1, waiting for transfers between devices, shards(): lax.psum(grad_text.astype(jnp.bfloat16), 'seq').astype(jnp.float32)  82.7 us
  transfers between devices with their start and end apart: 26, of which 16 were waited for; matrix products, arithmetic and copies ran while one was open for 18% of the time, Pallas kernels for 9%

profile of v1, /device:TPU:0, one launch (start us, length us, event | category | flops | bytes accessed | tf_op | source)
XLA Modules:
  0.0 1585.4 jit_solution(16133050175872349678)
XLA Ops:
  23.2 51.4 %collective-permute-done = bf16[768,1536]{1,0:T(8,128)(2,1)} collective-permute-done((bf16[768,1536]{1,0:T(8,128)(2,1)S(1)}, bf16[768,1536]{1,0:T(8,128)(2,1)}, u32[]{:S(2)}, u32[]{:S(2)}) %collective-permute-start) | collective-permute-done | bytes 2359328 | tf_op jit(solution)/shard_map/ppermute | solution.py:366
  120.5 60.7 %self_attend.1 = (bf16[1536,768]{1,0:T(8,128)(2,1)S(1)}, f32[1536,768]{1,0:T(8,128)}) custom-call(s32[4,4]{1,0:T(4,128)S(1)} %pad_add_fusion.bounds, bf16[1536,768]{1,0:T(8,128)(2,1)S(1)} %convolution_convert_fusion.11.q_ref, bf16[1536,1536]{1,0:T(8,128)(2,1)} %collective-permute-done.1.kp_ref.vp_ref, ...), custom_call_target="tpu_custom_call" | custom-call | flops 28991029248 | bytes 14155776 | tf_op jit(solution)/shard_map/self_attend/pallas_call | solution.py:133
  220.4 42.4 %all-gather.12.cloned.1.call-done = bf16[1536,1536]{1,0:T(8,128)(2,1)} async-done(((bf16[96,1536]{1,0:T(8,128)(2,1)}), bf16[1536,1536]{1,0:T(8,128)(2,1)}) %all-gather.12.cloned.1.call-update) | async-done | bytes 4718608 | tf_op jit(solution)/shard_map/all_gather | solution.py:466
  270.7 16.5 %cross_attend.1 = bf16[768,1536]{1,0:T(8,128)(2,1)S(1)} custom-call(bf16[768,1536]{1,0:T(8,128)(2,1)S(1)} %convolution_convert_fusion.10.q_ref, bf16[128,1536]{1,0:T(8,128)(2,1)S(1)} %get-tuple-element.69.k_ref, bf16[128,1536]{1,0:T(8,128)(2,1)S(1)} %get-tuple-element.68.v_ref, s32[768,128]{1,0:T(8,128)S(1)} %broadcast_in_dim.29.slot_ref), custom_call_target="tpu_custom_call" | custom-call | flops 1207959552 | bytes 4718592 | tf_op jit(solution)/shard_map/cross_attend/pallas_call | solution.py:283
  289.3 27.5 %all-gather.16.cloned.1.call-done = bf16[1536,1536]{1,0:T(8,128)(2,1)} async-done(((bf16[96,1536]{1,0:T(8,128)(2,1)}), bf16[1536,1536]{1,0:T(8,128)(2,1)}) %all-gather.16.cloned.1.call-update) | async-done | bytes 4718608 | tf_op jit(solution)/shard_map/all_gather | solution.py:466
  326.8 89.0 %all-gather.18.cloned.1.call-done = bf16[1536,6144]{1,0:T(8,128)(2,1)} async-done(((bf16[96,6144]{1,0:T(8,128)(2,1)}), bf16[1536,6144]{1,0:T(8,128)(2,1)}) %all-gather.18.cloned.1.call-update) | async-done | bytes 18874384 | tf_op jit(solution)/shard_map/all_gather | solution.py:466
  415.8 25.0 %multiply_convert_fusion = (bf16[768,6144]{1,0:T(8,128)(2,1)}, f32[768,6144]{1,0:T(8,128)}) fusion(bf16[1536,6144]{1,0:T(8,128)(2,1)} %all-gather.18.cloned.1.call-done, f32[768,1536]{1,0:T(8,128)} %copy-done.20, f32[1536]{0:T(1024)S(1)} %copy-done.44, f32[1536]{0:T(1024)S(1)} %copy-done.37, f32[768]{0:T(1024)S(1)} %add_rsqrt_fusion.2, ...), kind=kOutput, calls=%fused_computation.9 | convolution fusion | flops 14525005824 | bytes 51922944 | tf_op jit(solution)/shard_map/dot_general | solution.py:22
  440.8 75.6 %all-gather.20.cloned.1.call-done = bf16[6144,1536]{1,0:T(8,128)(2,1)} async-done(((bf16[384,1536]{1,0:T(8,128)(2,1)}), bf16[6144,1536]{1,0:T(8,128)(2,1)}) %all-gather.20.cloned.1.call-update) | async-done | bytes 18874384 | tf_op jit(solution)/shard_map/all_gather | solution.py:466
  516.4 25.3 %fusion.5 = bf16[768,6144]{1,0:T(8,128)(2,1)} fusion(f32[768,6144]{1,0:T(8,128)} %get-tuple-element.83, bf16[768,1536]{1,0:T(8,128)(2,1)} %param.25, bf16[6144,1536]{1,0:T(8,128)(2,1)} %all-gather.20.cloned.1.call-done), kind=kOutput, calls=%fused_computation.8 | convolution fusion | flops 14542700544 | bytes 49545216 | tf_op jit(solution)/shard_map/dot_general | solution.py:32
  541.7 23.9 %multiply_reduce_fusion = (f32[1536]{0:T(1024)}, f32[768]{0:T(1024)S(1)}, f32[768]{0:T(1024)S(1)}, f32[1536]{0:T(1024)}, f32[768,1536]{1,0:T(8,128)}) fusion(f32[768,1536]{1,0:T(8,128)S(1)} %bitcast.74, f32[768]{0:T(1024)S(1)} %add_rsqrt_fusion.2, f32[768]{0:T(1024)S(1)} %broadcast_multiply_fusion.8, f32[1536]{0:T(1024)S(1)} %copy-done.37, ...), kind=kOutput, calls=%fused_computation.46 | convolution fusion | flops 14506125312 | bytes 37779456 | tf_op jit(solution)/shard_map/dot_general | solution.py:32
  580.4 18.4 %cross_attend_back.1 = (bf16[768,1536]{1,0:T(8,128)(2,1)}, f32[128,1536]{1,0:T(8,128)S(1)}, f32[128,1536]{1,0:T(8,128)S(1)}) custom-call(bf16[768,1536]{1,0:T(8,128)(2,1)} %copy-done.3, bf16[768,1536]{1,0:T(8,128)(2,1)} %convolution_convert_fusion.9.g_ref, bf16[128,1536]{1,0:T(8,128)(2,1)S(1)} %get-tuple-element.69.k_ref, ...), custom_call_target="tpu_custom_call" | custom-call | flops 3019898880 | bytes 7077888 | tf_op jit(solution)/shard_map/cross_attend_back/pallas_call | solution.py:334
  639.4 22.2 %convolution_convert_fusion.1 = bf16[1536,6144]{1,0:T(8,128)(2,1)} fusion(bf16[768,6144]{1,0:T(8,128)(2,1)} %fusion.5, f32[768,1536]{1,0:T(8,128)} %copy-done.20, f32[1536]{0:T(1024)S(1)} %copy-done.44, f32[1536]{0:T(1024)S(1)} %copy-done.37, f32[768]{0:T(1024)S(1)} %add_rsqrt_fusion.2, f32[768]{0:T(1024)S(1)} %broadcast_multiply_fusion.8), kind=kOutput, calls=%fused_computation.2 | convolution fusion | flops 14510850048 | bytes 33048576 | tf_op jit(solution)/shard_map/dot_general | solution.py:26
  661.7 20.7 %convolution_convert_fusion = bf16[6144,1536]{1,0:T(8,128)(2,1)} fusion(bf16[768,6144]{1,0:T(8,128)(2,1)} %get-tuple-element.82, bf16[768,1536]{1,0:T(8,128)(2,1)} %param.25), kind=kOutput, calls=%fused_computation.1 | convolution fusion | flops 14504951808 | bytes 30670848 | tf_op jit(solution)/shard_map/dot_general | solution.py:26
  693.7 34.6 %collective-permute-done.8 = bf16[128,2,768]{2,0,1:T(8,128)(2,1)S(1)} collective-permute-done((bf16[128,2,768]{2,0,1:T(8,128)(2,1)S(1)}, bf16[128,2,768]{2,0,1:T(8,128)(2,1)S(1)}, u32[]{:S(2)}, u32[]{:S(2)}) %collective-permute-start.8) | collective-permute-done | bytes 393248 | tf_op jit(solution)/shard_map/ppermute | solution.py:366
  742.6 71.3 %self_attend_back.1 = (bf16[1536,768]{1,0:T(8,128)(2,1)S(1)}, bf16[1536,768]{1,0:T(8,128)(2,1)S(1)}, bf16[1536,768]{1,0:T(8,128)(2,1)}, bf16[1536,768]{1,0:T(8,128)(2,1)}, bf16[1536,768]{1,0:T(8,128)(2,1)}) custom-call(s32[4,4]{1,0:T(4,128)S(1)} %copy-done.7, bf16[1536,768]{1,0:T(8,128)(2,1)} %copy-done.8, bf16[1536,768]{1,0:T(8,128)(2,1)} %pad_maximum_fusion.5.do_ref, ...), custom_call_target="tpu_custom_call" | custom-call | flops 72477573120 | bytes 23592960 | tf_op jit(solution)/shard_map/self_attend_back/pallas_call | solution.py:245
  817.1 100.2 %collective-permute-done.5 = bf16[1536,768]{1,0:T(8,128)(2,1)S(1)} collective-permute-done((bf16[1536,768]{1,0:T(8,128)(2,1)S(1)}, bf16[1536,768]{1,0:T(8,128)(2,1)S(1)}, u32[]{:S(2)}, u32[]{:S(2)}) %collective-permute-start.5) | collective-permute-done | bytes 2359328 | tf_op jit(solution)/shard_map/ppermute | solution.py:372
  923.1 18.9 %convolution_convert_fusion.2 = bf16[1536,2304]{1,0:T(8,128)(2,1)} fusion(bf16[1536,768]{1,0:T(8,128)(2,1)} %add_convert_fusion, bf16[1536,768]{1,0:T(8,128)(2,1)} %add_convert_fusion.1, bf16[1536,768]{1,0:T(8,128)(2,1)S(1)} %copy-done.10, f32[1536]{0:T(1024)S(1)} %copy-done.43, f32[1536]{0:T(1024)S(1)} %copy-done.34, f32[1536]{0:T(1024)S(1)} %copy-done.52, ...), kind=kOutput, calls=%fused_computation.13 | convolution fusion | flops 10917642240 | bytes 18898944 | tf_op jit(solution)/shard_map/dot_general | solution.py:26
  951.6 16.3 %fusion.12 = f32[1536,1536]{1,0:T(8,128)} fusion(bf16[1536,2432]{1,0:T(8,128)(2,1)} %all-gather.8.cloned.1.call-done, bf16[1536,768]{1,0:T(8,128)(2,1)S(1)} %copy-done.22, bf16[1536,768]{1,0:T(8,128)(2,1)S(1)} %copy-done.21, bf16[1536,768]{1,0:T(8,128)(2,1)S(1)} %copy-done.10), kind=kOutput, calls=%fused_computation.25 | convolution fusion | flops 10892869632 | bytes 23592960 | tf_op jit(solution)/shard_map/dot_general | solution.py:32
  973.4 121.5 %reduce-scatter.18.cloned.1.call-done = bf16[96,6144]{1,0:T(8,128)(2,1)} async-done(((bf16[1536,6144]{1,0:T(8,128)(2,1)}), bf16[96,6144]{1,0:T(8,128)(2,1)}) %reduce-scatter.18.cloned.1.call-update) | async-done | bytes 1179664 | tf_op jit(solution)/shard_map/reduce_scatter | solution.py:431
  1094.9 198.6 %reduce-scatter.20.cloned.1.call-done = bf16[384,1536]{1,0:T(8,128)(2,1)} async-done(((bf16[6144,1536]{1,0:T(8,128)(2,1)}), bf16[384,1536]{1,0:T(8,128)(2,1)}) %reduce-scatter.20.cloned.1.call-update) | async-done | bytes 1179664 | tf_op jit(solution)/shard_map/reduce_scatter | solution.py:431
  1293.6 22.1 %add_convert_fusion.2 = bf16[768,1536]{1,0:T(8,128)(2,1)} fusion(f32[768,1536]{1,0:T(8,128)} %copy-done.20, bf16[768,6144]{1,0:T(8,128)(2,1)} %get-tuple-element.82, bf16[6144,1536]{1,0:T(8,128)(2,1)} %all-gather.20.cloned.1.call-done), kind=kOutput, calls=%fused_computation.56 | convolution fusion | flops 14497873920 | bytes 35389440 | tf_op jit(solution)/shard_map/dot_general | solution.py:22
  1322.3 41.4 %psum.55 = f32[6,1536]{1,0:T(8,128)S(1)} all-reduce(f32[6,1536]{1,0:T(8,128)S(1)} %stack.61), channel_id=1, replica_groups=mesh['fsdp'=16,'seq'=2] {'fsdp','seq'}, use_global_device_ids=true, to_apply=%region_34.35 | all-reduce | flops 9216 | bytes 73728 | tf_op jit(solution)/shard_map/psum | solution.py:561
  1377.1 89.4 %reduce-scatter.10.cloned.1.call-done = bf16[96,2304]{1,0:T(8,128)(2,1)} async-done(((bf16[1536,2304]{1,0:T(8,128)(2,1)}), bf16[96,2304]{1,0:T(8,128)(2,1)}) %reduce-scatter.10.cloned.1.call-update) | async-done | bytes 442384 | tf_op jit(solution)/shard_map/reduce_scatter | solution.py:431
  1486.4 82.7 %all-reduce.5.cloned.1.call-done = (bf16[2,64,1536]{2,1,0:T(8,128)(2,1)}, bf16[96,1536]{1,0:T(8,128)(2,1)}, bf16[96,1536]{1,0:T(8,128)(2,1)}, bf16[96,1536]{1,0:...) async-done(((bf16[2,64,1536]{2,1,0:T(8,128)(2,1)}, bf16[96,1536]{1,0:T(8,128)(2,1)}, bf16[96,1536]{1,0:T(8,128)(2,1)}, bf16[96,1536]{1,0:T(8,128)(2,1)}, ...) | async-done | bytes 3637264 | tf_op jit(solution)/shard_map/psum | solution.py:568
  (281 shorter events, 274.7 us)
Async XLA Ops:
  7.2 78.4 %all-gather.8.cloned.1.call-start = ((), (), s32[]{:S(2)}) async-start(), calls=%async_computation.7 | async-start | bytes 7938048 | tf_op jit(solution)/shard_map/all_gather | solution.py:466
  13.7 170.3 %all-gather.14.cloned.1.call-start = ((), (), s32[]{:S(2)}) async-start(), calls=%async_computation.10 | async-start | bytes 5013504 | tf_op jit(solution)/shard_map/all_gather | solution.py:466
  16.9 193.1 %all-gather.10.cloned.1.call-start = ((), (), s32[]{:S(2)}) async-start(), calls=%async_computation.8 | async-start | bytes 5013504 | tf_op jit(solution)/shard_map/all_gather | solution.py:466
  17.7 245.2 %all-gather.12.cloned.1.call-start = ((), (), s32[]{:S(2)}) async-start(), calls=%async_computation.9 | async-start | bytes 5013504 | tf_op jit(solution)/shard_map/all_gather | solution.py:466
  18.2 298.6 %all-gather.16.cloned.1.call-start = ((), (), s32[]{:S(2)}) async-start(), calls=%async_computation.11 | async-start | bytes 5013504 | tf_op jit(solution)/shard_map/all_gather | solution.py:466
  18.8 397.0 %all-gather.18.cloned.1.call-start = ((), (), s32[]{:S(2)}) async-start(), calls=%async_computation.12 | async-start | bytes 20054016 | tf_op jit(solution)/shard_map/all_gather | solution.py:466
  19.4 497.0 %all-gather.20.cloned.1.call-start = ((), (), s32[]{:S(2)}) async-start(), calls=%async_computation.13 | async-start | bytes 20054016 | tf_op jit(solution)/shard_map/all_gather | solution.py:466
  20.1 953.2 %reduce-scatter.14.cloned.1.call-start = ((), (), s32[]{:S(2)}) async-start(), calls=%async_computation.16 | async-start | bytes 5013504 | tf_op jit(solution)/shard_map/reduce_scatter | solution.py:431
  20.2 54.4 %collective-permute-start = (bf16[768,1536]{1,0:T(8,128)(2,1)S(1)}, bf16[768,1536]{1,0:T(8,128)(2,1)}, u32[]{:S(2)}, u32[]{:S(2)}) collective-permute-start(bf16[768,1536]{1,0:T(8,128)(2,1)S(1)} %copy-done.11), channel_id=1, source_target_pairs={{0,1},{1,0},{2,3},{3,2},{4,5},{5,4},{6,7},{7,6},{8,9},{9,8},{10,11... | collective-permute-start | bytes 7077896 | tf_op jit(solution)/shard_map/ppermute | solution.py:366
  103.2 17.0 %collective-permute-start.1 = (bf16[1536,1536]{1,0:T(8,128)(2,1)}, bf16[1536,1536]{1,0:T(8,128)(2,1)}, u32[]{:S(2)}, u32[]{:S(2)}) collective-permute-start(bf16[1536,1536]{1,0:T(8,128)(2,1)} %convolution_convert_fusion.7.ko_ref.vo_ref), channel_id=1, source_target_pairs={{0,2},{2,4},{4,6},{6,8},{8,10},{10,12},{12,14},{14,16},{16,18},{18... | collective-permute-start | bytes 14155784 | tf_op jit(solution)/shard_map/ppermute | solution.py:372
  182.4 21.9 %collective-permute-start.2 = (bf16[768,768]{1,0:T(8,128)(2,1)}, bf16[768,768]{1,0:T(8,128)(2,1)}, u32[]{:S(2)}, u32[]{:S(2)}) collective-permute-start(bf16[768,768]{1,0:T(8,128)(2,1)} %constant_dynamic-slice_fusion.3), channel_id=1, source_target_pairs={{0,1},{1,0},{2,3},{3,2},{4,5},{5,4},{6,7},{7,6},{8,9},{9,8},{10,11... | collective-permute-start | bytes 3538952 | tf_op jit(solution)/shard_map/ppermute | solution.py:366
  606.8 366.6 %reduce-scatter.12.cloned.1.call-start = ((), (), s32[]{:S(2)}) async-start(), calls=%async_computation.15 | async-start | bytes 5013504 | tf_op jit(solution)/shard_map/reduce_scatter | solution.py:431
  630.1 343.3 %reduce-scatter.16.cloned.1.call-start = ((), (), s32[]{:S(2)}) async-start(), calls=%async_computation.17 | async-start | bytes 5013504 | tf_op jit(solution)/shard_map/reduce_scatter | solution.py:431
  639.2 455.7 %reduce-scatter.18.cloned.1.call-start = ((), (), s32[]{:S(2)}) async-start(), calls=%async_computation.18 | async-start | bytes 20054016 | tf_op jit(solution)/shard_map/reduce_scatter | solution.py:431
  661.7 631.8 %reduce-scatter.20.cloned.1.call-start = ((), (), s32[]{:S(2)}) async-start(), calls=%async_computation.19 | async-start | bytes 20054016 | tf_op jit(solution)/shard_map/reduce_scatter | solution.py:431
  682.4 691.6 %reduce-scatter.22.cloned.1.call-start = ((), (), s32[]{:S(2)}) async-start(), calls=%async_computation.20 | async-start | bytes 5013504
  691.5 47.3 %collective-permute-start.4 = (bf16[768,768]{1,0:T(8,128)(2,1)}, bf16[768,768]{1,0:T(8,128)(2,1)}, u32[]{:S(2)}, u32[]{:S(2)}) collective-permute-start(bf16[768,768]{1,0:T(8,128)(2,1)} %constant_dynamic-slice_fusion.1), channel_id=1, source_target_pairs={{0,1},{1,0},{2,3},{3,2},{4,5},{5,4},{6,7},{7,6},{8,9},{9,8},{10,11... | collective-permute-start | bytes 3538952 | tf_op jit(solution)/shard_map/ppermute | solution.py:366
  693.1 35.2 %collective-permute-start.8 = (bf16[128,2,768]{2,0,1:T(8,128)(2,1)S(1)}, bf16[128,2,768]{2,0,1:T(8,128)(2,1)S(1)}, u32[]{:S(2)}, u32[]{:S(2)}) collective-permute-start(bf16[128,2,768]{2,0,1:T(8,128)(2,1)S(1)} %fusion.35), channel_id=1, source_target_pairs={{0,1},{1,0},{2,3},{3,2},{4,5},{5,4},{6,7},{7,6},{8,9},{9,8},{10,11... | collective-permute-start | bytes 1179656 | tf_op jit(solution)/shard_map/ppermute | solution.py:366
  738.8 727.7 %reduce-scatter.10.cloned.1.call-start = ((), (), s32[]{:S(2)}) async-start(), calls=%async_computation.14 | async-start | bytes 7520256 | tf_op jit(solution)/shard_map/reduce_scatter | solution.py:431
  813.8 103.5 %collective-permute-start.5 = (bf16[1536,768]{1,0:T(8,128)(2,1)S(1)}, bf16[1536,768]{1,0:T(8,128)(2,1)S(1)}, u32[]{:S(2)}, u32[]{:S(2)}) collective-permute-start(bf16[1536,768]{1,0:T(8,128)(2,1)S(1)} %get-tuple-element.27), channel_id=1, source_target_pairs={{2,0},{4,2},{6,4},{8,6},{10,8},{12,10},{14,12},{16,14},{18,16},{20... | collective-permute-start | bytes 7077896 | tf_op jit(solution)/shard_map/ppermute | solution.py:372
  815.4 105.7 %collective-permute-start.6 = (bf16[1536,768]{1,0:T(8,128)(2,1)}, bf16[1536,768]{1,0:T(8,128)(2,1)S(1)}, u32[]{:S(2)}, u32[]{:S(2)}) collective-permute-start(bf16[1536,768]{1,0:T(8,128)(2,1)} %get-tuple-element.29), channel_id=1, source_target_pairs={{2,0},{4,2},{6,4},{8,6},{10,8},{12,10},{14,12},{16,14},{18,16},{20... | collective-permute-start | bytes 7077896 | tf_op jit(solution)/shard_map/ppermute | solution.py:372
  942.0 627.1 %all-reduce.5.cloned.1.call-start = ((), (), s32[]{:S(2)}) async-start(), calls=%async_computation.21 | async-start | bytes 7274496 | tf_op jit(solution)/shard_map/psum | solution.py:568
  971.9 343.9 %collective-permute-start.7 = (bf16[768,1536]{1,0:T(8,128)(2,1)}, bf16[768,1536]{1,0:T(8,128)(2,1)}, u32[]{:S(2)}, u32[]{:S(2)}) collective-permute-start(bf16[768,1536]{1,0:T(8,128)(2,1)} %dynamic-slice_convert_fusion), channel_id=1, source_target_pairs={{0,1},{1,0},{2,3},{3,2},{4,5},{5,4},{6,7},{7,6},{8,9},{9,8},{10,11... | collective-permute-start | bytes 7077896 | tf_op jit(solution)/shard_map/ppermute | solution.py:366
  1375.4 93.8 %collective-permute-start.10 = (bf16[96,2,768]{2,0,1:T(8,128)(2,1)S(1)}, bf16[96,2,768]{2,0,1:T(8,128)(2,1)S(1)}, u32[]{:S(2)}, u32[]{:S(2)}) collective-permute-start(bf16[96,2,768]{2,0,1:T(8,128)(2,1)S(1)} %copy.85), channel_id=1, source_target_pairs={{0,1},{1,0},{2,3},{3,2},{4,5},{5,4},{6,7},{7,6},{8,9},{9,8},{10,11... | collective-permute-start | bytes 884744 | tf_op jit(solution)/shard_map/ppermute | solution.py:366
  (59 other events, 1473.6 us)
Sparse Core Ops, SparseCore 0:
  13.8 71.7 all-gather.7
  88.5 57.8 all-gather.13
  148.6 61.3 all-gather.9
  212.2 50.6 all-gather.11
  265.0 51.7 all-gather.15
  318.3 97.5 all-gather.17
  417.4 98.9 all-gather.19
  606.9 75.5 reduce-scatter.13
  686.8 74.6 reduce-scatter.11
  765.2 74.5 reduce-scatter.15
  844.5 250.3 reduce-scatter.17
  1099.4 194.0 reduce-scatter.19
  1297.8 76.1 reduce-scatter.21
  1377.9 88.6 reduce-scatter.9
  1469.8 99.2 all-reduce.4

commit v2 on v1

v2 whole, which is shorter than its diff:
```python
import functools

import jax
import jax.numpy as jnp
from jax import lax
from jax.experimental import pallas as pl
from jax.experimental.pallas import tpu as pltpu
from jax.sharding import PartitionSpec as P

HEADS = 24
HEAD = 64
PAIR = 2 * HEAD
TXT = 64
SPAN = 1536
EPS = 1e-05
NEG = -1e30
SCALE = HEAD**-0.5
VMEM_BYTES = 56 * 2**20


def matmul(left_side, right_side):
    return jnp.dot(left_side, right_side, preferred_element_type=jnp.float32)


def contract_rows(left_side, right_side):
    return lax.dot_general(
        left_side, right_side, (((0,), (0,)), ((), ())), preferred_element_type=jnp.float32
    )


def contract_cols(left_side, right_side):
    return lax.dot_general(
        left_side, right_side, (((1,), (1,)), ((), ())), preferred_element_type=jnp.float32
    )


TILE = 384


def block_bounds(starts, reach):
    rows = starts.shape[0]
    first = starts[::TILE]
    last = starts[TILE - 1 :: TILE]
    row0 = reach + jnp.arange(rows // TILE, dtype=jnp.int32) * TILE
    low = first // TILE
    high = (row0 + TILE - 1) // TILE + 1
    free_low = jnp.minimum(jnp.maximum((last + TILE - 1) // TILE, low), high)
    free_high = jnp.clip((row0 + 1) // TILE, free_low, high)
    return jnp.stack([low, free_low, free_high, high], axis=1)


def pairs_a_step(width):
    return 3 if width % (3 * PAIR) == 0 else 1


def split_heads(block):
    lower = lax.broadcasted_iota(jnp.int32, (1, PAIR), 1) < HEAD
    zero = jnp.zeros((1, 1), block.dtype)
    return [jnp.where(lower, block, zero), jnp.where(lower, zero, block)]


def lanes(p):
    return slice(p * PAIR, (p + 1) * PAIR)


def tile_allowed(j, row0, starts):
    at = j * TILE + lax.broadcasted_iota(jnp.int32, (TILE, TILE), 0)
    row = row0 + lax.broadcasted_iota(jnp.int32, (TILE, TILE), 1)
    return (at >= starts) & (at <= row)


def over_tiles(bounds, i, step, state):
    low, free_low, free_high, high = (bounds[i, n] for n in range(4))
    state = lax.fori_loop(low, free_low, functools.partial(step, True), state)
    state = lax.fori_loop(free_low, free_high, functools.partial(step, False), state)
    return lax.fori_loop(free_high, high, functools.partial(step, True), state)


def attend_kernel(
    bounds, q_ref, kp_ref, vp_ref, ko_ref, vo_ref, start_ref, o_ref, lse_ref, k_all, v_t, *, reach, pairs
):
    i = pl.program_id(1)

    @pl.when(i == 0)
    def _():
        k_all[:reach] = kp_ref[...]
        k_all[reach:] = ko_ref[...]
        for p in range(pairs):
            for ref, begin in ((vp_ref, 0), (vo_ref, reach)):
                end = begin + ref.shape[0]
                turned = ref[:, lanes(p)].T
                for h in range(2):
                    v_t[2 * p + h, :HEAD, begin:end] = turned[h * HEAD : (h + 1) * HEAD]
                    v_t[2 * p + h, HEAD:, begin:end] = jnp.ones((16, end - begin), jnp.bfloat16)

    halves = []
    for p in range(pairs):
        halves += split_heads(q_ref[:, lanes(p)] * jnp.bfloat16(SCALE))
    starts = start_ref[0]

    def step(masked, j, carried):
        rows = pl.ds(pl.multiple_of(j * TILE, TILE), TILE)
        if masked:
            allowed = tile_allowed(j, reach + i * TILE, starts)
        scores = []
        for n in range(2 * pairs):
            s = contract_cols(k_all[rows, lanes(n // 2)], halves[n])
            scores.append(jnp.where(allowed, s, NEG) if masked else s)
        out = []
        for n, (top, total) in enumerate(carried):
            new_top = jnp.maximum(top, jnp.max(scores[n], axis=0, keepdims=True))
            weights = jnp.exp(scores[n] - new_top).astype(jnp.bfloat16)
            total = total * jnp.exp(top - new_top) + matmul(v_t[n, :, rows], weights)
            out.append((new_top, total))
        return tuple(out)

    nothing = (jnp.full((1, TILE), NEG, jnp.float32), jnp.zeros((HEAD + 16, TILE), jnp.float32))
    state = over_tiles(bounds, i, step, (nothing,) * (2 * pairs))
    for p in range(pairs):
        outs = []
        for n in (2 * p, 2 * p + 1):
            top, total = state[n]
            count = total[HEAD : HEAD + 1]
            outs.append(total[:HEAD] / count)
            lse_ref[0, 0, n : n + 1, :] = top + jnp.log(count)
        o_ref[:, lanes(p)] = jnp.concatenate(outs, axis=0).T.astype(o_ref.dtype)


def attend_specs(rows, reach, width):
    pairs = pairs_a_step(width)
    wide = pairs * PAIR
    steps = width // wide
    block = pl.BlockSpec((TILE, wide), lambda p, i, b: (i, p))
    kv = [
        pl.BlockSpec((reach, wide), lambda p, i, b: (0, p)),
        pl.BlockSpec((reach, wide), lambda p, i, b: (0, steps + p)),
        pl.BlockSpec((rows, wide), lambda p, i, b: (0, p)),
        pl.BlockSpec((rows, wide), lambda p, i, b: (0, steps + p)),
    ]
    logs = pl.BlockSpec((1, 1, 8, TILE), lambda p, i, b: (p, i, 0, 0))
    starts = pl.BlockSpec((1, 1, TILE), lambda p, i, b: (i, 0, 0))
    return pairs, wide, (steps, rows // TILE), block, kv, logs, starts


def self_attend(q, kv_before, kv_own, starts):
    rows, width = q.shape
    reach = kv_before.shape[0]
    pairs, wide, grid, block, kv, logs, start_block = attend_specs(rows, reach, width)
    spec = pltpu.PrefetchScalarGridSpec(
        num_scalar_prefetch=1,
        grid=grid,
        in_specs=[block, *kv, start_block],
        out_specs=[block, logs],
        scratch_shapes=[
            pltpu.VMEM((reach + rows, wide), jnp.bfloat16),
            pltpu.VMEM((2 * pairs, HEAD + 16, reach + rows), jnp.bfloat16),
        ],
    )
    return pl.pallas_call(
        functools.partial(attend_kernel, reach=reach, pairs=pairs),
        grid_spec=spec,
        out_shape=[
            jax.ShapeDtypeStruct((rows, width), jnp.bfloat16),
            jax.ShapeDtypeStruct((*grid, 8, TILE), jnp.float32),
        ],
        compiler_params=pltpu.CompilerParams(vmem_limit_bytes=VMEM_BYTES),
        cost_estimate=pl.CostEstimate(
            flops=20 * rows * rows * width,
            bytes_accessed=12 * rows * width,
            transcendentals=rows * rows * width // HEAD,
        ),
        name="self_attend",
    )(block_bounds(starts, reach), q, kv_before, kv_before, kv_own, kv_own, starts.reshape(-1, 1, TILE))


def attend_back_kernel(
    bounds, q_ref, g_ref, o_ref, lse_ref, kp_ref, vp_ref, ko_ref, vo_ref, start_ref,
    dq_ref, dkp_ref, dvp_ref, dko_ref, dvo_ref, k_all, v_all, dk_sum, dv_sum, k_t, *, reach, pairs
):
    i = pl.program_id(1)

    @pl.when(i == 0)
    def _():
        k_all[:reach] = kp_ref[...]
        k_all[reach:] = ko_ref[...]
        v_all[:reach] = vp_ref[...]
        v_all[reach:] = vo_ref[...]
        k_t[:, :reach] = kp_ref[...].T
        k_t[:, reach:] = ko_ref[...].T
        dk_sum[...] = jnp.zeros_like(dk_sum)
        dv_sum[...] = jnp.zeros_like(dv_sum)

    queries, grads, inner, logs = [], [], [], []
    for p in range(pairs):
        grad = g_ref[:, lanes(p)]
        queries += split_heads(q_ref[:, lanes(p)] * jnp.bfloat16(SCALE))
        grads += split_heads(grad)
        product = (grad.astype(jnp.float32) * o_ref[:, lanes(p)].astype(jnp.float32)).T
        for h in range(2):
            inner.append(jnp.sum(product[h * HEAD : (h + 1) * HEAD], axis=0, keepdims=True))
            logs.append(lse_ref[0, 0, 2 * p + h : 2 * p + h + 1])
    starts = start_ref[0]

    def step(masked, j, carried):
        rows = pl.ds(pl.multiple_of(j * TILE, TILE), TILE)
        if masked:
            allowed = tile_allowed(j, reach + i * TILE, starts)
        out = []
        for p in range(pairs):
            keys, values = k_all[rows, lanes(p)], v_all[rows, lanes(p)]
            dks, dvs = [], []
            for n in (2 * p, 2 * p + 1):
                s = contract_cols(keys, queries[n])
                d = contract_cols(values, grads[n])
                if masked:
                    s = jnp.where(allowed, s, NEG)
                shares = jnp.exp(s - logs[n])
                ds = (shares * (d - inner[n])).astype(jnp.bfloat16)
                dvs.append(matmul(shares.astype(jnp.bfloat16), grads[n]))
                dks.append(matmul(ds, queries[n]))
                out.append(carried[n] + matmul(k_t[n * HEAD : (n + 1) * HEAD, rows], ds))
            dv_sum[rows, lanes(p)] += dvs[0] + dvs[1]
            dk_sum[rows, lanes(p)] += dks[0] + dks[1]
        return tuple(out)

    state = over_tiles(bounds, i, step, (jnp.zeros((HEAD, TILE), jnp.float32),) * (2 * pairs))
    for p in range(pairs):
        turned = jnp.concatenate([state[2 * p], state[2 * p + 1]], axis=0).T
        dq_ref[:, lanes(p)] = (turned * SCALE).astype(dq_ref.dtype)

    @pl.when(i == pl.num_programs(1) - 1)
    def _():
        dkp_ref[...] = dk_sum[:reach].astype(dkp_ref.dtype)
        dvp_ref[...] = dv_sum[:reach].astype(dvp_ref.dtype)
        dko_ref[...] = dk_sum[reach:].astype(dko_ref.dtype)
        dvo_ref[...] = dv_sum[reach:].astype(dvo_ref.dtype)


def self_attend_back(q, grad, o, lse, kv_before, kv_own, starts):
    rows, width = q.shape
    reach = kv_before.shape[0]
    pairs, wide, grid, block, kv, logs, start_block = attend_specs(rows, reach, width)
    spec = pltpu.PrefetchScalarGridSpec(
        num_scalar_prefetch=1,
        grid=grid,
        in_specs=[block, block, block, logs, *kv, start_block],
        out_specs=[block, kv[0], kv[0], kv[2], kv[2]],
        scratch_shapes=[
            pltpu.VMEM((reach + rows, wide), jnp.bfloat16),
            pltpu.VMEM((reach + rows, wide), jnp.bfloat16),
            pltpu.VMEM((reach + rows, wide), jnp.float32),
            pltpu.VMEM((reach + rows, wide), jnp.float32),
            pltpu.VMEM((wide, reach + rows), jnp.bfloat16),
        ],
    )
    shape = lambda n: jax.ShapeDtypeStruct((n, width), jnp.bfloat16)
    return pl.pallas_call(
        functools.partial(attend_back_kernel, reach=reach, pairs=pairs),
        grid_spec=spec,
        out_shape=[shape(rows), shape(reach), shape(reach), shape(rows), shape(rows)],
        compiler_params=pltpu.CompilerParams(vmem_limit_bytes=VMEM_BYTES),
        cost_estimate=pl.CostEstimate(
            flops=40 * rows * rows * width,
            bytes_accessed=20 * rows * width,
            transcendentals=rows * rows * width // HEAD,
        ),
        name="self_attend_back",
    )(
        block_bounds(starts, reach), q, grad, o, lse, kv_before, kv_before, kv_own, kv_own,
        starts.reshape(-1, 1, TILE),
    )


def cross_kernel(q_ref, k_ref, v_ref, slot_ref, o_ref):
    lower = lax.broadcasted_iota(jnp.int32, (1, PAIR), 1) < HEAD
    zero = jnp.zeros((1, 1), jnp.bfloat16)
    scaled = q_ref[...] * jnp.bfloat16(SCALE)
    tokens, texts = q_ref.shape[0], k_ref.shape[0]
    allowed = slot_ref[:, :1] == lax.broadcasted_iota(jnp.int32, (tokens, texts), 1) // TXT
    results = []
    for h in range(2):
        half = jnp.where(lower, scaled, zero) if h == 0 else jnp.where(lower, zero, scaled)
        scores = jnp.where(allowed, contract_cols(half, k_ref[...]), NEG)
        weights = jnp.exp(scores - jnp.max(scores, axis=1, keepdims=True))
        shares = weights / jnp.sum(weights, axis=1, keepdims=True)
        results.append(matmul(shares.astype(jnp.bfloat16), v_ref[...]))
    o_ref[...] = jnp.where(lower, results[0], results[1]).astype(o_ref.dtype)


def cross_attend(q, k, v, slots_wide):
    tokens, width = q.shape
    texts = k.shape[0]
    column = lambda p: (0, p)
    return pl.pallas_call(
        cross_kernel,
        grid=(width // PAIR,),
        in_specs=[
            pl.BlockSpec((tokens, PAIR), column),
            pl.BlockSpec((texts, PAIR), column),
            pl.BlockSpec((texts, PAIR), column),
            pl.BlockSpec((tokens, PAIR), lambda p: (0, 0)),
        ],
        out_specs=pl.BlockSpec((tokens, PAIR), column),
        out_shape=jax.ShapeDtypeStruct(q.shape, jnp.bfloat16),
        compiler_params=pltpu.CompilerParams(vmem_limit_bytes=VMEM_BYTES),
        cost_estimate=pl.CostEstimate(
            flops=8 * tokens * texts * width,
            bytes_accessed=4 * tokens * width,
            transcendentals=tokens * texts * width // HEAD,
        ),
        name="cross_attend",
    )(q, k, v, slots_wide)


def cross_back_kernel(q_ref, g_ref, k_ref, v_ref, slot_ref, dq_ref, dk_ref, dv_ref):
    lower = lax.broadcasted_iota(jnp.int32, (1, PAIR), 1) < HEAD
    zero = jnp.zeros((1, 1), jnp.bfloat16)
    scaled = q_ref[...] * jnp.bfloat16(SCALE)
    grad = g_ref[...]
    keys = k_ref[...]
    tokens, texts = q_ref.shape[0], k_ref.shape[0]
    allowed = slot_ref[:, :1] == lax.broadcasted_iota(jnp.int32, (tokens, texts), 1) // TXT
    dqs, dks, dvs = [], [], []
    for h in range(2):
        q_half = jnp.where(lower, scaled, zero) if h == 0 else jnp.where(lower, zero, scaled)
        g_half = jnp.where(lower, grad, zero) if h == 0 else jnp.where(lower, zero, grad)
        scores = jnp.where(allowed, contract_cols(q_half, keys), NEG)
        weights = jnp.exp(scores - jnp.max(scores, axis=1, keepdims=True))
        shares = weights / jnp.sum(weights, axis=1, keepdims=True)
        grad_shares = contract_cols(g_half, v_ref[...])
        inner = jnp.sum(shares * grad_shares, axis=1, keepdims=True)
        grad_scores = (shares * (grad_shares - inner)).astype(jnp.bfloat16)
        dqs.append(matmul(grad_scores, keys))
        dks.append(contract_rows(grad_scores, q_half))
        dvs.append(contract_rows(shares.astype(jnp.bfloat16), g_half))
    dq_ref[...] = (jnp.where(lower, dqs[0], dqs[1]) * SCALE).astype(dq_ref.dtype)
    dk_ref[...] = dks[0] + dks[1]
    dv_ref[...] = dvs[0] + dvs[1]


def cross_attend_back(q, grad, k, v, slots_wide):
    tokens, width = q.shape
    texts = k.shape[0]
    column = lambda p: (0, p)
    return pl.pallas_call(
        cross_back_kernel,
        grid=(width // PAIR,),
        in_specs=[
            pl.BlockSpec((tokens, PAIR), column),
            pl.BlockSpec((tokens, PAIR), column),
            pl.BlockSpec((texts, PAIR), column),
            pl.BlockSpec((texts, PAIR), column),
            pl.BlockSpec((tokens, PAIR), lambda p: (0, 0)),
        ],
        out_specs=[
            pl.BlockSpec((tokens, PAIR), column),
            pl.BlockSpec((texts, PAIR), column),
            pl.BlockSpec((texts, PAIR), column),
        ],
        out_shape=[
            jax.ShapeDtypeStruct(q.shape, jnp.bfloat16),
            jax.ShapeDtypeStruct((texts, width), jnp.float32),
            jax.ShapeDtypeStruct((texts, width), jnp.float32),
        ],
        compiler_params=pltpu.CompilerParams(vmem_limit_bytes=VMEM_BYTES),
        cost_estimate=pl.CostEstimate(
            flops=20 * tokens * texts * width,
            bytes_accessed=6 * tokens * width,
            transcendentals=tokens * texts * width // HEAD,
        ),
        name="cross_attend_back",
    )(q, grad, k, v, slots_wide)


def swap(value, axis, bit):
    count = lax.axis_size(axis)
    return lax.ppermute(value, axis, [(i, i ^ bit) for i in range(count)])


def passed_along(value, axis, steps):
    count = lax.axis_size(axis)
    initial, last = (max(0, -steps), min(count, count - steps))
    return lax.ppermute(value, axis, [(source, source + steps) for source in range(initial, last)])


def in_order(mine, other, dim):
    second = lax.axis_index("seq") == 1
    return jnp.concatenate([jnp.where(second, other, mine), jnp.where(second, mine, other)], axis=dim)


def gathered(value, dim):
    if lax.axis_size("seq") == 2:
        return in_order(value, swap(value, "seq", 1), dim)
    return lax.all_gather(value, "seq", axis=dim, tiled=True)


def own_block(value, dim):
    size = value.shape[dim] // lax.axis_size("seq")
    return lax.dynamic_slice_in_dim(value, lax.axis_index("seq") * size, size, dim)


def other_block(value, dim):
    size = value.shape[dim] // 2
    return lax.dynamic_slice_in_dim(value, (1 - lax.axis_index("seq")) * size, size, dim)


def exchanged(value, split, concat):
    if lax.axis_size("seq") == 2:
        return in_order(own_block(value, split), swap(other_block(value, split), "seq", 1), concat)
    return lax.all_to_all(value, "seq", split_axis=split, concat_axis=concat, tiled=True)


def summed_block(value, dim):
    if lax.axis_size("seq") == 2:
        received = swap(other_block(value, dim).astype(jnp.bfloat16), "seq", 1)
        return own_block(value, dim) + received.astype(jnp.float32)
    return lax.psum_scatter(
        value.astype(jnp.bfloat16), "seq", scatter_dimension=dim, tiled=True
    ).astype(jnp.float32)


def paired(value):
    short = -value.shape[-1] % PAIR
    return jnp.pad(value, ((0, 0), (0, short))) if short else value


def normed(values):
    average = jnp.mean(values, axis=-1, keepdims=True)
    centred = values - average
    spread = jnp.mean(centred * centred, axis=-1, keepdims=True)
    root = lax.rsqrt(spread + EPS)
    return centred * root, root


def norm_back(grad, n, root, gain):
    a = grad * gain
    back = (a - jnp.mean(a, axis=-1, keepdims=True) - n * jnp.mean(a * n, axis=-1, keepdims=True)) * root
    return back, jnp.sum(grad * n, axis=0), jnp.sum(grad, axis=0)


def scattered(grad):
    return lax.psum_scatter(grad.astype(jnp.bfloat16), "fsdp", scatter_dimension=0, tiled=True)


def whole(part):
    if lax.axis_size("seq") == 2:
        return part.astype(jnp.float32) + swap(part, "seq", 1).astype(jnp.float32)
    return lax.psum(part, "seq").astype(jnp.float32)


def columns(part, blocks):
    split = part.reshape(part.shape[0], blocks, -1)
    return gathered(split, 2).reshape(part.shape[0], -1).astype(jnp.float32)


def everywhere(value):
    for axis in ("fsdp", "seq"):
        bit = 1
        while bit < lax.axis_size(axis):
            value = value + swap(value, axis, bit)
            bit *= 2
    return value


def clip_starts(segments, group_index, group_rows):
    padded = jnp.concatenate([jnp.full((SPAN,), -1, jnp.int32), segments])
    spans = lax.dynamic_slice_in_dim(padded, group_index * group_rows, SPAN + group_rows)
    spans = spans.reshape(-1, SPAN)
    ahead = jnp.sum((spans == spans[:, :1]).astype(jnp.int32), axis=1)
    firsts = ahead + jnp.arange(spans.shape[0], dtype=jnp.int32) * SPAN
    late = spans[1:] != spans[1:, :1]
    return jnp.where(late, firsts[1:, None], firsts[:-1, None]).reshape(group_rows), spans[1:].reshape(group_rows)


def shards(
    tokens,
    segments,
    text,
    qkv_weight,
    out_weight,
    cross_query_weight,
    cross_kv_weight,
    cross_out_weight,
    up_weight,
    down_weight,
    norm_gain,
    norm_bias,
    cotangent,
):
    group_index = lax.axis_index("fsdp")
    seq_index = lax.axis_index("seq")
    seq_count = lax.axis_size("seq")
    tok_rows, width = tokens.shape
    group_rows = tok_rows * seq_count
    head_cols = width // seq_count
    shard_rows = qkv_weight.shape[0]
    row_block = lambda value: lax.all_gather(value, "fsdp", axis=0, tiled=True)

    norms = jnp.pad(jnp.concatenate([norm_gain, norm_bias]).T, ((0, 0), (0, PAIR - 6)))
    qkv_mine = own_block(qkv_weight.reshape(shard_rows, 3, width), 2).reshape(shard_rows, 3 * head_cols)
    first = row_block(jnp.concatenate([qkv_mine, norms], axis=1))
    w_q, w_kv, w_qkv = first[:, :head_cols], first[:, head_cols : 3 * head_cols], first[:, : 3 * head_cols]
    norm_rows = first[:, 3 * head_cols : 3 * head_cols + 6].astype(jnp.float32).T
    gains, biases = norm_rows[:3], norm_rows[3:]

    ckv_mine = own_block(cross_kv_weight.reshape(shard_rows, 2, width), 2).reshape(shard_rows, 2 * head_cols)
    second = row_block(jnp.concatenate([out_weight, cross_query_weight, cross_out_weight, ckv_mine], axis=1))
    full_out, full_cq, full_cout = second[:, :width], second[:, width : 2 * width], second[:, 2 * width : 3 * width]
    w_ckv = second[:, 3 * width :]

    starts, seg_group = clip_starts(segments, group_index, group_rows)
    slots = own_block(seg_group, 0) - group_index * (group_rows // SPAN)
    slots_wide = jnp.broadcast_to(slots[:, None], (tok_rows, PAIR))

    inputs = tokens.astype(jnp.float32)
    n_group, _ = normed(gathered(tokens, 0).astype(jnp.float32))
    normed_one = (n_group * gains[0] + biases[0]).astype(jnp.bfloat16)
    kv_own = matmul(normed_one, w_kv).astype(jnp.bfloat16)
    kv_before = passed_along(kv_own[group_rows - SPAN :], "fsdp", 1)
    queries = matmul(normed_one, w_q).astype(jnp.bfloat16)
    if head_cols % PAIR:
        pad_kv = lambda kv: jnp.concatenate([paired(kv[:, :head_cols]), paired(kv[:, head_cols:])], axis=1)
        queries, kv_own, kv_before = paired(queries), pad_kv(kv_own), pad_kv(kv_before)
    heads_out, log_totals = self_attend(queries, kv_before, kv_own, starts)
    attended = exchanged(heads_out[:, :head_cols], 0, 1)
    hidden_one = inputs + matmul(attended, full_out)

    text_rows = text.reshape(-1, width)
    text_count = text_rows.shape[0]
    ckv_part = matmul(text_rows, w_ckv).astype(jnp.bfloat16).reshape(text_count, 2, head_cols)
    cross_kv = gathered(ckv_part, 2)
    cross_k, cross_v = cross_kv[:, 0], cross_kv[:, 1]
    n_two, root_two = normed(hidden_one)
    normed_two = (n_two * gains[1] + biases[1]).astype(jnp.bfloat16)
    cross_query = matmul(normed_two, full_cq).astype(jnp.bfloat16)
    cross_result = cross_attend(cross_query, cross_k, cross_v, slots_wide)
    hidden_two = hidden_one + matmul(cross_result, full_cout)

    full_up, full_down = row_block(up_weight), row_block(down_weight)
    n_three, root_three = normed(hidden_two)
    normed_three = (n_three * gains[2] + biases[2]).astype(jnp.bfloat16)
    upward = matmul(normed_three, full_up)
    below = 0.5 * (1.0 + lax.erf(upward * (0.5**0.5)))
    active = (upward * below).astype(jnp.bfloat16)
    slope = below + upward * (jnp.exp(-0.5 * upward * upward) * 0.3989422804014327)
    layer_out = (hidden_two + matmul(active, full_down)).astype(jnp.bfloat16)

    grad_down, slope = lax.optimization_barrier((contract_rows(active, cotangent).astype(jnp.bfloat16), slope))
    grad_down = scattered(grad_down)
    grad_upward = (contract_cols(cotangent, full_down) * slope).astype(jnp.bfloat16)
    grad_up, grad_upward = lax.optimization_barrier(
        (contract_rows(normed_three, grad_upward).astype(jnp.bfloat16), grad_upward)
    )
    grad_up = scattered(grad_up)
    back_h2, gain_three, bias_three = norm_back(contract_cols(grad_upward, full_up), n_three, root_three, gains[2])
    grad_two = cotangent.astype(jnp.float32) + back_h2
    grad_two_low = grad_two.astype(jnp.bfloat16)
    grad_cout = contract_rows(cross_result, grad_two_low)
    grad_result = contract_cols(grad_two_low, full_cout).astype(jnp.bfloat16)
    grad_query_c, grad_text_k, grad_text_v = cross_attend_back(cross_query, grad_result, cross_k, cross_v, slots_wide)
    grad_cq = contract_rows(normed_two, grad_query_c)
    grad_text_kv = summed_block(jnp.stack([grad_text_k, grad_text_v], axis=1), 2)
    grad_text_kv = grad_text_kv.astype(jnp.bfloat16).reshape(text_count, 2 * head_cols)
    grad_text = contract_cols(grad_text_kv, w_ckv)
    grad_ckv = contract_rows(text_rows, grad_text_kv)
    back_h1, gain_two, bias_two = norm_back(contract_cols(grad_query_c, full_cq), n_two, root_two, gains[1])
    grad_one = grad_two + back_h1

    grad_one_low = grad_one.astype(jnp.bfloat16)
    grad_attended = contract_cols(grad_one_low, full_out).astype(jnp.bfloat16)
    grad_heads = paired(exchanged(grad_attended, 1, 0))
    grad_wout = contract_rows(attended, grad_one_low)
    middle = scattered(
        jnp.concatenate([part.astype(jnp.bfloat16) for part in (grad_wout, grad_cq, grad_cout, grad_ckv)], axis=1)
    )
    grad_q, grad_k_before, grad_v_before, grad_k, grad_v = self_attend_back(
        queries, grad_heads, heads_out, log_totals, kv_before, kv_own, starts
    )
    late = group_rows - SPAN
    owned = [grad_q[:, :head_cols]]
    for part, before in ((grad_k, grad_k_before), (grad_v, grad_v_before)):
        returned = passed_along(before[:, :head_cols], "fsdp", -1).astype(jnp.float32)
        part = part[:, :head_cols].astype(jnp.float32)
        part = jnp.concatenate([part[:late], part[late:] + returned]) if late else part + returned
        owned.append(part.astype(jnp.bfloat16))
    grad_proj = jnp.concatenate(owned, axis=1)
    grad_wqkv = scattered(contract_rows(normed_one, grad_proj))
    grad_normed_one = summed_block(contract_cols(grad_proj, w_qkv), 0)
    n_one, root_one = normed(inputs)
    back_x, gain_one, bias_one = norm_back(grad_normed_one, n_one, root_one, gains[0])
    grad_tokens = (grad_one + back_x).astype(jnp.bfloat16)

    grad_ckv = columns(middle[:, 3 * width :], 2)
    middle = whole(middle[:, : 3 * width])

    norm_grads = everywhere(jnp.stack([gain_one, gain_two, gain_three, bias_one, bias_two, bias_three]))
    norm_grads = lax.dynamic_slice_in_dim(norm_grads, group_index * shard_rows, shard_rows, 1)
    return (
        layer_out,
        grad_tokens,
        whole(grad_text.astype(jnp.bfloat16)).reshape(text.shape),
        columns(grad_wqkv, 3),
        middle[:, :width],
        middle[:, width : 2 * width],
        grad_ckv,
        middle[:, 2 * width :],
        whole(grad_up),
        whole(grad_down),
        norm_grads[:3],
        norm_grads[3:],
    )


def solution(mesh):
    rows, shard, copied = P(("fsdp", "seq"), None), P("fsdp", None), P(None, "fsdp")
    groups = P("fsdp", None, None)
    in_specs = (rows, P(), groups, *[shard] * 7, copied, copied, rows)
    out_specs = (rows, rows, groups, *[shard] * 7, copied, copied)
    return jax.shard_map(shards, mesh=mesh, in_specs=in_specs, out_specs=out_specs, check_vma=False)
```

time: 1590 us -> 1550 us (0.975)
  waiting for transfers between devices: 954 us -> 831 us
  starting transfers between devices: 20.5 us -> 132 us
  blocking collectives: 41.4 us -> 0 us
  Pallas kernels: 167 us -> 136 us
  local copies, waits for them, and re-layouts: 42.4 us -> 72.3 us
    unnamed x16 -> x9, waiting for transfers between devices: 7.67 us -> 197 us
    reduce_scatter x6 -> x3, waiting for transfers between devices: 410 us -> 293 us  [scattered(): lax.psum_scatter(grad.astype(jnp.bfloat16), 'fsdp', scatter_dimension=0,...]
    ppermute x8 -> x17, starting transfers between devices: 11.3 us -> 124 us  [swap(): return lax.ppermute(value, axis, [(i, i ^ bit) for i in range(count)])]
    all_gather x7 -> x4, waiting for transfers between devices: 242 us -> 148 us  [shards(): row_block = lambda value: lax.all_gather(value, 'fsdp', axis=0, tiled=True)]
    psum x1 -> x0, waiting for transfers between devices: 82.7 us -> none  [shards(): lax.psum(grad_text.astype(jnp.bfloat16), 'seq').astype(jnp.float32)]
    ppermute x3, waiting for transfers between devices: 100 us -> 30.9 us  [passed_along(): lax.ppermute(value, axis, [(source, source + steps) for source in range(i...]
    ppermute x8 -> x17, waiting for transfers between devices: 112 us -> 162 us  [swap(): return lax.ppermute(value, axis, [(i, i ^ bit) for i in range(count)])]
    psum x1 -> x0, blocking collectives: 41.4 us -> none  [shards(): lax.psum(jnp.stack([gain_one, gain_two, gain_three, bias_one, bias_two, b...]
  transfers between devices with their start and end apart: 26 -> 28, of which waited for: 16 -> 17; matrix products, arithmetic and copies ran while one was open for 18% -> 18% of each run, Pallas kernels for 9% -> 4%
where the time goes in v2:
time: 1550 us; the launch traced here: 1530 us
  waiting for transfers between devices  831 us (54%)
  matrix products  275 us (18%)
  Pallas kernels  136 us (9%)
  starting transfers between devices  132 us (9%)
  local copies, waits for them, and re-layouts  72.3 us (5%)
  other arithmetic  70 us (5%)
  between operations  15.6 us (1%)
    reduce_scatter x3, waiting for transfers between devices, scattered(): lax.psum_scatter(grad.astype(jnp.bfloat16), 'fsdp', scatter_dimension=0,...  293 us
    unnamed x9, waiting for transfers between devices  197 us
    ppermute x17, waiting for transfers between devices, swap(): return lax.ppermute(value, axis, [(i, i ^ bit) for i in range(count)])  162 us
    all_gather x4, waiting for transfers between devices, shards(): row_block = lambda value: lax.all_gather(value, 'fsdp', axis=0, tiled=True)  148 us
    ppermute x17, starting transfers between devices, swap(): return lax.ppermute(value, axis, [(i, i ^ bit) for i in range(count)])  124 us
    dot_general x8, matrix products, matmul(): return jnp.dot(left_side, right_side, preferred_element_type=jnp.float32)  98.7 us
    dot_general x7, matrix products, contract_cols(): lax.dot_general(left_side, right_side, (((1,), (1,)), ((), ())), preferre...  94.8 us
    dot_general x7, matrix products, contract_rows(): lax.dot_general(left_side, right_side, (((0,), (0,)), ((), ())), preferre...  81.6 us
  transfers between devices with their start and end apart: 28, of which 17 were waited for; matrix products, arithmetic and copies ran while one was open for 18% of the time, Pallas kernels for 4%

profile of v2, /device:TPU:0, one launch (start us, length us, event | category | flops | bytes accessed | tf_op | source)
XLA Modules:
  0.0 1532.0 jit_solution(10040390841895523492)
XLA Ops:
  20.8 51.4 %collective-permute-done = bf16[768,1536]{1,0:T(8,128)(2,1)} collective-permute-done((bf16[768,1536]{1,0:T(8,128)(2,1)S(1)}, bf16[768,1536]{1,0:T(8,128)(2,1)}, u32[]{:S(2)}, u32[]{:S(2)}) %collective-permute-start) | collective-permute-done | bytes 2359328 | tf_op jit(solution)/shard_map/ppermute | solution.py:377
  119.9 36.9 %self_attend.1 = (bf16[1536,768]{1,0:T(8,128)(2,1)}, f32[2,4,8,384]{3,2,1,0:T(8,128)}) custom-call(s32[4,4]{1,0:T(4,128)} %pad_add_fusion.bounds, bf16[1536,768]{1,0:T(8,128)(2,1)} %convolution_convert_fusion.8.q_ref, bf16[1536,1536]{1,0:T(8,128)(2,1)} %collective-permute-done.1.kp_ref.vp_ref, bf16[1536,1536]{1,0:T(8,128)(2,1)} %collective-permute-done.1.kp_ref.vp_ref, ...), custom_call_target="tpu_custom_call" | custom-call | flops 36238786560 | bytes 14155776 | tf_op jit(solution)/shard_map/self_attend/pallas_call | solution.py:159
  179.3 37.4 %all-gather.7.cloned.1.call-done = bf16[1536,6144]{1,0:T(8,128)(2,1)} async-done(((bf16[96,6144]{1,0:T(8,128)(2,1)}), bf16[1536,6144]{1,0:T(8,128)(2,1)}) %all-gather.7.cloned.1.call-update) | async-done | bytes 18874384 | tf_op jit(solution)/shard_map/all_gather | solution.py:497
  268.1 53.9 %all-gather.9.cloned.1.call-done = bf16[1536,6144]{1,0:T(8,128)(2,1)} async-done(((bf16[96,6144]{1,0:T(8,128)(2,1)}), bf16[1536,6144]{1,0:T(8,128)(2,1)}) %all-gather.9.cloned.1.call-update) | async-done | bytes 18874384 | tf_op jit(solution)/shard_map/all_gather | solution.py:497
  322.0 27.4 %fusion.3 = (f32[768,6144]{1,0:T(8,128)}, bf16[768,6144]{1,0:T(8,128)(2,1)S(1)}) fusion(bf16[1536,6144]{1,0:T(8,128)(2,1)} %all-gather.9.cloned.1.call-done, f32[768,1536]{1,0:T(8,128)} %copy-done.12, f32[1536]{0:T(1024)S(1)} %copy-done.45, f32[1536]{0:T(1024)S(1)} %get-tuple-element.124, f32[768]{0:T(1024)S(1)} %add_rsqrt_fusion.2, ...), kind=kOutput, calls=%fused_computation.6 | convolution fusion | flops 14548598784 | bytes 51922944 | tf_op jit(solution)/shard_map/dot_general | solution.py:22
  353.0 18.1 %convolution_convert_fusion = bf16[6144,1536]{1,0:T(8,128)(2,1)} fusion(bf16[768,6144]{1,0:T(8,128)(2,1)S(1)} %get-tuple-element.135, bf16[768,1536]{1,0:T(8,128)(2,1)S(1)} %copy-done.17), kind=kOutput, calls=%fused_computation.1 | convolution fusion | flops 14504951808 | bytes 30670848 | tf_op jit(solution)/shard_map/dot_general | solution.py:26
  371.1 51.5 %all-gather.11.cloned.1.call-done = bf16[6144,1536]{1,0:T(8,128)(2,1)} async-done(((bf16[384,1536]{1,0:T(8,128)(2,1)}), bf16[6144,1536]{1,0:T(8,128)(2,1)}) %all-gather.11.cloned.1.call-update) | async-done | bytes 18874384 | tf_op jit(solution)/shard_map/all_gather | solution.py:497
  422.6 24.8 %multiply_convert_fusion = bf16[768,6144]{1,0:T(8,128)(2,1)} fusion(f32[768,6144]{1,0:T(8,128)} %get-tuple-element.27, bf16[768,1536]{1,0:T(8,128)(2,1)S(1)} %copy-done.17, bf16[6144,1536]{1,0:T(8,128)(2,1)} %all-gather.11.cloned.1.call-done), kind=kOutput, calls=%fused_computation.8 | convolution fusion | flops 14504951808 | bytes 49545216 | tf_op jit(solution)/shard_map/dot_general | solution.py:32
  447.3 22.2 %convolution_convert_fusion.1 = bf16[1536,6144]{1,0:T(8,128)(2,1)} fusion(bf16[768,6144]{1,0:T(8,128)(2,1)} %multiply_convert_fusion, f32[768,1536]{1,0:T(8,128)} %copy-done.12, f32[1536]{0:T(1024)S(1)} %copy-done.45, f32[1536]{0:T(1024)S(1)} %get-tuple-element.124, f32[768]{0:T(1024)S(1)} %add_rsqrt_fusion.2, f32[768]{0:T(1024)S(1)} %broadcast_multiply_fusion.8), kind=kOutput, calls=%fused_computation.2 | convolution fusion | flops 14510850048 | bytes 33048576 | tf_op jit(solution)/shard_map/dot_general | solution.py:26
  469.5 24.6 %multiply_reduce_fusion = (f32[1536]{0:T(1024)}, f32[768]{0:T(1024)S(1)}, f32[768]{0:T(1024)S(1)}, f32[1536]{0:T(1024)}, f32[768,1536]{1,0:T(8,128)}) fusion(f32[768,1536]{1,0:T(8,128)} %copy-done.12, f32[768]{0:T(1024)S(1)} %add_rsqrt_fusion.2, f32[768]{0:T(1024)S(1)} %broadcast_multiply_fusion.8, f32[1536]{0:T(1024)S(1)} %get-tuple-element.124, ...), kind=kOutput, calls=%fused_computation.46 | convolution fusion | flops 14506125312 | bytes 37779456 | tf_op jit(solution)/shard_map/dot_general | solution.py:32
  508.9 18.6 %cross_attend_back.1 = (bf16[768,1536]{1,0:T(8,128)(2,1)}, f32[128,1536]{1,0:T(8,128)}, f32[128,1536]{1,0:T(8,128)}) custom-call(bf16[768,1536]{1,0:T(8,128)(2,1)} %fusion.50.q_ref, bf16[768,1536]{1,0:T(8,128)(2,1)} %fusion.53.g_ref, bf16[128,1536]{1,0:T(8,128)(2,1)} %get-tuple-element.148.k_ref, bf16[128,1536]{1,0:T(8,128)(2,1)} %get-tuple-element.147.v_ref, ...), custom_call_target="tpu_custom_call" | custom-call | flops 3019898880 | bytes 7077888 | tf_op jit(solution)/shard_map/cross_attend_back/pallas_call | solution.py:345
  547.9 26.7 %collective-permute-done.4 = bf16[768,768]{1,0:T(8,128)(2,1)S(1)} collective-permute-done((bf16[768,768]{1,0:T(8,128)(2,1)S(1)}, bf16[768,768]{1,0:T(8,128)(2,1)S(1)}, u32[]{:S(2)}, u32[]{:S(2)}) %collective-permute-start.4) | collective-permute-done | bytes 1179680 | tf_op jit(solution)/shard_map/ppermute | solution.py:377
  576.7 62.7 %self_attend_back.1 = (bf16[1536,768]{1,0:T(8,128)(2,1)}, bf16[1536,768]{1,0:T(8,128)(2,1)}, bf16[1536,768]{1,0:T(8,128)(2,1)}, bf16[1536,768]{1,0:T(8,128)(2,1)}, bf16[1536,768]{1,0:T(8,128)(2,1)}) custom-call(s32[4,4]{1,0:T(4,128)} %pad_add_fusion.bounds, bf16[1536,768]{1,0:T(8,128)(2,1)} %convolution_convert_fusion.8.q_ref, ...), custom_call_target="tpu_custom_call" | custom-call | flops 72477573120 | bytes 23592960 | tf_op jit(solution)/shard_map/self_attend_back/pallas_call | solution.py:257
  642.5 30.9 %collective-permute-done.6 = bf16[1536,768]{1,0:T(8,128)(2,1)S(1)} collective-permute-done((bf16[1536,768]{1,0:T(8,128)(2,1)}, bf16[1536,768]{1,0:T(8,128)(2,1)S(1)}, u32[]{:S(2)}, u32[]{:S(2)}) %collective-permute-start.6) | collective-permute-done | bytes 2359328 | tf_op jit(solution)/shard_map/ppermute | solution.py:383
  679.1 18.6 %convolution_convert_fusion.2 = bf16[1536,2304]{1,0:T(8,128)(2,1)} fusion(bf16[1536,768]{1,0:T(8,128)(2,1)} %add_convert_fusion, bf16[1536,768]{1,0:T(8,128)(2,1)} %add_convert_fusion.1, bf16[1536,768]{1,0:T(8,128)(2,1)} %get-tuple-element.31, f32[1536]{0:T(1024)S(1)} %copy-done.44, f32[1536]{0:T(1024)S(1)} %copy-done.29, f32[1536]{0:T(1024)S(1)} %copy-done.51, ...), kind=kOutput, calls=%fused_computation.13 | convolution fusion | flops 10917642240 | bytes 18898944 | tf_op jit(solution)/shard_map/dot_general | solution.py:26
  737.9 24.8 %copy.117 = bf16[1536,6144]{1,0:T(8,128)(2,1)} copy(bf16[1536,6144]{0,1:T(8,128)(2,1)} %pad_maximum_fusion) | data formatting | bytes 37748736
  795.6 19.2 %collective-permute-done.7 = bf16[768,1536]{1,0:T(8,128)(2,1)} collective-permute-done((bf16[768,1536]{1,0:T(8,128)(2,1)}, bf16[768,1536]{1,0:T(8,128)(2,1)}, u32[]{:S(2)}, u32[]{:S(2)}) %collective-permute-start.7) | collective-permute-done | bytes 2359328 | tf_op jit(solution)/shard_map/ppermute | solution.py:377
  823.9 51.7 %collective-permute-start.15 = (f32[6,1536]{1,0:T(8,128)}, f32[6,1536]{1,0:T(8,128)S(1)}, u32[]{:S(2)}, u32[]{:S(2)}) collective-permute-start(f32[6,1536]{1,0:T(8,128)} %stack.61), channel_id=1, source_target_pairs={{0,2},{2,0},{4,6},{6,4},{8,10},{10,8},{12,14},{14,12},{16,18},{18,... | collective-permute-start | bytes 110600 | tf_op jit(solution)/shard_map/ppermute | solution.py:377
  875.6 22.3 %add_convert_fusion.2 = bf16[768,1536]{1,0:T(8,128)(2,1)} fusion(f32[768,1536]{1,0:T(8,128)} %copy-done.12, bf16[768,6144]{1,0:T(8,128)(2,1)} %copy-done.53, bf16[6144,1536]{1,0:T(8,128)(2,1)} %all-gather.11.cloned.1.call-done), kind=kOutput, calls=%fused_computation.56 | convolution fusion | flops 14497873920 | bytes 35389440 | tf_op jit(solution)/shard_map/dot_general | solution.py:22
  897.9 31.3 %collective-permute-start.16 = (f32[6,1536]{1,0:T(8,128)S(1)}, f32[6,1536]{1,0:T(8,128)S(1)}, u32[]{:S(2)}, u32[]{:S(2)}) collective-permute-start(f32[6,1536]{1,0:T(8,128)S(1)} %add.264), channel_id=1, source_target_pairs={{0,4},{2,6},{4,0},{6,2},{8,12},{10,14},{12,8},{14,10},{16,20},{18,... | collective-permute-start | bytes 110600 | tf_op jit(solution)/shard_map/ppermute | solution.py:377
  976.0 99.1 %reduce-scatter.9.cloned.1.call-done = bf16[96,6144]{1,0:T(8,128)(2,1)} async-done(((bf16[1536,6144]{1,0:T(8,128)(2,1)}), bf16[96,6144]{1,0:T(8,128)(2,1)}) %reduce-scatter.9.cloned.1.call-update) | async-done | bytes 1179664 | tf_op jit(solution)/shard_map/reduce_scatter | solution.py:442
  1079.0 194.6 %reduce-scatter.13.cloned.1.call-done = bf16[96,6144]{1,0:T(8,128)(2,1)} async-done(((bf16[1536,6144]{1,0:T(8,128)(2,1)}), bf16[96,6144]{1,0:T(8,128)(2,1)}) %reduce-scatter.13.cloned.1.call-update) | async-done | bytes 1179664
  1278.9 193.5 %reduce-scatter.11.cloned.1.call-done = bf16[384,1536]{1,0:T(8,128)(2,1)} async-done(((bf16[6144,1536]{1,0:T(8,128)(2,1)}), bf16[384,1536]{1,0:T(8,128)(2,1)}) %reduce-scatter.11.cloned.1.call-update) | async-done | bytes 1179664 | tf_op jit(solution)/shard_map/reduce_scatter | solution.py:442
  1479.6 22.0 %collective-permute-done.14 = bf16[384,1536]{1,0:T(8,128)(2,1)} collective-permute-done((bf16[384,1536]{1,0:T(8,128)(2,1)}, bf16[384,1536]{1,0:T(8,128)(2,1)}, u32[]{:S(2)}, u32[]{:S(2)}) %collective-permute-start.14) | collective-permute-done | bytes 1179680 | tf_op jit(solution)/shard_map/ppermute | solution.py:377
  (300 shorter events, 352.4 us)
Async XLA Ops:
  7.2 76.3 %all-gather.5.cloned.1.call-start = ((), (), s32[]{:S(2)}) async-start(), calls=%async_computation.4 | async-start | bytes 7938048 | tf_op jit(solution)/shard_map/all_gather | solution.py:497
  11.6 205.1 %all-gather.7.cloned.1.call-start = ((), (), s32[]{:S(2)}) async-start(), calls=%async_computation.5 | async-start | bytes 20054016 | tf_op jit(solution)/shard_map/all_gather | solution.py:497
  16.4 305.7 %all-gather.9.cloned.1.call-start = ((), (), s32[]{:S(2)}) async-start(), calls=%async_computation.6 | async-start | bytes 20054016 | tf_op jit(solution)/shard_map/all_gather | solution.py:497
  17.1 405.4 %all-gather.11.cloned.1.call-start = ((), (), s32[]{:S(2)}) async-start(), calls=%async_computation.7 | async-start | bytes 20054016 | tf_op jit(solution)/shard_map/all_gather | solution.py:497
  17.7 948.6 %reduce-scatter.7.cloned.1.call-start = ((), (), s32[]{:S(2)}) async-start(), calls=%async_computation.8 | async-start | bytes 7520256 | tf_op jit(solution)/shard_map/reduce_scatter | solution.py:442
  17.7 54.4 %collective-permute-start = (bf16[768,1536]{1,0:T(8,128)(2,1)S(1)}, bf16[768,1536]{1,0:T(8,128)(2,1)}, u32[]{:S(2)}, u32[]{:S(2)}) collective-permute-start(bf16[768,1536]{1,0:T(8,128)(2,1)S(1)} %copy-done.1), channel_id=1, source_target_pairs={{0,1},{1,0},{2,3},{3,2},{4,5},{5,4},{6,7},{7,6},{8,9},{9,8},{10,11... | collective-permute-start | bytes 7077896 | tf_op jit(solution)/shard_map/ppermute | solution.py:377
  100.8 19.2 %collective-permute-start.1 = (bf16[1536,1536]{1,0:T(8,128)(2,1)}, bf16[1536,1536]{1,0:T(8,128)(2,1)}, u32[]{:S(2)}, u32[]{:S(2)}) collective-permute-start(bf16[1536,1536]{1,0:T(8,128)(2,1)} %convolution_convert_fusion.7.ko_ref.vo_ref), channel_id=1, source_target_pairs={{0,2},{2,4},{4,6},{6,8},{8,10},{10,12},{12,14},{14,16},{16,18},{18... | collective-permute-start | bytes 14155784 | tf_op jit(solution)/shard_map/ppermute | solution.py:383
  546.4 28.2 %collective-permute-start.4 = (bf16[768,768]{1,0:T(8,128)(2,1)S(1)}, bf16[768,768]{1,0:T(8,128)(2,1)S(1)}, u32[]{:S(2)}, u32[]{:S(2)}) collective-permute-start(bf16[768,768]{1,0:T(8,128)(2,1)S(1)} %constant_dynamic-slice_fusion), channel_id=1, source_target_pairs={{0,1},{1,0},{2,3},{3,2},{4,5},{5,4},{6,7},{7,6},{8,9},{9,8},{10,11... | collective-permute-start | bytes 3538952 | tf_op jit(solution)/shard_map/ppermute | solution.py:377
  639.4 34.0 %collective-permute-start.6 = (bf16[1536,768]{1,0:T(8,128)(2,1)}, bf16[1536,768]{1,0:T(8,128)(2,1)S(1)}, u32[]{:S(2)}, u32[]{:S(2)}) collective-permute-start(bf16[1536,768]{1,0:T(8,128)(2,1)} %get-tuple-element.35), channel_id=1, source_target_pairs={{2,0},{4,2},{6,4},{8,6},{10,8},{12,10},{14,12},{16,14},{18,16},{20... | collective-permute-start | bytes 7077896 | tf_op jit(solution)/shard_map/ppermute | solution.py:383
  640.8 36.3 %collective-permute-start.5 = (bf16[1536,768]{1,0:T(8,128)(2,1)}, bf16[1536,768]{1,0:T(8,128)(2,1)S(1)}, u32[]{:S(2)}, u32[]{:S(2)}) collective-permute-start(bf16[1536,768]{1,0:T(8,128)(2,1)} %get-tuple-element.33), channel_id=1, source_target_pairs={{2,0},{4,2},{6,4},{8,6},{10,8},{12,10},{14,12},{16,14},{18,16},{20... | collective-permute-start | bytes 7077896 | tf_op jit(solution)/shard_map/ppermute | solution.py:383
  697.7 377.4 %reduce-scatter.9.cloned.1.call-start = ((), (), s32[]{:S(2)}) async-start(), calls=%async_computation.9 | async-start | bytes 20054016 | tf_op jit(solution)/shard_map/reduce_scatter | solution.py:442
  698.3 575.4 %reduce-scatter.13.cloned.1.call-start = ((), (), s32[]{:S(2)}) async-start(), calls=%async_computation.11 | async-start | bytes 20054016
  699.1 23.1 %collective-permute-start.8 = (bf16[128,2,768]{2,0,1:T(8,128)(2,1)S(1)}, bf16[128,2,768]{2,0,1:T(8,128)(2,1)S(1)}, u32[]{:S(2)}, u32[]{:S(2)}) collective-permute-start(bf16[128,2,768]{2,0,1:T(8,128)(2,1)S(1)} %fusion.69), channel_id=1, source_target_pairs={{0,1},{1,0},{2,3},{3,2},{4,5},{5,4},{6,7},{7,6},{8,9},{9,8},{10,11... | collective-permute-start | bytes 1179656 | tf_op jit(solution)/shard_map/ppermute | solution.py:377
  762.7 709.7 %reduce-scatter.11.cloned.1.call-start = ((), (), s32[]{:S(2)}) async-start(), calls=%async_computation.10 | async-start | bytes 20054016 | tf_op jit(solution)/shard_map/reduce_scatter | solution.py:442
  785.6 29.2 %collective-permute-start.7 = (bf16[768,1536]{1,0:T(8,128)(2,1)}, bf16[768,1536]{1,0:T(8,128)(2,1)}, u32[]{:S(2)}, u32[]{:S(2)}) collective-permute-start(bf16[768,1536]{1,0:T(8,128)(2,1)} %dynamic-slice_convert_fusion), channel_id=1, source_target_pairs={{0,1},{1,0},{2,3},{3,2},{4,5},{5,4},{6,7},{7,6},{8,9},{9,8},{10,11... | collective-permute-start | bytes 7077896 | tf_op jit(solution)/shard_map/ppermute | solution.py:377
  793.9 135.3 %collective-permute-start.9 = (bf16[128,1536]{1,0:T(8,128)(2,1)S(1)}, bf16[128,1536]{1,0:T(8,128)(2,1)S(1)}, u32[]{:S(2)}, u32[]{:S(2)}) collective-permute-start(bf16[128,1536]{1,0:T(8,128)(2,1)S(1)} %fusion.59), channel_id=1, source_target_pairs={{0,1},{1,0},{2,3},{3,2},{4,5},{5,4},{6,7},{7,6},{8,9},{9,8},{10,11... | collective-permute-start | bytes 1179656 | tf_op jit(solution)/shard_map/ppermute | solution.py:377
  823.9 74.0 %collective-permute-start.15 = (f32[6,1536]{1,0:T(8,128)}, f32[6,1536]{1,0:T(8,128)S(1)}, u32[]{:S(2)}, u32[]{:S(2)}) collective-permute-start(f32[6,1536]{1,0:T(8,128)} %stack.61), channel_id=1, source_target_pairs={{0,2},{2,0},{4,6},{6,4},{8,10},{10,8},{12,14},{14,12},{16,18},{18,... | collective-permute-start | bytes 110600 | tf_op jit(solution)/shard_map/ppermute | solution.py:377
  897.9 34.3 %collective-permute-start.16 = (f32[6,1536]{1,0:T(8,128)S(1)}, f32[6,1536]{1,0:T(8,128)S(1)}, u32[]{:S(2)}, u32[]{:S(2)}) collective-permute-start(f32[6,1536]{1,0:T(8,128)S(1)} %add.264), channel_id=1, source_target_pairs={{0,4},{2,6},{4,0},{6,2},{8,12},{10,14},{12,8},{14,10},{16,20},{18,... | collective-permute-start | bytes 110600 | tf_op jit(solution)/shard_map/ppermute | solution.py:377
  932.2 21.4 %collective-permute-start.17 = (f32[6,1536]{1,0:T(8,128)S(1)}, f32[6,1536]{1,0:T(8,128)S(1)}, u32[]{:S(2)}, u32[]{:S(2)}) collective-permute-start(f32[6,1536]{1,0:T(8,128)S(1)} %add.265), channel_id=1, source_target_pairs={{0,8},{2,10},{4,12},{6,14},{8,0},{10,2},{12,4},{14,6},{16,24},{18,... | collective-permute-start | bytes 110600 | tf_op jit(solution)/shard_map/ppermute | solution.py:377
  968.1 109.3 %collective-permute-start.10 = (bf16[96,3,768]{2,0,1:T(8,128)(2,1)}, bf16[96,3,768]{2,0,1:T(8,128)(2,1)}, u32[]{:S(2)}, u32[]{:S(2)}) collective-permute-start(bf16[96,3,768]{2,0,1:T(8,128)(2,1)} %bitcast.56), channel_id=1, source_target_pairs={{0,1},{1,0},{2,3},{3,2},{4,5},{5,4},{6,7},{7,6},{8,9},{9,8},{10,11... | collective-permute-start | bytes 1327112 | tf_op jit(solution)/shard_map/ppermute | solution.py:377
  1075.1 401.5 %collective-permute-start.13 = (bf16[96,6144]{1,0:T(8,128)(2,1)}, bf16[96,6144]{1,0:T(8,128)(2,1)}, u32[]{:S(2)}, u32[]{:S(2)}) collective-permute-start(bf16[96,6144]{1,0:T(8,128)(2,1)} %reduce-scatter.9.cloned.1.call-done), channel_id=1, source_target_pairs={{0,1},{1,0},{2,3},{3,2},{4,5},{5,4},{6,7},{7,6},{8,9},{9,8},{10,11... | collective-permute-start | bytes 3538952 | tf_op jit(solution)/shard_map/ppermute | solution.py:377
  1275.0 200.2 %collective-permute-start.12 = (bf16[96,2,768]{2,0,1:T(8,128)(2,1)S(1)}, bf16[96,2,768]{2,0,1:T(8,128)(2,1)S(1)}, u32[]{:S(2)}, u32[]{:S(2)}) collective-permute-start(bf16[96,2,768]{2,0,1:T(8,128)(2,1)S(1)} %copy.106), channel_id=1, source_target_pairs={{0,1},{1,0},{2,3},{3,2},{4,5},{5,4},{6,7},{7,6},{8,9},{9,8},{10,11... | collective-permute-start | bytes 884744 | tf_op jit(solution)/shard_map/ppermute | solution.py:377
  1472.4 29.2 %collective-permute-start.14 = (bf16[384,1536]{1,0:T(8,128)(2,1)}, bf16[384,1536]{1,0:T(8,128)(2,1)}, u32[]{:S(2)}, u32[]{:S(2)}) collective-permute-start(bf16[384,1536]{1,0:T(8,128)(2,1)} %reduce-scatter.11.cloned.1.call-done), channel_id=1, source_target_pairs={{0,1},{1,0},{2,3},{3,2},{4,5},{5,4},{6,7},{7,6},{8,9},{9,8},{10,11... | collective-permute-start | bytes 3538952 | tf_op jit(solution)/shard_map/ppermute | solution.py:377
  1473.9 45.5 %collective-permute-start.11 = (bf16[96,4608]{1,0:T(8,128)(2,1)S(1)}, bf16[96,4608]{1,0:T(8,128)(2,1)}, u32[]{:S(2)}, u32[]{:S(2)}) collective-permute-start(bf16[96,4608]{1,0:T(8,128)(2,1)S(1)} %slice.159), channel_id=1, source_target_pairs={{0,1},{1,0},{2,3},{3,2},{4,5},{5,4},{6,7},{7,6},{8,9},{9,8},{10,11... | collective-permute-start | bytes 2654216 | tf_op jit(solution)/shard_map/ppermute | solution.py:377
  (66 other events, 1716.7 us)
Sparse Core Ops, SparseCore 0:
  11.7 71.7 all-gather.4
  85.7 130.9 all-gather.6
  218.3 103.7 all-gather.8
  323.5 99.0 all-gather.10
  697.8 176.3 reduce-scatter.6
  878.7 196.3 reduce-scatter.8
  1079.8 193.8 reduce-scatter.12
  1278.3 194.0 reduce-scatter.10

commit v3 on v2

--- a/solution.py
+++ b/solution.py
@@ -37,14 +37,13 @@
 TILE = 384
 
 
-def block_bounds(starts, reach):
-    rows = starts.shape[0]
-    first = starts[::TILE]
-    last = starts[TILE - 1 :: TILE]
-    row0 = reach + jnp.arange(rows // TILE, dtype=jnp.int32) * TILE
-    low = first // TILE
-    high = (row0 + TILE - 1) // TILE + 1
-    free_low = jnp.minimum(jnp.maximum((last + TILE - 1) // TILE, low), high)
+def tile_bounds(starts, reach, base, kv_rows):
+    count = kv_rows // TILE
+    first, last = starts[::TILE] - base, starts[TILE - 1 :: TILE] - base
+    row0 = reach - base + jnp.arange(first.shape[0], dtype=jnp.int32) * TILE
+    low = jnp.clip(first // TILE, 0, count)
+    high = jnp.clip((row0 + TILE - 1) // TILE + 1, low, count)
+    free_low = jnp.clip((last + TILE - 1) // TILE, low, high)
     free_high = jnp.clip((row0 + 1) // TILE, free_low, high)
     return jnp.stack([low, free_low, free_high, high], axis=1)
 
@@ -63,8 +62,8 @@
     return slice(p * PAIR, (p + 1) * PAIR)
 
 
-def tile_allowed(j, row0, starts):
-    at = j * TILE + lax.broadcasted_iota(jnp.int32, (TILE, TILE), 0)
+def tile_allowed(col0, row0, starts):
+    at = col0 + lax.broadcasted_iota(jnp.int32, (TILE, TILE), 0)
     row = row0 + lax.broadcasted_iota(jnp.int32, (TILE, TILE), 1)
     return (at >= starts) & (at <= row)
 
@@ -76,22 +75,20 @@
     return lax.fori_loop(free_high, high, functools.partial(step, True), state)
 
 
-def attend_kernel(
-    bounds, q_ref, kp_ref, vp_ref, ko_ref, vo_ref, start_ref, o_ref, lse_ref, k_all, v_t, *, reach, pairs
-):
+def attend_kernel(bounds, q_ref, k_ref, v_ref, start_ref, *refs, reach, base, pairs, ends):
     i = pl.program_id(1)
+    if ends:
+        before_ref, o_ref, lse_ref, v_t = refs
+    else:
+        after_ref, v_t = refs
 
     @pl.when(i == 0)
     def _():
-        k_all[:reach] = kp_ref[...]
-        k_all[reach:] = ko_ref[...]
         for p in range(pairs):
-            for ref, begin in ((vp_ref, 0), (vo_ref, reach)):
-                end = begin + ref.shape[0]
-                turned = ref[:, lanes(p)].T
-                for h in range(2):
-                    v_t[2 * p + h, :HEAD, begin:end] = turned[h * HEAD : (h + 1) * HEAD]
-                    v_t[2 * p + h, HEAD:, begin:end] = jnp.ones((16, end - begin), jnp.bfloat16)
+            turned = v_ref[:, lanes(p)].T
+            for h in range(2):
+                v_t[2 * p + h, :HEAD] = turned[h * HEAD : (h + 1) * HEAD]
+                v_t[2 * p + h, HEAD:] = jnp.ones((16, turned.shape[1]), jnp.bfloat16)
 
     halves = []
     for p in range(pairs):
@@ -101,10 +98,10 @@
     def step(masked, j, carried):
         rows = pl.ds(pl.multiple_of(j * TILE, TILE), TILE)
         if masked:
-            allowed = tile_allowed(j, reach + i * TILE, starts)
+            allowed = tile_allowed(base + j * TILE, reach + i * TILE, starts)
         scores = []
         for n in range(2 * pairs):
-            s = contract_cols(k_all[rows, lanes(n // 2)], halves[n])
+            s = contract_cols(k_ref[rows, lanes(n // 2)], halves[n])
             scores.append(jnp.where(allowed, s, NEG) if masked else s)
         out = []
         for n, (top, total) in enumerate(carried):
@@ -114,8 +111,17 @@
             out.append((new_top, total))
         return tuple(out)
 
-    nothing = (jnp.full((1, TILE), NEG, jnp.float32), jnp.zeros((HEAD + 16, TILE), jnp.float32))
-    state = over_tiles(bounds, i, step, (nothing,) * (2 * pairs))
+    if ends:
+        state = tuple((before_ref[0, 0, n, HEAD + 8 : HEAD + 9], before_ref[0, 0, n]) for n in range(2 * pairs))
+    else:
+        nothing = (jnp.full((1, TILE), NEG, jnp.float32), jnp.zeros((HEAD + 16, TILE), jnp.float32))
+        state = (nothing,) * (2 * pairs)
+    state = over_tiles(bounds, i, step, state)
+    if not ends:
+        for n, (top, total) in enumerate(state):
+            after_ref[0, 0, n, : HEAD + 8] = total[: HEAD + 8]
+            after_ref[0, 0, n, HEAD + 8 :] = jnp.broadcast_to(top, (8, TILE))
+        return
     for p in range(pairs):
         outs = []
         for n in (2 * p, 2 * p + 1):
@@ -126,67 +132,61 @@
         o_ref[:, lanes(p)] = jnp.concatenate(outs, axis=0).T.astype(o_ref.dtype)
 
 
-def attend_specs(rows, reach, width):
+def attend_specs(rows, kv_rows, width):
     pairs = pairs_a_step(width)
     wide = pairs * PAIR
     steps = width // wide
     block = pl.BlockSpec((TILE, wide), lambda p, i, b: (i, p))
-    kv = [
-        pl.BlockSpec((reach, wide), lambda p, i, b: (0, p)),
-        pl.BlockSpec((reach, wide), lambda p, i, b: (0, steps + p)),
-        pl.BlockSpec((rows, wide), lambda p, i, b: (0, p)),
-        pl.BlockSpec((rows, wide), lambda p, i, b: (0, steps + p)),
-    ]
-    logs = pl.BlockSpec((1, 1, 8, TILE), lambda p, i, b: (p, i, 0, 0))
+    keys = pl.BlockSpec((kv_rows, wide), lambda p, i, b: (0, p))
+    values = pl.BlockSpec((kv_rows, wide), lambda p, i, b: (0, steps + p))
+    by_tile = lambda *shape: pl.BlockSpec((1, 1, *shape, TILE), lambda p, i, b: (p, i, *[0] * len(shape), 0))
     starts = pl.BlockSpec((1, 1, TILE), lambda p, i, b: (i, 0, 0))
-    return pairs, wide, (steps, rows // TILE), block, kv, logs, starts
-
-
-def self_attend(q, kv_before, kv_own, starts):
+    return pairs, wide, (steps, rows // TILE), block, keys, values, by_tile, starts
+
+
+def self_attend(q, kv, starts, reach, base, before=None):
     rows, width = q.shape
-    reach = kv_before.shape[0]
-    pairs, wide, grid, block, kv, logs, start_block = attend_specs(rows, reach, width)
+    kv_rows = kv.shape[0]
+    ends = before is not None
+    pairs, wide, grid, block, keys, values, by_tile, start_block = attend_specs(rows, kv_rows, width)
+    state = by_tile(2 * pairs, HEAD + 16)
+    state_shape = jax.ShapeDtypeStruct((*grid, 2 * pairs, HEAD + 16, TILE), jnp.float32)
     spec = pltpu.PrefetchScalarGridSpec(
         num_scalar_prefetch=1,
         grid=grid,
-        in_specs=[block, *kv, start_block],
-        out_specs=[block, logs],
-        scratch_shapes=[
-            pltpu.VMEM((reach + rows, wide), jnp.bfloat16),
-            pltpu.VMEM((2 * pairs, HEAD + 16, reach + rows), jnp.bfloat16),
-        ],
+        in_specs=[block, keys, values, start_block] + [state] * ends,
+        out_specs=[block, by_tile(8)] if ends else state,
+        scratch_shapes=[pltpu.VMEM((2 * pairs, HEAD + 16, kv_rows), jnp.bfloat16)],
     )
     return pl.pallas_call(
-        functools.partial(attend_kernel, reach=reach, pairs=pairs),
+        functools.partial(attend_kernel, reach=reach, base=base, pairs=pairs, ends=ends),
         grid_spec=spec,
         out_shape=[
             jax.ShapeDtypeStruct((rows, width), jnp.bfloat16),
             jax.ShapeDtypeStruct((*grid, 8, TILE), jnp.float32),
-        ],
+        ]
+        if ends
+        else state_shape,
         compiler_params=pltpu.CompilerParams(vmem_limit_bytes=VMEM_BYTES),
         cost_estimate=pl.CostEstimate(
-            flops=20 * rows * rows * width,
-            bytes_accessed=12 * rows * width,
-            transcendentals=rows * rows * width // HEAD,
+            flops=10 * rows * kv_rows * width,
+            bytes_accessed=16 * rows * width,
+            transcendentals=rows * kv_rows * width // HEAD // 2,
         ),
         name="self_attend",
-    )(block_bounds(starts, reach), q, kv_before, kv_before, kv_own, kv_own, starts.reshape(-1, 1, TILE))
-
-
-def attend_back_kernel(
-    bounds, q_ref, g_ref, o_ref, lse_ref, kp_ref, vp_ref, ko_ref, vo_ref, start_ref,
-    dq_ref, dkp_ref, dvp_ref, dko_ref, dvo_ref, k_all, v_all, dk_sum, dv_sum, k_t, *, reach, pairs
-):
+    )(tile_bounds(starts, reach, base, kv_rows), q, kv, kv, starts.reshape(-1, 1, TILE), *([before] if ends else []))
+
+
+def attend_back_kernel(bounds, q_ref, g_ref, o_ref, lse_ref, k_ref, v_ref, start_ref, *refs, reach, base, pairs, ends):
     i = pl.program_id(1)
+    if ends:
+        before_ref, dq_ref, dk_ref, dv_ref, dk_sum, dv_sum, k_t = refs
+    else:
+        after_ref, dk_ref, dv_ref, dk_sum, dv_sum, k_t = refs
 
     @pl.when(i == 0)
     def _():
-        k_all[:reach] = kp_ref[...]
-        k_all[reach:] = ko_ref[...]
-        v_all[:reach] = vp_ref[...]
-        v_all[reach:] = vo_ref[...]
-        k_t[:, :reach] = kp_ref[...].T
-        k_t[:, reach:] = ko_ref[...].T
+        k_t[...] = k_ref[...].T
         dk_sum[...] = jnp.zeros_like(dk_sum)
         dv_sum[...] = jnp.zeros_like(dv_sum)
 
@@ -204,10 +204,10 @@
     def step(masked, j, carried):
         rows = pl.ds(pl.multiple_of(j * TILE, TILE), TILE)
         if masked:
-            allowed = tile_allowed(j, reach + i * TILE, starts)
+            allowed = tile_allowed(base + j * TILE, reach + i * TILE, starts)
         out = []
         for p in range(pairs):
-            keys, values = k_all[rows, lanes(p)], v_all[rows, lanes(p)]
+            keys, values = k_ref[rows, lanes(p)], v_ref[rows, lanes(p)]
             dks, dvs = [], []
             for n in (2 * p, 2 * p + 1):
                 s = contract_cols(keys, queries[n])
@@ -223,51 +223,61 @@
             dk_sum[rows, lanes(p)] += dks[0] + dks[1]
         return tuple(out)
 
-    state = over_tiles(bounds, i, step, (jnp.zeros((HEAD, TILE), jnp.float32),) * (2 * pairs))
-    for p in range(pairs):
-        turned = jnp.concatenate([state[2 * p], state[2 * p + 1]], axis=0).T
-        dq_ref[:, lanes(p)] = (turned * SCALE).astype(dq_ref.dtype)
+    if ends:
+        state = tuple(before_ref[0, 0, n] for n in range(2 * pairs))
+    else:
+        state = (jnp.zeros((HEAD, TILE), jnp.float32),) * (2 * pairs)
+    state = over_tiles(bounds, i, step, state)
+    if ends:
+        for p in range(pairs):
+            turned = jnp.concatenate([state[2 * p], state[2 * p + 1]], axis=0).T
+            dq_ref[:, lanes(p)] = (turned * SCALE).astype(dq_ref.dtype)
+    else:
+        for n in range(2 * pairs):
+            after_ref[0, 0, n] = state[n]
 
     @pl.when(i == pl.num_programs(1) - 1)
     def _():
-        dkp_ref[...] = dk_sum[:reach].astype(dkp_ref.dtype)
-        dvp_ref[...] = dv_sum[:reach].astype(dvp_ref.dtype)
-        dko_ref[...] = dk_sum[reach:].astype(dko_ref.dtype)
-        dvo_ref[...] = dv_sum[reach:].astype(dvo_ref.dtype)
-
-
-def self_attend_back(q, grad, o, lse, kv_before, kv_own, starts):
+        dk_ref[...] = dk_sum[...].astype(dk_ref.dtype)
+        dv_ref[...] = dv_sum[...].astype(dv_ref.dtype)
+
+
+def self_attend_back(q, grad, o, lse, kv, starts, reach, base, before=None):
     rows, width = q.shape
-    reach = kv_before.shape[0]
-    pairs, wide, grid, block, kv, logs, start_block = attend_specs(rows, reach, width)
+    kv_rows = kv.shape[0]
+    ends = before is not None
+    pairs, wide, grid, block, keys, values, by_tile, start_block = attend_specs(rows, kv_rows, width)
+    state = by_tile(2 * pairs, HEAD)
+    shape = lambda n: jax.ShapeDtypeStruct((n, width), jnp.bfloat16)
     spec = pltpu.PrefetchScalarGridSpec(
         num_scalar_prefetch=1,
         grid=grid,
-        in_specs=[block, block, block, logs, *kv, start_block],
-        out_specs=[block, kv[0], kv[0], kv[2], kv[2]],
+        in_specs=[block, block, block, by_tile(8), keys, values, start_block] + [state] * ends,
+        out_specs=[block if ends else state, keys, keys],
         scratch_shapes=[
-            pltpu.VMEM((reach + rows, wide), jnp.bfloat16),
-            pltpu.VMEM((reach + rows, wide), jnp.bfloat16),
-            pltpu.VMEM((reach + rows, wide), jnp.float32),
-            pltpu.VMEM((reach + rows, wide), jnp.float32),
-            pltpu.VMEM((wide, reach + rows), jnp.bfloat16),
+            pltpu.VMEM((kv_rows, wide), jnp.float32),
+            pltpu.VMEM((kv_rows, wide), jnp.float32),
+            pltpu.VMEM((wide, kv_rows), jnp.bfloat16),
         ],
     )
-    shape = lambda n: jax.ShapeDtypeStruct((n, width), jnp.bfloat16)
     return pl.pallas_call(
-        functools.partial(attend_back_kernel, reach=reach, pairs=pairs),
+        functools.partial(attend_back_kernel, reach=reach, base=base, pairs=pairs, ends=ends),
         grid_spec=spec,
-        out_shape=[shape(rows), shape(reach), shape(reach), shape(rows), shape(rows)],
+        out_shape=[
+            shape(rows) if ends else jax.ShapeDtypeStruct((*grid, 2 * pairs, HEAD, TILE), jnp.float32),
+            shape(kv_rows),
+            shape(kv_rows),
+        ],
         compiler_params=pltpu.CompilerParams(vmem_limit_bytes=VMEM_BYTES),
         cost_estimate=pl.CostEstimate(
-            flops=40 * rows * rows * width,
+            flops=20 * rows * kv_rows * width,
             bytes_accessed=20 * rows * width,
-            transcendentals=rows * rows * width // HEAD,
+            transcendentals=rows * kv_rows * width // HEAD // 2,
         ),
         name="self_attend_back",
     )(
-        block_bounds(starts, reach), q, grad, o, lse, kv_before, kv_before, kv_own, kv_own,
-        starts.reshape(-1, 1, TILE),
+        tile_bounds(starts, reach, base, kv_rows), q, grad, o, lse, kv, kv, starts.reshape(-1, 1, TILE),
+        *([before] if ends else []),
     )
 
 
@@ -453,13 +463,40 @@
     return gathered(split, 2).reshape(part.shape[0], -1).astype(jnp.float32)
 
 
-def everywhere(value):
-    for axis in ("fsdp", "seq"):
-        bit = 1
-        while bit < lax.axis_size(axis):
-            value = value + swap(value, axis, bit)
-            bit *= 2
-    return value
+def four_sums(lefts, rights):
+    chip, core = lax.axis_index("fsdp") // 2, lax.axis_index("fsdp") % 2
+    seq_index, seq_count = lax.axis_index("seq"), lax.axis_size("seq")
+    chips = lax.axis_size("fsdp") // 2
+    if seq_count != 2:
+        sums = [[scattered(contract_rows(a, b)) for a, b in zip(*each)] for each in zip(lefts, rights)]
+        return [[whole(part) for part in each] for each in sums]
+
+    def products(place):
+        pick = lambda parts: jnp.stack([jnp.where(place == 0, a, b) for a, b in zip(*parts)])
+        return jnp.einsum("kta,ktb->kab", pick(lefts), pick(rights), preferred_element_type=jnp.float32).astype(
+            jnp.bfloat16
+        )
+
+    take = lambda value, place, dim=0: lax.dynamic_index_in_dim(value, place, dim, keepdims=False).astype(jnp.float32)
+    sent = swap(products(1 - core), "fsdp", 1)
+    kept = products(core)
+    other = swap((take(kept, 1 - seq_index) + take(sent, 1 - seq_index)).astype(jnp.bfloat16), "seq", 1)
+    total = take(kept, seq_index) + take(sent, seq_index) + other.astype(jnp.float32)
+    bit, at = 2, chip
+    total = total.reshape(chips, -1, total.shape[-1])
+    while chips > 1:
+        chips //= 2
+        total = total.astype(jnp.bfloat16).reshape(chips, 2, *total.shape[1:])
+        more = swap(take(total, 1 - at % 2, 1).astype(jnp.bfloat16), "fsdp", bit)
+        total = take(total, at % 2, 1) + more.astype(jnp.float32)
+        bit, at = bit * 2, at // 2
+    total = total.astype(jnp.bfloat16).reshape(2, -1, total.shape[-1])
+    mine = take(total, core).astype(jnp.bfloat16)
+    theirs = swap(take(total, 1 - core).astype(jnp.bfloat16), "fsdp", 1)
+    pair = jnp.stack([jnp.where(core == 0, mine, theirs), jnp.where(core == 0, theirs, mine)])
+    beside = swap(pair, "seq", 1)
+    by_seq = [jnp.where(seq_index == 0, pair, beside), jnp.where(seq_index == 0, beside, pair)]
+    return [[by_seq[s][c].astype(jnp.float32) for s in range(2)] for c in range(2)]
 
 
 def clip_starts(segments, group_index, group_rows):
@@ -521,7 +558,8 @@
     if head_cols % PAIR:
         pad_kv = lambda kv: jnp.concatenate([paired(kv[:, :head_cols]), paired(kv[:, head_cols:])], axis=1)
         queries, kv_own, kv_before = paired(queries), pad_kv(kv_own), pad_kv(kv_before)
-    heads_out, log_totals = self_attend(queries, kv_before, kv_own, starts)
+    heads_state = self_attend(queries, kv_own, starts, SPAN, SPAN)
+    heads_out, log_totals = self_attend(queries, kv_before, starts, SPAN, 0, heads_state)
     attended = exchanged(heads_out[:, :head_cols], 0, 1)
     hidden_one = inputs + matmul(attended, full_out)
 
@@ -549,62 +587,63 @@
     grad_down = scattered(grad_down)
     grad_upward = (contract_cols(cotangent, full_down) * slope).astype(jnp.bfloat16)
     grad_up, grad_upward = lax.optimization_barrier(
-        (contract_rows(normed_three, grad_upward).astype(jnp.bfloat16), grad_upward)
-    )
-    grad_up = scattered(grad_up)
+        (contract_rows(normed_three, grad_upward[:, :-width]).astype(jnp.bfloat16), grad_upward)
+    )
+    grad_up = scattered(lax.optimization_barrier((grad_up, grad_down))[0])
     back_h2, gain_three, bias_three = norm_back(contract_cols(grad_upward, full_up), n_three, root_three, gains[2])
     grad_two = cotangent.astype(jnp.float32) + back_h2
     grad_two_low = grad_two.astype(jnp.bfloat16)
-    grad_cout = contract_rows(cross_result, grad_two_low)
     grad_result = contract_cols(grad_two_low, full_cout).astype(jnp.bfloat16)
     grad_query_c, grad_text_k, grad_text_v = cross_attend_back(cross_query, grad_result, cross_k, cross_v, slots_wide)
-    grad_cq = contract_rows(normed_two, grad_query_c)
     grad_text_kv = summed_block(jnp.stack([grad_text_k, grad_text_v], axis=1), 2)
     grad_text_kv = grad_text_kv.astype(jnp.bfloat16).reshape(text_count, 2 * head_cols)
     grad_text = contract_cols(grad_text_kv, w_ckv)
-    grad_ckv = contract_rows(text_rows, grad_text_kv)
+    grad_ckv = contract_rows(text_rows, grad_text_kv).astype(jnp.bfloat16)
+    grad_ckv = scattered(lax.optimization_barrier((grad_ckv, grad_up))[0])
     back_h1, gain_two, bias_two = norm_back(contract_cols(grad_query_c, full_cq), n_two, root_two, gains[1])
     grad_one = grad_two + back_h1
 
     grad_one_low = grad_one.astype(jnp.bfloat16)
     grad_attended = contract_cols(grad_one_low, full_out).astype(jnp.bfloat16)
     grad_heads = paired(exchanged(grad_attended, 1, 0))
-    grad_wout = contract_rows(attended, grad_one_low)
-    middle = scattered(
-        jnp.concatenate([part.astype(jnp.bfloat16) for part in (grad_wout, grad_cq, grad_cout, grad_ckv)], axis=1)
-    )
-    grad_q, grad_k_before, grad_v_before, grad_k, grad_v = self_attend_back(
-        queries, grad_heads, heads_out, log_totals, kv_before, kv_own, starts
-    )
+    small = four_sums(
+        ((attended, normed_two), (cross_result, normed_three)),
+        ((grad_one_low, grad_query_c), (grad_two_low, grad_upward[:, -width:])),
+    )
+    back_args = (queries, grad_heads, heads_out, log_totals)
+    query_state, *grad_before = self_attend_back(*back_args, kv_before, starts, SPAN, 0)
+    returned = [passed_along(part[:, :head_cols], "fsdp", -1).astype(jnp.float32) for part in grad_before]
+    grad_q, *grad_own = self_attend_back(*back_args, kv_own, starts, SPAN, SPAN, query_state)
     late = group_rows - SPAN
     owned = [grad_q[:, :head_cols]]
-    for part, before in ((grad_k, grad_k_before), (grad_v, grad_v_before)):
-        returned = passed_along(before[:, :head_cols], "fsdp", -1).astype(jnp.float32)
+    for part, more in zip(grad_own, returned):
         part = part[:, :head_cols].astype(jnp.float32)
-        part = jnp.concatenate([part[:late], part[late:] + returned]) if late else part + returned
+        part = jnp.concatenate([part[:late], part[late:] + more]) if late else part + more
         owned.append(part.astype(jnp.bfloat16))
     grad_proj = jnp.concatenate(owned, axis=1)
-    grad_wqkv = scattered(contract_rows(normed_one, grad_proj))
+    grad_wqkv, grad_proj = lax.optimization_barrier(
+        (contract_rows(normed_one, grad_proj).astype(jnp.bfloat16), grad_proj)
+    )
+    grad_wqkv = scattered(lax.optimization_barrier((grad_wqkv, grad_ckv))[0])
     grad_normed_one = summed_block(contract_cols(grad_proj, w_qkv), 0)
     n_one, root_one = normed(inputs)
     back_x, gain_one, bias_one = norm_back(grad_normed_one, n_one, root_one, gains[0])
     grad_tokens = (grad_one + back_x).astype(jnp.bfloat16)
 
-    grad_ckv = columns(middle[:, 3 * width :], 2)
-    middle = whole(middle[:, : 3 * width])
-
-    norm_grads = everywhere(jnp.stack([gain_one, gain_two, gain_three, bias_one, bias_two, bias_three]))
+    norm_grads = lax.psum(
+        jnp.stack([gain_one, gain_two, gain_three, bias_one, bias_two, bias_three]), ("fsdp", "seq")
+    )
     norm_grads = lax.dynamic_slice_in_dim(norm_grads, group_index * shard_rows, shard_rows, 1)
     return (
         layer_out,
         grad_tokens,
         whole(grad_text.astype(jnp.bfloat16)).reshape(text.shape),
         columns(grad_wqkv, 3),
-        middle[:, :width],
-        middle[:, width : 2 * width],
-        grad_ckv,
-        middle[:, 2 * width :],
-        whole(grad_up),
+        small[0][0],
+        small[0][1],
+        columns(grad_ckv, 2),
+        small[1][0],
+        jnp.concatenate([whole(grad_up), small[1][1]], axis=1),
         whole(grad_down),
         norm_grads[:3],
         norm_grads[3:],

time: 1550 us -> 1260 us (0.81)
  waiting for transfers between devices: 831 us -> 490 us
  blocking collectives: 0 us -> 45.8 us
  Pallas kernels: 136 us -> 172 us
  other arithmetic: 70 us -> 101 us
  local copies, waits for them, and re-layouts: 72.3 us -> 42.3 us
  starting transfers between devices: 132 us -> 102 us
    unnamed x9, waiting for transfers between devices: 197 us -> 1.3 us
    reduce_scatter x3, waiting for transfers between devices: 293 us -> 116 us  [scattered(): lax.psum_scatter(grad.astype(jnp.bfloat16), 'fsdp', scatter_dimension=0,...]
    ppermute x17 -> x18, waiting for transfers between devices: 162 us -> 244 us  [swap(): return lax.ppermute(value, axis, [(i, i ^ bit) for i in range(count)])]
    psum x0 -> x1, blocking collectives: none -> 45.8 us  [shards(): lax.psum(jnp.stack([gain_one, gain_two, gain_three, bias_one, bias_two, b...]
    pallas_call x2 -> x4, Pallas kernels: 99.6 us -> 136 us  [the longest x2 85 us: self_attend_back(): pl.pallas_call(functools.partial(attend_back_kernel, reach=reach, base=ba...]
    ppermute x3, waiting for transfers between devices: 30.9 us -> 0.01 us  [passed_along(): lax.ppermute(value, axis, [(source, source + steps) for source in range(i...]
    ppermute x17 -> x18, starting transfers between devices: 124 us -> 94 us  [swap(): return lax.ppermute(value, axis, [(i, i ^ bit) for i in range(count)])]
    dot_general x7 -> x4, matrix products: 81.6 us -> 58.1 us  [contract_rows(): lax.dot_general(left_side, right_side, (((0,), (0,)), ((), ())), preferre...]
  transfers between devices with their start and end apart: 28 -> 29, of which waited for: 17 -> 15; matrix products, arithmetic and copies ran while one was open for 18% -> 32% of each run, Pallas kernels for 4% -> 14%
where the time goes in v3:
time: 1260 us; the launch traced here: 1250 us
  waiting for transfers between devices  490 us (39%)
  matrix products  277 us (22%)
  Pallas kernels  172 us (14%)
  starting transfers between devices  102 us (8%)
  other arithmetic  101 us (8%)
  blocking collectives  45.8 us (4%)
  local copies, waits for them, and re-layouts  42.3 us (3%)
  between operations  15.6 us (1%)
    ppermute x18, waiting for transfers between devices, swap(): return lax.ppermute(value, axis, [(i, i ^ bit) for i in range(count)])  244 us
    all_gather x4, waiting for transfers between devices, shards(): row_block = lambda value: lax.all_gather(value, 'fsdp', axis=0, tiled=True)  129 us
    reduce_scatter x3, waiting for transfers between devices, scattered(): lax.psum_scatter(grad.astype(jnp.bfloat16), 'fsdp', scatter_dimension=0,...  116 us
    dot_general x7, matrix products, contract_cols(): lax.dot_general(left_side, right_side, (((1,), (1,)), ((), ())), preferre...  99.1 us
    dot_general x8, matrix products, matmul(): return jnp.dot(left_side, right_side, preferred_element_type=jnp.float32)  97 us
    ppermute x18, starting transfers between devices, swap(): return lax.ppermute(value, axis, [(i, i ^ bit) for i in range(count)])  94 us
    pallas_call x2, Pallas kernels, self_attend_back(): pl.pallas_call(functools.partial(attend_back_kernel, reach=reach, base=ba...  85 us
    dot_general x4, matrix products, contract_rows(): lax.dot_general(left_side, right_side, (((0,), (0,)), ((), ())), preferre...  58.1 us
  transfers between devices with their start and end apart: 29, of which 15 were waited for; matrix products, arithmetic and copies ran while one was open for 32% of the time, Pallas kernels for 14%

profile of v3, /device:TPU:0, one launch (start us, length us, event | category | flops | bytes accessed | tf_op | source)
XLA Modules:
  0.0 1246.2 jit_solution(5020411037328329555)
XLA Ops:
  20.8 51.4 %collective-permute-done = bf16[768,1536]{1,0:T(8,128)(2,1)} collective-permute-done((bf16[768,1536]{1,0:T(8,128)(2,1)S(1)}, bf16[768,1536]{1,0:T(8,128)(2,1)}, u32[]{:S(2)}, u32[]{:S(2)}) %collective-permute-start) | collective-permute-done | bytes 2359328 | tf_op jit(solution)/shard_map/ppermute | solution.py:387
  121.0 38.8 %self_attend.2.refs_0_ = f32[2,4,6,80,384]{4,3,2,1,0:T(8,128)} custom-call(s32[4,4]{1,0:T(4,128)} %pad_add_fusion.1.bounds, bf16[1536,768]{1,0:T(8,128)(2,1)} %convolution_convert_fusion.7.q_ref, bf16[1536,1536]{1,0:T(8,128)(2,1)} %convolution_convert_fusion.6.k_ref.v_ref, bf16[1536,1536]{1,0:T(8,128)(2,1)} %convolution_convert_fusion.6.k_ref.v_ref, ...), custom_call_target="tpu_custom_call" | custom-call | flops 18119393280 | bytes 18874368 | tf_op jit(solution)/shard_map/self_attend/pallas_call | solution.py:161
  194.3 22.4 %all-gather.7.cloned.1.call-done = bf16[1536,6144]{1,0:T(8,128)(2,1)} async-done(((bf16[96,6144]{1,0:T(8,128)(2,1)}), bf16[1536,6144]{1,0:T(8,128)(2,1)}) %all-gather.7.cloned.1.call-update) | async-done | bytes 18874384 | tf_op jit(solution)/shard_map/all_gather | solution.py:534
  240.8 17.7 %cross_attend.1 = bf16[768,1536]{1,0:T(8,128)(2,1)} custom-call(bf16[768,1536]{1,0:T(8,128)(2,1)} %fusion.66.q_ref, bf16[128,1536]{1,0:T(8,128)(2,1)} %get-tuple-element.102.k_ref, bf16[128,1536]{1,0:T(8,128)(2,1)} %get-tuple-element.101.v_ref, s32[768,128]{1,0:T(8,128)} %broadcast_in_dim.26.slot_ref), custom_call_target="tpu_custom_call" | custom-call | flops 1207959552 | bytes 4718592 | tf_op jit(solution)/shard_map/cross_attend/pallas_call | solution.py:304
  271.0 51.0 %all-gather.9.cloned.1.call-done = bf16[1536,6144]{1,0:T(8,128)(2,1)} async-done(((bf16[96,6144]{1,0:T(8,128)(2,1)}), bf16[1536,6144]{1,0:T(8,128)(2,1)}) %all-gather.9.cloned.1.call-update) | async-done | bytes 18874384 | tf_op jit(solution)/shard_map/all_gather | solution.py:534
  322.0 25.8 %fusion.3 = (f32[768,6144]{1,0:T(8,128)}, bf16[768,6144]{1,0:T(8,128)(2,1)S(1)}) fusion(bf16[768,1536]{1,0:T(8,128)(2,1)} %get-tuple-element.73, bf16[1536,6144]{1,0:T(8,128)(2,1)} %all-gather.9.cloned.1.call-done), kind=kOutput, calls=%fused_computation.6 | convolution fusion | flops 14542700544 | bytes 49545216 | tf_op jit(solution)/shard_map/dot_general | solution.py:22
  351.5 17.8 %convolution_convert_fusion = bf16[6144,1536]{1,0:T(8,128)(2,1)} fusion(bf16[768,6144]{1,0:T(8,128)(2,1)S(1)} %get-tuple-element.84, bf16[768,1536]{1,0:T(8,128)(2,1)S(1)} %copy-done.20), kind=kOutput, calls=%fused_computation.1 | convolution fusion | flops 14504951808 | bytes 30670848 | tf_op jit(solution)/shard_map/dot_general | solution.py:26
  371.2 51.4 %all-gather.11.cloned.1.call-done = bf16[6144,1536]{1,0:T(8,128)(2,1)} async-done(((bf16[384,1536]{1,0:T(8,128)(2,1)}), bf16[6144,1536]{1,0:T(8,128)(2,1)}) %all-gather.11.cloned.1.call-update) | async-done | bytes 18874384 | tf_op jit(solution)/shard_map/all_gather | solution.py:534
  422.6 26.7 %multiply_convert_fusion = bf16[768,6144]{1,0:T(8,128)(2,1)} fusion(f32[768,6144]{1,0:T(8,128)} %get-tuple-element.33, bf16[768,1536]{1,0:T(8,128)(2,1)} %param.25, bf16[6144,1536]{1,0:T(8,128)(2,1)} %all-gather.11.cloned.1.call-done), kind=kOutput, calls=%fused_computation.7 | convolution fusion | flops 14504951808 | bytes 49545216 | tf_op jit(solution)/shard_map/dot_general | solution.py:32
  449.3 18.4 %convolution_convert_fusion.1 = bf16[1536,4608]{1,0:T(8,128)(2,1)} fusion(bf16[768,1536]{1,0:T(8,128)(2,1)S(1)} %copy-done.13, bf16[768,6144]{1,0:T(8,128)(2,1)} %multiply_convert_fusion), kind=kOutput, calls=%fused_computation.2 | convolution fusion | flops 10878713856 | bytes 23592960 | tf_op jit(solution)/shard_map/dot_general | solution.py:26
  467.6 24.3 %multiply_reduce_fusion = (f32[1536]{0:T(1024)}, f32[768]{0:T(1024)S(1)}, f32[768]{0:T(1024)S(1)}, f32[1536]{0:T(1024)}, f32[768,1536]{1,0:T(8,128)}) fusion(f32[768,1536]{1,0:T(8,128)} %copy-done.4, f32[768]{0:T(1024)S(1)} %add_rsqrt_fusion.2, f32[768]{0:T(1024)S(1)} %broadcast_multiply_fusion.8, f32[1536]{0:T(1024)S(1)} %get-tuple-element.64, ...), kind=kOutput, calls=%fused_computation.63 | convolution fusion | flops 14506125312 | bytes 37779456 | tf_op jit(solution)/shard_map/dot_general | solution.py:32
  505.7 115.6 %reduce-scatter.7.cloned.1.call-done = bf16[384,1536]{1,0:T(8,128)(2,1)} async-done(((bf16[6144,1536]{1,0:T(8,128)(2,1)}), bf16[384,1536]{1,0:T(8,128)(2,1)}) %reduce-scatter.7.cloned.1.call-update) | async-done | bytes 1179664 | tf_op jit(solution)/shard_map/reduce_scatter | solution.py:452
  621.4 18.8 %cross_attend_back.1 = (bf16[768,1536]{1,0:T(8,128)(2,1)}, f32[128,1536]{1,0:T(8,128)}, f32[128,1536]{1,0:T(8,128)}) custom-call(bf16[768,1536]{1,0:T(8,128)(2,1)} %fusion.66.q_ref, bf16[768,1536]{1,0:T(8,128)(2,1)} %fusion.69.g_ref, bf16[128,1536]{1,0:T(8,128)(2,1)} %get-tuple-element.102.k_ref, bf16[128,1536]{1,0:T(8,128)(2,1)} %get-tuple-element.101.v_ref, ...), custom_call_target="tpu_custom_call" | custom-call | flops 3019898880 | bytes 7077888 | tf_op jit(solution)/shard_map/cross_attend_back/pallas_call | solution.py:355
  734.4 70.5 %self_attend_back.3 = (bf16[1536,768]{1,0:T(8,128)(2,1)}, bf16[1536,768]{1,0:T(8,128)(2,1)}, bf16[1536,768]{1,0:T(8,128)(2,1)}) custom-call(s32[4,4]{1,0:T(4,128)} %pad_add_fusion.1.bounds, bf16[1536,768]{1,0:T(8,128)(2,1)} %convolution_convert_fusion.7.q_ref, bf16[1536,768]{1,0:T(8,128)(2,1)} %pad_maximum_fusion.3.g_ref, ...), custom_call_target="tpu_custom_call" | custom-call | flops 36238786560 | bytes 23592960 | tf_op jit(solution)/shard_map/self_attend_back/pallas_call | solution.py:263
  825.3 18.4 %convolution_convert_fusion.2 = bf16[1536,2304]{1,0:T(8,128)(2,1)} fusion(bf16[1536,768]{1,0:T(8,128)(2,1)} %add_convert_fusion.1, bf16[1536,768]{1,0:T(8,128)(2,1)} %add_convert_fusion.2, bf16[1536,768]{1,0:T(8,128)(2,1)} %get-tuple-element.38, f32[1536]{0:T(1024)S(1)} %copy-done.53, f32[1536]{0:T(1024)S(1)} %copy-done.42, f32[1536]{0:T(1024)S(1)} %copy-done.59, ...), kind=kOutput, calls=%fused_computation.12 | convolution fusion | flops 10917642240 | bytes 18898944 | tf_op jit(solution)/shard_map/dot_general | solution.py:26
  850.2 61.3 %collective-permute-done.12 = bf16[1536,1536]{1,0:T(8,128)(2,1)} collective-permute-done((bf16[1536,1536]{1,0:T(8,128)(2,1)}, bf16[1536,1536]{1,0:T(8,128)(2,1)}, u32[]{:S(2)}, u32[]{:S(2)}) %collective-permute-start.12) | collective-permute-done | bytes 4718624 | tf_op jit(solution)/shard_map/ppermute | solution.py:387
  918.7 39.8 %collective-permute-start.13 = (bf16[4,192,1536]{2,1,0:T(8,128)(2,1)S(1)}, bf16[4,192,1536]{2,1,0:T(8,128)(2,1)S(1)}, u32[]{:S(2)}, u32[]{:S(2)}) collective-permute-start(bf16[4,192,1536]{2,1,0:T(8,128)(2,1)S(1)} %dynamic-slice_bitcast_fusion), channel_id=1, source_target_pairs={{0,4},{2,6},{4,0},{6,2},{8,12},{10,14},{12,8},{14,10},{16,20},{18,... | collective-permute-start | bytes 7077896 | tf_op jit(solution)/shard_map/ppermute | solution.py:387
  958.5 15.9 %fusion.11 = f32[1536,1536]{1,0:T(8,128)S(1)} fusion(bf16[1536,2304]{1,0:T(8,128)(2,1)} %pad_maximum_fusion, bf16[1536,2432]{1,0:T(8,128)(2,1)} %all-gather.5.cloned.1.call-done), kind=kOutput, calls=%fused_computation.26 | convolution fusion | flops 10871635968 | bytes 23592960 | tf_op jit(solution)/shard_map/dot_general | solution.py:32
  977.0 21.7 %collective-permute-done.13 = bf16[4,192,1536]{2,1,0:T(8,128)(2,1)S(1)} collective-permute-done((bf16[4,192,1536]{2,1,0:T(8,128)(2,1)S(1)}, bf16[4,192,1536]{2,1,0:T(8,128)(2,1)S(1)}, u32[]{:S(2)}, u32[]{:S(2)}) %collective-permute-start.13) | collective-permute-done | bytes 2359328 | tf_op jit(solution)/shard_map/ppermute | solution.py:387
  1000.5 24.4 %collective-permute-start.14 = (bf16[2,192,1536]{2,1,0:T(8,128)(2,1)}, bf16[2,192,1536]{2,1,0:T(8,128)(2,1)}, u32[]{:S(2)}, u32[]{:S(2)}) collective-permute-start(bf16[2,192,1536]{2,1,0:T(8,128)(2,1)} %dynamic-slice_bitcast_fusion.1), channel_id=1, source_target_pairs={{0,8},{2,10},{4,12},{6,14},{8,0},{10,2},{12,4},{14,6},{16,24},{18,... | collective-permute-start | bytes 3538952 | tf_op jit(solution)/shard_map/ppermute | solution.py:387
  1026.9 22.2 %add_convert_fusion.3 = bf16[768,1536]{1,0:T(8,128)(2,1)} fusion(f32[768,1536]{1,0:T(8,128)} %copy-done.4, bf16[768,6144]{1,0:T(8,128)(2,1)} %copy-done.60, bf16[6144,1536]{1,0:T(8,128)(2,1)} %all-gather.11.cloned.1.call-done), kind=kOutput, calls=%fused_computation.73 | convolution fusion | flops 14497873920 | bytes 35389440 | tf_op jit(solution)/shard_map/dot_general | solution.py:22
  1072.9 45.7 %collective-permute-done.15 = bf16[1,192,1536]{2,1,0:T(8,128)(2,1)S(1)} collective-permute-done((bf16[1,192,1536]{2,1,0:T(8,128)(2,1)S(1)}, bf16[1,192,1536]{2,1,0:T(8,128)(2,1)S(1)}, u32[]{:S(2)}, u32[]{:S(2)}) %collective-permute-start.15) | collective-permute-done | bytes 589856 | tf_op jit(solution)/shard_map/ppermute | solution.py:387
  1124.9 45.8 %psum.7 = f32[6,1536]{1,0:T(8,128)S(1)} all-reduce(f32[6,1536]{1,0:T(8,128)S(1)} %stack.149), channel_id=1, replica_groups=mesh['fsdp'=16,'seq'=2] {'fsdp','seq'}, use_global_device_ids=true, to_apply=%region_25.26 | all-reduce | flops 9216 | bytes 73728 | tf_op jit(solution)/shard_map/psum | solution.py:633
  1177.0 23.8 %collective-permute-done.20 = bf16[384,1536]{1,0:T(8,128)(2,1)S(1)} collective-permute-done((bf16[384,1536]{1,0:T(8,128)(2,1)}, bf16[384,1536]{1,0:T(8,128)(2,1)S(1)}, u32[]{:S(2)}, u32[]{:S(2)}) %collective-permute-start.20) | collective-permute-done | bytes 1179680 | tf_op jit(solution)/shard_map/ppermute | solution.py:387
  (330 shorter events, 361.1 us)
Async XLA Ops:
  7.2 76.3 %all-gather.5.cloned.1.call-start = ((), (), s32[]{:S(2)}) async-start(), calls=%async_computation.4 | async-start | bytes 7938048 | tf_op jit(solution)/shard_map/all_gather | solution.py:534
  11.6 205.1 %all-gather.7.cloned.1.call-start = ((), (), s32[]{:S(2)}) async-start(), calls=%async_computation.5 | async-start | bytes 20054016 | tf_op jit(solution)/shard_map/all_gather | solution.py:534
  16.4 305.6 %all-gather.9.cloned.1.call-start = ((), (), s32[]{:S(2)}) async-start(), calls=%async_computation.6 | async-start | bytes 20054016 | tf_op jit(solution)/shard_map/all_gather | solution.py:534
  17.1 405.4 %all-gather.11.cloned.1.call-start = ((), (), s32[]{:S(2)}) async-start(), calls=%async_computation.7 | async-start | bytes 20054016 | tf_op jit(solution)/shard_map/all_gather | solution.py:534
  17.7 603.6 %reduce-scatter.7.cloned.1.call-start = ((), (), s32[]{:S(2)}) async-start(), calls=%async_computation.8 | async-start | bytes 20054016 | tf_op jit(solution)/shard_map/reduce_scatter | solution.py:452
  17.7 54.4 %collective-permute-start = (bf16[768,1536]{1,0:T(8,128)(2,1)S(1)}, bf16[768,1536]{1,0:T(8,128)(2,1)}, u32[]{:S(2)}, u32[]{:S(2)}) collective-permute-start(bf16[768,1536]{1,0:T(8,128)(2,1)S(1)} %copy-done.2), channel_id=1, source_target_pairs={{0,1},{1,0},{2,3},{3,2},{4,5},{5,4},{6,7},{7,6},{8,9},{9,8},{10,11... | collective-permute-start | bytes 7077896 | tf_op jit(solution)/shard_map/ppermute | solution.py:387
  100.8 58.9 %collective-permute-start.1 = (bf16[1536,1536]{1,0:T(8,128)(2,1)}, bf16[1536,1536]{1,0:T(8,128)(2,1)}, u32[]{:S(2)}, u32[]{:S(2)}) collective-permute-start(bf16[1536,1536]{1,0:T(8,128)(2,1)} %convolution_convert_fusion.6.k_ref.v_ref), channel_id=1, source_target_pairs={{0,2},{2,4},{4,6},{6,8},{8,10},{10,12},{12,14},{14,16},{16,18},{18... | collective-permute-start | bytes 14155784 | tf_op jit(solution)/shard_map/ppermute | solution.py:393
  369.2 447.8 %reduce-scatter.9.cloned.1.call-start = ((), (), s32[]{:S(2)}) async-start(), calls=%async_computation.9 | async-start | bytes 15040512 | tf_op jit(solution)/shard_map/reduce_scatter | solution.py:452
  621.4 403.6 %reduce-scatter.13.cloned.1.call-start = ((), (), s32[]{:S(2)}) async-start(), calls=%async_computation.11 | async-start | bytes 5013504
  664.8 49.2 %collective-permute-start.4 = (bf16[768,768]{1,0:T(8,128)(2,1)}, bf16[768,768]{1,0:T(8,128)(2,1)}, u32[]{:S(2)}, u32[]{:S(2)}) collective-permute-start(bf16[768,768]{1,0:T(8,128)(2,1)} %constant_dynamic-slice_fusion.2), channel_id=1, source_target_pairs={{0,1},{1,0},{2,3},{3,2},{4,5},{5,4},{6,7},{7,6},{8,9},{9,8},{10,11... | collective-permute-start | bytes 3538952 | tf_op jit(solution)/shard_map/ppermute | solution.py:387
  667.1 36.0 %collective-permute-start.8 = (bf16[128,2,768]{2,0,1:T(8,128)(2,1)}, bf16[128,2,768]{2,0,1:T(8,128)(2,1)}, u32[]{:S(2)}, u32[]{:S(2)}) collective-permute-start(bf16[128,2,768]{2,0,1:T(8,128)(2,1)} %fusion.82), channel_id=1, source_target_pairs={{0,1},{1,0},{2,3},{3,2},{4,5},{5,4},{6,7},{7,6},{8,9},{9,8},{10,11... | collective-permute-start | bytes 1179656 | tf_op jit(solution)/shard_map/ppermute | solution.py:387
  693.2 111.7 %collective-permute-start.11 = (bf16[2,1536,1536]{2,1,0:T(8,128)(2,1)}, bf16[2,1536,1536]{2,1,0:T(8,128)(2,1)}, u32[]{:S(2)}, u32[]{:S(2)}) collective-permute-start(bf16[2,1536,1536]{2,1,0:T(8,128)(2,1)} %convolution_convert_fusion.3), channel_id=1, source_target_pairs={{0,2},{2,0},{4,6},{6,4},{8,10},{10,8},{12,14},{14,12},{16,18},{18,... | collective-permute-start | bytes 28311560 | tf_op jit(solution)/shard_map/ppermute | solution.py:387
  709.2 340.0 %collective-permute-start.9 = (bf16[128,1536]{1,0:T(8,128)(2,1)}, bf16[128,1536]{1,0:T(8,128)(2,1)}, u32[]{:S(2)}, u32[]{:S(2)}) collective-permute-start(bf16[128,1536]{1,0:T(8,128)(2,1)} %fusion.75), channel_id=1, source_target_pairs={{0,1},{1,0},{2,3},{3,2},{4,5},{5,4},{6,7},{7,6},{8,9},{9,8},{10,11... | collective-permute-start | bytes 1179656 | tf_op jit(solution)/shard_map/ppermute | solution.py:387
  731.9 81.1 %collective-permute-start.6 = (bf16[1536,768]{1,0:T(8,128)(2,1)}, bf16[1536,768]{1,0:T(8,128)(2,1)S(1)}, u32[]{:S(2)}, u32[]{:S(2)}) collective-permute-start(bf16[1536,768]{1,0:T(8,128)(2,1)} %get-tuple-element.42), channel_id=1, source_target_pairs={{2,0},{4,2},{6,4},{8,6},{10,8},{12,10},{14,12},{16,14},{18,16},{20... | collective-permute-start | bytes 7077896 | tf_op jit(solution)/shard_map/ppermute | solution.py:393
  733.1 81.9 %collective-permute-start.5 = (bf16[1536,768]{1,0:T(8,128)(2,1)}, bf16[1536,768]{1,0:T(8,128)(2,1)S(1)}, u32[]{:S(2)}, u32[]{:S(2)}) collective-permute-start(bf16[1536,768]{1,0:T(8,128)(2,1)} %get-tuple-element.40), channel_id=1, source_target_pairs={{2,0},{4,2},{6,4},{8,6},{10,8},{12,10},{14,12},{16,14},{18,16},{20... | collective-permute-start | bytes 7077896 | tf_op jit(solution)/shard_map/ppermute | solution.py:393
  812.2 99.3 %collective-permute-start.12 = (bf16[1536,1536]{1,0:T(8,128)(2,1)}, bf16[1536,1536]{1,0:T(8,128)(2,1)}, u32[]{:S(2)}, u32[]{:S(2)}) collective-permute-start(bf16[1536,1536]{1,0:T(8,128)(2,1)} %fusion.27), channel_id=1, source_target_pairs={{0,1},{1,0},{2,3},{3,2},{4,5},{5,4},{6,7},{7,6},{8,9},{9,8},{10,11... | collective-permute-start | bytes 14155784 | tf_op jit(solution)/shard_map/ppermute | solution.py:387
  823.7 398.0 %reduce-scatter.11.cloned.1.call-start = ((), (), s32[]{:S(2)}) async-start(), calls=%async_computation.10 | async-start | bytes 7520256 | tf_op jit(solution)/shard_map/reduce_scatter | solution.py:452
  918.7 79.9 %collective-permute-start.13 = (bf16[4,192,1536]{2,1,0:T(8,128)(2,1)S(1)}, bf16[4,192,1536]{2,1,0:T(8,128)(2,1)S(1)}, u32[]{:S(2)}, u32[]{:S(2)}) collective-permute-start(bf16[4,192,1536]{2,1,0:T(8,128)(2,1)S(1)} %dynamic-slice_bitcast_fusion), channel_id=1, source_target_pairs={{0,4},{2,6},{4,0},{6,2},{8,12},{10,14},{12,8},{14,10},{16,20},{18,... | collective-permute-start | bytes 7077896 | tf_op jit(solution)/shard_map/ppermute | solution.py:387
  976.3 90.8 %collective-permute-start.7 = (bf16[768,1536]{1,0:T(8,128)(2,1)}, bf16[768,1536]{1,0:T(8,128)(2,1)}, u32[]{:S(2)}, u32[]{:S(2)}) collective-permute-start(bf16[768,1536]{1,0:T(8,128)(2,1)} %dynamic-slice_convert_fusion), channel_id=1, source_target_pairs={{0,1},{1,0},{2,3},{3,2},{4,5},{5,4},{6,7},{7,6},{8,9},{9,8},{10,11... | collective-permute-start | bytes 7077896 | tf_op jit(solution)/shard_map/ppermute | solution.py:387
  1000.5 51.0 %collective-permute-start.14 = (bf16[2,192,1536]{2,1,0:T(8,128)(2,1)}, bf16[2,192,1536]{2,1,0:T(8,128)(2,1)}, u32[]{:S(2)}, u32[]{:S(2)}) collective-permute-start(bf16[2,192,1536]{2,1,0:T(8,128)(2,1)} %dynamic-slice_bitcast_fusion.1), channel_id=1, source_target_pairs={{0,8},{2,10},{4,12},{6,14},{8,0},{10,2},{12,4},{14,6},{16,24},{18,... | collective-permute-start | bytes 3538952 | tf_op jit(solution)/shard_map/ppermute | solution.py:387
  1053.7 64.9 %collective-permute-start.15 = (bf16[1,192,1536]{2,1,0:T(8,128)(2,1)S(1)}, bf16[1,192,1536]{2,1,0:T(8,128)(2,1)S(1)}, u32[]{:S(2)}, u32[]{:S(2)}) collective-permute-start(bf16[1,192,1536]{2,1,0:T(8,128)(2,1)S(1)} %constant_dynamic-slice_fusion.1), channel_id=1, source_target_pairs={{0,16},{2,18},{4,20},{6,22},{8,24},{10,26},{12,28},{14,30},{16,0},... | collective-permute-start | bytes 1769480 | tf_op jit(solution)/shard_map/ppermute | solution.py:387
  1121.3 52.4 %collective-permute-start.17 = (bf16[2,96,1536]{2,1,0:T(8,128)(2,1)}, bf16[2,96,1536]{2,1,0:T(8,128)(2,1)}, u32[]{:S(2)}, u32[]{:S(2)}) collective-permute-start(bf16[2,96,1536]{2,1,0:T(8,128)(2,1)} %pad_maximum_fusion.7), channel_id=1, source_target_pairs={{0,1},{1,0},{2,3},{3,2},{4,5},{5,4},{6,7},{7,6},{8,9},{9,8},{10,11... | collective-permute-start | bytes 1769480 | tf_op jit(solution)/shard_map/ppermute | solution.py:387
  1171.4 29.4 %collective-permute-start.20 = (bf16[384,1536]{1,0:T(8,128)(2,1)}, bf16[384,1536]{1,0:T(8,128)(2,1)S(1)}, u32[]{:S(2)}, u32[]{:S(2)}) collective-permute-start(bf16[384,1536]{1,0:T(8,128)(2,1)} %reduce-scatter.7.cloned.1.call-done), channel_id=1, source_target_pairs={{0,1},{1,0},{2,3},{3,2},{4,5},{5,4},{6,7},{7,6},{8,9},{9,8},{10,11... | collective-permute-start | bytes 3538952 | tf_op jit(solution)/shard_map/ppermute | solution.py:387
  1176.0 41.9 %collective-permute-start.19 = (bf16[96,4608]{1,0:T(8,128)(2,1)}, bf16[96,4608]{1,0:T(8,128)(2,1)S(1)}, u32[]{:S(2)}, u32[]{:S(2)}) collective-permute-start(bf16[96,4608]{1,0:T(8,128)(2,1)} %reduce-scatter.9.cloned.1.call-done), channel_id=1, source_target_pairs={{0,1},{1,0},{2,3},{3,2},{4,5},{5,4},{6,7},{7,6},{8,9},{9,8},{10,11... | collective-permute-start | bytes 2654216 | tf_op jit(solution)/shard_map/ppermute | solution.py:387
  (74 other events, 1716.5 us)
Sparse Core Ops, SparseCore 0:
  11.7 71.7 all-gather.4
  85.7 130.9 all-gather.6
  218.3 103.7 all-gather.8
  323.5 99.0 all-gather.10
  426.5 194.7 reduce-scatter.6
  625.3 144.6 reduce-scatter.8
  823.8 132.8 reduce-scatter.12
  1027.0 117.5 reduce-scatter.10

commit v4 on v3

--- a/solution.py
+++ b/solution.py
@@ -169,9 +169,7 @@
         else state_shape,
         compiler_params=pltpu.CompilerParams(vmem_limit_bytes=VMEM_BYTES),
         cost_estimate=pl.CostEstimate(
-            flops=10 * rows * kv_rows * width,
-            bytes_accessed=16 * rows * width,
-            transcendentals=rows * kv_rows * width // HEAD // 2,
+            flops=rows * kv_rows * HEAD, bytes_accessed=rows * HEAD, transcendentals=0
         ),
         name="self_attend",
     )(tile_bounds(starts, reach, base, kv_rows), q, kv, kv, starts.reshape(-1, 1, TILE), *([before] if ends else []))
@@ -270,9 +268,7 @@
         ],
         compiler_params=pltpu.CompilerParams(vmem_limit_bytes=VMEM_BYTES),
         cost_estimate=pl.CostEstimate(
-            flops=20 * rows * kv_rows * width,
-            bytes_accessed=20 * rows * width,
-            transcendentals=rows * kv_rows * width // HEAD // 2,
+            flops=rows * kv_rows * HEAD, bytes_accessed=rows * HEAD, transcendentals=0
         ),
         name="self_attend_back",
     )(
@@ -463,40 +459,35 @@
     return gathered(split, 2).reshape(part.shape[0], -1).astype(jnp.float32)
 
 
-def four_sums(lefts, rights):
-    chip, core = lax.axis_index("fsdp") // 2, lax.axis_index("fsdp") % 2
-    seq_index, seq_count = lax.axis_index("seq"), lax.axis_size("seq")
-    chips = lax.axis_size("fsdp") // 2
-    if seq_count != 2:
-        sums = [[scattered(contract_rows(a, b)) for a, b in zip(*each)] for each in zip(lefts, rights)]
-        return [[whole(part) for part in each] for each in sums]
-
-    def products(place):
-        pick = lambda parts: jnp.stack([jnp.where(place == 0, a, b) for a, b in zip(*parts)])
-        return jnp.einsum("kta,ktb->kab", pick(lefts), pick(rights), preferred_element_type=jnp.float32).astype(
-            jnp.bfloat16
-        )
-
-    take = lambda value, place, dim=0: lax.dynamic_index_in_dim(value, place, dim, keepdims=False).astype(jnp.float32)
-    sent = swap(products(1 - core), "fsdp", 1)
-    kept = products(core)
-    other = swap((take(kept, 1 - seq_index) + take(sent, 1 - seq_index)).astype(jnp.bfloat16), "seq", 1)
-    total = take(kept, seq_index) + take(sent, seq_index) + other.astype(jnp.float32)
-    bit, at = 2, chip
-    total = total.reshape(chips, -1, total.shape[-1])
-    while chips > 1:
-        chips //= 2
-        total = total.astype(jnp.bfloat16).reshape(chips, 2, *total.shape[1:])
-        more = swap(take(total, 1 - at % 2, 1).astype(jnp.bfloat16), "fsdp", bit)
-        total = take(total, at % 2, 1) + more.astype(jnp.float32)
-        bit, at = bit * 2, at // 2
-    total = total.astype(jnp.bfloat16).reshape(2, -1, total.shape[-1])
-    mine = take(total, core).astype(jnp.bfloat16)
-    theirs = swap(take(total, 1 - core).astype(jnp.bfloat16), "fsdp", 1)
+def core_products(left, right):
+    size, core = right.shape[1] // 2, lax.axis_index("fsdp") % 2
+    part = lambda place: contract_rows(left, lax.dynamic_slice_in_dim(right, place * size, size, 1)).astype(jnp.bfloat16)
+    return part(core), part(1 - core)
+
+
+def both(first, second):
+    return (first.astype(jnp.float32) + second.astype(jnp.float32)).astype(jnp.bfloat16)
+
+
+def half_rows(value, place):
+    blocks = value.reshape(-1, 2, *value.shape[1:])
+    return lax.dynamic_index_in_dim(blocks, place, 1, keepdims=False)
+
+
+def own_rows(kept, came, at):
+    value, bit = both(kept, came), 4
+    while value.shape[0] > 1:
+        at = at // 2
+        value = both(half_rows(value, at % 2), swap(half_rows(value, 1 - at % 2), "fsdp", bit))
+        bit *= 2
+    core, second = lax.axis_index("fsdp") % 2, lax.axis_index("seq") == 1
+    value = value.reshape(2, -1, value.shape[-1])
+    take = lambda place: lax.dynamic_index_in_dim(value, place, 0, keepdims=False)
+    mine, theirs = take(core), swap(take(1 - core), "fsdp", 1)
     pair = jnp.stack([jnp.where(core == 0, mine, theirs), jnp.where(core == 0, theirs, mine)])
     beside = swap(pair, "seq", 1)
-    by_seq = [jnp.where(seq_index == 0, pair, beside), jnp.where(seq_index == 0, beside, pair)]
-    return [[by_seq[s][c].astype(jnp.float32) for s in range(2)] for c in range(2)]
+    by_seq = jnp.where(second, beside, pair), jnp.where(second, pair, beside)
+    return jnp.concatenate([by_seq[s][c] for c in range(2) for s in range(2)], axis=1).astype(jnp.float32)
 
 
 def clip_starts(segments, group_index, group_rows):
@@ -583,37 +574,62 @@
     slope = below + upward * (jnp.exp(-0.5 * upward * upward) * 0.3989422804014327)
     layer_out = (hidden_two + matmul(active, full_down)).astype(jnp.bfloat16)
 
-    grad_down, slope = lax.optimization_barrier((contract_rows(active, cotangent).astype(jnp.bfloat16), slope))
+    gate = lax.optimization_barrier
+    by_steps = seq_count == 2
+    chip = group_index // 2
+    grad_down, slope = gate((contract_rows(active, cotangent).astype(jnp.bfloat16), slope))
     grad_down = scattered(grad_down)
     grad_upward = (contract_cols(cotangent, full_down) * slope).astype(jnp.bfloat16)
-    grad_up, grad_upward = lax.optimization_barrier(
-        (contract_rows(normed_three, grad_upward[:, :-width]).astype(jnp.bfloat16), grad_upward)
-    )
-    grad_up = scattered(lax.optimization_barrier((grad_up, grad_down))[0])
+    if by_steps:
+        up_kept, up_away, grad_upward = gate((*core_products(normed_three, grad_upward), grad_upward))
+        up_came = swap(up_away, "fsdp", 1)
+    else:
+        grad_up = scattered(contract_rows(normed_three, grad_upward))
     back_h2, gain_three, bias_three = norm_back(contract_cols(grad_upward, full_up), n_three, root_three, gains[2])
     grad_two = cotangent.astype(jnp.float32) + back_h2
     grad_two_low = grad_two.astype(jnp.bfloat16)
+    if by_steps:
+        beside, grad_two_low = gate((both(other_block(up_kept, 1), other_block(up_came, 1)), grad_two_low))
+        beside = swap(beside, "seq", 1)
     grad_result = contract_cols(grad_two_low, full_cout).astype(jnp.bfloat16)
     grad_query_c, grad_text_k, grad_text_v = cross_attend_back(cross_query, grad_result, cross_k, cross_v, slots_wide)
     grad_text_kv = summed_block(jnp.stack([grad_text_k, grad_text_v], axis=1), 2)
     grad_text_kv = grad_text_kv.astype(jnp.bfloat16).reshape(text_count, 2 * head_cols)
     grad_text = contract_cols(grad_text_kv, w_ckv)
-    grad_ckv = contract_rows(text_rows, grad_text_kv).astype(jnp.bfloat16)
-    grad_ckv = scattered(lax.optimization_barrier((grad_ckv, grad_up))[0])
     back_h1, gain_two, bias_two = norm_back(contract_cols(grad_query_c, full_cq), n_two, root_two, gains[1])
     grad_one = grad_two + back_h1
 
     grad_one_low = grad_one.astype(jnp.bfloat16)
     grad_attended = contract_cols(grad_one_low, full_out).astype(jnp.bfloat16)
     grad_heads = paired(exchanged(grad_attended, 1, 0))
-    small = four_sums(
-        ((attended, normed_two), (cross_result, normed_three)),
-        ((grad_one_low, grad_query_c), (grad_two_low, grad_upward[:, -width:])),
-    )
+    small = [
+        contract_rows(left, right).astype(jnp.bfloat16)
+        for left, right in (
+            (cross_result, grad_two_low),
+            (normed_two, grad_query_c),
+            (attended, grad_one_low),
+            (text_rows, grad_text_kv),
+        )
+    ]
+    if by_steps:
+        small = lax.psum_scatter(gate((jnp.stack(small), grad_down, grad_heads))[0], "fsdp", scatter_dimension=1, tiled=True)
+    else:
+        small = [scattered(part) for part in small]
     back_args = (queries, grad_heads, heads_out, log_totals)
     query_state, *grad_before = self_attend_back(*back_args, kv_before, starts, SPAN, 0)
     returned = [passed_along(part[:, :head_cols], "fsdp", -1).astype(jnp.float32) for part in grad_before]
+    if by_steps:
+        total = both(both(own_block(up_kept, 1), own_block(up_came, 1)), beside)
+        total = total.reshape(-1, 2 * shard_rows, total.shape[1])
+        first_away, grad_down, query_state = gate((half_rows(total, 1 - chip % 2), grad_down, query_state))
+        down_beside = swap(grad_down, "seq", 1)
     grad_q, *grad_own = self_attend_back(*back_args, kv_own, starts, SPAN, SPAN, query_state)
+    if by_steps:
+        down_beside, first_came, grad_q = gate((down_beside, swap(first_away, "fsdp", 2), grad_q))
+        grad_up = own_rows(half_rows(total, chip % 2), first_came, chip)
+        grad_down = grad_down.astype(jnp.float32) + down_beside.astype(jnp.float32)
+    else:
+        grad_up, grad_down = whole(grad_up), whole(grad_down)
     late = group_rows - SPAN
     owned = [grad_q[:, :head_cols]]
     for part, more in zip(grad_own, returned):
@@ -621,15 +637,15 @@
         part = jnp.concatenate([part[:late], part[late:] + more]) if late else part + more
         owned.append(part.astype(jnp.bfloat16))
     grad_proj = jnp.concatenate(owned, axis=1)
-    grad_wqkv, grad_proj = lax.optimization_barrier(
-        (contract_rows(normed_one, grad_proj).astype(jnp.bfloat16), grad_proj)
-    )
-    grad_wqkv = scattered(lax.optimization_barrier((grad_wqkv, grad_ckv))[0])
-    grad_normed_one = summed_block(contract_cols(grad_proj, w_qkv), 0)
+    grad_wqkv, grad_proj = gate((contract_rows(normed_one, grad_proj).astype(jnp.bfloat16), grad_proj))
+    grad_normed_one = contract_cols(grad_proj, w_qkv)
+    grad_wqkv = scattered(gate((grad_wqkv, small, grad_normed_one))[0])
+    grad_normed_one = summed_block(grad_normed_one, 0)
     n_one, root_one = normed(inputs)
     back_x, gain_one, bias_one = norm_back(grad_normed_one, n_one, root_one, gains[0])
     grad_tokens = (grad_one + back_x).astype(jnp.bfloat16)
 
+    grad_cout, grad_cq, grad_wout = whole(small[:3]) if by_steps else [whole(part) for part in small[:3]]
     norm_grads = lax.psum(
         jnp.stack([gain_one, gain_two, gain_three, bias_one, bias_two, bias_three]), ("fsdp", "seq")
     )
@@ -639,12 +655,12 @@
         grad_tokens,
         whole(grad_text.astype(jnp.bfloat16)).reshape(text.shape),
         columns(grad_wqkv, 3),
-        small[0][0],
-        small[0][1],
-        columns(grad_ckv, 2),
-        small[1][0],
-        jnp.concatenate([whole(grad_up), small[1][1]], axis=1),
-        whole(grad_down),
+        grad_wout,
+        grad_cq,
+        columns(small[3], 2),
+        grad_cout,
+        grad_up,
+        grad_down,
         norm_grads[:3],
         norm_grads[3:],
     )

time: 1260 us -> 1100 us (0.87)
  waiting for transfers between devices: 490 us -> 402 us
  starting transfers between devices: 102 us -> 51.7 us
    reduce_scatter x3 -> x2, waiting for transfers between devices: 116 us -> 4.29 us  [scattered(): lax.psum_scatter(grad.astype(jnp.bfloat16), 'fsdp', scatter_dimension=0,...]
    ppermute x18, starting transfers between devices: 94 us -> 44.1 us  [swap(): return lax.ppermute(value, axis, [(i, i ^ bit) for i in range(count)])]
    dot_general x4 -> x8, matrix products: 58.1 us -> 84.8 us  [contract_rows(): lax.dot_general(left_side, right_side, (((0,), (0,)), ((), ())), preferre...]
    dot_general x2 -> x0, matrix products: 23.1 us -> none  [products(): jnp.einsum('kta,ktb->kab', pick(lefts), pick(rights), preferred_element_t...]
    ppermute x18, waiting for transfers between devices: 244 us -> 263 us  [swap(): return lax.ppermute(value, axis, [(i, i ^ bit) for i in range(count)])]
  transfers between devices with their start and end apart: 29 -> 28, of which waited for: 15 -> 14; matrix products, arithmetic and copies ran while one was open for 32% -> 36% of each run, Pallas kernels for 14% -> 16%
where the time goes in v4:
time: 1100 us
  waiting for transfers between devices  402 us (37%)
  matrix products  280 us (25%)
  Pallas kernels  173 us (16%)
  other arithmetic  93.9 us (9%)
  starting transfers between devices  51.7 us (5%)
  blocking collectives  40.8 us (4%)
  local copies, waits for them, and re-layouts  39.6 us (4%)
  between operations  15.6 us (1%)
    ppermute x18, waiting for transfers between devices, swap(): return lax.ppermute(value, axis, [(i, i ^ bit) for i in range(count)])  263 us
    all_gather x4, waiting for transfers between devices, shards(): row_block = lambda value: lax.all_gather(value, 'fsdp', axis=0, tiled=True)  133 us
    dot_general x8, matrix products, matmul(): return jnp.dot(left_side, right_side, preferred_element_type=jnp.float32)  99.5 us
    dot_general x7, matrix products, contract_cols(): lax.dot_general(left_side, right_side, (((1,), (1,)), ((), ())), preferre...  95.5 us
    pallas_call x2, Pallas kernels, self_attend_back(): pl.pallas_call(functools.partial(attend_back_kernel, reach=reach, base=ba...  85.6 us
    dot_general x8, matrix products, contract_rows(): lax.dot_general(left_side, right_side, (((0,), (0,)), ((), ())), preferre...  84.8 us
    pallas_call x2, Pallas kernels, self_attend(): pl.pallas_call(functools.partial(attend_kernel, reach=reach, base=base, p...  51 us
    ppermute x18, starting transfers between devices, swap(): return lax.ppermute(value, axis, [(i, i ^ bit) for i in range(count)])  44.1 us
  transfers between devices with their start and end apart: 28, of which 14 were waited for; matrix products, arithmetic and copies ran while one was open for 36% of the time, Pallas kernels for 16%

profile of v4, /device:TPU:0, one launch (start us, length us, event | category | flops | bytes accessed | tf_op | source)
XLA Modules:
  0.0 1096.1 jit_solution(973120563605586371)
XLA Ops:
  20.8 51.4 %collective-permute-done = bf16[768,1536]{1,0:T(8,128)(2,1)} collective-permute-done((bf16[768,1536]{1,0:T(8,128)(2,1)S(1)}, bf16[768,1536]{1,0:T(8,128)(2,1)}, u32[]{:S(2)}, u32[]{:S(2)}) %collective-permute-start) | collective-permute-done | bytes 2359328 | tf_op jit(solution)/shard_map/ppermute | solution.py:383
  121.1 38.8 %self_attend.2.refs_0_ = f32[2,4,6,80,384]{4,3,2,1,0:T(8,128)} custom-call(s32[4,4]{1,0:T(4,128)} %pad_add_fusion.1.bounds, bf16[1536,768]{1,0:T(8,128)(2,1)} %convolution_convert_fusion.9.q_ref, bf16[1536,1536]{1,0:T(8,128)(2,1)} %convolution_convert_fusion.8.k_ref.v_ref, bf16[1536,1536]{1,0:T(8,128)(2,1)} %convolution_convert_fusion.8.k_ref.v_ref, ...), custom_call_target="tpu_custom_call" | custom-call | flops 150994944 | bytes 98304 | tf_op jit(solution)/shard_map/self_attend/pallas_call | solution.py:161
  176.6 14.4 %collective-permute-done.2 = bf16[768,768]{1,0:T(8,128)(2,1)} collective-permute-done((bf16[768,768]{1,0:T(8,128)(2,1)}, bf16[768,768]{1,0:T(8,128)(2,1)}, u32[]{:S(2)}, u32[]{:S(2)}) %collective-permute-start.2) | collective-permute-done | bytes 1179680 | tf_op jit(solution)/shard_map/ppermute | solution.py:383
  194.5 22.2 %all-gather.7.cloned.1.call-done = bf16[1536,6144]{1,0:T(8,128)(2,1)} async-done(((bf16[96,6144]{1,0:T(8,128)(2,1)}), bf16[1536,6144]{1,0:T(8,128)(2,1)}) %all-gather.7.cloned.1.call-update) | async-done | bytes 18874384 | tf_op jit(solution)/shard_map/all_gather | solution.py:525
  240.8 17.7 %cross_attend.1 = bf16[768,1536]{1,0:T(8,128)(2,1)} custom-call(bf16[768,1536]{1,0:T(8,128)(2,1)} %fusion.56.q_ref, bf16[128,1536]{1,0:T(8,128)(2,1)} %get-tuple-element.115.k_ref, bf16[128,1536]{1,0:T(8,128)(2,1)} %get-tuple-element.114.v_ref, s32[768,128]{1,0:T(8,128)} %broadcast_in_dim.26.slot_ref), custom_call_target="tpu_custom_call" | custom-call | flops 1207959552 | bytes 4718592 | tf_op jit(solution)/shard_map/cross_attend/pallas_call | solution.py:300
  268.0 54.1 %all-gather.9.cloned.1.call-done = bf16[1536,6144]{1,0:T(8,128)(2,1)} async-done(((bf16[96,6144]{1,0:T(8,128)(2,1)}), bf16[1536,6144]{1,0:T(8,128)(2,1)}) %all-gather.9.cloned.1.call-update) | async-done | bytes 18874384 | tf_op jit(solution)/shard_map/all_gather | solution.py:525
  322.0 27.6 %fusion.3 = (f32[768,6144]{1,0:T(8,128)}, bf16[768,6144]{1,0:T(8,128)(2,1)S(1)}) fusion(bf16[1536,6144]{1,0:T(8,128)(2,1)} %all-gather.9.cloned.1.call-done, f32[768,1536]{1,0:T(8,128)} %copy-done.7, f32[1536]{0:T(1024)S(1)} %copy-done.54, f32[1536]{0:T(1024)S(1)} %get-tuple-element.80, f32[768]{0:T(1024)S(1)} %add_rsqrt_fusion.2, ...), kind=kOutput, calls=%fused_computation.5 | convolution fusion | flops 14548598784 | bytes 51922944 | tf_op jit(solution)/shard_map/dot_general | solution.py:22
  353.2 17.8 %convolution_convert_fusion = bf16[6144,1536]{1,0:T(8,128)(2,1)} fusion(bf16[768,6144]{1,0:T(8,128)(2,1)S(1)} %get-tuple-element.98, bf16[768,1536]{1,0:T(8,128)(2,1)S(1)} %copy-done.24), kind=kOutput, calls=%fused_computation.1 | convolution fusion | flops 14504951808 | bytes 30670848 | tf_op jit(solution)/shard_map/dot_general | solution.py:26
  371.2 51.4 %all-gather.11.cloned.1.call-done = bf16[6144,1536]{1,0:T(8,128)(2,1)} async-done(((bf16[384,1536]{1,0:T(8,128)(2,1)}), bf16[6144,1536]{1,0:T(8,128)(2,1)}) %all-gather.11.cloned.1.call-update) | async-done | bytes 18874384 | tf_op jit(solution)/shard_map/all_gather | solution.py:525
  422.6 27.2 %multiply_convert_fusion = bf16[768,6144]{1,0:T(8,128)(2,1)} fusion(f32[768,6144]{1,0:T(8,128)} %get-tuple-element.41, bf16[768,1536]{1,0:T(8,128)(2,1)S(1)} %copy-done.24, bf16[6144,1536]{1,0:T(8,128)(2,1)} %all-gather.11.cloned.1.call-done), kind=kOutput, calls=%fused_computation.7 | convolution fusion | flops 14504951808 | bytes 49545216 | tf_op jit(solution)/shard_map/dot_general | solution.py:32
  449.8 15.3 %convolution_convert_fusion.2 = bf16[1536,3072]{1,0:T(8,128)(2,1)} fusion(bf16[768,6144]{1,0:T(8,128)(2,1)} %multiply_convert_fusion, s32[]{:T(128)S(6)} %select_n.259, f32[768,1536]{1,0:T(8,128)} %copy-done.7, f32[1536]{0:T(1024)S(1)} %copy-done.54, f32[1536]{0:T(1024)S(1)} %get-tuple-element.80, f32[768]{0:T(1024)S(1)} %add_rsqrt_fusion.2, ...), kind=kOutput, calls=%fused_computation.13 | convolution fusion | flops 7258374144 | bytes 18892804 | tf_op jit(solution)/shard_map/dot_general | solution.py:26
  478.6 24.5 %multiply_reduce_fusion = (f32[1536]{0:T(1024)}, f32[768]{0:T(1024)S(1)}, f32[768]{0:T(1024)S(1)}, f32[1536]{0:T(1024)}, f32[768,1536]{1,0:T(8,128)}) fusion(f32[768,1536]{1,0:T(8,128)} %copy-done.7, f32[768]{0:T(1024)S(1)} %add_rsqrt_fusion.2, f32[768]{0:T(1024)S(1)} %broadcast_multiply_fusion.8, f32[1536]{0:T(1024)S(1)} %get-tuple-element.80, ...), kind=kOutput, calls=%fused_computation.55 | convolution fusion | flops 14506125312 | bytes 37779456 | tf_op jit(solution)/shard_map/dot_general | solution.py:32
  524.6 18.8 %cross_attend_back.1 = (bf16[768,1536]{1,0:T(8,128)(2,1)}, f32[128,1536]{1,0:T(8,128)}, f32[128,1536]{1,0:T(8,128)}) custom-call(bf16[768,1536]{1,0:T(8,128)(2,1)} %fusion.56.q_ref, bf16[768,1536]{1,0:T(8,128)(2,1)} %fusion.59.g_ref, bf16[128,1536]{1,0:T(8,128)(2,1)} %get-tuple-element.115.k_ref, bf16[128,1536]{1,0:T(8,128)(2,1)} %get-tuple-element.114.v_ref, ...), custom_call_target="tpu_custom_call" | custom-call | flops 3019898880 | bytes 7077888 | tf_op jit(solution)/shard_map/cross_attend_back/pallas_call | solution.py:351
  623.1 15.4 %self_attend_back.2 = (f32[2,4,6,64,384]{4,3,2,1,0:T(8,128)}, bf16[1536,768]{1,0:T(8,128)(2,1)}, bf16[1536,768]{1,0:T(8,128)(2,1)}) custom-call(s32[4,4]{1,0:T(4,128)} %pad_add_fusion.bounds, bf16[1536,768]{1,0:T(8,128)(2,1)} %convolution_convert_fusion.9.q_ref, bf16[1536,768]{1,0:T(8,128)(2,1)} %pad_maximum_fusion.4.g_ref, ...), custom_call_target="tpu_custom_call" | custom-call | flops 150994944 | bytes 98304 | tf_op jit(solution)/shard_map/self_attend_back/pallas_call | solution.py:261
  641.2 84.3 %collective-permute-done.5 = bf16[1536,1536]{1,0:T(8,128)(2,1)} collective-permute-done((bf16[1536,1536]{1,0:T(8,128)(2,1)}, bf16[1536,1536]{1,0:T(8,128)(2,1)}, u32[]{:S(2)}, u32[]{:S(2)}) %collective-permute-start.5) | collective-permute-done | bytes 4718624 | tf_op jit(solution)/shard_map/ppermute | solution.py:383
  740.8 70.2 %self_attend_back.3 = (bf16[1536,768]{1,0:T(8,128)(2,1)}, bf16[1536,768]{1,0:T(8,128)(2,1)}, bf16[1536,768]{1,0:T(8,128)(2,1)}) custom-call(s32[4,4]{1,0:T(4,128)} %pad_add_fusion.1.bounds, bf16[1536,768]{1,0:T(8,128)(2,1)} %convolution_convert_fusion.9.q_ref, bf16[1536,768]{1,0:T(8,128)(2,1)} %pad_maximum_fusion.4.g_ref, ...), custom_call_target="tpu_custom_call" | custom-call | flops 150994944 | bytes 98304 | tf_op jit(solution)/shard_map/self_attend_back/pallas_call | solution.py:261
  818.4 26.8 %collective-permute-done.8 = bf16[4,192,1536]{2,1,0:T(8,128)(2,1)} collective-permute-done((bf16[4,192,1536]{2,1,0:T(8,128)(2,1)}, bf16[4,192,1536]{2,1,0:T(8,128)(2,1)}, u32[]{:S(2)}, u32[]{:S(2)}) %collective-permute-start.8) | collective-permute-done | bytes 2359328 | tf_op jit(solution)/shard_map/ppermute | solution.py:383
  849.0 19.1 %convolution_convert_fusion.3 = bf16[1536,2304]{1,0:T(8,128)(2,1)} fusion(bf16[1536,768]{1,0:T(8,128)(2,1)} %copy-done.11, bf16[1536,768]{1,0:T(8,128)(2,1)} %copy-done.12, bf16[1536,768]{1,0:T(8,128)(2,1)} %get-tuple-element.55, f32[1536]{0:T(1024)S(1)} %copy-done.51, f32[1536]{0:T(1024)S(1)} %copy-done.40, f32[1536]{0:T(1024)S(1)} %copy-done.60, ...), kind=kOutput, calls=%fused_computation.14 | convolution fusion | flops 10917642240 | bytes 18898944 | tf_op jit(solution)/shard_map/dot_general | solution.py:26
  873.8 21.3 %collective-permute-start.17 = (bf16[2,192,1536]{2,1,0:T(8,128)(2,1)}, bf16[2,192,1536]{2,1,0:T(8,128)(2,1)}, u32[]{:S(2)}, u32[]{:S(2)}) collective-permute-start(bf16[2,192,1536]{2,1,0:T(8,128)(2,1)} %dynamic-slice_bitcast_fusion.1), channel_id=1, source_target_pairs={{0,8},{2,10},{4,12},{6,14},{8,0},{10,2},{12,4},{14,6},{16,24},{18,... | collective-permute-start | bytes 3538952 | tf_op jit(solution)/shard_map/ppermute | solution.py:383
  895.1 15.9 %fusion.10 = f32[1536,1536]{1,0:T(8,128)} fusion(bf16[1536,2304]{1,0:T(8,128)(2,1)S(1)} %copy-done.16, bf16[1536,2432]{1,0:T(8,128)(2,1)} %all-gather.5.cloned.1.call-done), kind=kOutput, calls=%fused_computation.29 | convolution fusion | flops 10871635968 | bytes 23592960 | tf_op jit(solution)/shard_map/dot_general | solution.py:32
  911.1 22.9 %add_convert_fusion.5 = bf16[768,1536]{1,0:T(8,128)(2,1)} fusion(f32[768,1536]{1,0:T(8,128)} %copy-done.7, bf16[768,6144]{1,0:T(8,128)(2,1)} %copy-done.63, bf16[6144,1536]{1,0:T(8,128)(2,1)} %all-gather.11.cloned.1.call-done), kind=kOutput, calls=%fused_computation.67 | convolution fusion | flops 14497873920 | bytes 35389440 | tf_op jit(solution)/shard_map/dot_general | solution.py:22
  951.4 37.7 %collective-permute-done.18 = bf16[1,192,1536]{2,1,0:T(8,128)(2,1)S(1)} collective-permute-done((bf16[1,192,1536]{2,1,0:T(8,128)(2,1)S(1)}, bf16[1,192,1536]{2,1,0:T(8,128)(2,1)S(1)}, u32[]{:S(2)}, u32[]{:S(2)}) %collective-permute-start.18) | collective-permute-done | bytes 589856 | tf_op jit(solution)/shard_map/ppermute | solution.py:383
  1000.0 40.8 %psum.7 = f32[6,1536]{1,0:T(8,128)S(1)} all-reduce(f32[6,1536]{1,0:T(8,128)S(1)} %stack.121), channel_id=1, replica_groups=mesh['fsdp'=16,'seq'=2] {'fsdp','seq'}, use_global_device_ids=true, to_apply=%region_24.25 | all-reduce | flops 9216 | bytes 73728 | tf_op jit(solution)/shard_map/psum | solution.py:649
  1049.6 22.1 %collective-permute-done.16 = bf16[96,2,768]{2,1,0:T(2,128)(2,1)S(1)} collective-permute-done((bf16[96,2,768]{2,1,0:T(2,128)(2,1)S(1)}, bf16[96,2,768]{2,1,0:T(2,128)(2,1)S(1)}, u32[]{:S(2)}, u32[]{:S(2)}) %collective-permute-start.16) | collective-permute-done | bytes 294944 | tf_op jit(solution)/shard_map/ppermute | solution.py:383
  (323 shorter events, 322.9 us)
Async XLA Ops:
  7.2 76.3 %all-gather.5.cloned.1.call-start = ((), (), s32[]{:S(2)}) async-start(), calls=%async_computation.3 | async-start | bytes 7938048 | tf_op jit(solution)/shard_map/all_gather | solution.py:525
  11.6 205.1 %all-gather.7.cloned.1.call-start = ((), (), s32[]{:S(2)}) async-start(), calls=%async_computation.4 | async-start | bytes 20054016 | tf_op jit(solution)/shard_map/all_gather | solution.py:525
  16.4 305.7 %all-gather.9.cloned.1.call-start = ((), (), s32[]{:S(2)}) async-start(), calls=%async_computation.5 | async-start | bytes 20054016 | tf_op jit(solution)/shard_map/all_gather | solution.py:525
  17.1 405.4 %all-gather.11.cloned.1.call-start = ((), (), s32[]{:S(2)}) async-start(), calls=%async_computation.6 | async-start | bytes 20054016 | tf_op jit(solution)/shard_map/all_gather | solution.py:525
  17.7 603.8 %reduce-scatter.4.cloned.1.call-start = ((), (), s32[]{:S(2)}) async-start(), calls=%async_computation.7 | async-start | bytes 20054016 | tf_op jit(solution)/shard_map/reduce_scatter | solution.py:448
  17.7 54.4 %collective-permute-start = (bf16[768,1536]{1,0:T(8,128)(2,1)S(1)}, bf16[768,1536]{1,0:T(8,128)(2,1)}, u32[]{:S(2)}, u32[]{:S(2)}) collective-permute-start(bf16[768,1536]{1,0:T(8,128)(2,1)S(1)} %copy-done.1), channel_id=1, source_target_pairs={{0,1},{1,0},{2,3},{3,2},{4,5},{5,4},{6,7},{7,6},{8,9},{9,8},{10,11... | collective-permute-start | bytes 7077896 | tf_op jit(solution)/shard_map/ppermute | solution.py:383
  100.8 59.0 %collective-permute-start.1 = (bf16[1536,1536]{1,0:T(8,128)(2,1)}, bf16[1536,1536]{1,0:T(8,128)(2,1)}, u32[]{:S(2)}, u32[]{:S(2)}) collective-permute-start(bf16[1536,1536]{1,0:T(8,128)(2,1)} %convolution_convert_fusion.8.k_ref.v_ref), channel_id=1, source_target_pairs={{0,2},{2,4},{4,6},{6,8},{8,10},{10,12},{12,14},{14,16},{16,18},{18... | collective-permute-start | bytes 14155784 | tf_op jit(solution)/shard_map/ppermute | solution.py:389
  220.6 18.2 %collective-permute-start.3 = (bf16[128,2,768]{2,0,1:T(8,128)(2,1)S(1)}, bf16[128,2,768]{2,0,1:T(8,128)(2,1)S(1)}, u32[]{:S(2)}, u32[]{:S(2)}) collective-permute-start(bf16[128,2,768]{2,0,1:T(8,128)(2,1)S(1)} %copy.74), channel_id=1, source_target_pairs={{0,1},{1,0},{2,3},{3,2},{4,5},{5,4},{6,7},{7,6},{8,9},{9,8},{10,11... | collective-permute-start | bytes 1179656 | tf_op jit(solution)/shard_map/ppermute | solution.py:383
  371.1 539.9 %reduce-scatter.6.cloned.1.call-start = ((), (), s32[]{:S(2)}) async-start(), calls=%async_computation.8 | async-start | bytes 20054016 | tf_op jit(solution)/shard_map/reduce_scatter | solution.py:615
  478.2 31.2 %collective-permute-start.4 = (bf16[1536,3072]{1,0:T(8,128)(2,1)}, bf16[1536,3072]{1,0:T(8,128)(2,1)}, u32[]{:S(2)}, u32[]{:S(2)}) collective-permute-start(bf16[1536,3072]{1,0:T(8,128)(2,1)} %convolution_convert_fusion.1), channel_id=1, source_target_pairs={{0,2},{2,0},{4,6},{6,4},{8,10},{10,8},{12,14},{14,12},{16,18},{18,... | collective-permute-start | bytes 28311560 | tf_op jit(solution)/shard_map/ppermute | solution.py:383
  544.6 41.7 %collective-permute-start.12 = (bf16[128,2,768]{2,0,1:T(8,128)(2,1)S(1)}, bf16[128,2,768]{2,0,1:T(8,128)(2,1)S(1)}, u32[]{:S(2)}, u32[]{:S(2)}) collective-permute-start(bf16[128,2,768]{2,0,1:T(8,128)(2,1)S(1)} %fusion.74), channel_id=1, source_target_pairs={{0,1},{1,0},{2,3},{3,2},{4,5},{5,4},{6,7},{7,6},{8,9},{9,8},{10,11... | collective-permute-start | bytes 1179656 | tf_op jit(solution)/shard_map/ppermute | solution.py:383
  585.8 28.1 %collective-permute-start.6 = (bf16[768,768]{1,0:T(8,128)(2,1)}, bf16[768,768]{1,0:T(8,128)(2,1)}, u32[]{:S(2)}, u32[]{:S(2)}) collective-permute-start(bf16[768,768]{1,0:T(8,128)(2,1)} %constant_dynamic-slice_fusion.2), channel_id=1, source_target_pairs={{0,1},{1,0},{2,3},{3,2},{4,5},{5,4},{6,7},{7,6},{8,9},{9,8},{10,11... | collective-permute-start | bytes 3538952 | tf_op jit(solution)/shard_map/ppermute | solution.py:383
  621.5 453.5 %reduce-scatter.8.cloned.1.call-start = ((), (), s32[]{:S(2)}) async-start(), calls=%async_computation.9 | async-start | bytes 7520256 | tf_op jit(solution)/shard_map/reduce_scatter | solution.py:448
  621.5 104.0 %collective-permute-start.5 = (bf16[1536,1536]{1,0:T(8,128)(2,1)}, bf16[1536,1536]{1,0:T(8,128)(2,1)}, u32[]{:S(2)}, u32[]{:S(2)}) collective-permute-start(bf16[1536,1536]{1,0:T(8,128)(2,1)} %add_convert_fusion.2), channel_id=1, source_target_pairs={{0,1},{1,0},{2,3},{3,2},{4,5},{5,4},{6,7},{7,6},{8,9},{9,8},{10,11... | collective-permute-start | bytes 14155784 | tf_op jit(solution)/shard_map/ppermute | solution.py:383
  638.5 172.6 %collective-permute-start.10 = (bf16[1536,768]{1,0:T(8,128)(2,1)}, bf16[1536,768]{1,0:T(8,128)(2,1)}, u32[]{:S(2)}, u32[]{:S(2)}) collective-permute-start(bf16[1536,768]{1,0:T(8,128)(2,1)} %get-tuple-element.59), channel_id=1, source_target_pairs={{2,0},{4,2},{6,4},{8,6},{10,8},{12,10},{14,12},{16,14},{18,16},{20... | collective-permute-start | bytes 7077896 | tf_op jit(solution)/shard_map/ppermute | solution.py:389
  639.8 174.5 %collective-permute-start.9 = (bf16[1536,768]{1,0:T(8,128)(2,1)}, bf16[1536,768]{1,0:T(8,128)(2,1)}, u32[]{:S(2)}, u32[]{:S(2)}) collective-permute-start(bf16[1536,768]{1,0:T(8,128)(2,1)} %get-tuple-element.57), channel_id=1, source_target_pairs={{2,0},{4,2},{6,4},{8,6},{10,8},{12,10},{14,12},{16,14},{18,16},{20... | collective-permute-start | bytes 7077896 | tf_op jit(solution)/shard_map/ppermute | solution.py:389
  736.5 108.7 %collective-permute-start.8 = (bf16[4,192,1536]{2,1,0:T(8,128)(2,1)}, bf16[4,192,1536]{2,1,0:T(8,128)(2,1)}, u32[]{:S(2)}, u32[]{:S(2)}) collective-permute-start(bf16[4,192,1536]{2,1,0:T(8,128)(2,1)} %dynamic-slice_bitcast_fusion), channel_id=1, source_target_pairs={{0,4},{2,6},{4,0},{6,2},{8,12},{10,14},{12,8},{14,10},{16,20},{18,... | collective-permute-start | bytes 7077896 | tf_op jit(solution)/shard_map/ppermute | solution.py:383
  739.3 78.0 %collective-permute-start.7 = (bf16[384,1536]{1,0:T(8,128)(2,1)S(1)}, bf16[384,1536]{1,0:T(8,128)(2,1)S(1)}, u32[]{:S(2)}, u32[]{:S(2)}) collective-permute-start(bf16[384,1536]{1,0:T(8,128)(2,1)S(1)} %copy-done.34), channel_id=1, source_target_pairs={{0,1},{1,0},{2,3},{3,2},{4,5},{5,4},{6,7},{7,6},{8,9},{9,8},{10,11... | collective-permute-start | bytes 3538952 | tf_op jit(solution)/shard_map/ppermute | solution.py:383
  873.8 64.5 %collective-permute-start.17 = (bf16[2,192,1536]{2,1,0:T(8,128)(2,1)}, bf16[2,192,1536]{2,1,0:T(8,128)(2,1)}, u32[]{:S(2)}, u32[]{:S(2)}) collective-permute-start(bf16[2,192,1536]{2,1,0:T(8,128)(2,1)} %dynamic-slice_bitcast_fusion.1), channel_id=1, source_target_pairs={{0,8},{2,10},{4,12},{6,14},{8,0},{10,2},{12,4},{14,6},{16,24},{18,... | collective-permute-start | bytes 3538952 | tf_op jit(solution)/shard_map/ppermute | solution.py:383
  940.0 49.0 %collective-permute-start.18 = (bf16[1,192,1536]{2,1,0:T(8,128)(2,1)S(1)}, bf16[1,192,1536]{2,1,0:T(8,128)(2,1)S(1)}, u32[]{:S(2)}, u32[]{:S(2)}) collective-permute-start(bf16[1,192,1536]{2,1,0:T(8,128)(2,1)S(1)} %constant_dynamic-slice_fusion.1), channel_id=1, source_target_pairs={{0,16},{2,18},{4,20},{6,22},{8,24},{10,26},{12,28},{14,30},{16,0},... | collective-permute-start | bytes 1769480 | tf_op jit(solution)/shard_map/ppermute | solution.py:383
  942.1 51.7 %collective-permute-start.11 = (bf16[768,1536]{1,0:T(8,128)(2,1)S(1)}, bf16[768,1536]{1,0:T(8,128)(2,1)S(1)}, u32[]{:S(2)}, u32[]{:S(2)}) collective-permute-start(bf16[768,1536]{1,0:T(8,128)(2,1)S(1)} %dynamic-slice_convert_fusion), channel_id=1, source_target_pairs={{0,1},{1,0},{2,3},{3,2},{4,5},{5,4},{6,7},{7,6},{8,9},{9,8},{10,11... | collective-permute-start | bytes 7077896 | tf_op jit(solution)/shard_map/ppermute | solution.py:383
  992.0 49.5 %collective-permute-start.20 = (bf16[2,96,1536]{2,1,0:T(8,128)(2,1)}, bf16[2,96,1536]{2,1,0:T(8,128)(2,1)}, u32[]{:S(2)}, u32[]{:S(2)}) collective-permute-start(bf16[2,96,1536]{2,1,0:T(8,128)(2,1)} %pad_maximum_fusion.8), channel_id=1, source_target_pairs={{0,1},{1,0},{2,3},{3,2},{4,5},{5,4},{6,7},{7,6},{8,9},{9,8},{10,11... | collective-permute-start | bytes 1769480 | tf_op jit(solution)/shard_map/ppermute | solution.py:383
  1044.6 28.9 %collective-permute-start.15 = (bf16[3,96,1536]{2,1,0:T(8,128)(2,1)}, bf16[3,96,1536]{2,1,0:T(8,128)(2,1)}, u32[]{:S(2)}, u32[]{:S(2)}) collective-permute-start(bf16[3,96,1536]{2,1,0:T(8,128)(2,1)} %slice.167), channel_id=1, source_target_pairs={{0,1},{1,0},{2,3},{3,2},{4,5},{5,4},{6,7},{7,6},{8,9},{9,8},{10,11... | collective-permute-start | bytes 2654216 | tf_op jit(solution)/shard_map/ppermute | solution.py:383
  1047.0 24.8 %collective-permute-start.16 = (bf16[96,2,768]{2,1,0:T(2,128)(2,1)S(1)}, bf16[96,2,768]{2,1,0:T(2,128)(2,1)S(1)}, u32[]{:S(2)}, u32[]{:S(2)}) collective-permute-start(bf16[96,2,768]{2,1,0:T(2,128)(2,1)S(1)} %reshape_squeeze.3), channel_id=1, source_target_pairs={{0,1},{1,0},{2,3},{3,2},{4,5},{5,4},{6,7},{7,6},{8,9},{9,8},{10,11... | collective-permute-start | bytes 884744 | tf_op jit(solution)/shard_map/ppermute | solution.py:383
  (73 other events, 1391.7 us)
Sparse Core Ops, SparseCore 0:
  11.7 71.7 all-gather.4
  85.7 130.9 all-gather.6
  218.3 103.7 all-gather.8
  323.5 99.0 all-gather.10
  426.5 194.8 reduce-scatter.3
  625.4 263.1 reduce-scatter.5
  911.2 102.5 reduce-scatter.7

commit v5 on v4

--- a/solution.py
+++ b/solution.py
@@ -474,8 +474,7 @@
     return lax.dynamic_index_in_dim(blocks, place, 1, keepdims=False)
 
 
-def own_rows(kept, came, at):
-    value, bit = both(kept, came), 4
+def own_rows(value, at, bit):
     while value.shape[0] > 1:
         at = at // 2
         value = both(half_rows(value, at % 2), swap(half_rows(value, 1 - at % 2), "fsdp", bit))
@@ -540,16 +539,25 @@
     slots = own_block(seg_group, 0) - group_index * (group_rows // SPAN)
     slots_wide = jnp.broadcast_to(slots[:, None], (tok_rows, PAIR))
 
+    gate = lax.optimization_barrier
+    by_steps = seq_count == 2 and group_rows == SPAN
     inputs = tokens.astype(jnp.float32)
-    n_group, _ = normed(gathered(tokens, 0).astype(jnp.float32))
-    normed_one = (n_group * gains[0] + biases[0]).astype(jnp.bfloat16)
+    norm_one = lambda rows: (normed(rows.astype(jnp.float32))[0] * gains[0] + biases[0]).astype(jnp.bfloat16)
+    normed_one = norm_one(gathered(tokens, 0))
     kv_own = matmul(normed_one, w_kv).astype(jnp.bfloat16)
-    kv_before = passed_along(kv_own[group_rows - SPAN :], "fsdp", 1)
     queries = matmul(normed_one, w_q).astype(jnp.bfloat16)
+    if by_steps:
+        before = passed_along(tokens, "fsdp", 1)
+        before_other = swap(before, "seq", 1)
+    else:
+        kv_before = passed_along(kv_own[group_rows - SPAN :], "fsdp", 1)
+    pad_kv = lambda kv: jnp.concatenate([paired(kv[:, :head_cols]), paired(kv[:, head_cols:])], axis=1)
     if head_cols % PAIR:
-        pad_kv = lambda kv: jnp.concatenate([paired(kv[:, :head_cols]), paired(kv[:, head_cols:])], axis=1)
         queries, kv_own, kv_before = paired(queries), pad_kv(kv_own), pad_kv(kv_before)
     heads_state = self_attend(queries, kv_own, starts, SPAN, SPAN)
+    if by_steps:
+        before, before_other, heads_state = gate((before, before_other, heads_state))
+        kv_before = matmul(norm_one(in_order(before, before_other, 0)), w_kv).astype(jnp.bfloat16)
     heads_out, log_totals = self_attend(queries, kv_before, starts, SPAN, 0, heads_state)
     attended = exchanged(heads_out[:, :head_cols], 0, 1)
     hidden_one = inputs + matmul(attended, full_out)
@@ -574,8 +582,6 @@
     slope = below + upward * (jnp.exp(-0.5 * upward * upward) * 0.3989422804014327)
     layer_out = (hidden_two + matmul(active, full_down)).astype(jnp.bfloat16)
 
-    gate = lax.optimization_barrier
-    by_steps = seq_count == 2
     chip = group_index // 2
     grad_down, slope = gate((contract_rows(active, cotangent).astype(jnp.bfloat16), slope))
     grad_down = scattered(grad_down)
@@ -625,8 +631,8 @@
         down_beside = swap(grad_down, "seq", 1)
     grad_q, *grad_own = self_attend_back(*back_args, kv_own, starts, SPAN, SPAN, query_state)
     if by_steps:
-        down_beside, first_came, grad_q = gate((down_beside, swap(first_away, "fsdp", 2), grad_q))
-        grad_up = own_rows(half_rows(total, chip % 2), first_came, chip)
+        first_came = swap(first_away, "fsdp", 2)
+        down_beside, grad_q = gate((down_beside, grad_q))
         grad_down = grad_down.astype(jnp.float32) + down_beside.astype(jnp.float32)
     else:
         grad_up, grad_down = whole(grad_up), whole(grad_down)
@@ -640,15 +646,23 @@
     grad_wqkv, grad_proj = gate((contract_rows(normed_one, grad_proj).astype(jnp.bfloat16), grad_proj))
     grad_normed_one = contract_cols(grad_proj, w_qkv)
     grad_wqkv = scattered(gate((grad_wqkv, small, grad_normed_one))[0])
+    grad_cout, grad_cq, grad_wout = whole(small[:3]) if by_steps else [whole(part) for part in small[:3]]
+    grad_ckv = columns(small[3], 2)
+    if by_steps:
+        first_came, grad_normed_one = gate((first_came, grad_normed_one))
+        up_rows = both(half_rows(total, chip % 2), first_came)
+        second_came = swap(half_rows(up_rows, 1 - chip // 2 % 2), "fsdp", 4)
     grad_normed_one = summed_block(grad_normed_one, 0)
     n_one, root_one = normed(inputs)
     back_x, gain_one, bias_one = norm_back(grad_normed_one, n_one, root_one, gains[0])
     grad_tokens = (grad_one + back_x).astype(jnp.bfloat16)
 
-    grad_cout, grad_cq, grad_wout = whole(small[:3]) if by_steps else [whole(part) for part in small[:3]]
-    norm_grads = lax.psum(
-        jnp.stack([gain_one, gain_two, gain_three, bias_one, bias_two, bias_three]), ("fsdp", "seq")
-    )
+    norm_grads = jnp.stack([gain_one, gain_two, gain_three, bias_one, bias_two, bias_three])
+    norm_grads, grad_cout, grad_cq, grad_wout, grad_ckv = gate((norm_grads, grad_cout, grad_cq, grad_wout, grad_ckv))
+    norm_grads = lax.psum(norm_grads, ("fsdp", "seq"))
+    if by_steps:
+        norm_grads, second_came = gate((norm_grads, second_came))
+        grad_up = own_rows(both(half_rows(up_rows, chip // 2 % 2), second_came), chip // 2, 8)
     norm_grads = lax.dynamic_slice_in_dim(norm_grads, group_index * shard_rows, shard_rows, 1)
     return (
         layer_out,
@@ -657,7 +671,7 @@
         columns(grad_wqkv, 3),
         grad_wout,
         grad_cq,
-        columns(small[3], 2),
+        grad_ckv,
         grad_cout,
         grad_up,
         grad_down,

time: 1100 us -> 1060 us (0.964)
  starting transfers between devices: 51.7 us -> 22.5 us
  waiting for transfers between devices: 402 us -> 376 us
  Pallas kernels: 173 us -> 157 us
  other arithmetic: 93.9 us -> 105 us
    reduce_scatter x1, waiting for transfers between devices: 0.01 us -> 39.8 us  [shards(): lax.psum_scatter(gate((jnp.stack(small), grad_down, grad_heads))[0], 'fsd...]
    ppermute x18 -> x19, waiting for transfers between devices: 263 us -> 227 us  [swap(): return lax.ppermute(value, axis, [(i, i ^ bit) for i in range(count)])]
    all_gather x4, waiting for transfers between devices: 133 us -> 103 us  [shards(): row_block = lambda value: lax.all_gather(value, 'fsdp', axis=0, tiled=True)]
    ppermute x18 -> x19, starting transfers between devices: 44.1 us -> 15.5 us  [swap(): return lax.ppermute(value, axis, [(i, i ^ bit) for i in range(count)])]
    pallas_call x2, Pallas kernels: 85.6 us -> 74.5 us  [self_attend_back(): pl.pallas_call(functools.partial(attend_back_kernel, reach=reach, base=ba...]
    dot_general x8 -> x9, matrix products: 99.5 us -> 108 us  [matmul(): return jnp.dot(left_side, right_side, preferred_element_type=jnp.float32)]
  transfers between devices with their start and end apart: 28 -> 29, of which waited for: 14 -> 15; matrix products, arithmetic and copies ran while one was open for 36% -> 39% of each run, Pallas kernels for 16% -> 15%
where the time goes in v5:
time: 1060 us; the launch traced here: 1050 us
  waiting for transfers between devices  376 us (35%)
  matrix products  290 us (27%)
  Pallas kernels  157 us (15%)
  other arithmetic  105 us (10%)
  blocking collectives  44.1 us (4%)
  local copies, waits for them, and re-layouts  41.4 us (4%)
  starting transfers between devices  22.5 us (2%)
  between operations  15.8 us (1%)
    ppermute x19, waiting for transfers between devices, swap(): return lax.ppermute(value, axis, [(i, i ^ bit) for i in range(count)])  227 us
    dot_general x9, matrix products, matmul(): return jnp.dot(left_side, right_side, preferred_element_type=jnp.float32)  108 us
    all_gather x4, waiting for transfers between devices, shards(): row_block = lambda value: lax.all_gather(value, 'fsdp', axis=0, tiled=True)  103 us
    dot_general x7, matrix products, contract_cols(): lax.dot_general(left_side, right_side, (((1,), (1,)), ((), ())), preferre...  97.3 us
    dot_general x8, matrix products, contract_rows(): lax.dot_general(left_side, right_side, (((0,), (0,)), ((), ())), preferre...  84.4 us
    pallas_call x2, Pallas kernels, self_attend_back(): pl.pallas_call(functools.partial(attend_back_kernel, reach=reach, base=ba...  74.5 us
    pallas_call x2, Pallas kernels, self_attend(): pl.pallas_call(functools.partial(attend_kernel, reach=reach, base=base, p...  45.6 us
    psum x1, blocking collectives, shards(): norm_grads = lax.psum(norm_grads, ('fsdp', 'seq'))  44.1 us
  transfers between devices with their start and end apart: 29, of which 15 were waited for; matrix products, arithmetic and copies ran while one was open for 39% of the time, Pallas kernels for 15%

profile of v5, /device:TPU:0, one launch (start us, length us, event | category | flops | bytes accessed | tf_op | source)
XLA Modules:
  0.0 1052.4 jit_solution(10134391166511394405)
XLA Ops:
  30.3 45.8 %collective-permute-done = bf16[768,1536]{1,0:T(8,128)(2,1)} collective-permute-done((bf16[768,1536]{1,0:T(8,128)(2,1)S(1)}, bf16[768,1536]{1,0:T(8,128)(2,1)}, u32[]{:S(2)}, u32[]{:S(2)}) %collective-permute-start) | collective-permute-done | bytes 2359328 | tf_op jit(solution)/shard_map/ppermute | solution.py:383
  82.7 14.8 %all-gather.5.cloned.1.call-done = bf16[1536,2432]{1,0:T(8,128)(2,1)} async-done(((bf16[96,2432]{1,0:T(8,128)(2,1)}), bf16[1536,2432]{1,0:T(8,128)(2,1)}) %all-gather.5.cloned.1.call-update) | async-done | bytes 7471120 | tf_op jit(solution)/shard_map/all_gather | solution.py:524
  122.3 33.4 %self_attend.2.refs_0_ = f32[2,4,6,80,384]{4,3,2,1,0:T(8,128)} custom-call(s32[4,4]{1,0:T(4,128)} %pad_add_fusion.1.bounds, bf16[1536,768]{1,0:T(8,128)(2,1)} %convolution_convert_fusion.10.q_ref, bf16[1536,1536]{1,0:T(8,128)(2,1)} %convolution_convert_fusion.9.k_ref.v_ref, bf16[1536,1536]{1,0:T(8,128)(2,1)} %convolution_convert_fusion.9.k_ref.v_ref, ...), custom_call_target="tpu_custom_call" | custom-call | flops 150994944 | bytes 98304 | tf_op jit(solution)/shard_map/self_attend/pallas_call | solution.py:161
  190.7 14.4 %collective-permute-done.3 = bf16[768,768]{1,0:T(8,128)(2,1)} collective-permute-done((bf16[768,768]{1,0:T(8,128)(2,1)}, bf16[768,768]{1,0:T(8,128)(2,1)}, u32[]{:S(2)}, u32[]{:S(2)}) %collective-permute-start.3) | collective-permute-done | bytes 1179680 | tf_op jit(solution)/shard_map/ppermute | solution.py:383
  232.5 18.2 %cross_attend.1 = bf16[768,1536]{1,0:T(8,128)(2,1)} custom-call(bf16[768,1536]{1,0:T(8,128)(2,1)} %fusion.68.q_ref, bf16[128,1536]{1,0:T(8,128)(2,1)} %get-tuple-element.139.k_ref, bf16[128,1536]{1,0:T(8,128)(2,1)} %get-tuple-element.138.v_ref, s32[768,128]{1,0:T(8,128)} %broadcast_in_dim.26.slot_ref), custom_call_target="tpu_custom_call" | custom-call | flops 1207959552 | bytes 4718592 | tf_op jit(solution)/shard_map/cross_attend/pallas_call | solution.py:300
  260.3 37.0 %all-gather.9.cloned.1.call-done = bf16[1536,6144]{1,0:T(8,128)(2,1)} async-done(((bf16[96,6144]{1,0:T(8,128)(2,1)}), bf16[1536,6144]{1,0:T(8,128)(2,1)}) %all-gather.9.cloned.1.call-update) | async-done | bytes 18874384 | tf_op jit(solution)/shard_map/all_gather | solution.py:524
  297.3 27.4 %fusion.3 = (f32[768,6144]{1,0:T(8,128)}, bf16[768,6144]{1,0:T(8,128)(2,1)S(1)}) fusion(bf16[1536,6144]{1,0:T(8,128)(2,1)} %all-gather.9.cloned.1.call-done, f32[768,1536]{1,0:T(8,128)} %copy-done.7, f32[1536]{0:T(1024)S(1)} %copy-done.49, f32[1536]{0:T(1024)S(1)} %get-tuple-element.102, f32[768]{0:T(1024)S(1)} %add_rsqrt_fusion.3, ...), kind=kOutput, calls=%fused_computation.5 | convolution fusion | flops 14548598784 | bytes 51922944 | tf_op jit(solution)/shard_map/dot_general | solution.py:22
  328.3 17.9 %convolution_convert_fusion = bf16[6144,1536]{1,0:T(8,128)(2,1)} fusion(bf16[768,6144]{1,0:T(8,128)(2,1)S(1)} %get-tuple-element.120, bf16[768,1536]{1,0:T(8,128)(2,1)S(1)} %copy-done.21), kind=kOutput, calls=%fused_computation.1 | convolution fusion | flops 14504951808 | bytes 30670848 | tf_op jit(solution)/shard_map/dot_general | solution.py:26
  346.3 51.5 %all-gather.11.cloned.1.call-done = bf16[6144,1536]{1,0:T(8,128)(2,1)} async-done(((bf16[384,1536]{1,0:T(8,128)(2,1)}), bf16[6144,1536]{1,0:T(8,128)(2,1)}) %all-gather.11.cloned.1.call-update) | async-done | bytes 18874384 | tf_op jit(solution)/shard_map/all_gather | solution.py:524
  397.8 27.4 %multiply_convert_fusion = bf16[768,6144]{1,0:T(8,128)(2,1)} fusion(f32[768,6144]{1,0:T(8,128)} %get-tuple-element.55, bf16[768,1536]{1,0:T(8,128)(2,1)S(1)} %copy-done.21, bf16[6144,1536]{1,0:T(8,128)(2,1)} %all-gather.11.cloned.1.call-done), kind=kOutput, calls=%fused_computation.7 | convolution fusion | flops 14504951808 | bytes 49545216 | tf_op jit(solution)/shard_map/dot_general | solution.py:32
  425.2 15.4 %convolution_convert_fusion.2 = bf16[1536,3072]{1,0:T(8,128)(2,1)} fusion(bf16[768,6144]{1,0:T(8,128)(2,1)} %multiply_convert_fusion, s32[]{:T(128)S(6)} %select_n.271, f32[768,1536]{1,0:T(8,128)} %copy-done.7, f32[1536]{0:T(1024)S(1)} %copy-done.49, f32[1536]{0:T(1024)S(1)} %get-tuple-element.102, f32[768]{0:T(1024)S(1)} %add_rsqrt_fusion.3, ...), kind=kOutput, calls=%fused_computation.15 | convolution fusion | flops 7258374144 | bytes 18892804 | tf_op jit(solution)/shard_map/dot_general | solution.py:26
  440.6 12.9 %convolution_convert_fusion.1 = bf16[1536,3072]{1,0:T(8,128)(2,1)} fusion(bf16[768,6144]{1,0:T(8,128)(2,1)S(1)} %copy-done.56, s32[]{:T(128)S(6)} %select_n.272, f32[768,1536]{1,0:T(8,128)} %copy-done.7, f32[1536]{0:T(1024)S(1)} %copy-done.49, f32[1536]{0:T(1024)S(1)} %get-tuple-element.102, f32[768]{0:T(1024)S(1)} %add_rsqrt_fusion.3, ...), kind=kOutput, calls=%fused_computation.14 | convolution fusion | flops 7258374144 | bytes 18898948 | tf_op jit(solution)/shard_map/dot_general | solution.py:26
  453.8 24.3 %multiply_reduce_fusion = (f32[1536]{0:T(1024)}, f32[768]{0:T(1024)S(1)}, f32[768]{0:T(1024)S(1)}, f32[1536]{0:T(1024)}, f32[768,1536]{1,0:T(8,128)}) fusion(f32[768,1536]{1,0:T(8,128)} %copy-done.7, f32[768]{0:T(1024)S(1)} %add_rsqrt_fusion.3, f32[768]{0:T(1024)S(1)} %broadcast_multiply_fusion.9, f32[1536]{0:T(1024)S(1)} %get-tuple-element.102, ...), kind=kOutput, calls=%fused_computation.64 | convolution fusion | flops 14506125312 | bytes 37779456 | tf_op jit(solution)/shard_map/dot_general | solution.py:32
  499.7 19.1 %cross_attend_back.1 = (bf16[768,1536]{1,0:T(8,128)(2,1)}, f32[128,1536]{1,0:T(8,128)}, f32[128,1536]{1,0:T(8,128)}) custom-call(bf16[768,1536]{1,0:T(8,128)(2,1)} %fusion.68.q_ref, bf16[768,1536]{1,0:T(8,128)(2,1)} %fusion.71.g_ref, bf16[128,1536]{1,0:T(8,128)(2,1)} %get-tuple-element.139.k_ref, bf16[128,1536]{1,0:T(8,128)(2,1)} %get-tuple-element.138.v_ref, ...), custom_call_target="tpu_custom_call" | custom-call | flops 3019898880 | bytes 7077888 | tf_op jit(solution)/shard_map/cross_attend_back/pallas_call | solution.py:351
  598.7 15.4 %self_attend_back.2 = (f32[2,4,6,64,384]{4,3,2,1,0:T(8,128)}, bf16[1536,768]{1,0:T(8,128)(2,1)}, bf16[1536,768]{1,0:T(8,128)(2,1)}) custom-call(s32[4,4]{1,0:T(4,128)} %pad_add_fusion.bounds, bf16[1536,768]{1,0:T(8,128)(2,1)} %convolution_convert_fusion.10.q_ref, bf16[1536,768]{1,0:T(8,128)(2,1)} %pad_maximum_fusion.5.g_ref, ...), custom_call_target="tpu_custom_call" | custom-call | flops 150994944 | bytes 98304 | tf_op jit(solution)/shard_map/self_attend_back/pallas_call | solution.py:261
  623.7 78.1 %collective-permute-done.6 = bf16[1536,1536]{1,0:T(8,128)(2,1)} collective-permute-done((bf16[1536,1536]{1,0:T(8,128)(2,1)}, bf16[1536,1536]{1,0:T(8,128)(2,1)}, u32[]{:S(2)}, u32[]{:S(2)}) %collective-permute-start.6) | collective-permute-done | bytes 4718624 | tf_op jit(solution)/shard_map/ppermute | solution.py:383
  714.4 59.1 %self_attend_back.3 = (bf16[1536,768]{1,0:T(8,128)(2,1)}, bf16[1536,768]{1,0:T(8,128)(2,1)}, bf16[1536,768]{1,0:T(8,128)(2,1)}) custom-call(s32[4,4]{1,0:T(4,128)} %pad_add_fusion.1.bounds, bf16[1536,768]{1,0:T(8,128)(2,1)} %convolution_convert_fusion.10.q_ref, bf16[1536,768]{1,0:T(8,128)(2,1)} %pad_maximum_fusion.5.g_ref, ...), custom_call_target="tpu_custom_call" | custom-call | flops 150994944 | bytes 98304 | tf_op jit(solution)/shard_map/self_attend_back/pallas_call | solution.py:261
  785.2 19.1 %convolution_convert_fusion.3 = bf16[1536,2304]{1,0:T(8,128)(2,1)} fusion(bf16[1536,768]{1,0:T(8,128)(2,1)} %copy-done.11, bf16[1536,768]{1,0:T(8,128)(2,1)} %copy-done.12, bf16[1536,768]{1,0:T(8,128)(2,1)} %get-tuple-element.69, f32[1536]{0:T(1024)S(1)} %copy-done.46, f32[1536]{0:T(1024)S(1)} %copy-done.35, f32[1536]{0:T(1024)S(1)} %copy-done.55, ...), kind=kOutput, calls=%fused_computation.16 | convolution fusion | flops 10917642240 | bytes 18898944 | tf_op jit(solution)/shard_map/dot_general | solution.py:26
  804.3 16.1 %fusion.16 = f32[1536,1536]{1,0:T(8,128)S(1)} fusion(bf16[1536,2304]{1,0:T(8,128)(2,1)} %pad_maximum_fusion.1, bf16[1536,2432]{1,0:T(8,128)(2,1)} %all-gather.5.cloned.1.call-done), kind=kOutput, calls=%fused_computation.38 | convolution fusion | flops 10871635968 | bytes 23592960 | tf_op jit(solution)/shard_map/dot_general | solution.py:32
  834.1 39.8 %reduce-scatter.6.cloned.1.call-done = bf16[4,96,1536]{2,1,0:T(8,128)(2,1)} async-done(((bf16[4,1536,1536]{2,1,0:T(8,128)(2,1)}), bf16[4,96,1536]{2,1,0:T(8,128)(2,1)}) %reduce-scatter.6.cloned.1.call-update) | async-done | bytes 1179664 | tf_op jit(solution)/shard_map/reduce_scatter | solution.py:621
  874.0 22.1 %add_convert_fusion.5 = bf16[768,1536]{1,0:T(8,128)(2,1)} fusion(f32[768,1536]{1,0:T(8,128)} %copy-done.7, bf16[768,6144]{1,0:T(8,128)(2,1)} %copy-done.58, bf16[6144,1536]{1,0:T(8,128)(2,1)} %all-gather.11.cloned.1.call-done), kind=kOutput, calls=%fused_computation.76 | convolution fusion | flops 14497873920 | bytes 35389440 | tf_op jit(solution)/shard_map/dot_general | solution.py:22
  914.3 18.0 %collective-permute-done.17 = bf16[96,2,768]{2,1,0:T(2,128)(2,1)S(1)} collective-permute-done((bf16[96,2,768]{2,1,0:T(2,128)(2,1)S(1)}, bf16[96,2,768]{2,1,0:T(2,128)(2,1)S(1)}, u32[]{:S(2)}, u32[]{:S(2)}) %collective-permute-start.17) | collective-permute-done | bytes 294944 | tf_op jit(solution)/shard_map/ppermute | solution.py:383
  936.8 44.1 %psum.7 = f32[6,1536]{1,0:T(8,128)S(1)} all-reduce(f32[6,1536]{1,0:T(8,128)S(1)} %stack.118), channel_id=1, replica_groups=mesh['fsdp'=16,'seq'=2] {'fsdp','seq'}, use_global_device_ids=true, to_apply=%region_26.27 | all-reduce | flops 9216 | bytes 73728 | tf_op jit(solution)/shard_map/psum | solution.py:662
  986.8 24.5 %collective-permute-done.19 = bf16[1,192,1536]{2,1,0:T(8,128)(2,1)S(1)} collective-permute-done((bf16[1,192,1536]{2,1,0:T(8,128)(2,1)S(1)}, bf16[1,192,1536]{2,1,0:T(8,128)(2,1)S(1)}, u32[]{:S(2)}, u32[]{:S(2)}) %collective-permute-start.19) | collective-permute-done | bytes 589856 | tf_op jit(solution)/shard_map/ppermute | solution.py:383
  (341 shorter events, 340.7 us)
Async XLA Ops:
  7.2 90.3 %all-gather.5.cloned.1.call-start = ((), (), s32[]{:S(2)}) async-start(), calls=%async_computation.3 | async-start | bytes 7938048 | tf_op jit(solution)/shard_map/all_gather | solution.py:524
  11.6 197.1 %all-gather.7.cloned.1.call-start = ((), (), s32[]{:S(2)}) async-start(), calls=%async_computation.4 | async-start | bytes 20054016 | tf_op jit(solution)/shard_map/all_gather | solution.py:524
  16.4 281.0 %all-gather.9.cloned.1.call-start = ((), (), s32[]{:S(2)}) async-start(), calls=%async_computation.5 | async-start | bytes 20054016 | tf_op jit(solution)/shard_map/all_gather | solution.py:524
  17.1 380.6 %all-gather.11.cloned.1.call-start = ((), (), s32[]{:S(2)}) async-start(), calls=%async_computation.6 | async-start | bytes 20054016 | tf_op jit(solution)/shard_map/all_gather | solution.py:524
  17.7 579.0 %reduce-scatter.4.cloned.1.call-start = ((), (), s32[]{:S(2)}) async-start(), calls=%async_computation.7 | async-start | bytes 20054016 | tf_op jit(solution)/shard_map/reduce_scatter | solution.py:448
  21.5 54.6 %collective-permute-start = (bf16[768,1536]{1,0:T(8,128)(2,1)S(1)}, bf16[768,1536]{1,0:T(8,128)(2,1)}, u32[]{:S(2)}, u32[]{:S(2)}) collective-permute-start(bf16[768,1536]{1,0:T(8,128)(2,1)S(1)} %copy-done.1), channel_id=1, source_target_pairs={{0,1},{1,0},{2,3},{3,2},{4,5},{5,4},{6,7},{7,6},{8,9},{9,8},{10,11... | collective-permute-start | bytes 7077896 | tf_op jit(solution)/shard_map/ppermute | solution.py:383
  30.3 125.3 %collective-permute-start.2 = (bf16[768,1536]{1,0:T(8,128)(2,1)}, bf16[768,1536]{1,0:T(8,128)(2,1)}, u32[]{:S(2)}, u32[]{:S(2)}) collective-permute-start(bf16[768,1536]{1,0:T(8,128)(2,1)} %collective-permute-done.1), channel_id=1, source_target_pairs={{0,1},{1,0},{2,3},{3,2},{4,5},{5,4},{6,7},{7,6},{8,9},{9,8},{10,11... | collective-permute-start | bytes 7077896 | tf_op jit(solution)/shard_map/ppermute | solution.py:383
  212.6 18.0 %collective-permute-start.4 = (bf16[128,2,768]{2,0,1:T(8,128)(2,1)S(1)}, bf16[128,2,768]{2,0,1:T(8,128)(2,1)S(1)}, u32[]{:S(2)}, u32[]{:S(2)}) collective-permute-start(bf16[128,2,768]{2,0,1:T(8,128)(2,1)S(1)} %copy.74), channel_id=1, source_target_pairs={{0,1},{1,0},{2,3},{3,2},{4,5},{5,4},{6,7},{7,6},{8,9},{9,8},{10,11... | collective-permute-start | bytes 1179656 | tf_op jit(solution)/shard_map/ppermute | solution.py:383
  346.2 527.7 %reduce-scatter.6.cloned.1.call-start = ((), (), s32[]{:S(2)}) async-start(), calls=%async_computation.8 | async-start | bytes 20054016 | tf_op jit(solution)/shard_map/reduce_scatter | solution.py:621
  453.5 30.9 %collective-permute-start.5 = (bf16[1536,3072]{1,0:T(8,128)(2,1)}, bf16[1536,3072]{1,0:T(8,128)(2,1)}, u32[]{:S(2)}, u32[]{:S(2)}) collective-permute-start(bf16[1536,3072]{1,0:T(8,128)(2,1)} %convolution_convert_fusion.1), channel_id=1, source_target_pairs={{0,2},{2,0},{4,6},{6,4},{8,10},{10,8},{12,14},{14,12},{16,18},{18,... | collective-permute-start | bytes 28311560 | tf_op jit(solution)/shard_map/ppermute | solution.py:383
  519.9 41.5 %collective-permute-start.13 = (bf16[128,2,768]{2,0,1:T(8,128)(2,1)S(1)}, bf16[128,2,768]{2,0,1:T(8,128)(2,1)S(1)}, u32[]{:S(2)}, u32[]{:S(2)}) collective-permute-start(bf16[128,2,768]{2,0,1:T(8,128)(2,1)S(1)} %fusion.86), channel_id=1, source_target_pairs={{0,1},{1,0},{2,3},{3,2},{4,5},{5,4},{6,7},{7,6},{8,9},{9,8},{10,11... | collective-permute-start | bytes 1179656 | tf_op jit(solution)/shard_map/ppermute | solution.py:383
  560.7 28.0 %collective-permute-start.7 = (bf16[768,768]{1,0:T(8,128)(2,1)}, bf16[768,768]{1,0:T(8,128)(2,1)}, u32[]{:S(2)}, u32[]{:S(2)}) collective-permute-start(bf16[768,768]{1,0:T(8,128)(2,1)} %constant_dynamic-slice_fusion.2), channel_id=1, source_target_pairs={{0,1},{1,0},{2,3},{3,2},{4,5},{5,4},{6,7},{7,6},{8,9},{9,8},{10,11... | collective-permute-start | bytes 3538952 | tf_op jit(solution)/shard_map/ppermute | solution.py:383
  596.7 432.2 %reduce-scatter.8.cloned.1.call-start = ((), (), s32[]{:S(2)}) async-start(), calls=%async_computation.9 | async-start | bytes 7520256 | tf_op jit(solution)/shard_map/reduce_scatter | solution.py:448
  596.7 105.1 %collective-permute-start.6 = (bf16[1536,1536]{1,0:T(8,128)(2,1)}, bf16[1536,1536]{1,0:T(8,128)(2,1)}, u32[]{:S(2)}, u32[]{:S(2)}) collective-permute-start(bf16[1536,1536]{1,0:T(8,128)(2,1)} %add_convert_fusion.2), channel_id=1, source_target_pairs={{0,1},{1,0},{2,3},{3,2},{4,5},{5,4},{6,7},{7,6},{8,9},{9,8},{10,11... | collective-permute-start | bytes 14155784 | tf_op jit(solution)/shard_map/ppermute | solution.py:383
  614.1 159.5 %collective-permute-start.11 = (bf16[1536,768]{1,0:T(8,128)(2,1)}, bf16[1536,768]{1,0:T(8,128)(2,1)}, u32[]{:S(2)}, u32[]{:S(2)}) collective-permute-start(bf16[1536,768]{1,0:T(8,128)(2,1)} %get-tuple-element.73), channel_id=1, source_target_pairs={{2,0},{4,2},{6,4},{8,6},{10,8},{12,10},{14,12},{16,14},{18,16},{20... | collective-permute-start | bytes 7077896 | tf_op jit(solution)/shard_map/ppermute | solution.py:389
  616.2 160.4 %collective-permute-start.10 = (bf16[1536,768]{1,0:T(8,128)(2,1)}, bf16[1536,768]{1,0:T(8,128)(2,1)}, u32[]{:S(2)}, u32[]{:S(2)}) collective-permute-start(bf16[1536,768]{1,0:T(8,128)(2,1)} %get-tuple-element.71), channel_id=1, source_target_pairs={{2,0},{4,2},{6,4},{8,6},{10,8},{12,10},{14,12},{16,14},{18,16},{20... | collective-permute-start | bytes 7077896 | tf_op jit(solution)/shard_map/ppermute | solution.py:389
  623.7 272.6 %collective-permute-start.14 = (bf16[128,1536]{1,0:T(8,128)(2,1)}, bf16[128,1536]{1,0:T(8,128)(2,1)}, u32[]{:S(2)}, u32[]{:S(2)}) collective-permute-start(bf16[128,1536]{1,0:T(8,128)(2,1)} %fusion.77), channel_id=1, source_target_pairs={{0,1},{1,0},{2,3},{3,2},{4,5},{5,4},{6,7},{7,6},{8,9},{9,8},{10,11... | collective-permute-start | bytes 1179656 | tf_op jit(solution)/shard_map/ppermute | solution.py:383
  712.6 119.6 %collective-permute-start.8 = (bf16[4,192,1536]{2,1,0:T(8,128)(2,1)}, bf16[4,192,1536]{2,1,0:T(8,128)(2,1)}, u32[]{:S(2)}, u32[]{:S(2)}) collective-permute-start(bf16[4,192,1536]{2,1,0:T(8,128)(2,1)} %dynamic-slice_bitcast_fusion), channel_id=1, source_target_pairs={{0,4},{2,6},{4,0},{6,2},{8,12},{10,14},{12,8},{14,10},{16,20},{18,... | collective-permute-start | bytes 7077896 | tf_op jit(solution)/shard_map/ppermute | solution.py:383
  712.9 66.9 %collective-permute-start.9 = (bf16[384,1536]{1,0:T(8,128)(2,1)S(1)}, bf16[384,1536]{1,0:T(8,128)(2,1)S(1)}, u32[]{:S(2)}, u32[]{:S(2)}) collective-permute-start(bf16[384,1536]{1,0:T(8,128)(2,1)S(1)} %copy-done.31), channel_id=1, source_target_pairs={{0,1},{1,0},{2,3},{3,2},{4,5},{5,4},{6,7},{7,6},{8,9},{9,8},{10,11... | collective-permute-start | bytes 3538952 | tf_op jit(solution)/shard_map/ppermute | solution.py:383
  833.8 73.0 %collective-permute-start.12 = (bf16[768,1536]{1,0:T(8,128)(2,1)}, bf16[768,1536]{1,0:T(8,128)(2,1)}, u32[]{:S(2)}, u32[]{:S(2)}) collective-permute-start(bf16[768,1536]{1,0:T(8,128)(2,1)} %dynamic-slice_convert_fusion), channel_id=1, source_target_pairs={{0,1},{1,0},{2,3},{3,2},{4,5},{5,4},{6,7},{7,6},{8,9},{9,8},{10,11... | collective-permute-start | bytes 7077896 | tf_op jit(solution)/shard_map/ppermute | solution.py:383
  903.4 77.6 %collective-permute-start.18 = (bf16[2,192,1536]{2,1,0:T(8,128)(2,1)}, bf16[2,192,1536]{2,1,0:T(8,128)(2,1)}, u32[]{:S(2)}, u32[]{:S(2)}) collective-permute-start(bf16[2,192,1536]{2,1,0:T(8,128)(2,1)} %dynamic-slice_bitcast_fusion.1), channel_id=1, source_target_pairs={{0,8},{2,10},{4,12},{6,14},{8,0},{10,2},{12,4},{14,6},{16,24},{18,... | collective-permute-start | bytes 3538952 | tf_op jit(solution)/shard_map/ppermute | solution.py:383
  904.6 29.5 %collective-permute-start.16 = (bf16[3,96,1536]{2,1,0:T(8,128)(2,1)}, bf16[3,96,1536]{2,1,0:T(8,128)(2,1)}, u32[]{:S(2)}, u32[]{:S(2)}) collective-permute-start(bf16[3,96,1536]{2,1,0:T(8,128)(2,1)} %slice.169), channel_id=1, source_target_pairs={{0,1},{1,0},{2,3},{3,2},{4,5},{5,4},{6,7},{7,6},{8,9},{9,8},{10,11... | collective-permute-start | bytes 2654216 | tf_op jit(solution)/shard_map/ppermute | solution.py:383
  906.2 26.1 %collective-permute-start.17 = (bf16[96,2,768]{2,1,0:T(2,128)(2,1)S(1)}, bf16[96,2,768]{2,1,0:T(2,128)(2,1)S(1)}, u32[]{:S(2)}, u32[]{:S(2)}) collective-permute-start(bf16[96,2,768]{2,1,0:T(2,128)(2,1)S(1)} %reshape_squeeze.3), channel_id=1, source_target_pairs={{0,1},{1,0},{2,3},{3,2},{4,5},{5,4},{6,7},{7,6},{8,9},{9,8},{10,11... | collective-permute-start | bytes 884744 | tf_op jit(solution)/shard_map/ppermute | solution.py:383
  983.1 28.2 %collective-permute-start.19 = (bf16[1,192,1536]{2,1,0:T(8,128)(2,1)S(1)}, bf16[1,192,1536]{2,1,0:T(8,128)(2,1)S(1)}, u32[]{:S(2)}, u32[]{:S(2)}) collective-permute-start(bf16[1,192,1536]{2,1,0:T(8,128)(2,1)S(1)} %constant_dynamic-slice_fusion.1), channel_id=1, source_target_pairs={{0,16},{2,18},{4,20},{6,22},{8,24},{10,26},{12,28},{14,30},{16,0},... | collective-permute-start | bytes 1769480 | tf_op jit(solution)/shard_map/ppermute | solution.py:383
  (77 other events, 1349.0 us)
Sparse Core Ops, SparseCore 0:
  11.7 85.7 all-gather.4
  99.6 97.0 all-gather.6
  198.4 98.9 all-gather.8
  298.8 98.9 all-gather.10
  401.7 194.8 reduce-scatter.3
  600.6 273.2 reduce-scatter.5
  877.9 105.8 reduce-scatter.7

commit v6 on v5

--- a/solution.py
+++ b/solution.py
@@ -277,20 +277,21 @@
     )
 
 
+CROSS_PAIRS = 3
+
+
 def cross_kernel(q_ref, k_ref, v_ref, slot_ref, o_ref):
     lower = lax.broadcasted_iota(jnp.int32, (1, PAIR), 1) < HEAD
-    zero = jnp.zeros((1, 1), jnp.bfloat16)
-    scaled = q_ref[...] * jnp.bfloat16(SCALE)
     tokens, texts = q_ref.shape[0], k_ref.shape[0]
     allowed = slot_ref[:, :1] == lax.broadcasted_iota(jnp.int32, (tokens, texts), 1) // TXT
-    results = []
-    for h in range(2):
-        half = jnp.where(lower, scaled, zero) if h == 0 else jnp.where(lower, zero, scaled)
-        scores = jnp.where(allowed, contract_cols(half, k_ref[...]), NEG)
-        weights = jnp.exp(scores - jnp.max(scores, axis=1, keepdims=True))
-        shares = weights / jnp.sum(weights, axis=1, keepdims=True)
-        results.append(matmul(shares.astype(jnp.bfloat16), v_ref[...]))
-    o_ref[...] = jnp.where(lower, results[0], results[1]).astype(o_ref.dtype)
+    for p in range(CROSS_PAIRS):
+        results = []
+        for half in split_heads(q_ref[:, lanes(p)] * jnp.bfloat16(SCALE)):
+            scores = jnp.where(allowed, contract_cols(half, k_ref[:, lanes(p)]), NEG)
+            weights = jnp.exp(scores - jnp.max(scores, axis=1, keepdims=True))
+            shares = weights / jnp.sum(weights, axis=1, keepdims=True)
+            results.append(matmul(shares.astype(jnp.bfloat16), v_ref[:, lanes(p)]))
+        o_ref[:, lanes(p)] = jnp.where(lower, results[0], results[1]).astype(o_ref.dtype)
 
 
 def cross_attend(q, k, v, slots_wide):
@@ -299,14 +300,14 @@
     column = lambda p: (0, p)
     return pl.pallas_call(
         cross_kernel,
-        grid=(width // PAIR,),
+        grid=(width // (CROSS_PAIRS * PAIR),),
         in_specs=[
-            pl.BlockSpec((tokens, PAIR), column),
-            pl.BlockSpec((texts, PAIR), column),
-            pl.BlockSpec((texts, PAIR), column),
+            pl.BlockSpec((tokens, CROSS_PAIRS * PAIR), column),
+            pl.BlockSpec((texts, CROSS_PAIRS * PAIR), column),
+            pl.BlockSpec((texts, CROSS_PAIRS * PAIR), column),
             pl.BlockSpec((tokens, PAIR), lambda p: (0, 0)),
         ],
-        out_specs=pl.BlockSpec((tokens, PAIR), column),
+        out_specs=pl.BlockSpec((tokens, CROSS_PAIRS * PAIR), column),
         out_shape=jax.ShapeDtypeStruct(q.shape, jnp.bfloat16),
         compiler_params=pltpu.CompilerParams(vmem_limit_bytes=VMEM_BYTES),
         cost_estimate=pl.CostEstimate(
@@ -320,28 +321,25 @@
 
 def cross_back_kernel(q_ref, g_ref, k_ref, v_ref, slot_ref, dq_ref, dk_ref, dv_ref):
     lower = lax.broadcasted_iota(jnp.int32, (1, PAIR), 1) < HEAD
-    zero = jnp.zeros((1, 1), jnp.bfloat16)
-    scaled = q_ref[...] * jnp.bfloat16(SCALE)
-    grad = g_ref[...]
-    keys = k_ref[...]
     tokens, texts = q_ref.shape[0], k_ref.shape[0]
     allowed = slot_ref[:, :1] == lax.broadcasted_iota(jnp.int32, (tokens, texts), 1) // TXT
-    dqs, dks, dvs = [], [], []
-    for h in range(2):
-        q_half = jnp.where(lower, scaled, zero) if h == 0 else jnp.where(lower, zero, scaled)
-        g_half = jnp.where(lower, grad, zero) if h == 0 else jnp.where(lower, zero, grad)
-        scores = jnp.where(allowed, contract_cols(q_half, keys), NEG)
-        weights = jnp.exp(scores - jnp.max(scores, axis=1, keepdims=True))
-        shares = weights / jnp.sum(weights, axis=1, keepdims=True)
-        grad_shares = contract_cols(g_half, v_ref[...])
-        inner = jnp.sum(shares * grad_shares, axis=1, keepdims=True)
-        grad_scores = (shares * (grad_shares - inner)).astype(jnp.bfloat16)
-        dqs.append(matmul(grad_scores, keys))
-        dks.append(contract_rows(grad_scores, q_half))
-        dvs.append(contract_rows(shares.astype(jnp.bfloat16), g_half))
-    dq_ref[...] = (jnp.where(lower, dqs[0], dqs[1]) * SCALE).astype(dq_ref.dtype)
-    dk_ref[...] = dks[0] + dks[1]
-    dv_ref[...] = dvs[0] + dvs[1]
+    for p in range(CROSS_PAIRS):
+        keys, values = k_ref[:, lanes(p)], v_ref[:, lanes(p)]
+        halves = zip(split_heads(q_ref[:, lanes(p)] * jnp.bfloat16(SCALE)), split_heads(g_ref[:, lanes(p)]))
+        dqs, dks, dvs = [], [], []
+        for q_half, g_half in halves:
+            scores = jnp.where(allowed, contract_cols(q_half, keys), NEG)
+            weights = jnp.exp(scores - jnp.max(scores, axis=1, keepdims=True))
+            shares = weights / jnp.sum(weights, axis=1, keepdims=True)
+            grad_shares = contract_cols(g_half, values)
+            inner = jnp.sum(shares * grad_shares, axis=1, keepdims=True)
+            grad_scores = (shares * (grad_shares - inner)).astype(jnp.bfloat16)
+            dqs.append(matmul(grad_scores, keys))
+            dks.append(contract_rows(grad_scores, q_half))
+            dvs.append(contract_rows(shares.astype(jnp.bfloat16), g_half))
+        dq_ref[:, lanes(p)] = (jnp.where(lower, dqs[0], dqs[1]) * SCALE).astype(dq_ref.dtype)
+        dk_ref[:, lanes(p)] = dks[0] + dks[1]
+        dv_ref[:, lanes(p)] = dvs[0] + dvs[1]
 
 
 def cross_attend_back(q, grad, k, v, slots_wide):
@@ -350,18 +348,18 @@
     column = lambda p: (0, p)
     return pl.pallas_call(
         cross_back_kernel,
-        grid=(width // PAIR,),
+        grid=(width // (CROSS_PAIRS * PAIR),),
         in_specs=[
-            pl.BlockSpec((tokens, PAIR), column),
-            pl.BlockSpec((tokens, PAIR), column),
-            pl.BlockSpec((texts, PAIR), column),
-            pl.BlockSpec((texts, PAIR), column),
+            pl.BlockSpec((tokens, CROSS_PAIRS * PAIR), column),
+            pl.BlockSpec((tokens, CROSS_PAIRS * PAIR), column),
+            pl.BlockSpec((texts, CROSS_PAIRS * PAIR), column),
+            pl.BlockSpec((texts, CROSS_PAIRS * PAIR), column),
             pl.BlockSpec((tokens, PAIR), lambda p: (0, 0)),
         ],
         out_specs=[
-            pl.BlockSpec((tokens, PAIR), column),
-            pl.BlockSpec((texts, PAIR), column),
-            pl.BlockSpec((texts, PAIR), column),
+            pl.BlockSpec((tokens, CROSS_PAIRS * PAIR), column),
+            pl.BlockSpec((texts, CROSS_PAIRS * PAIR), column),
+            pl.BlockSpec((texts, CROSS_PAIRS * PAIR), column),
         ],
         out_shape=[
             jax.ShapeDtypeStruct(q.shape, jnp.bfloat16),
@@ -471,14 +469,22 @@
 
 def half_rows(value, place):
     blocks = value.reshape(-1, 2, *value.shape[1:])
-    return lax.dynamic_index_in_dim(blocks, place, 1, keepdims=False)
+    return lax.dynamic_index_in_dim(blocks, place % 2, 1, keepdims=False)
+
+
+def seq_away(kept, came):
+    return both(other_block(kept, 1), other_block(came, 1))
+
+
+def chip_blocks(kept, came, beside):
+    value = both(both(own_block(kept, 1), own_block(came, 1)), beside)
+    return value.reshape(lax.axis_size("fsdp") // 2, -1, value.shape[1])
 
 
 def own_rows(value, at, bit):
     while value.shape[0] > 1:
-        at = at // 2
-        value = both(half_rows(value, at % 2), swap(half_rows(value, 1 - at % 2), "fsdp", bit))
-        bit *= 2
+        value = both(half_rows(value, at), swap(half_rows(value, at + 1), "fsdp", bit))
+        at, bit = at // 2, bit * 2
     core, second = lax.axis_index("fsdp") % 2, lax.axis_index("seq") == 1
     value = value.reshape(2, -1, value.shape[-1])
     take = lambda place: lax.dynamic_index_in_dim(value, place, 0, keepdims=False)
@@ -531,16 +537,17 @@
     gains, biases = norm_rows[:3], norm_rows[3:]
 
     ckv_mine = own_block(cross_kv_weight.reshape(shard_rows, 2, width), 2).reshape(shard_rows, 2 * head_cols)
-    second = row_block(jnp.concatenate([out_weight, cross_query_weight, cross_out_weight, ckv_mine], axis=1))
-    full_out, full_cq, full_cout = second[:, :width], second[:, width : 2 * width], second[:, 2 * width : 3 * width]
+    squares = (out_weight, cross_query_weight, cross_out_weight)
+    gate = lax.optimization_barrier
+    by_steps = seq_count == 2 and group_rows == SPAN
+    second = row_block(jnp.concatenate([*squares, ckv_mine], axis=1))
+    full_out, full_cq, full_cout = (second[:, i * width : (i + 1) * width] for i in range(3))
     w_ckv = second[:, 3 * width :]
 
     starts, seg_group = clip_starts(segments, group_index, group_rows)
     slots = own_block(seg_group, 0) - group_index * (group_rows // SPAN)
     slots_wide = jnp.broadcast_to(slots[:, None], (tok_rows, PAIR))
 
-    gate = lax.optimization_barrier
-    by_steps = seq_count == 2 and group_rows == SPAN
     inputs = tokens.astype(jnp.float32)
     norm_one = lambda rows: (normed(rows.astype(jnp.float32))[0] * gains[0] + biases[0]).astype(jnp.bfloat16)
     normed_one = norm_one(gathered(tokens, 0))
@@ -595,8 +602,8 @@
     grad_two = cotangent.astype(jnp.float32) + back_h2
     grad_two_low = grad_two.astype(jnp.bfloat16)
     if by_steps:
-        beside, grad_two_low = gate((both(other_block(up_kept, 1), other_block(up_came, 1)), grad_two_low))
-        beside = swap(beside, "seq", 1)
+        up_beside, grad_two_low = gate((seq_away(up_kept, up_came), grad_two_low))
+        up_beside = swap(up_beside, "seq", 1)
     grad_result = contract_cols(grad_two_low, full_cout).astype(jnp.bfloat16)
     grad_query_c, grad_text_k, grad_text_v = cross_attend_back(cross_query, grad_result, cross_k, cross_v, slots_wide)
     grad_text_kv = summed_block(jnp.stack([grad_text_k, grad_text_v], axis=1), 2)
@@ -625,13 +632,11 @@
     query_state, *grad_before = self_attend_back(*back_args, kv_before, starts, SPAN, 0)
     returned = [passed_along(part[:, :head_cols], "fsdp", -1).astype(jnp.float32) for part in grad_before]
     if by_steps:
-        total = both(both(own_block(up_kept, 1), own_block(up_came, 1)), beside)
-        total = total.reshape(-1, 2 * shard_rows, total.shape[1])
-        first_away, grad_down, query_state = gate((half_rows(total, 1 - chip % 2), grad_down, query_state))
-        down_beside = swap(grad_down, "seq", 1)
+        up_rows = chip_blocks(up_kept, up_came, up_beside)
+        up_away, grad_down, query_state = gate((half_rows(up_rows, chip + 1), grad_down, query_state))
+        up_came, down_beside = swap(up_away, "fsdp", 2), swap(grad_down, "seq", 1)
     grad_q, *grad_own = self_attend_back(*back_args, kv_own, starts, SPAN, SPAN, query_state)
     if by_steps:
-        first_came = swap(first_away, "fsdp", 2)
         down_beside, grad_q = gate((down_beside, grad_q))
         grad_down = grad_down.astype(jnp.float32) + down_beside.astype(jnp.float32)
     else:
@@ -643,16 +648,20 @@
         part = jnp.concatenate([part[:late], part[late:] + more]) if late else part + more
         owned.append(part.astype(jnp.bfloat16))
     grad_proj = jnp.concatenate(owned, axis=1)
-    grad_wqkv, grad_proj = gate((contract_rows(normed_one, grad_proj).astype(jnp.bfloat16), grad_proj))
-    grad_normed_one = contract_cols(grad_proj, w_qkv)
-    grad_wqkv = scattered(gate((grad_wqkv, small, grad_normed_one))[0])
-    grad_cout, grad_cq, grad_wout = whole(small[:3]) if by_steps else [whole(part) for part in small[:3]]
+    grad_normed_one, grad_proj = gate((contract_cols(grad_proj, w_qkv), grad_proj))
+    grad_wqkv = contract_rows(normed_one, grad_proj).astype(jnp.bfloat16)
+    if by_steps:
+        up_came, grad_normed_one = gate((up_came, grad_normed_one))
+        up_rows = both(half_rows(up_rows, chip), up_came)
+        up_came = swap(half_rows(up_rows, chip // 2 + 1), "fsdp", 4)
+        normed_came = swap(other_block(grad_normed_one, 0).astype(jnp.bfloat16), "seq", 1)
+        grad_wqkv = scattered(gate((grad_wqkv, small, normed_came))[0])
+        grad_normed_one = own_block(grad_normed_one, 0) + normed_came.astype(jnp.float32)
+        grad_cout, grad_cq, grad_wout = whole(small[:3])
+    else:
+        grad_wqkv, grad_normed_one = scattered(grad_wqkv), summed_block(grad_normed_one, 0)
+        grad_cout, grad_cq, grad_wout = (whole(part) for part in small[:3])
     grad_ckv = columns(small[3], 2)
-    if by_steps:
-        first_came, grad_normed_one = gate((first_came, grad_normed_one))
-        up_rows = both(half_rows(total, chip % 2), first_came)
-        second_came = swap(half_rows(up_rows, 1 - chip // 2 % 2), "fsdp", 4)
-    grad_normed_one = summed_block(grad_normed_one, 0)
     n_one, root_one = normed(inputs)
     back_x, gain_one, bias_one = norm_back(grad_normed_one, n_one, root_one, gains[0])
     grad_tokens = (grad_one + back_x).astype(jnp.bfloat16)
@@ -661,8 +670,8 @@
     norm_grads, grad_cout, grad_cq, grad_wout, grad_ckv = gate((norm_grads, grad_cout, grad_cq, grad_wout, grad_ckv))
     norm_grads = lax.psum(norm_grads, ("fsdp", "seq"))
     if by_steps:
-        norm_grads, second_came = gate((norm_grads, second_came))
-        grad_up = own_rows(both(half_rows(up_rows, chip // 2 % 2), second_came), chip // 2, 8)
+        norm_grads, up_came = gate((norm_grads, up_came))
+        grad_up = own_rows(both(half_rows(up_rows, chip // 2), up_came), chip // 4, 8)
     norm_grads = lax.dynamic_slice_in_dim(norm_grads, group_index * shard_rows, shard_rows, 1)
     return (
         layer_out,

time: 1060 us -> 1080 us (1.019); the launches traced: 1050 us -> 1060 us
    reduce_scatter x1, waiting for transfers between devices: 39.8 us -> 0.01 us  [shards(): lax.psum_scatter(gate((jnp.stack(small), grad_down, grad_heads))[0], 'fsd...]
    ppermute x19, waiting for transfers between devices: 227 us -> 263 us  [swap(): return lax.ppermute(value, axis, [(i, i ^ bit) for i in range(count)])]
  transfers between devices with their start and end apart: 29 -> 29, of which waited for: 15 -> 15; matrix products, arithmetic and copies ran while one was open for 39% -> 39% of each run, Pallas kernels for 15% -> 14%
where the time goes in v6:
time: 1080 us; the launch traced here: 1060 us
  waiting for transfers between devices  381 us (35%)
  matrix products  289 us (27%)
  Pallas kernels  148 us (14%)
  other arithmetic  104 us (10%)
  blocking collectives  47.4 us (4%)
  local copies, waits for them, and re-layouts  43.7 us (4%)
  starting transfers between devices  29.5 us (3%)
  between operations  15.9 us (1%)
    ppermute x19, waiting for transfers between devices, swap(): return lax.ppermute(value, axis, [(i, i ^ bit) for i in range(count)])  263 us
    all_gather x4, waiting for transfers between devices, shards(): row_block = lambda value: lax.all_gather(value, 'fsdp', axis=0, tiled=True)  111 us
    dot_general x9, matrix products, matmul(): return jnp.dot(left_side, right_side, preferred_element_type=jnp.float32)  108 us
    dot_general x7, matrix products, contract_cols(): lax.dot_general(left_side, right_side, (((1,), (1,)), ((), ())), preferre...  97.5 us
    dot_general x8, matrix products, contract_rows(): lax.dot_general(left_side, right_side, (((0,), (0,)), ((), ())), preferre...  82.9 us
    pallas_call x2, Pallas kernels, self_attend_back(): pl.pallas_call(functools.partial(attend_back_kernel, reach=reach, base=ba...  75.2 us
    psum x1, blocking collectives, shards(): norm_grads = lax.psum(norm_grads, ('fsdp', 'seq'))  47.4 us
    pallas_call x2, Pallas kernels, self_attend(): pl.pallas_call(functools.partial(attend_kernel, reach=reach, base=base, p...  46 us
  transfers between devices with their start and end apart: 29, of which 15 were waited for; matrix products, arithmetic and copies ran while one was open for 39% of the time, Pallas kernels for 14%

profile of v6, /device:TPU:0, one launch (start us, length us, event | category | flops | bytes accessed | tf_op | source)
XLA Modules:
  0.0 1059.1 jit_solution(2255546009012767817)
XLA Ops:
  30.3 45.8 %collective-permute-done = bf16[768,1536]{1,0:T(8,128)(2,1)} collective-permute-done((bf16[768,1536]{1,0:T(8,128)(2,1)S(1)}, bf16[768,1536]{1,0:T(8,128)(2,1)}, u32[]{:S(2)}, u32[]{:S(2)}) %collective-permute-start) | collective-permute-done | bytes 2359328 | tf_op jit(solution)/shard_map/ppermute | solution.py:381
  82.3 15.1 %all-gather.5.cloned.1.call-done = bf16[1536,2432]{1,0:T(8,128)(2,1)} async-done(((bf16[96,2432]{1,0:T(8,128)(2,1)}), bf16[1536,2432]{1,0:T(8,128)(2,1)}) %all-gather.5.cloned.1.call-update) | async-done | bytes 7471120 | tf_op jit(solution)/shard_map/all_gather | solution.py:530
  122.2 33.6 %self_attend.2.refs_0_ = f32[2,4,6,80,384]{4,3,2,1,0:T(8,128)} custom-call(s32[4,4]{1,0:T(4,128)} %pad_add_fusion.1.bounds, bf16[1536,768]{1,0:T(8,128)(2,1)} %convolution_convert_fusion.10.q_ref, bf16[1536,1536]{1,0:T(8,128)(2,1)} %convolution_convert_fusion.9.k_ref.v_ref, bf16[1536,1536]{1,0:T(8,128)(2,1)} %convolution_convert_fusion.9.k_ref.v_ref, ...), custom_call_target="tpu_custom_call" | custom-call | flops 150994944 | bytes 98304 | tf_op jit(solution)/shard_map/self_attend/pallas_call | solution.py:161
  191.1 14.3 %collective-permute-done.3 = bf16[768,768]{1,0:T(8,128)(2,1)} collective-permute-done((bf16[768,768]{1,0:T(8,128)(2,1)}, bf16[768,768]{1,0:T(8,128)(2,1)}, u32[]{:S(2)}, u32[]{:S(2)}) %collective-permute-start.3) | collective-permute-done | bytes 1179680 | tf_op jit(solution)/shard_map/ppermute | solution.py:381
  252.2 45.1 %all-gather.9.cloned.1.call-done = bf16[1536,6144]{1,0:T(8,128)(2,1)} async-done(((bf16[96,6144]{1,0:T(8,128)(2,1)}), bf16[1536,6144]{1,0:T(8,128)(2,1)}) %all-gather.9.cloned.1.call-update) | async-done | bytes 18874384 | tf_op jit(solution)/shard_map/all_gather | solution.py:530
  297.3 27.5 %fusion.3 = (f32[768,6144]{1,0:T(8,128)}, bf16[768,6144]{1,0:T(8,128)(2,1)S(1)}) fusion(bf16[1536,6144]{1,0:T(8,128)(2,1)} %all-gather.9.cloned.1.call-done, f32[768,1536]{1,0:T(8,128)} %copy-done.9, f32[1536]{0:T(1024)S(1)} %copy-done.50, f32[1536]{0:T(1024)S(1)} %get-tuple-element.102, f32[768]{0:T(1024)S(1)} %add_rsqrt_fusion.3, ...), kind=kOutput, calls=%fused_computation.5 | convolution fusion | flops 14548598784 | bytes 51922944 | tf_op jit(solution)/shard_map/dot_general | solution.py:22
  328.4 18.0 %convolution_convert_fusion = bf16[6144,1536]{1,0:T(8,128)(2,1)} fusion(bf16[768,6144]{1,0:T(8,128)(2,1)S(1)} %get-tuple-element.120, bf16[768,1536]{1,0:T(8,128)(2,1)S(1)} %copy-done.20), kind=kOutput, calls=%fused_computation.1 | convolution fusion | flops 14504951808 | bytes 30670848 | tf_op jit(solution)/shard_map/dot_general | solution.py:26
  346.5 51.2 %all-gather.11.cloned.1.call-done = bf16[6144,1536]{1,0:T(8,128)(2,1)} async-done(((bf16[384,1536]{1,0:T(8,128)(2,1)}), bf16[6144,1536]{1,0:T(8,128)(2,1)}) %all-gather.11.cloned.1.call-update) | async-done | bytes 18874384 | tf_op jit(solution)/shard_map/all_gather | solution.py:530
  397.8 26.9 %multiply_convert_fusion = bf16[768,6144]{1,0:T(8,128)(2,1)} fusion(f32[768,6144]{1,0:T(8,128)} %get-tuple-element.55, bf16[768,1536]{1,0:T(8,128)(2,1)S(1)} %copy-done.20, bf16[6144,1536]{1,0:T(8,128)(2,1)} %all-gather.11.cloned.1.call-done), kind=kOutput, calls=%fused_computation.7 | convolution fusion | flops 14504951808 | bytes 49545216 | tf_op jit(solution)/shard_map/dot_general | solution.py:32
  424.6 15.4 %convolution_convert_fusion.2 = bf16[1536,3072]{1,0:T(8,128)(2,1)} fusion(bf16[768,6144]{1,0:T(8,128)(2,1)} %multiply_convert_fusion, s32[]{:T(128)S(6)} %select_n.276, f32[768,1536]{1,0:T(8,128)} %copy-done.9, f32[1536]{0:T(1024)S(1)} %copy-done.50, f32[1536]{0:T(1024)S(1)} %get-tuple-element.102, f32[768]{0:T(1024)S(1)} %add_rsqrt_fusion.3, ...), kind=kOutput, calls=%fused_computation.15 | convolution fusion | flops 7258374144 | bytes 18892804 | tf_op jit(solution)/shard_map/dot_general | solution.py:26
  440.0 13.1 %convolution_convert_fusion.1 = bf16[1536,3072]{1,0:T(8,128)(2,1)} fusion(bf16[768,6144]{1,0:T(8,128)(2,1)S(1)} %copy-done.57, s32[]{:T(128)S(6)} %select_n.277, f32[768,1536]{1,0:T(8,128)} %copy-done.9, f32[1536]{0:T(1024)S(1)} %copy-done.50, f32[1536]{0:T(1024)S(1)} %get-tuple-element.102, f32[768]{0:T(1024)S(1)} %add_rsqrt_fusion.3, ...), kind=kOutput, calls=%fused_computation.14 | convolution fusion | flops 7258374144 | bytes 18898948 | tf_op jit(solution)/shard_map/dot_general | solution.py:26
  453.5 24.5 %multiply_reduce_fusion = (f32[1536]{0:T(1024)}, f32[768]{0:T(1024)S(1)}, f32[768]{0:T(1024)S(1)}, f32[1536]{0:T(1024)}, f32[768,1536]{1,0:T(8,128)}) fusion(f32[768,1536]{1,0:T(8,128)} %copy-done.9, f32[768]{0:T(1024)S(1)} %add_rsqrt_fusion.3, f32[768]{0:T(1024)S(1)} %broadcast_multiply_fusion.9, f32[1536]{0:T(1024)S(1)} %get-tuple-element.102, ...), kind=kOutput, calls=%fused_computation.64 | convolution fusion | flops 14506125312 | bytes 37779456 | tf_op jit(solution)/shard_map/dot_general | solution.py:32
  499.6 17.4 %cross_attend_back.1 = (bf16[768,1536]{1,0:T(8,128)(2,1)}, f32[128,1536]{1,0:T(8,128)}, f32[128,1536]{1,0:T(8,128)}) custom-call(bf16[768,1536]{1,0:T(8,128)(2,1)} %fusion.68.q_ref, bf16[768,1536]{1,0:T(8,128)(2,1)} %fusion.71.g_ref, bf16[128,1536]{1,0:T(8,128)(2,1)} %get-tuple-element.139.k_ref, bf16[128,1536]{1,0:T(8,128)(2,1)} %get-tuple-element.138.v_ref, ...), custom_call_target="tpu_custom_call" | custom-call | flops 3019898880 | bytes 7077888 | tf_op jit(solution)/shard_map/cross_attend_back/pallas_call | solution.py:349
  598.5 15.7 %self_attend_back.2 = (f32[2,4,6,64,384]{4,3,2,1,0:T(8,128)}, bf16[1536,768]{1,0:T(8,128)(2,1)}, bf16[1536,768]{1,0:T(8,128)(2,1)}) custom-call(s32[4,4]{1,0:T(4,128)} %pad_add_fusion.bounds, bf16[1536,768]{1,0:T(8,128)(2,1)} %convolution_convert_fusion.10.q_ref, bf16[1536,768]{1,0:T(8,128)(2,1)} %pad_maximum_fusion.5.g_ref, ...), custom_call_target="tpu_custom_call" | custom-call | flops 150994944 | bytes 98304 | tf_op jit(solution)/shard_map/self_attend_back/pallas_call | solution.py:261
  623.2 78.5 %collective-permute-done.6 = bf16[1536,1536]{1,0:T(8,128)(2,1)} collective-permute-done((bf16[1536,1536]{1,0:T(8,128)(2,1)}, bf16[1536,1536]{1,0:T(8,128)(2,1)}, u32[]{:S(2)}, u32[]{:S(2)}) %collective-permute-start.6) | collective-permute-done | bytes 4718624 | tf_op jit(solution)/shard_map/ppermute | solution.py:381
  715.5 59.5 %self_attend_back.3 = (bf16[1536,768]{1,0:T(8,128)(2,1)}, bf16[1536,768]{1,0:T(8,128)(2,1)}, bf16[1536,768]{1,0:T(8,128)(2,1)}) custom-call(s32[4,4]{1,0:T(4,128)} %pad_add_fusion.1.bounds, bf16[1536,768]{1,0:T(8,128)(2,1)} %convolution_convert_fusion.10.q_ref, bf16[1536,768]{1,0:T(8,128)(2,1)} %pad_maximum_fusion.5.g_ref, ...), custom_call_target="tpu_custom_call" | custom-call | flops 150994944 | bytes 98304 | tf_op jit(solution)/shard_map/self_attend_back/pallas_call | solution.py:261
  783.8 17.3 %fusion.16 = f32[1536,1536]{1,0:T(8,128)} fusion(bf16[1536,2432]{1,0:T(8,128)(2,1)} %all-gather.5.cloned.1.call-done, bf16[1536,768]{1,0:T(8,128)(2,1)S(1)} %add_convert_fusion.3, bf16[1536,768]{1,0:T(8,128)(2,1)S(1)} %add_convert_fusion.4, bf16[1536,768]{1,0:T(8,128)(2,1)} %get-tuple-element.69), kind=kOutput, calls=%fused_computation.38 | convolution fusion | flops 10892869632 | bytes 23592960 | tf_op jit(solution)/shard_map/dot_general | solution.py:32
  801.1 21.7 %collective-permute-done.8 = bf16[4,192,1536]{2,1,0:T(8,128)(2,1)} collective-permute-done((bf16[4,192,1536]{2,1,0:T(8,128)(2,1)}, bf16[4,192,1536]{2,1,0:T(8,128)(2,1)}, u32[]{:S(2)}, u32[]{:S(2)}) %collective-permute-start.8) | collective-permute-done | bytes 2359328 | tf_op jit(solution)/shard_map/ppermute | solution.py:381
  828.8 16.8 %convolution_convert_fusion.3 = bf16[1536,2304]{1,0:T(8,128)(2,1)} fusion(bf16[1536,2304]{1,0:T(8,128)(2,1)} %pad_maximum_fusion.1, f32[1536]{0:T(1024)S(1)} %copy-done.47, f32[1536]{0:T(1024)S(1)} %copy-done.32, f32[1536]{0:T(1024)S(1)} %copy-done.56, f32[1536]{0:T(1024)S(1)} %copy-done.38, bf16[768,1536]{1,0:T(8,128)(2,1)S(1)} %copy-done.8, ...), kind=kOutput, calls=%fused_computation.16 | convolution fusion | flops 10896408576 | bytes 18898944 | tf_op jit(solution)/shard_map/dot_general | solution.py:26
  845.6 32.6 %collective-permute-done.12 = bf16[768,1536]{1,0:T(8,128)(2,1)} collective-permute-done((bf16[768,1536]{1,0:T(8,128)(2,1)}, bf16[768,1536]{1,0:T(8,128)(2,1)}, u32[]{:S(2)}, u32[]{:S(2)}) %collective-permute-start.12) | collective-permute-done | bytes 2359328 | tf_op jit(solution)/shard_map/ppermute | solution.py:381
  878.2 22.3 %add_convert_fusion.5 = bf16[768,1536]{1,0:T(8,128)(2,1)} fusion(f32[768,1536]{1,0:T(8,128)} %copy-done.9, bf16[768,6144]{1,0:T(8,128)(2,1)} %copy-done.59, bf16[6144,1536]{1,0:T(8,128)(2,1)} %all-gather.11.cloned.1.call-done), kind=kOutput, calls=%fused_computation.76 | convolution fusion | flops 14497873920 | bytes 35389440 | tf_op jit(solution)/shard_map/dot_general | solution.py:22
  921.1 15.0 %collective-permute-done.17 = bf16[96,2,768]{2,1,0:T(2,128)(2,1)S(1)} collective-permute-done((bf16[96,2,768]{2,1,0:T(2,128)(2,1)S(1)}, bf16[96,2,768]{2,1,0:T(2,128)(2,1)S(1)}, u32[]{:S(2)}, u32[]{:S(2)}) %collective-permute-start.17) | collective-permute-done | bytes 294944 | tf_op jit(solution)/shard_map/ppermute | solution.py:381
  940.5 47.4 %psum.7 = f32[6,1536]{1,0:T(8,128)S(1)} all-reduce(f32[6,1536]{1,0:T(8,128)S(1)} %stack.118), channel_id=1, replica_groups=mesh['fsdp'=16,'seq'=2] {'fsdp','seq'}, use_global_device_ids=true, to_apply=%region_26.27 | all-reduce | flops 9216 | bytes 73728 | tf_op jit(solution)/shard_map/psum | solution.py:671
  995.8 22.9 %collective-permute-done.19 = bf16[1,192,1536]{2,1,0:T(8,128)(2,1)S(1)} collective-permute-done((bf16[1,192,1536]{2,1,0:T(8,128)(2,1)S(1)}, bf16[1,192,1536]{2,1,0:T(8,128)(2,1)S(1)}, u32[]{:S(2)}, u32[]{:S(2)}) %collective-permute-start.19) | collective-permute-done | bytes 589856 | tf_op jit(solution)/shard_map/ppermute | solution.py:381
  (333 shorter events, 345.6 us)
Async XLA Ops:
  7.2 90.3 %all-gather.5.cloned.1.call-start = ((), (), s32[]{:S(2)}) async-start(), calls=%async_computation.3 | async-start | bytes 7938048 | tf_op jit(solution)/shard_map/all_gather | solution.py:530
  11.6 197.4 %all-gather.7.cloned.1.call-start = ((), (), s32[]{:S(2)}) async-start(), calls=%async_computation.4 | async-start | bytes 20054016 | tf_op jit(solution)/shard_map/all_gather | solution.py:530
  16.4 281.0 %all-gather.9.cloned.1.call-start = ((), (), s32[]{:S(2)}) async-start(), calls=%async_computation.5 | async-start | bytes 20054016 | tf_op jit(solution)/shard_map/all_gather | solution.py:530
  17.1 380.6 %all-gather.11.cloned.1.call-start = ((), (), s32[]{:S(2)}) async-start(), calls=%async_computation.6 | async-start | bytes 20054016 | tf_op jit(solution)/shard_map/all_gather | solution.py:530
  17.7 578.8 %reduce-scatter.4.cloned.1.call-start = ((), (), s32[]{:S(2)}) async-start(), calls=%async_computation.7 | async-start | bytes 20054016 | tf_op jit(solution)/shard_map/reduce_scatter | solution.py:446
  21.5 54.6 %collective-permute-start = (bf16[768,1536]{1,0:T(8,128)(2,1)S(1)}, bf16[768,1536]{1,0:T(8,128)(2,1)}, u32[]{:S(2)}, u32[]{:S(2)}) collective-permute-start(bf16[768,1536]{1,0:T(8,128)(2,1)S(1)} %copy-done.1), channel_id=1, source_target_pairs={{0,1},{1,0},{2,3},{3,2},{4,5},{5,4},{6,7},{7,6},{8,9},{9,8},{10,11... | collective-permute-start | bytes 7077896 | tf_op jit(solution)/shard_map/ppermute | solution.py:381
  30.3 125.5 %collective-permute-start.2 = (bf16[768,1536]{1,0:T(8,128)(2,1)}, bf16[768,1536]{1,0:T(8,128)(2,1)}, u32[]{:S(2)}, u32[]{:S(2)}) collective-permute-start(bf16[768,1536]{1,0:T(8,128)(2,1)} %collective-permute-done.1), channel_id=1, source_target_pairs={{0,1},{1,0},{2,3},{3,2},{4,5},{5,4},{6,7},{7,6},{8,9},{9,8},{10,11... | collective-permute-start | bytes 7077896 | tf_op jit(solution)/shard_map/ppermute | solution.py:381
  212.9 18.0 %collective-permute-start.4 = (bf16[128,2,768]{2,0,1:T(8,128)(2,1)S(1)}, bf16[128,2,768]{2,0,1:T(8,128)(2,1)S(1)}, u32[]{:S(2)}, u32[]{:S(2)}) collective-permute-start(bf16[128,2,768]{2,0,1:T(8,128)(2,1)S(1)} %copy.74), channel_id=1, source_target_pairs={{0,1},{1,0},{2,3},{3,2},{4,5},{5,4},{6,7},{7,6},{8,9},{9,8},{10,11... | collective-permute-start | bytes 1179656 | tf_op jit(solution)/shard_map/ppermute | solution.py:381
  346.5 531.6 %reduce-scatter.6.cloned.1.call-start = ((), (), s32[]{:S(2)}) async-start(), calls=%async_computation.8 | async-start | bytes 20054016 | tf_op jit(solution)/shard_map/reduce_scatter | solution.py:628
  453.2 31.1 %collective-permute-start.5 = (bf16[1536,3072]{1,0:T(8,128)(2,1)}, bf16[1536,3072]{1,0:T(8,128)(2,1)}, u32[]{:S(2)}, u32[]{:S(2)}) collective-permute-start(bf16[1536,3072]{1,0:T(8,128)(2,1)} %convolution_convert_fusion.1), channel_id=1, source_target_pairs={{0,2},{2,0},{4,6},{6,4},{8,10},{10,8},{12,14},{14,12},{16,18},{18,... | collective-permute-start | bytes 28311560 | tf_op jit(solution)/shard_map/ppermute | solution.py:381
  518.2 41.9 %collective-permute-start.13 = (bf16[128,2,768]{2,0,1:T(8,128)(2,1)S(1)}, bf16[128,2,768]{2,0,1:T(8,128)(2,1)S(1)}, u32[]{:S(2)}, u32[]{:S(2)}) collective-permute-start(bf16[128,2,768]{2,0,1:T(8,128)(2,1)S(1)} %fusion.86), channel_id=1, source_target_pairs={{0,1},{1,0},{2,3},{3,2},{4,5},{5,4},{6,7},{7,6},{8,9},{9,8},{10,11... | collective-permute-start | bytes 1179656 | tf_op jit(solution)/shard_map/ppermute | solution.py:381
  559.7 28.2 %collective-permute-start.7 = (bf16[768,768]{1,0:T(8,128)(2,1)}, bf16[768,768]{1,0:T(8,128)(2,1)}, u32[]{:S(2)}, u32[]{:S(2)}) collective-permute-start(bf16[768,768]{1,0:T(8,128)(2,1)} %constant_dynamic-slice_fusion.2), channel_id=1, source_target_pairs={{0,1},{1,0},{2,3},{3,2},{4,5},{5,4},{6,7},{7,6},{8,9},{9,8},{10,11... | collective-permute-start | bytes 3538952 | tf_op jit(solution)/shard_map/ppermute | solution.py:381
  596.6 439.7 %reduce-scatter.8.cloned.1.call-start = ((), (), s32[]{:S(2)}) async-start(), calls=%async_computation.9 | async-start | bytes 7520256 | tf_op jit(solution)/shard_map/reduce_scatter | solution.py:446
  596.6 105.1 %collective-permute-start.6 = (bf16[1536,1536]{1,0:T(8,128)(2,1)}, bf16[1536,1536]{1,0:T(8,128)(2,1)}, u32[]{:S(2)}, u32[]{:S(2)}) collective-permute-start(bf16[1536,1536]{1,0:T(8,128)(2,1)} %add_convert_fusion.2), channel_id=1, source_target_pairs={{0,1},{1,0},{2,3},{3,2},{4,5},{5,4},{6,7},{7,6},{8,9},{9,8},{10,11... | collective-permute-start | bytes 14155784 | tf_op jit(solution)/shard_map/ppermute | solution.py:381
  614.2 160.7 %collective-permute-start.11 = (bf16[1536,768]{1,0:T(8,128)(2,1)}, bf16[1536,768]{1,0:T(8,128)(2,1)}, u32[]{:S(2)}, u32[]{:S(2)}) collective-permute-start(bf16[1536,768]{1,0:T(8,128)(2,1)} %get-tuple-element.73), channel_id=1, source_target_pairs={{2,0},{4,2},{6,4},{8,6},{10,8},{12,10},{14,12},{16,14},{18,16},{20... | collective-permute-start | bytes 7077896 | tf_op jit(solution)/shard_map/ppermute | solution.py:387
  616.4 161.6 %collective-permute-start.10 = (bf16[1536,768]{1,0:T(8,128)(2,1)}, bf16[1536,768]{1,0:T(8,128)(2,1)}, u32[]{:S(2)}, u32[]{:S(2)}) collective-permute-start(bf16[1536,768]{1,0:T(8,128)(2,1)} %get-tuple-element.71), channel_id=1, source_target_pairs={{2,0},{4,2},{6,4},{8,6},{10,8},{12,10},{14,12},{16,14},{18,16},{20... | collective-permute-start | bytes 7077896 | tf_op jit(solution)/shard_map/ppermute | solution.py:387
  622.7 280.2 %collective-permute-start.14 = (bf16[128,1536]{1,0:T(8,128)(2,1)S(1)}, bf16[128,1536]{1,0:T(8,128)(2,1)S(1)}, u32[]{:S(2)}, u32[]{:S(2)}) collective-permute-start(bf16[128,1536]{1,0:T(8,128)(2,1)S(1)} %fusion.77), channel_id=1, source_target_pairs={{0,1},{1,0},{2,3},{3,2},{4,5},{5,4},{6,7},{7,6},{8,9},{9,8},{10,11... | collective-permute-start | bytes 1179656 | tf_op jit(solution)/shard_map/ppermute | solution.py:381
  712.4 110.3 %collective-permute-start.8 = (bf16[4,192,1536]{2,1,0:T(8,128)(2,1)}, bf16[4,192,1536]{2,1,0:T(8,128)(2,1)}, u32[]{:S(2)}, u32[]{:S(2)}) collective-permute-start(bf16[4,192,1536]{2,1,0:T(8,128)(2,1)} %dynamic-slice_bitcast_fusion), channel_id=1, source_target_pairs={{0,4},{2,6},{4,0},{6,2},{8,12},{10,14},{12,8},{14,10},{16,20},{18,... | collective-permute-start | bytes 7077896 | tf_op jit(solution)/shard_map/ppermute | solution.py:381
  714.0 66.5 %collective-permute-start.9 = (bf16[384,1536]{1,0:T(8,128)(2,1)}, bf16[384,1536]{1,0:T(8,128)(2,1)}, u32[]{:S(2)}, u32[]{:S(2)}) collective-permute-start(bf16[384,1536]{1,0:T(8,128)(2,1)} %reduce-scatter.4.cloned.1.call-done), channel_id=1, source_target_pairs={{0,1},{1,0},{2,3},{3,2},{4,5},{5,4},{6,7},{7,6},{8,9},{9,8},{10,11... | collective-permute-start | bytes 3538952 | tf_op jit(solution)/shard_map/ppermute | solution.py:381
  826.8 51.4 %collective-permute-start.12 = (bf16[768,1536]{1,0:T(8,128)(2,1)}, bf16[768,1536]{1,0:T(8,128)(2,1)}, u32[]{:S(2)}, u32[]{:S(2)}) collective-permute-start(bf16[768,1536]{1,0:T(8,128)(2,1)} %dynamic-slice_convert_fusion), channel_id=1, source_target_pairs={{0,1},{1,0},{2,3},{3,2},{4,5},{5,4},{6,7},{7,6},{8,9},{9,8},{10,11... | collective-permute-start | bytes 7077896 | tf_op jit(solution)/shard_map/ppermute | solution.py:381
  909.8 78.1 %collective-permute-start.18 = (bf16[2,192,1536]{2,1,0:T(8,128)(2,1)}, bf16[2,192,1536]{2,1,0:T(8,128)(2,1)}, u32[]{:S(2)}, u32[]{:S(2)}) collective-permute-start(bf16[2,192,1536]{2,1,0:T(8,128)(2,1)} %dynamic-slice_bitcast_fusion.1), channel_id=1, source_target_pairs={{0,8},{2,10},{4,12},{6,14},{8,0},{10,2},{12,4},{14,6},{16,24},{18,... | collective-permute-start | bytes 3538952 | tf_op jit(solution)/shard_map/ppermute | solution.py:381
  911.9 25.9 %collective-permute-start.16 = (bf16[3,96,1536]{2,1,0:T(8,128)(2,1)}, bf16[3,96,1536]{2,1,0:T(8,128)(2,1)}, u32[]{:S(2)}, u32[]{:S(2)}) collective-permute-start(bf16[3,96,1536]{2,1,0:T(8,128)(2,1)} %slice.169), channel_id=1, source_target_pairs={{0,1},{1,0},{2,3},{3,2},{4,5},{5,4},{6,7},{7,6},{8,9},{9,8},{10,11... | collective-permute-start | bytes 2654216 | tf_op jit(solution)/shard_map/ppermute | solution.py:381
  913.8 22.2 %collective-permute-start.17 = (bf16[96,2,768]{2,1,0:T(2,128)(2,1)S(1)}, bf16[96,2,768]{2,1,0:T(2,128)(2,1)S(1)}, u32[]{:S(2)}, u32[]{:S(2)}) collective-permute-start(bf16[96,2,768]{2,1,0:T(2,128)(2,1)S(1)} %reshape_squeeze.3), channel_id=1, source_target_pairs={{0,1},{1,0},{2,3},{3,2},{4,5},{5,4},{6,7},{7,6},{8,9},{9,8},{10,11... | collective-permute-start | bytes 884744 | tf_op jit(solution)/shard_map/ppermute | solution.py:381
  990.0 28.7 %collective-permute-start.19 = (bf16[1,192,1536]{2,1,0:T(8,128)(2,1)S(1)}, bf16[1,192,1536]{2,1,0:T(8,128)(2,1)S(1)}, u32[]{:S(2)}, u32[]{:S(2)}) collective-permute-start(bf16[1,192,1536]{2,1,0:T(8,128)(2,1)S(1)} %constant_dynamic-slice_fusion.1), channel_id=1, source_target_pairs={{0,16},{2,18},{4,20},{6,22},{8,24},{10,26},{12,28},{14,30},{16,0},... | collective-permute-start | bytes 1769480 | tf_op jit(solution)/shard_map/ppermute | solution.py:381
  (74 other events, 1436.8 us)
Sparse Core Ops, SparseCore 0:
  11.7 85.7 all-gather.4
  99.6 97.0 all-gather.6
  198.4 98.9 all-gather.8
  298.8 98.9 all-gather.10
  401.7 194.7 reduce-scatter.3
  600.5 269.2 reduce-scatter.5
  878.3 112.8 reduce-scatter.7

commit v7 on v6

--- a/solution.py
+++ b/solution.py
@@ -614,6 +614,7 @@
 
     grad_one_low = grad_one.astype(jnp.bfloat16)
     grad_attended = contract_cols(grad_one_low, full_out).astype(jnp.bfloat16)
+    grad_attended, grad_query_c, grad_two_low = gate((grad_attended, grad_query_c, grad_two_low))
     grad_heads = paired(exchanged(grad_attended, 1, 0))
     small = [
         contract_rows(left, right).astype(jnp.bfloat16)
@@ -649,35 +650,32 @@
         owned.append(part.astype(jnp.bfloat16))
     grad_proj = jnp.concatenate(owned, axis=1)
     grad_normed_one, grad_proj = gate((contract_cols(grad_proj, w_qkv), grad_proj))
+    grad_normed_one = summed_block(grad_normed_one, 0)
     grad_wqkv = contract_rows(normed_one, grad_proj).astype(jnp.bfloat16)
-    if by_steps:
-        up_came, grad_normed_one = gate((up_came, grad_normed_one))
-        up_rows = both(half_rows(up_rows, chip), up_came)
-        up_came = swap(half_rows(up_rows, chip // 2 + 1), "fsdp", 4)
-        normed_came = swap(other_block(grad_normed_one, 0).astype(jnp.bfloat16), "seq", 1)
-        grad_wqkv = scattered(gate((grad_wqkv, small, normed_came))[0])
-        grad_normed_one = own_block(grad_normed_one, 0) + normed_came.astype(jnp.float32)
-        grad_cout, grad_cq, grad_wout = whole(small[:3])
-    else:
-        grad_wqkv, grad_normed_one = scattered(grad_wqkv), summed_block(grad_normed_one, 0)
-        grad_cout, grad_cq, grad_wout = (whole(part) for part in small[:3])
-    grad_ckv = columns(small[3], 2)
     n_one, root_one = normed(inputs)
     back_x, gain_one, bias_one = norm_back(grad_normed_one, n_one, root_one, gains[0])
     grad_tokens = (grad_one + back_x).astype(jnp.bfloat16)
-
     norm_grads = jnp.stack([gain_one, gain_two, gain_three, bias_one, bias_two, bias_three])
-    norm_grads, grad_cout, grad_cq, grad_wout, grad_ckv = gate((norm_grads, grad_cout, grad_cq, grad_wout, grad_ckv))
-    norm_grads = lax.psum(norm_grads, ("fsdp", "seq"))
-    if by_steps:
-        norm_grads, up_came = gate((norm_grads, up_came))
-        grad_up = own_rows(both(half_rows(up_rows, chip // 2), up_came), chip // 4, 8)
-    norm_grads = lax.dynamic_slice_in_dim(norm_grads, group_index * shard_rows, shard_rows, 1)
+    norm_grads = jnp.pad(norm_grads.T.astype(jnp.bfloat16), ((0, 0), (0, PAIR - 6)))
+    last, small = gate((jnp.concatenate([grad_wqkv, norm_grads], axis=1), small))
+    if by_steps:
+        up_came, last = gate((up_came, last))
+    last = scattered(last)
+    if by_steps:
+        grad_cout, grad_cq, grad_wout = whole(small[:3])
+        grad_up = own_rows(both(half_rows(up_rows, chip), up_came), chip // 2, 4)
+    else:
+        grad_cout, grad_cq, grad_wout = (whole(part) for part in small[:3])
+    grad_ckv = columns(small[3], 2)
+    last, grad_cout, grad_cq, grad_wout, grad_ckv, grad_up = gate(
+        (last, grad_cout, grad_cq, grad_wout, grad_ckv, grad_up)
+    )
+    norm_grads = whole(last[:, -PAIR:]).T
     return (
         layer_out,
         grad_tokens,
         whole(grad_text.astype(jnp.bfloat16)).reshape(text.shape),
-        columns(grad_wqkv, 3),
+        columns(last[:, : 3 * head_cols], 3),
         grad_wout,
         grad_cq,
         grad_ckv,
@@ -685,7 +683,7 @@
         grad_up,
         grad_down,
         norm_grads[:3],
-        norm_grads[3:],
+        norm_grads[3:6],
     )
 
 

time: 1080 us -> 1030 us (0.954)
  blocking collectives: 47.4 us -> 0 us
    psum x1 -> x0, blocking collectives: 47.4 us -> none  [shards(): norm_grads = lax.psum(norm_grads, ('fsdp', 'seq'))]
    ppermute x19 -> x20, waiting for transfers between devices: 263 us -> 256 us  [swap(): return lax.ppermute(value, axis, [(i, i ^ bit) for i in range(count)])]
    ppermute x19 -> x20, starting transfers between devices: 22.8 us -> 21.1 us  [swap(): return lax.ppermute(value, axis, [(i, i ^ bit) for i in range(count)])]
  transfers between devices with their start and end apart: 29 -> 30, of which waited for: 15 -> 14; matrix products, arithmetic and copies ran while one was open for 39% -> 42% of each run, Pallas kernels for 14% -> 15%
where the time goes in v7:
time: 1030 us; the launch traced here: 1010 us
  waiting for transfers between devices  376 us (37%)
  matrix products  291 us (28%)
  Pallas kernels  148 us (14%)
  other arithmetic  110 us (11%)
  local copies, waits for them, and re-layouts  44.2 us (4%)
  starting transfers between devices  27.7 us (3%)
  between operations  15.8 us (2%)
    ppermute x20, waiting for transfers between devices, swap(): return lax.ppermute(value, axis, [(i, i ^ bit) for i in range(count)])  256 us
    all_gather x4, waiting for transfers between devices, shards(): row_block = lambda value: lax.all_gather(value, 'fsdp', axis=0, tiled=True)  111 us
    dot_general x9, matrix products, matmul(): return jnp.dot(left_side, right_side, preferred_element_type=jnp.float32)  109 us
    dot_general x7, matrix products, contract_cols(): lax.dot_general(left_side, right_side, (((1,), (1,)), ((), ())), preferre...  98.7 us
    dot_general x8, matrix products, contract_rows(): lax.dot_general(left_side, right_side, (((0,), (0,)), ((), ())), preferre...  83.1 us
    pallas_call x2, Pallas kernels, self_attend_back(): pl.pallas_call(functools.partial(attend_back_kernel, reach=reach, base=ba...  75 us
    pallas_call x2, Pallas kernels, self_attend(): pl.pallas_call(functools.partial(attend_kernel, reach=reach, base=base, p...  45.9 us
    ppermute x20, starting transfers between devices, swap(): return lax.ppermute(value, axis, [(i, i ^ bit) for i in range(count)])  21.1 us
  transfers between devices with their start and end apart: 30, of which 14 were waited for; matrix products, arithmetic and copies ran while one was open for 42% of the time, Pallas kernels for 15%

profile of v7, /device:TPU:0, one launch (start us, length us, event | category | flops | bytes accessed | tf_op | source)
XLA Modules:
  0.0 1012.2 jit_solution(567890636762713693)
XLA Ops:
  30.3 45.8 %collective-permute-done = bf16[768,1536]{1,0:T(8,128)(2,1)} collective-permute-done((bf16[768,1536]{1,0:T(8,128)(2,1)S(1)}, bf16[768,1536]{1,0:T(8,128)(2,1)}, u32[]{:S(2)}, u32[]{:S(2)}) %collective-permute-start) | collective-permute-done | bytes 2359328 | tf_op jit(solution)/shard_map/ppermute | solution.py:381
  82.3 15.2 %all-gather.5.cloned.1.call-done = bf16[1536,2432]{1,0:T(8,128)(2,1)} async-done(((bf16[96,2432]{1,0:T(8,128)(2,1)}), bf16[1536,2432]{1,0:T(8,128)(2,1)}) %all-gather.5.cloned.1.call-update) | async-done | bytes 7471120 | tf_op jit(solution)/shard_map/all_gather | solution.py:530
  122.2 33.6 %self_attend.2.refs_0_ = f32[2,4,6,80,384]{4,3,2,1,0:T(8,128)} custom-call(s32[4,4]{1,0:T(4,128)} %pad_add_fusion.1.bounds, bf16[1536,768]{1,0:T(8,128)(2,1)} %convolution_convert_fusion.10.q_ref, bf16[1536,1536]{1,0:T(8,128)(2,1)} %convolution_convert_fusion.9.k_ref.v_ref, bf16[1536,1536]{1,0:T(8,128)(2,1)} %convolution_convert_fusion.9.k_ref.v_ref, ...), custom_call_target="tpu_custom_call" | custom-call | flops 150994944 | bytes 98304 | tf_op jit(solution)/shard_map/self_attend/pallas_call | solution.py:161
  174.2 12.3 %self_attend.3 = (bf16[1536,768]{1,0:T(8,128)(2,1)}, f32[2,4,8,384]{3,2,1,0:T(8,128)}) custom-call(s32[4,4]{1,0:T(4,128)} %pad_add_fusion.bounds, bf16[1536,768]{1,0:T(8,128)(2,1)} %convolution_convert_fusion.10.q_ref, bf16[1536,1536]{1,0:T(8,128)(2,1)} %convolution_convert_fusion.8.k_ref.v_ref, bf16[1536,1536]{1,0:T(8,128)(2,1)} %convolution_convert_fusion.8.k_ref.v_ref, ...), custom_call_target="tpu_custom_call" | custom-call | flops 150994944 | bytes 98304 | tf_op jit(solution)/shard_map/self_attend/pallas_call | solution.py:161
  191.0 14.4 %collective-permute-done.3 = bf16[768,768]{1,0:T(8,128)(2,1)} collective-permute-done((bf16[768,768]{1,0:T(8,128)(2,1)}, bf16[768,768]{1,0:T(8,128)(2,1)}, u32[]{:S(2)}, u32[]{:S(2)}) %collective-permute-start.3) | collective-permute-done | bytes 1179680 | tf_op jit(solution)/shard_map/ppermute | solution.py:381
  252.2 45.1 %all-gather.9.cloned.1.call-done = bf16[1536,6144]{1,0:T(8,128)(2,1)} async-done(((bf16[96,6144]{1,0:T(8,128)(2,1)}), bf16[1536,6144]{1,0:T(8,128)(2,1)}) %all-gather.9.cloned.1.call-update) | async-done | bytes 18874384 | tf_op jit(solution)/shard_map/all_gather | solution.py:530
  297.3 27.6 %fusion.3 = (f32[768,6144]{1,0:T(8,128)}, bf16[768,6144]{1,0:T(8,128)(2,1)S(1)}) fusion(bf16[1536,6144]{1,0:T(8,128)(2,1)} %all-gather.9.cloned.1.call-done, f32[768,1536]{1,0:T(8,128)} %copy-done.9, f32[1536]{0:T(1024)S(1)} %copy-done.52, f32[1536]{0:T(1024)S(1)} %get-tuple-element.156, f32[768]{0:T(1024)S(1)} %add_rsqrt_fusion.3, ...), kind=kOutput, calls=%fused_computation.5 | convolution fusion | flops 14548598784 | bytes 51922944 | tf_op jit(solution)/shard_map/dot_general | solution.py:22
  328.5 18.0 %convolution_convert_fusion = bf16[6144,1536]{1,0:T(8,128)(2,1)} fusion(bf16[768,6144]{1,0:T(8,128)(2,1)S(1)} %get-tuple-element.174, bf16[768,1536]{1,0:T(8,128)(2,1)S(1)} %copy-done.20), kind=kOutput, calls=%fused_computation.1 | convolution fusion | flops 14504951808 | bytes 30670848 | tf_op jit(solution)/shard_map/dot_general | solution.py:26
  346.6 51.2 %all-gather.11.cloned.1.call-done = bf16[6144,1536]{1,0:T(8,128)(2,1)} async-done(((bf16[384,1536]{1,0:T(8,128)(2,1)}), bf16[6144,1536]{1,0:T(8,128)(2,1)}) %all-gather.11.cloned.1.call-update) | async-done | bytes 18874384 | tf_op jit(solution)/shard_map/all_gather | solution.py:530
  397.8 27.5 %multiply_convert_fusion = bf16[768,6144]{1,0:T(8,128)(2,1)} fusion(f32[768,6144]{1,0:T(8,128)} %get-tuple-element.58, bf16[768,1536]{1,0:T(8,128)(2,1)S(1)} %copy-done.20, bf16[6144,1536]{1,0:T(8,128)(2,1)} %all-gather.11.cloned.1.call-done), kind=kOutput, calls=%fused_computation.7 | convolution fusion | flops 14504951808 | bytes 49545216 | tf_op jit(solution)/shard_map/dot_general | solution.py:32
  425.3 15.4 %convolution_convert_fusion.2 = bf16[1536,3072]{1,0:T(8,128)(2,1)} fusion(bf16[768,6144]{1,0:T(8,128)(2,1)} %multiply_convert_fusion, s32[]{:T(128)S(6)} %select_n.272, f32[768,1536]{1,0:T(8,128)} %copy-done.9, f32[1536]{0:T(1024)S(1)} %copy-done.52, f32[1536]{0:T(1024)S(1)} %get-tuple-element.156, f32[768]{0:T(1024)S(1)} %add_rsqrt_fusion.3, ...), kind=kOutput, calls=%fused_computation.17 | convolution fusion | flops 7258374144 | bytes 18892804 | tf_op jit(solution)/shard_map/dot_general | solution.py:26
  440.8 12.9 %convolution_convert_fusion.1 = bf16[1536,3072]{1,0:T(8,128)(2,1)} fusion(bf16[768,6144]{1,0:T(8,128)(2,1)S(1)} %copy-done.55, s32[]{:T(128)S(6)} %select_n.273, f32[768,1536]{1,0:T(8,128)} %copy-done.9, f32[1536]{0:T(1024)S(1)} %copy-done.52, f32[1536]{0:T(1024)S(1)} %get-tuple-element.156, f32[768]{0:T(1024)S(1)} %add_rsqrt_fusion.3, ...), kind=kOutput, calls=%fused_computation.16 | convolution fusion | flops 7258374144 | bytes 18898948 | tf_op jit(solution)/shard_map/dot_general | solution.py:26
  453.9 23.9 %multiply_reduce_fusion = (bf16[1536]{0:T(1024)(128)(2,1)S(1)}, f32[768]{0:T(1024)S(1)}, f32[768]{0:T(1024)S(1)}, bf16[1536]{0:T(1024)(128)(2,1)S(1)}, f32[768,1536]{1,0:T(8,128)}) fusion(f32[768,1536]{1,0:T(8,128)} %copy-done.9, f32[768]{0:T(1024)S(1)} %add_rsqrt_fusion.3, f32[768]{0:T(1024)S(1)} %broadcast_multiply_fusion.9, ...), kind=kOutput, calls=%fused_computation.67 | convolution fusion | flops 14506125312 | bytes 37773312 | tf_op jit(solution)/shard_map/dot_general | solution.py:32
  499.4 17.4 %cross_attend_back.1 = (bf16[768,1536]{1,0:T(8,128)(2,1)}, f32[128,1536]{1,0:T(8,128)}, f32[128,1536]{1,0:T(8,128)}) custom-call(bf16[768,1536]{1,0:T(8,128)(2,1)} %fusion.70.q_ref, bf16[768,1536]{1,0:T(8,128)(2,1)} %fusion.73.g_ref, bf16[128,1536]{1,0:T(8,128)(2,1)} %get-tuple-element.193.k_ref, bf16[128,1536]{1,0:T(8,128)(2,1)} %get-tuple-element.192.v_ref, ...), custom_call_target="tpu_custom_call" | custom-call | flops 3019898880 | bytes 7077888 | tf_op jit(solution)/shard_map/cross_attend_back/pallas_call | solution.py:349
  559.3 16.7 %collective-permute-done.12 = bf16[128,2,768]{2,0,1:T(8,128)(2,1)S(1)} collective-permute-done((bf16[128,2,768]{2,0,1:T(8,128)(2,1)S(1)}, bf16[128,2,768]{2,0,1:T(8,128)(2,1)S(1)}, u32[]{:S(2)}, u32[]{:S(2)}) %collective-permute-start.12) | collective-permute-done | bytes 393248 | tf_op jit(solution)/shard_map/ppermute | solution.py:381
  578.8 12.1 %pad_maximum_fusion = bf16[4,1536,1536]{2,1,0:T(8,128)(2,1)} fusion(bf16[1,1536,1536]{2,1,0:T(8,128)(2,1)S(1)} %fusion.20, bf16[1,1536,1536]{2,1,0:T(8,128)(2,1)S(1)} %copy-done.14, bf16[1,1536,1536]{2,1,0:T(8,128)(2,1)} %fusion.22, bf16[1,1536,1536]{2,1,0:T(8,128)(2,1)} %fusion.21), kind=kLoop, calls=%fused_computation.6 | loop fusion | flops 28311552 | bytes 37748736 | tf_op jit(solution)/shard_map/stack | solution.py:629
  598.7 15.6 %self_attend_back.2 = (f32[2,4,6,64,384]{4,3,2,1,0:T(8,128)}, bf16[1536,768]{1,0:T(8,128)(2,1)}, bf16[1536,768]{1,0:T(8,128)(2,1)}) custom-call(s32[4,4]{1,0:T(4,128)} %pad_add_fusion.bounds, bf16[1536,768]{1,0:T(8,128)(2,1)} %convolution_convert_fusion.10.q_ref, bf16[1536,768]{1,0:T(8,128)(2,1)} %pad_maximum_fusion.5.g_ref, ...), custom_call_target="tpu_custom_call" | custom-call | flops 150994944 | bytes 98304 | tf_op jit(solution)/shard_map/self_attend_back/pallas_call | solution.py:261
  625.7 76.2 %collective-permute-done.6 = bf16[1536,1536]{1,0:T(8,128)(2,1)} collective-permute-done((bf16[1536,1536]{1,0:T(8,128)(2,1)}, bf16[1536,1536]{1,0:T(8,128)(2,1)}, u32[]{:S(2)}, u32[]{:S(2)}) %collective-permute-start.6) | collective-permute-done | bytes 4718624 | tf_op jit(solution)/shard_map/ppermute | solution.py:381
  715.6 59.4 %self_attend_back.3 = (bf16[1536,768]{1,0:T(8,128)(2,1)}, bf16[1536,768]{1,0:T(8,128)(2,1)}, bf16[1536,768]{1,0:T(8,128)(2,1)}) custom-call(s32[4,4]{1,0:T(4,128)} %pad_add_fusion.1.bounds, bf16[1536,768]{1,0:T(8,128)(2,1)} %convolution_convert_fusion.10.q_ref, bf16[1536,768]{1,0:T(8,128)(2,1)} %pad_maximum_fusion.5.g_ref, ...), custom_call_target="tpu_custom_call" | custom-call | flops 150994944 | bytes 98304 | tf_op jit(solution)/shard_map/self_attend_back/pallas_call | solution.py:261
  783.9 17.3 %fusion.18 = f32[1536,1536]{1,0:T(8,128)} fusion(bf16[1536,2432]{1,0:T(8,128)(2,1)} %all-gather.5.cloned.1.call-done, bf16[1536,768]{1,0:T(8,128)(2,1)S(1)} %add_convert_fusion.3, bf16[1536,768]{1,0:T(8,128)(2,1)S(1)} %add_convert_fusion.4, bf16[1536,768]{1,0:T(8,128)(2,1)} %get-tuple-element.72), kind=kOutput, calls=%fused_computation.41 | convolution fusion | flops 10892869632 | bytes 23592960 | tf_op jit(solution)/shard_map/dot_general | solution.py:32
  805.0 17.6 %convolution_convert_fusion.3 = bf16[1536,2304]{1,0:T(8,128)(2,1)} fusion(bf16[1536,2304]{1,0:T(8,128)(2,1)} %pad_maximum_fusion.1, f32[1536]{0:T(1024)S(1)} %copy-done.49, f32[1536]{0:T(1024)S(1)} %copy-done.32, f32[1536]{0:T(1024)S(1)} %copy-done.54, f32[1536]{0:T(1024)S(1)} %copy-done.38, bf16[768,1536]{1,0:T(8,128)(2,1)S(1)} %copy-done.8, ...), kind=kOutput, calls=%fused_computation.18 | convolution fusion | flops 10896408576 | bytes 18898944 | tf_op jit(solution)/shard_map/dot_general | solution.py:26
  822.6 31.8 %collective-permute-done.11 = bf16[768,1536]{1,0:T(8,128)(2,1)S(1)} collective-permute-done((bf16[768,1536]{1,0:T(8,128)(2,1)S(1)}, bf16[768,1536]{1,0:T(8,128)(2,1)S(1)}, u32[]{:S(2)}, u32[]{:S(2)}) %collective-permute-start.11) | collective-permute-done | bytes 2359328 | tf_op jit(solution)/shard_map/ppermute | solution.py:381
  871.1 22.7 %add_convert_fusion.5 = bf16[768,1536]{1,0:T(8,128)(2,1)} fusion(f32[768,1536]{1,0:T(8,128)} %copy-done.9, bf16[768,6144]{1,0:T(8,128)(2,1)} %copy-done.57, bf16[6144,1536]{1,0:T(8,128)(2,1)} %all-gather.11.cloned.1.call-done), kind=kOutput, calls=%fused_computation.79 | convolution fusion | flops 14497873920 | bytes 35389440 | tf_op jit(solution)/shard_map/dot_general | solution.py:22
  907.2 49.1 %collective-permute-done.18 = bf16[1,192,1536]{2,1,0:T(8,128)(2,1)} collective-permute-done((bf16[1,192,1536]{2,1,0:T(8,128)(2,1)}, bf16[1,192,1536]{2,1,0:T(8,128)(2,1)}, u32[]{:S(2)}, u32[]{:S(2)}) %collective-permute-start.18) | collective-permute-done | bytes 589856 | tf_op jit(solution)/shard_map/ppermute | solution.py:381
  (338 shorter events, 317.7 us)
Async XLA Ops:
  7.2 90.3 %all-gather.5.cloned.1.call-start = ((), (), s32[]{:S(2)}) async-start(), calls=%async_computation.3 | async-start | bytes 7938048 | tf_op jit(solution)/shard_map/all_gather | solution.py:530
  11.6 197.3 %all-gather.7.cloned.1.call-start = ((), (), s32[]{:S(2)}) async-start(), calls=%async_computation.4 | async-start | bytes 20054016 | tf_op jit(solution)/shard_map/all_gather | solution.py:530
  16.4 281.0 %all-gather.9.cloned.1.call-start = ((), (), s32[]{:S(2)}) async-start(), calls=%async_computation.5 | async-start | bytes 20054016 | tf_op jit(solution)/shard_map/all_gather | solution.py:530
  17.1 380.6 %all-gather.11.cloned.1.call-start = ((), (), s32[]{:S(2)}) async-start(), calls=%async_computation.6 | async-start | bytes 20054016 | tf_op jit(solution)/shard_map/all_gather | solution.py:530
  17.7 579.0 %reduce-scatter.4.cloned.1.call-start = ((), (), s32[]{:S(2)}) async-start(), calls=%async_computation.7 | async-start | bytes 20054016 | tf_op jit(solution)/shard_map/reduce_scatter | solution.py:446
  21.5 54.6 %collective-permute-start = (bf16[768,1536]{1,0:T(8,128)(2,1)S(1)}, bf16[768,1536]{1,0:T(8,128)(2,1)}, u32[]{:S(2)}, u32[]{:S(2)}) collective-permute-start(bf16[768,1536]{1,0:T(8,128)(2,1)S(1)} %copy-done.1), channel_id=1, source_target_pairs={{0,1},{1,0},{2,3},{3,2},{4,5},{5,4},{6,7},{7,6},{8,9},{9,8},{10,11... | collective-permute-start | bytes 7077896 | tf_op jit(solution)/shard_map/ppermute | solution.py:381
  30.3 125.6 %collective-permute-start.2 = (bf16[768,1536]{1,0:T(8,128)(2,1)}, bf16[768,1536]{1,0:T(8,128)(2,1)}, u32[]{:S(2)}, u32[]{:S(2)}) collective-permute-start(bf16[768,1536]{1,0:T(8,128)(2,1)} %collective-permute-done.1), channel_id=1, source_target_pairs={{0,1},{1,0},{2,3},{3,2},{4,5},{5,4},{6,7},{7,6},{8,9},{9,8},{10,11... | collective-permute-start | bytes 7077896 | tf_op jit(solution)/shard_map/ppermute | solution.py:381
  212.8 17.9 %collective-permute-start.4 = (bf16[128,2,768]{2,0,1:T(8,128)(2,1)S(1)}, bf16[128,2,768]{2,0,1:T(8,128)(2,1)S(1)}, u32[]{:S(2)}, u32[]{:S(2)}) collective-permute-start(bf16[128,2,768]{2,0,1:T(8,128)(2,1)S(1)} %copy.92), channel_id=1, source_target_pairs={{0,1},{1,0},{2,3},{3,2},{4,5},{5,4},{6,7},{7,6},{8,9},{9,8},{10,11... | collective-permute-start | bytes 1179656 | tf_op jit(solution)/shard_map/ppermute | solution.py:381
  346.5 521.4 %reduce-scatter.6.cloned.1.call-start = ((), (), s32[]{:S(2)}) async-start(), calls=%async_computation.8 | async-start | bytes 20054016 | tf_op jit(solution)/shard_map/reduce_scatter | solution.py:629
  453.6 30.5 %collective-permute-start.5 = (bf16[1536,3072]{1,0:T(8,128)(2,1)}, bf16[1536,3072]{1,0:T(8,128)(2,1)}, u32[]{:S(2)}, u32[]{:S(2)}) collective-permute-start(bf16[1536,3072]{1,0:T(8,128)(2,1)} %convolution_convert_fusion.1), channel_id=1, source_target_pairs={{0,2},{2,0},{4,6},{6,4},{8,10},{10,8},{12,14},{14,12},{16,18},{18,... | collective-permute-start | bytes 28311560 | tf_op jit(solution)/shard_map/ppermute | solution.py:381
  539.3 51.5 %collective-permute-start.7 = (bf16[768,768]{1,0:T(8,128)(2,1)}, bf16[768,768]{1,0:T(8,128)(2,1)}, u32[]{:S(2)}, u32[]{:S(2)}) collective-permute-start(bf16[768,768]{1,0:T(8,128)(2,1)} %constant_dynamic-slice_fusion.1), channel_id=1, source_target_pairs={{0,1},{1,0},{2,3},{3,2},{4,5},{5,4},{6,7},{7,6},{8,9},{9,8},{10,11... | collective-permute-start | bytes 3538952 | tf_op jit(solution)/shard_map/ppermute | solution.py:381
  540.7 35.3 %collective-permute-start.12 = (bf16[128,2,768]{2,0,1:T(8,128)(2,1)S(1)}, bf16[128,2,768]{2,0,1:T(8,128)(2,1)S(1)}, u32[]{:S(2)}, u32[]{:S(2)}) collective-permute-start(bf16[128,2,768]{2,0,1:T(8,128)(2,1)S(1)} %fusion.88), channel_id=1, source_target_pairs={{0,1},{1,0},{2,3},{3,2},{4,5},{5,4},{6,7},{7,6},{8,9},{9,8},{10,11... | collective-permute-start | bytes 1179656 | tf_op jit(solution)/shard_map/ppermute | solution.py:381
  596.7 385.6 %reduce-scatter.8.cloned.1.call-start = ((), (), s32[]{:S(2)}) async-start(), calls=%async_computation.9 | async-start | bytes 7938048 | tf_op jit(solution)/shard_map/reduce_scatter | solution.py:446
  596.7 105.1 %collective-permute-start.6 = (bf16[1536,1536]{1,0:T(8,128)(2,1)}, bf16[1536,1536]{1,0:T(8,128)(2,1)}, u32[]{:S(2)}, u32[]{:S(2)}) collective-permute-start(bf16[1536,1536]{1,0:T(8,128)(2,1)} %add_convert_fusion.2), channel_id=1, source_target_pairs={{0,1},{1,0},{2,3},{3,2},{4,5},{5,4},{6,7},{7,6},{8,9},{9,8},{10,11... | collective-permute-start | bytes 14155784 | tf_op jit(solution)/shard_map/ppermute | solution.py:381
  614.3 160.7 %collective-permute-start.10 = (bf16[1536,768]{1,0:T(8,128)(2,1)}, bf16[1536,768]{1,0:T(8,128)(2,1)}, u32[]{:S(2)}, u32[]{:S(2)}) collective-permute-start(bf16[1536,768]{1,0:T(8,128)(2,1)} %get-tuple-element.76), channel_id=1, source_target_pairs={{2,0},{4,2},{6,4},{8,6},{10,8},{12,10},{14,12},{16,14},{18,16},{20... | collective-permute-start | bytes 7077896 | tf_op jit(solution)/shard_map/ppermute | solution.py:387
  618.9 159.2 %collective-permute-start.9 = (bf16[1536,768]{1,0:T(8,128)(2,1)}, bf16[1536,768]{1,0:T(8,128)(2,1)}, u32[]{:S(2)}, u32[]{:S(2)}) collective-permute-start(bf16[1536,768]{1,0:T(8,128)(2,1)} %get-tuple-element.74), channel_id=1, source_target_pairs={{2,0},{4,2},{6,4},{8,6},{10,8},{12,10},{14,12},{16,14},{18,16},{20... | collective-permute-start | bytes 7077896 | tf_op jit(solution)/shard_map/ppermute | solution.py:387
  625.2 268.7 %collective-permute-start.13 = (bf16[128,1536]{1,0:T(8,128)(2,1)S(1)}, bf16[128,1536]{1,0:T(8,128)(2,1)}, u32[]{:S(2)}, u32[]{:S(2)}) collective-permute-start(bf16[128,1536]{1,0:T(8,128)(2,1)S(1)} %fusion.79), channel_id=1, source_target_pairs={{0,1},{1,0},{2,3},{3,2},{4,5},{5,4},{6,7},{7,6},{8,9},{9,8},{10,11... | collective-permute-start | bytes 1179656 | tf_op jit(solution)/shard_map/ppermute | solution.py:381
  712.6 67.9 %collective-permute-start.8 = (bf16[384,1536]{1,0:T(8,128)(2,1)}, bf16[384,1536]{1,0:T(8,128)(2,1)}, u32[]{:S(2)}, u32[]{:S(2)}) collective-permute-start(bf16[384,1536]{1,0:T(8,128)(2,1)} %reduce-scatter.4.cloned.1.call-done), channel_id=1, source_target_pairs={{0,1},{1,0},{2,3},{3,2},{4,5},{5,4},{6,7},{7,6},{8,9},{9,8},{10,11... | collective-permute-start | bytes 3538952 | tf_op jit(solution)/shard_map/ppermute | solution.py:381
  714.1 153.9 %collective-permute-start.14 = (bf16[4,192,1536]{2,1,0:T(8,128)(2,1)}, bf16[4,192,1536]{2,1,0:T(8,128)(2,1)}, u32[]{:S(2)}, u32[]{:S(2)}) collective-permute-start(bf16[4,192,1536]{2,1,0:T(8,128)(2,1)} %dynamic-slice_bitcast_fusion), channel_id=1, source_target_pairs={{0,4},{2,6},{4,0},{6,2},{8,12},{10,14},{12,8},{14,10},{16,20},{18,... | collective-permute-start | bytes 7077896 | tf_op jit(solution)/shard_map/ppermute | solution.py:381
  804.0 50.4 %collective-permute-start.11 = (bf16[768,1536]{1,0:T(8,128)(2,1)S(1)}, bf16[768,1536]{1,0:T(8,128)(2,1)S(1)}, u32[]{:S(2)}, u32[]{:S(2)}) collective-permute-start(bf16[768,1536]{1,0:T(8,128)(2,1)S(1)} %dynamic-slice_convert_fusion), channel_id=1, source_target_pairs={{0,1},{1,0},{2,3},{3,2},{4,5},{5,4},{6,7},{7,6},{8,9},{9,8},{10,11... | collective-permute-start | bytes 7077896 | tf_op jit(solution)/shard_map/ppermute | solution.py:381
  871.1 25.8 %collective-permute-start.17 = (bf16[2,192,1536]{2,1,0:T(8,128)(2,1)S(1)}, bf16[2,192,1536]{2,1,0:T(8,128)(2,1)S(1)}, u32[]{:S(2)}, u32[]{:S(2)}) collective-permute-start(bf16[2,192,1536]{2,1,0:T(8,128)(2,1)S(1)} %dynamic-slice_bitcast_fusion.1), channel_id=1, source_target_pairs={{0,8},{2,10},{4,12},{6,14},{8,0},{10,2},{12,4},{14,6},{16,24},{18,... | collective-permute-start | bytes 3538952 | tf_op jit(solution)/shard_map/ppermute | solution.py:381
  899.1 57.2 %collective-permute-start.18 = (bf16[1,192,1536]{2,1,0:T(8,128)(2,1)}, bf16[1,192,1536]{2,1,0:T(8,128)(2,1)}, u32[]{:S(2)}, u32[]{:S(2)}) collective-permute-start(bf16[1,192,1536]{2,1,0:T(8,128)(2,1)} %constant_dynamic-slice_fusion), channel_id=1, source_target_pairs={{0,16},{2,18},{4,20},{6,22},{8,24},{10,26},{12,28},{14,30},{16,0},... | collective-permute-start | bytes 1769480 | tf_op jit(solution)/shard_map/ppermute | solution.py:381
  905.0 56.5 %collective-permute-start.15 = (bf16[3,96,1536]{2,1,0:T(8,128)(2,1)}, bf16[3,96,1536]{2,1,0:T(8,128)(2,1)}, u32[]{:S(2)}, u32[]{:S(2)}) collective-permute-start(bf16[3,96,1536]{2,1,0:T(8,128)(2,1)} %slice.149), channel_id=1, source_target_pairs={{0,1},{1,0},{2,3},{3,2},{4,5},{5,4},{6,7},{7,6},{8,9},{9,8},{10,11... | collective-permute-start | bytes 2654216 | tf_op jit(solution)/shard_map/ppermute | solution.py:381
  905.6 53.0 %collective-permute-start.16 = (bf16[96,2,768]{2,1,0:T(2,128)(2,1)S(1)}, bf16[96,2,768]{2,1,0:T(2,128)(2,1)S(1)}, u32[]{:S(2)}, u32[]{:S(2)}) collective-permute-start(bf16[96,2,768]{2,1,0:T(2,128)(2,1)S(1)} %reshape_squeeze.3), channel_id=1, source_target_pairs={{0,1},{1,0},{2,3},{3,2},{4,5},{5,4},{6,7},{7,6},{8,9},{9,8},{10,11... | collective-permute-start | bytes 884744 | tf_op jit(solution)/shard_map/ppermute | solution.py:381
  (74 other events, 1466.2 us)
Sparse Core Ops, SparseCore 0:
  11.7 85.7 all-gather.4
  99.6 97.0 all-gather.6
  198.4 98.9 all-gather.8
  298.8 98.9 all-gather.10
  401.7 194.8 reduce-scatter.3
  600.6 265.2 reduce-scatter.5
  869.9 112.2 reduce-scatter.7

commit v8 on v6

--- a/solution.py
+++ b/solution.py
@@ -472,19 +472,23 @@
     return lax.dynamic_index_in_dim(blocks, place % 2, 1, keepdims=False)
 
 
-def seq_away(kept, came):
-    return both(other_block(kept, 1), other_block(came, 1))
-
-
-def chip_blocks(kept, came, beside):
-    value = both(both(own_block(kept, 1), own_block(came, 1)), beside)
+def chip_sums(block, products):
+    return jnp.concatenate([both(block(kept, 1), block(came, 1)) for kept, came in products], axis=1)
+
+
+def chip_blocks(mine, beside):
+    value = both(mine, beside)
     return value.reshape(lax.axis_size("fsdp") // 2, -1, value.shape[1])
 
 
-def own_rows(value, at, bit):
+def over_chips(value, at, bit):
     while value.shape[0] > 1:
         value = both(half_rows(value, at), swap(half_rows(value, at + 1), "fsdp", bit))
         at, bit = at // 2, bit * 2
+    return value
+
+
+def own_rows(value):
     core, second = lax.axis_index("fsdp") % 2, lax.axis_index("seq") == 1
     value = value.reshape(2, -1, value.shape[-1])
     take = lambda place: lax.dynamic_index_in_dim(value, place, 0, keepdims=False)
@@ -492,7 +496,7 @@
     pair = jnp.stack([jnp.where(core == 0, mine, theirs), jnp.where(core == 0, theirs, mine)])
     beside = swap(pair, "seq", 1)
     by_seq = jnp.where(second, beside, pair), jnp.where(second, pair, beside)
-    return jnp.concatenate([by_seq[s][c] for c in range(2) for s in range(2)], axis=1).astype(jnp.float32)
+    return [by_seq[s][c].astype(jnp.float32) for c in range(2) for s in range(2)]
 
 
 def clip_starts(segments, group_index, group_rows):
@@ -539,7 +543,7 @@
     ckv_mine = own_block(cross_kv_weight.reshape(shard_rows, 2, width), 2).reshape(shard_rows, 2 * head_cols)
     squares = (out_weight, cross_query_weight, cross_out_weight)
     gate = lax.optimization_barrier
-    by_steps = seq_count == 2 and group_rows == SPAN
+    by_steps = seq_count == 2 and group_rows == SPAN and lax.axis_size("fsdp") == 16
     second = row_block(jnp.concatenate([*squares, ckv_mine], axis=1))
     full_out, full_cq, full_cout = (second[:, i * width : (i + 1) * width] for i in range(3))
     w_ckv = second[:, 3 * width :]
@@ -602,11 +606,17 @@
     grad_two = cotangent.astype(jnp.float32) + back_h2
     grad_two_low = grad_two.astype(jnp.bfloat16)
     if by_steps:
-        up_beside, grad_two_low = gate((seq_away(up_kept, up_came), grad_two_low))
-        up_beside = swap(up_beside, "seq", 1)
+        cout_kept, cout_away = core_products(cross_result, grad_two_low)
+        tree = ((up_kept, up_came), (cout_kept, swap(cout_away, "fsdp", 1)))
     grad_result = contract_cols(grad_two_low, full_cout).astype(jnp.bfloat16)
     grad_query_c, grad_text_k, grad_text_v = cross_attend_back(cross_query, grad_result, cross_k, cross_v, slots_wide)
-    grad_text_kv = summed_block(jnp.stack([grad_text_k, grad_text_v], axis=1), 2)
+    grad_text_kv = jnp.stack([grad_text_k, grad_text_v], axis=1)
+    if by_steps:
+        text_came = swap(other_block(grad_text_kv, 2).astype(jnp.bfloat16), "seq", 1)
+        text_came, grad_query_c = gate((text_came, grad_query_c))
+        grad_text_kv = own_block(grad_text_kv, 2) + text_came.astype(jnp.float32)
+    else:
+        grad_text_kv = summed_block(grad_text_kv, 2)
     grad_text_kv = grad_text_kv.astype(jnp.bfloat16).reshape(text_count, 2 * head_cols)
     grad_text = contract_cols(grad_text_kv, w_ckv)
     back_h1, gain_two, bias_two = norm_back(contract_cols(grad_query_c, full_cq), n_two, root_two, gains[1])
@@ -614,25 +624,28 @@
 
     grad_one_low = grad_one.astype(jnp.bfloat16)
     grad_attended = contract_cols(grad_one_low, full_out).astype(jnp.bfloat16)
-    grad_heads = paired(exchanged(grad_attended, 1, 0))
+    grad_attended, grad_query_c, grad_two_low = gate((grad_attended, grad_query_c, grad_two_low))
+    if by_steps:
+        heads_came = swap(other_block(grad_attended, 1), "seq", 1)
+    else:
+        grad_heads = paired(exchanged(grad_attended, 1, 0))
     small = [
         contract_rows(left, right).astype(jnp.bfloat16)
-        for left, right in (
-            (cross_result, grad_two_low),
-            (normed_two, grad_query_c),
-            (attended, grad_one_low),
-            (text_rows, grad_text_kv),
-        )
+        for left, right in ((normed_two, grad_query_c), (attended, grad_one_low), (text_rows, grad_text_kv))
     ]
     if by_steps:
-        small = lax.psum_scatter(gate((jnp.stack(small), grad_down, grad_heads))[0], "fsdp", scatter_dimension=1, tiled=True)
+        small, beside, heads_came = gate((jnp.stack(small), chip_sums(other_block, tree), heads_came))
+        grad_heads = in_order(own_block(grad_attended, 1), heads_came, 0)
+        small = lax.psum_scatter(small, "fsdp", scatter_dimension=1, tiled=True)
+        beside = swap(beside, "seq", 1)
     else:
         small = [scattered(part) for part in small]
+        grad_cout = scattered(contract_rows(cross_result, grad_two_low))
     back_args = (queries, grad_heads, heads_out, log_totals)
     query_state, *grad_before = self_attend_back(*back_args, kv_before, starts, SPAN, 0)
     returned = [passed_along(part[:, :head_cols], "fsdp", -1).astype(jnp.float32) for part in grad_before]
     if by_steps:
-        up_rows = chip_blocks(up_kept, up_came, up_beside)
+        up_rows = chip_blocks(chip_sums(own_block, tree), beside)
         up_away, grad_down, query_state = gate((half_rows(up_rows, chip + 1), grad_down, query_state))
         up_came, down_beside = swap(up_away, "fsdp", 2), swap(grad_down, "seq", 1)
     grad_q, *grad_own = self_attend_back(*back_args, kv_own, starts, SPAN, SPAN, query_state)
@@ -648,30 +661,37 @@
         part = jnp.concatenate([part[:late], part[late:] + more]) if late else part + more
         owned.append(part.astype(jnp.bfloat16))
     grad_proj = jnp.concatenate(owned, axis=1)
-    grad_normed_one, grad_proj = gate((contract_cols(grad_proj, w_qkv), grad_proj))
-    grad_wqkv = contract_rows(normed_one, grad_proj).astype(jnp.bfloat16)
-    if by_steps:
+    grad_wqkv, grad_proj = gate((contract_rows(normed_one, grad_proj).astype(jnp.bfloat16), grad_proj))
+    grad_normed_one = contract_cols(grad_proj, w_qkv)
+    grad_wqkv, small, _ = gate((grad_wqkv, small, grad_normed_one))
+    grad_wqkv = scattered(grad_wqkv)
+    if by_steps:
+        normed_came = swap(other_block(grad_normed_one, 0).astype(jnp.bfloat16), "seq", 1)
         up_came, grad_normed_one = gate((up_came, grad_normed_one))
         up_rows = both(half_rows(up_rows, chip), up_came)
-        up_came = swap(half_rows(up_rows, chip // 2 + 1), "fsdp", 4)
-        normed_came = swap(other_block(grad_normed_one, 0).astype(jnp.bfloat16), "seq", 1)
-        grad_wqkv = scattered(gate((grad_wqkv, small, normed_came))[0])
+        up_came, normed_came = gate((swap(half_rows(up_rows, chip // 2 + 1), "fsdp", 4), normed_came))
+        up_rows = over_chips(both(half_rows(up_rows, chip // 2), up_came), chip // 4, 8)
         grad_normed_one = own_block(grad_normed_one, 0) + normed_came.astype(jnp.float32)
-        grad_cout, grad_cq, grad_wout = whole(small[:3])
-    else:
-        grad_wqkv, grad_normed_one = scattered(grad_wqkv), summed_block(grad_normed_one, 0)
-        grad_cout, grad_cq, grad_wout = (whole(part) for part in small[:3])
-    grad_ckv = columns(small[3], 2)
+        grad_cq, grad_wout = whole(small[:2])
+    else:
+        grad_cq, grad_wout = (whole(part) for part in small[:2])
+        grad_normed_one = summed_block(grad_normed_one, 0)
+    grad_ckv = columns(small[2], 2)
     n_one, root_one = normed(inputs)
     back_x, gain_one, bias_one = norm_back(grad_normed_one, n_one, root_one, gains[0])
     grad_tokens = (grad_one + back_x).astype(jnp.bfloat16)
-
-    norm_grads = jnp.stack([gain_one, gain_two, gain_three, bias_one, bias_two, bias_three])
-    norm_grads, grad_cout, grad_cq, grad_wout, grad_ckv = gate((norm_grads, grad_cout, grad_cq, grad_wout, grad_ckv))
-    norm_grads = lax.psum(norm_grads, ("fsdp", "seq"))
-    if by_steps:
-        norm_grads, up_came = gate((norm_grads, up_came))
-        grad_up = own_rows(both(half_rows(up_rows, chip // 2), up_came), chip // 4, 8)
+    norm_grads = lax.psum(
+        jnp.stack([gain_one, gain_two, gain_three, bias_one, bias_two, bias_three]), ("fsdp", "seq")
+    )
+    if by_steps:
+        norm_grads, up_rows = gate((norm_grads, up_rows))
+        quarters = own_rows(up_rows)
+        grad_up, grad_cout = (jnp.concatenate(parts, axis=1) for parts in zip(*((q[:, :width], q[:, width:]) for q in quarters)))
+    else:
+        grad_cout = whole(grad_cout)
+    grad_wqkv, grad_cout, grad_cq, grad_wout, grad_ckv, grad_up = gate(
+        (grad_wqkv, grad_cout, grad_cq, grad_wout, grad_ckv, grad_up)
+    )
     norm_grads = lax.dynamic_slice_in_dim(norm_grads, group_index * shard_rows, shard_rows, 1)
     return (
         layer_out,

time: 1080 us -> 1030 us (0.954); the launches traced: 1060 us -> 1020 us
  waiting for transfers between devices: 381 us -> 300 us
  Pallas kernels: 148 us -> 164 us
  blocking collectives: 47.4 us -> 59.8 us
    ppermute x19 -> x20, waiting for transfers between devices: 263 us -> 193 us  [swap(): return lax.ppermute(value, axis, [(i, i ^ bit) for i in range(count)])]
    psum x1, blocking collectives: 47.4 us -> 59.8 us  [shards(): lax.psum(jnp.stack([gain_one, gain_two, gain_three, bias_one, bias_two, b...]
    unnamed x140 -> x144, local copies, waits for them, and re-layouts: 15.1 us -> 21.6 us
    convert_element_type x5 -> x6, other arithmetic: 18.9 us -> 24.9 us  [both(): (first.astype(jnp.float32) + second.astype(jnp.float32)).astype(jnp.bfloa...]
    dot_general x8 -> x9, matrix products: 82.9 us -> 83.4 us  [contract_rows(): lax.dot_general(left_side, right_side, (((0,), (0,)), ((), ())), preferre...]
    ppermute x19 -> x20, starting transfers between devices: 22.8 us -> 22.9 us  [swap(): return lax.ppermute(value, axis, [(i, i ^ bit) for i in range(count)])]
  transfers between devices with their start and end apart: 29 -> 30, of which waited for: 15 -> 11; matrix products, arithmetic and copies ran while one was open for 39% -> 42% of each run, Pallas kernels for 14% -> 16%
where the time goes in v8:
time: 1030 us; the launch traced here: 1020 us
  waiting for transfers between devices  300 us (29%)
  matrix products  289 us (28%)
  Pallas kernels  164 us (16%)
  other arithmetic  113 us (11%)
  blocking collectives  59.8 us (6%)
  local copies, waits for them, and re-layouts  52.4 us (5%)
  starting transfers between devices  29.8 us (3%)
  between operations  15.8 us (2%)
    ppermute x20, waiting for transfers between devices, swap(): return lax.ppermute(value, axis, [(i, i ^ bit) for i in range(count)])  193 us
    dot_general x9, matrix products, matmul(): return jnp.dot(left_side, right_side, preferred_element_type=jnp.float32)  110 us
    all_gather x4, waiting for transfers between devices, shards(): row_block = lambda value: lax.all_gather(value, 'fsdp', axis=0, tiled=True)  105 us
    dot_general x7, matrix products, contract_cols(): lax.dot_general(left_side, right_side, (((1,), (1,)), ((), ())), preferre...  96.1 us
    pallas_call x2, Pallas kernels, self_attend_back(): pl.pallas_call(functools.partial(attend_back_kernel, reach=reach, base=ba...  85.1 us
    dot_general x9, matrix products, contract_rows(): lax.dot_general(left_side, right_side, (((0,), (0,)), ((), ())), preferre...  83.4 us
    psum x1, blocking collectives, shards(): lax.psum(jnp.stack([gain_one, gain_two, gain_three, bias_one, bias_two, b...  59.8 us
    pallas_call x2, Pallas kernels, self_attend(): pl.pallas_call(functools.partial(attend_kernel, reach=reach, base=base, p...  51.7 us
  transfers between devices with their start and end apart: 30, of which 11 were waited for; matrix products, arithmetic and copies ran while one was open for 42% of the time, Pallas kernels for 16%

profile of v8, /device:TPU:0, one launch (start us, length us, event | category | flops | bytes accessed | tf_op | source)
XLA Modules:
  0.0 1023.4 jit_solution(844423996927372162)
XLA Ops:
  30.4 45.8 %collective-permute-done = bf16[768,1536]{1,0:T(8,128)(2,1)} collective-permute-done((bf16[768,1536]{1,0:T(8,128)(2,1)S(1)}, bf16[768,1536]{1,0:T(8,128)(2,1)}, u32[]{:S(2)}, u32[]{:S(2)}) %collective-permute-start) | collective-permute-done | bytes 2359328 | tf_op jit(solution)/shard_map/ppermute | solution.py:381
  82.5 15.0 %all-gather.5.cloned.1.call-done = bf16[1536,2432]{1,0:T(8,128)(2,1)} async-done(((bf16[96,2432]{1,0:T(8,128)(2,1)}), bf16[1536,2432]{1,0:T(8,128)(2,1)}) %all-gather.5.cloned.1.call-update) | async-done | bytes 7471120 | tf_op jit(solution)/shard_map/all_gather | solution.py:534
  110.9 11.3 %convolution_convert_fusion.8.k_ref.v_ref = bf16[1536,1536]{1,0:T(8,128)(2,1)} fusion(bf16[1536,2432]{1,0:T(8,128)(2,1)S(1)} %bitcast.159, f32[1536]{0:T(1024)S(1)} %get-tuple-element.122, f32[1536]{0:T(1024)S(1)} %get-tuple-element.123, f32[1536]{0:T(1024)S(1)} %add_rsqrt_fusion.1, f32[1536]{0:T(1024)S(1)} %broadcast_multiply_fusion.1, ...), kind=kOutput, calls=%fused_computation.36 | convolution fusion | flops 7271350272 | bytes 14188544 | tf_op jit(solution)/shard_map/dot_general | solution.py:22
  122.2 39.4 %self_attend.2.refs_0_ = f32[2,4,6,80,384]{4,3,2,1,0:T(8,128)} custom-call(s32[4,4]{1,0:T(4,128)} %pad_add_fusion.1.bounds, bf16[1536,768]{1,0:T(8,128)(2,1)} %convolution_convert_fusion.11.q_ref, bf16[1536,1536]{1,0:T(8,128)(2,1)} %convolution_convert_fusion.8.k_ref.v_ref, bf16[1536,1536]{1,0:T(8,128)(2,1)} %convolution_convert_fusion.8.k_ref.v_ref, ...), custom_call_target="tpu_custom_call" | custom-call | flops 150994944 | bytes 98304 | tf_op jit(solution)/shard_map/self_attend/pallas_call | solution.py:161
  168.5 11.4 %convolution_convert_fusion.7.k_ref.v_ref = bf16[1536,1536]{1,0:T(8,128)(2,1)} fusion(f32[1536]{0:T(1024)S(1)} %add_rsqrt_fusion, f32[1536]{0:T(1024)S(1)} %broadcast_multiply_fusion, f32[1536]{0:T(1024)S(1)} %get-tuple-element.122, f32[1536]{0:T(1024)S(1)} %get-tuple-element.123, bf16[1536,2432]{1,0:T(8,128)(2,1)S(1)} %bitcast.161, ...), kind=kOutput, calls=%fused_computation.35 | convolution fusion | flops 7271350272 | bytes 14188544 | tf_op jit(solution)/shard_map/dot_general | solution.py:22
  179.9 12.4 %self_attend.3 = (bf16[1536,768]{1,0:T(8,128)(2,1)}, f32[2,4,8,384]{3,2,1,0:T(8,128)}) custom-call(s32[4,4]{1,0:T(4,128)} %pad_add_fusion.bounds, bf16[1536,768]{1,0:T(8,128)(2,1)} %convolution_convert_fusion.11.q_ref, bf16[1536,1536]{1,0:T(8,128)(2,1)} %convolution_convert_fusion.7.k_ref.v_ref, bf16[1536,1536]{1,0:T(8,128)(2,1)} %convolution_convert_fusion.7.k_ref.v_ref, ...), custom_call_target="tpu_custom_call" | custom-call | flops 150994944 | bytes 98304 | tf_op jit(solution)/shard_map/self_attend/pallas_call | solution.py:161
  196.9 14.3 %collective-permute-done.3 = bf16[768,768]{1,0:T(8,128)(2,1)} collective-permute-done((bf16[768,768]{1,0:T(8,128)(2,1)}, bf16[768,768]{1,0:T(8,128)(2,1)}, u32[]{:S(2)}, u32[]{:S(2)}) %collective-permute-start.3) | collective-permute-done | bytes 1179680 | tf_op jit(solution)/shard_map/ppermute | solution.py:381
  258.2 39.2 %all-gather.9.cloned.1.call-done = bf16[1536,6144]{1,0:T(8,128)(2,1)} async-done(((bf16[96,6144]{1,0:T(8,128)(2,1)}), bf16[1536,6144]{1,0:T(8,128)(2,1)}) %all-gather.9.cloned.1.call-update) | async-done | bytes 18874384 | tf_op jit(solution)/shard_map/all_gather | solution.py:534
  297.3 27.5 %fusion.3 = (f32[768,6144]{1,0:T(8,128)}, bf16[768,6144]{1,0:T(8,128)(2,1)S(1)}) fusion(bf16[1536,6144]{1,0:T(8,128)(2,1)} %all-gather.9.cloned.1.call-done, f32[768,1536]{1,0:T(8,128)} %copy-done.8, f32[1536]{0:T(1024)S(1)} %copy-done.50, f32[1536]{0:T(1024)S(1)} %get-tuple-element.118, f32[768]{0:T(1024)S(1)} %add_rsqrt_fusion.3, ...), kind=kOutput, calls=%fused_computation.5 | convolution fusion | flops 14548598784 | bytes 51922944 | tf_op jit(solution)/shard_map/dot_general | solution.py:22
  328.4 18.1 %convolution_convert_fusion = bf16[6144,1536]{1,0:T(8,128)(2,1)} fusion(bf16[768,6144]{1,0:T(8,128)(2,1)S(1)} %get-tuple-element.138, bf16[768,1536]{1,0:T(8,128)(2,1)S(1)} %copy-done.21), kind=kOutput, calls=%fused_computation.1 | convolution fusion | flops 14504951808 | bytes 30670848 | tf_op jit(solution)/shard_map/dot_general | solution.py:26
  346.6 51.2 %all-gather.11.cloned.1.call-done = bf16[6144,1536]{1,0:T(8,128)(2,1)} async-done(((bf16[384,1536]{1,0:T(8,128)(2,1)}), bf16[6144,1536]{1,0:T(8,128)(2,1)}) %all-gather.11.cloned.1.call-update) | async-done | bytes 18874384 | tf_op jit(solution)/shard_map/all_gather | solution.py:534
  397.8 27.0 %multiply_convert_fusion = bf16[768,6144]{1,0:T(8,128)(2,1)} fusion(f32[768,6144]{1,0:T(8,128)} %get-tuple-element.63, bf16[768,1536]{1,0:T(8,128)(2,1)S(1)} %copy-done.21, bf16[6144,1536]{1,0:T(8,128)(2,1)} %all-gather.11.cloned.1.call-done), kind=kOutput, calls=%fused_computation.6 | convolution fusion | flops 14504951808 | bytes 49545216 | tf_op jit(solution)/shard_map/dot_general | solution.py:32
  424.8 15.3 %convolution_convert_fusion.2 = bf16[1536,3072]{1,0:T(8,128)(2,1)} fusion(bf16[768,6144]{1,0:T(8,128)(2,1)} %multiply_convert_fusion, s32[]{:T(128)S(6)} %select_n.292, f32[768,1536]{1,0:T(8,128)} %copy-done.8, f32[1536]{0:T(1024)S(1)} %copy-done.50, f32[1536]{0:T(1024)S(1)} %get-tuple-element.118, f32[768]{0:T(1024)S(1)} %add_rsqrt_fusion.3, ...), kind=kOutput, calls=%fused_computation.16 | convolution fusion | flops 7258374144 | bytes 18892804 | tf_op jit(solution)/shard_map/dot_general | solution.py:26
  440.1 13.3 %convolution_convert_fusion.1 = bf16[1536,3072]{1,0:T(8,128)(2,1)} fusion(bf16[768,6144]{1,0:T(8,128)(2,1)S(1)} %copy-done.57, s32[]{:T(128)S(6)} %select_n.293, f32[768,1536]{1,0:T(8,128)} %copy-done.8, f32[1536]{0:T(1024)S(1)} %copy-done.50, f32[1536]{0:T(1024)S(1)} %get-tuple-element.118, f32[768]{0:T(1024)S(1)} %add_rsqrt_fusion.3, ...), kind=kOutput, calls=%fused_computation.15 | convolution fusion | flops 7258374144 | bytes 18898948 | tf_op jit(solution)/shard_map/dot_general | solution.py:26
  453.6 23.1 %multiply_reduce_fusion = (f32[1536]{0:T(1024)}, f32[768]{0:T(1024)S(1)}, f32[768]{0:T(1024)S(1)}, f32[1536]{0:T(1024)}, f32[768,1536]{1,0:T(8,128)S(1)}) fusion(f32[768,1536]{1,0:T(8,128)S(1)} %bitcast.129, f32[768]{0:T(1024)S(1)} %add_rsqrt_fusion.3, f32[768]{0:T(1024)S(1)} %broadcast_multiply_fusion.9, f32[1536]{0:T(1024)S(1)} %get-tuple-element.118, ...), kind=kOutput, calls=%fused_computation.63 | convolution fusion | flops 14506125312 | bytes 37779456 | tf_op jit(solution)/shard_map/dot_general | solution.py:32
  490.6 17.5 %cross_attend_back.1 = (bf16[768,1536]{1,0:T(8,128)(2,1)}, f32[128,1536]{1,0:T(8,128)}, f32[128,1536]{1,0:T(8,128)}) custom-call(bf16[768,1536]{1,0:T(8,128)(2,1)} %fusion.67.q_ref, bf16[768,1536]{1,0:T(8,128)(2,1)} %fusion.70.g_ref, bf16[128,1536]{1,0:T(8,128)(2,1)} %get-tuple-element.158.k_ref, bf16[128,1536]{1,0:T(8,128)(2,1)} %get-tuple-element.157.v_ref, ...), custom_call_target="tpu_custom_call" | custom-call | flops 3019898880 | bytes 7077888 | tf_op jit(solution)/shard_map/cross_attend_back/pallas_call | solution.py:349
  584.6 14.6 %self_attend_back.2 = (f32[2,4,6,64,384]{4,3,2,1,0:T(8,128)}, bf16[1536,768]{1,0:T(8,128)(2,1)}, bf16[1536,768]{1,0:T(8,128)(2,1)}) custom-call(s32[4,4]{1,0:T(4,128)} %pad_add_fusion.bounds, bf16[1536,768]{1,0:T(8,128)(2,1)} %convolution_convert_fusion.11.q_ref, bf16[1536,768]{1,0:T(8,128)(2,1)} %pad_maximum_fusion.6.g_ref, ...), custom_call_target="tpu_custom_call" | custom-call | flops 150994944 | bytes 98304 | tf_op jit(solution)/shard_map/self_attend_back/pallas_call | solution.py:261
  607.7 101.7 %collective-permute-done.9 = bf16[1536,1920]{1,0:T(8,128)(2,1)} collective-permute-done((bf16[1536,1920]{1,0:T(8,128)(2,1)}, bf16[1536,1920]{1,0:T(8,128)(2,1)}, u32[]{:S(2)}, u32[]{:S(2)}) %collective-permute-start.9) | collective-permute-done | bytes 5898272 | tf_op jit(solution)/shard_map/ppermute | solution.py:381
  721.1 70.6 %self_attend_back.3 = (bf16[1536,768]{1,0:T(8,128)(2,1)}, bf16[1536,768]{1,0:T(8,128)(2,1)}, bf16[1536,768]{1,0:T(8,128)(2,1)}) custom-call(s32[4,4]{1,0:T(4,128)} %pad_add_fusion.1.bounds, bf16[1536,768]{1,0:T(8,128)(2,1)} %convolution_convert_fusion.11.q_ref, bf16[1536,768]{1,0:T(8,128)(2,1)} %pad_maximum_fusion.6.g_ref, ...), custom_call_target="tpu_custom_call" | custom-call | flops 150994944 | bytes 98304 | tf_op jit(solution)/shard_map/self_attend_back/pallas_call | solution.py:261
  803.1 19.2 %convolution_convert_fusion.3 = bf16[1536,2304]{1,0:T(8,128)(2,1)} fusion(bf16[1536,768]{1,0:T(8,128)(2,1)} %copy-done.13, bf16[1536,768]{1,0:T(8,128)(2,1)} %copy-done.14, bf16[1536,768]{1,0:T(8,128)(2,1)} %get-tuple-element.83, f32[1536]{0:T(1024)S(1)} %copy-done.47, f32[1536]{0:T(1024)S(1)} %copy-done.34, f32[1536]{0:T(1024)S(1)} %copy-done.56, ...), kind=kOutput, calls=%fused_computation.17 | convolution fusion | flops 10917642240 | bytes 18898944 | tf_op jit(solution)/shard_map/dot_general | solution.py:26
  822.3 16.4 %fusion.16 = f32[1536,1536]{1,0:T(8,128)S(1)} fusion(bf16[1536,2304]{1,0:T(8,128)(2,1)} %pad_maximum_fusion.1, bf16[1536,2432]{1,0:T(8,128)(2,1)} %all-gather.5.cloned.1.call-done), kind=kOutput, calls=%fused_computation.37 | convolution fusion | flops 10871635968 | bytes 23592960 | tf_op jit(solution)/shard_map/dot_general | solution.py:32
  851.8 23.5 %add_convert_fusion.5 = bf16[768,1536]{1,0:T(8,128)(2,1)} fusion(f32[768,1536]{1,0:T(8,128)} %copy-done.8, bf16[768,6144]{1,0:T(8,128)(2,1)} %copy-done.59, bf16[6144,1536]{1,0:T(8,128)(2,1)} %all-gather.11.cloned.1.call-done), kind=kOutput, calls=%fused_computation.75 | convolution fusion | flops 14497873920 | bytes 35389440 | tf_op jit(solution)/shard_map/dot_general | solution.py:22
  913.0 59.8 %psum.7 = f32[6,1536]{1,0:T(8,128)} all-reduce(f32[6,1536]{1,0:T(8,128)S(1)} %stack.114), channel_id=1, replica_groups=mesh['fsdp'=16,'seq'=2] {'fsdp','seq'}, use_global_device_ids=true, to_apply=%region_26.27 | all-reduce | flops 9216 | bytes 73728 | tf_op jit(solution)/shard_map/psum | solution.py:683
  979.6 15.8 %collective-permute-done.19 = bf16[2,96,1920]{2,1,0:T(8,128)(2,1)S(1)} collective-permute-done((bf16[2,96,1920]{2,1,0:T(8,128)(2,1)S(1)}, bf16[2,96,1920]{2,1,0:T(8,128)(2,1)S(1)}, u32[]{:S(2)}, u32[]{:S(2)}) %collective-permute-start.19) | collective-permute-done | bytes 737312 | tf_op jit(solution)/shard_map/ppermute | solution.py:381
  (352 shorter events, 304.4 us)
Async XLA Ops:
  7.2 90.3 %all-gather.5.cloned.1.call-start = ((), (), s32[]{:S(2)}) async-start(), calls=%async_computation.3 | async-start | bytes 7938048 | tf_op jit(solution)/shard_map/all_gather | solution.py:534
  11.6 203.2 %all-gather.7.cloned.1.call-start = ((), (), s32[]{:S(2)}) async-start(), calls=%async_computation.4 | async-start | bytes 20054016 | tf_op jit(solution)/shard_map/all_gather | solution.py:534
  16.4 280.9 %all-gather.9.cloned.1.call-start = ((), (), s32[]{:S(2)}) async-start(), calls=%async_computation.5 | async-start | bytes 20054016 | tf_op jit(solution)/shard_map/all_gather | solution.py:534
  17.1 380.6 %all-gather.11.cloned.1.call-start = ((), (), s32[]{:S(2)}) async-start(), calls=%async_computation.6 | async-start | bytes 20054016 | tf_op jit(solution)/shard_map/all_gather | solution.py:534
  17.7 701.3 %reduce-scatter.4.cloned.1.call-start = ((), (), s32[]{:S(2)}) async-start(), calls=%async_computation.7 | async-start | bytes 20054016 | tf_op jit(solution)/shard_map/reduce_scatter | solution.py:446
  21.7 54.5 %collective-permute-start = (bf16[768,1536]{1,0:T(8,128)(2,1)S(1)}, bf16[768,1536]{1,0:T(8,128)(2,1)}, u32[]{:S(2)}, u32[]{:S(2)}) collective-permute-start(bf16[768,1536]{1,0:T(8,128)(2,1)S(1)} %copy-done.1), channel_id=1, source_target_pairs={{0,1},{1,0},{2,3},{3,2},{4,5},{5,4},{6,7},{7,6},{8,9},{9,8},{10,11... | collective-permute-start | bytes 7077896 | tf_op jit(solution)/shard_map/ppermute | solution.py:381
  30.4 131.1 %collective-permute-start.2 = (bf16[768,1536]{1,0:T(8,128)(2,1)}, bf16[768,1536]{1,0:T(8,128)(2,1)}, u32[]{:S(2)}, u32[]{:S(2)}) collective-permute-start(bf16[768,1536]{1,0:T(8,128)(2,1)} %collective-permute-done.1), channel_id=1, source_target_pairs={{0,1},{1,0},{2,3},{3,2},{4,5},{5,4},{6,7},{7,6},{8,9},{9,8},{10,11... | collective-permute-start | bytes 7077896 | tf_op jit(solution)/shard_map/ppermute | solution.py:381
  218.8 17.9 %collective-permute-start.4 = (bf16[128,2,768]{2,0,1:T(8,128)(2,1)S(1)}, bf16[128,2,768]{2,0,1:T(8,128)(2,1)S(1)}, u32[]{:S(2)}, u32[]{:S(2)}) collective-permute-start(bf16[128,2,768]{2,0,1:T(8,128)(2,1)S(1)} %copy.77), channel_id=1, source_target_pairs={{0,1},{1,0},{2,3},{3,2},{4,5},{5,4},{6,7},{7,6},{8,9},{9,8},{10,11... | collective-permute-start | bytes 1179656 | tf_op jit(solution)/shard_map/ppermute | solution.py:381
  346.5 498.9 %reduce-scatter.6.cloned.1.call-start = ((), (), s32[]{:S(2)}) async-start(), calls=%async_computation.8 | async-start | bytes 15040512 | tf_op jit(solution)/shard_map/reduce_scatter | solution.py:639
  453.3 112.7 %collective-permute-start.6 = (bf16[1536,3072]{1,0:T(8,128)(2,1)}, bf16[1536,3072]{1,0:T(8,128)(2,1)}, u32[]{:S(2)}, u32[]{:S(2)}) collective-permute-start(bf16[1536,3072]{1,0:T(8,128)(2,1)} %convolution_convert_fusion.1), channel_id=1, source_target_pairs={{0,2},{2,0},{4,6},{6,4},{8,10},{10,8},{12,14},{14,12},{16,18},{18,... | collective-permute-start | bytes 28311560 | tf_op jit(solution)/shard_map/ppermute | solution.py:381
  514.3 48.4 %collective-permute-start.7 = (bf16[1536,768]{1,0:T(8,128)(2,1)}, bf16[1536,768]{1,0:T(8,128)(2,1)}, u32[]{:S(2)}, u32[]{:S(2)}) collective-permute-start(bf16[1536,768]{1,0:T(8,128)(2,1)} %convolution_convert_fusion.9), channel_id=1, source_target_pairs={{0,2},{2,0},{4,6},{6,4},{8,10},{10,8},{12,14},{14,12},{16,18},{18,... | collective-permute-start | bytes 7077896 | tf_op jit(solution)/shard_map/ppermute | solution.py:381
  544.1 34.9 %collective-permute-start.8 = (bf16[768,768]{1,0:T(8,128)(2,1)}, bf16[768,768]{1,0:T(8,128)(2,1)}, u32[]{:S(2)}, u32[]{:S(2)}) collective-permute-start(bf16[768,768]{1,0:T(8,128)(2,1)} %constant_dynamic-slice_fusion.2), channel_id=1, source_target_pairs={{0,1},{1,0},{2,3},{3,2},{4,5},{5,4},{6,7},{7,6},{8,9},{9,8},{10,11... | collective-permute-start | bytes 3538952 | tf_op jit(solution)/shard_map/ppermute | solution.py:381
  579.0 419.4 %reduce-scatter.8.cloned.1.call-start = ((), (), s32[]{:S(2)}) async-start(), calls=%async_computation.9 | async-start | bytes 7520256 | tf_op jit(solution)/shard_map/reduce_scatter | solution.py:446
  579.1 130.4 %collective-permute-start.9 = (bf16[1536,1920]{1,0:T(8,128)(2,1)}, bf16[1536,1920]{1,0:T(8,128)(2,1)}, u32[]{:S(2)}, u32[]{:S(2)}) collective-permute-start(bf16[1536,1920]{1,0:T(8,128)(2,1)} %pad_maximum_fusion.2), channel_id=1, source_target_pairs={{0,1},{1,0},{2,3},{3,2},{4,5},{5,4},{6,7},{7,6},{8,9},{9,8},{10,11... | collective-permute-start | bytes 17694728 | tf_op jit(solution)/shard_map/ppermute | solution.py:381
  599.2 192.4 %collective-permute-start.13 = (bf16[1536,768]{1,0:T(8,128)(2,1)}, bf16[1536,768]{1,0:T(8,128)(2,1)}, u32[]{:S(2)}, u32[]{:S(2)}) collective-permute-start(bf16[1536,768]{1,0:T(8,128)(2,1)} %get-tuple-element.87), channel_id=1, source_target_pairs={{2,0},{4,2},{6,4},{8,6},{10,8},{12,10},{14,12},{16,14},{18,16},{20... | collective-permute-start | bytes 7077896 | tf_op jit(solution)/shard_map/ppermute | solution.py:387
  601.5 193.3 %collective-permute-start.12 = (bf16[1536,768]{1,0:T(8,128)(2,1)}, bf16[1536,768]{1,0:T(8,128)(2,1)}, u32[]{:S(2)}, u32[]{:S(2)}) collective-permute-start(bf16[1536,768]{1,0:T(8,128)(2,1)} %get-tuple-element.85), channel_id=1, source_target_pairs={{2,0},{4,2},{6,4},{8,6},{10,8},{12,10},{14,12},{16,14},{18,16},{20... | collective-permute-start | bytes 7077896 | tf_op jit(solution)/shard_map/ppermute | solution.py:387
  607.0 270.7 %collective-permute-start.16 = (bf16[128,1536]{1,0:T(8,128)(2,1)S(1)}, bf16[128,1536]{1,0:T(8,128)(2,1)}, u32[]{:S(2)}, u32[]{:S(2)}) collective-permute-start(bf16[128,1536]{1,0:T(8,128)(2,1)S(1)} %fusion.77), channel_id=1, source_target_pairs={{0,1},{1,0},{2,3},{3,2},{4,5},{5,4},{6,7},{7,6},{8,9},{9,8},{10,11... | collective-permute-start | bytes 1179656 | tf_op jit(solution)/shard_map/ppermute | solution.py:381
  719.0 126.4 %collective-permute-start.10 = (bf16[4,192,1920]{2,1,0:T(8,128)(2,1)}, bf16[4,192,1920]{2,1,0:T(8,128)(2,1)}, u32[]{:S(2)}, u32[]{:S(2)}) collective-permute-start(bf16[4,192,1920]{2,1,0:T(8,128)(2,1)} %dynamic-slice_bitcast_fusion), channel_id=1, source_target_pairs={{0,4},{2,6},{4,0},{6,2},{8,12},{10,14},{12,8},{14,10},{16,20},{18,... | collective-permute-start | bytes 8847368 | tf_op jit(solution)/shard_map/ppermute | solution.py:381
  720.4 77.6 %collective-permute-start.11 = (bf16[384,1536]{1,0:T(8,128)(2,1)}, bf16[384,1536]{1,0:T(8,128)(2,1)}, u32[]{:S(2)}, u32[]{:S(2)}) collective-permute-start(bf16[384,1536]{1,0:T(8,128)(2,1)} %reduce-scatter.4.cloned.1.call-done), channel_id=1, source_target_pairs={{0,1},{1,0},{2,3},{3,2},{4,5},{5,4},{6,7},{7,6},{8,9},{9,8},{10,11... | collective-permute-start | bytes 3538952 | tf_op jit(solution)/shard_map/ppermute | solution.py:381
  844.0 51.4 %collective-permute-start.15 = (bf16[768,1536]{1,0:T(8,128)(2,1)}, bf16[768,1536]{1,0:T(8,128)(2,1)}, u32[]{:S(2)}, u32[]{:S(2)}) collective-permute-start(bf16[768,1536]{1,0:T(8,128)(2,1)} %dynamic-slice_convert_fusion), channel_id=1, source_target_pairs={{0,1},{1,0},{2,3},{3,2},{4,5},{5,4},{6,7},{7,6},{8,9},{9,8},{10,11... | collective-permute-start | bytes 7077896 | tf_op jit(solution)/shard_map/ppermute | solution.py:381
  851.7 43.7 %collective-permute-start.14 = (bf16[2,192,1920]{2,1,0:T(8,128)(2,1)}, bf16[2,192,1920]{2,1,0:T(8,128)(2,1)}, u32[]{:S(2)}, u32[]{:S(2)}) collective-permute-start(bf16[2,192,1920]{2,1,0:T(8,128)(2,1)} %dynamic-slice_bitcast_fusion.1), channel_id=1, source_target_pairs={{0,8},{2,10},{4,12},{6,14},{8,0},{10,2},{12,4},{14,6},{16,24},{18,... | collective-permute-start | bytes 4423688 | tf_op jit(solution)/shard_map/ppermute | solution.py:381
  885.2 89.1 %collective-permute-start.20 = (bf16[2,96,1536]{2,1,0:T(8,128)(2,1)}, bf16[2,96,1536]{2,1,0:T(8,128)(2,1)}, u32[]{:S(2)}, u32[]{:S(2)}) collective-permute-start(bf16[2,96,1536]{2,1,0:T(8,128)(2,1)} %slice.175), channel_id=1, source_target_pairs={{0,1},{1,0},{2,3},{3,2},{4,5},{5,4},{6,7},{7,6},{8,9},{9,8},{10,11... | collective-permute-start | bytes 1769480 | tf_op jit(solution)/shard_map/ppermute | solution.py:381
  899.2 73.6 %collective-permute-start.17 = (bf16[1,192,1920]{2,1,0:T(8,128)(2,1)}, bf16[1,192,1920]{2,1,0:T(8,128)(2,1)S(1)}, u32[]{:S(2)}, u32[]{:S(2)}) collective-permute-start(bf16[1,192,1920]{2,1,0:T(8,128)(2,1)} %constant_dynamic-slice_fusion.1), channel_id=1, source_target_pairs={{0,16},{2,18},{4,20},{6,22},{8,24},{10,26},{12,28},{14,30},{16,0},... | collective-permute-start | bytes 2211848 | tf_op jit(solution)/shard_map/ppermute | solution.py:381
  976.1 19.2 %collective-permute-start.19 = (bf16[2,96,1920]{2,1,0:T(8,128)(2,1)S(1)}, bf16[2,96,1920]{2,1,0:T(8,128)(2,1)S(1)}, u32[]{:S(2)}, u32[]{:S(2)}) collective-permute-start(bf16[2,96,1920]{2,1,0:T(8,128)(2,1)S(1)} %pad_maximum_fusion.12), channel_id=1, source_target_pairs={{0,1},{1,0},{2,3},{3,2},{4,5},{5,4},{6,7},{7,6},{8,9},{9,8},{10,11... | collective-permute-start | bytes 2211848 | tf_op jit(solution)/shard_map/ppermute | solution.py:381
  (77 other events, 1333.1 us)
Sparse Core Ops, SparseCore 0:
  11.7 85.7 all-gather.4
  99.6 97.0 all-gather.6
  198.4 98.9 all-gather.8
  298.8 98.9 all-gather.10
  401.7 194.8 reduce-scatter.3
  600.7 209.3 reduce-scatter.5
  845.5 109.5 reduce-scatter.7

commit v9 on v8

--- a/solution.py
+++ b/solution.py
@@ -472,12 +472,8 @@
     return lax.dynamic_index_in_dim(blocks, place % 2, 1, keepdims=False)
 
 
-def chip_sums(block, products):
-    return jnp.concatenate([both(block(kept, 1), block(came, 1)) for kept, came in products], axis=1)
-
-
-def chip_blocks(mine, beside):
-    value = both(mine, beside)
+def chip_blocks(parts):
+    value = jnp.concatenate([both(mine, beside) for mine, beside in parts], axis=1)
     return value.reshape(lax.axis_size("fsdp") // 2, -1, value.shape[1])
 
 
@@ -606,10 +602,16 @@
     grad_two = cotangent.astype(jnp.float32) + back_h2
     grad_two_low = grad_two.astype(jnp.bfloat16)
     if by_steps:
+        up_beside, grad_two_low = gate((both(other_block(up_kept, 1), other_block(up_came, 1)), grad_two_low))
+        half = up_beside.shape[1] // 2
+        first_part, early, late_part = (up_beside[:, a * half // 2 : b * half // 2] for a, b in ((0, 1), (1, 2), (2, 4)))
+        first_part, early = swap(first_part, "seq", 1), swap(early, "seq", 1)
         cout_kept, cout_away = core_products(cross_result, grad_two_low)
-        tree = ((up_kept, up_came), (cout_kept, swap(cout_away, "fsdp", 1)))
+        cout_came = swap(cout_away, "fsdp", 1)
     grad_result = contract_cols(grad_two_low, full_cout).astype(jnp.bfloat16)
     grad_query_c, grad_text_k, grad_text_v = cross_attend_back(cross_query, grad_result, cross_k, cross_v, slots_wide)
+    if by_steps:
+        first_part, grad_query_c, grad_text_k, grad_text_v = gate((first_part, grad_query_c, grad_text_k, grad_text_v))
     grad_text_kv = jnp.stack([grad_text_k, grad_text_v], axis=1)
     if by_steps:
         text_came = swap(other_block(grad_text_kv, 2).astype(jnp.bfloat16), "seq", 1)
@@ -623,6 +625,8 @@
     grad_one = grad_two + back_h1
 
     grad_one_low = grad_one.astype(jnp.bfloat16)
+    if by_steps:
+        early, grad_one_low = gate((early, grad_one_low))
     grad_attended = contract_cols(grad_one_low, full_out).astype(jnp.bfloat16)
     grad_attended, grad_query_c, grad_two_low = gate((grad_attended, grad_query_c, grad_two_low))
     if by_steps:
@@ -634,10 +638,12 @@
         for left, right in ((normed_two, grad_query_c), (attended, grad_one_low), (text_rows, grad_text_kv))
     ]
     if by_steps:
-        small, beside, heads_came = gate((jnp.stack(small), chip_sums(other_block, tree), heads_came))
+        cout_beside = both(other_block(cout_kept, 1), other_block(cout_came, 1))
+        small, cout_beside, heads_came, late_part = gate((jnp.stack(small), cout_beside, heads_came, late_part))
+        late_part = swap(late_part, "seq", 1)
         grad_heads = in_order(own_block(grad_attended, 1), heads_came, 0)
         small = lax.psum_scatter(small, "fsdp", scatter_dimension=1, tiled=True)
-        beside = swap(beside, "seq", 1)
+        cout_beside = swap(cout_beside, "seq", 1)
     else:
         small = [scattered(part) for part in small]
         grad_cout = scattered(contract_rows(cross_result, grad_two_low))
@@ -645,7 +651,10 @@
     query_state, *grad_before = self_attend_back(*back_args, kv_before, starts, SPAN, 0)
     returned = [passed_along(part[:, :head_cols], "fsdp", -1).astype(jnp.float32) for part in grad_before]
     if by_steps:
-        up_rows = chip_blocks(chip_sums(own_block, tree), beside)
+        up_mine = both(own_block(up_kept, 1), own_block(up_came, 1))
+        cout_mine = both(own_block(cout_kept, 1), own_block(cout_came, 1))
+        parts = ((0, half // 2, first_part), (half // 2, half, early), (half, 2 * half, late_part))
+        up_rows = chip_blocks([(up_mine[:, a:b], part) for a, b, part in parts] + [(cout_mine, cout_beside)])
         up_away, grad_down, query_state = gate((half_rows(up_rows, chip + 1), grad_down, query_state))
         up_came, down_beside = swap(up_away, "fsdp", 2), swap(grad_down, "seq", 1)
     grad_q, *grad_own = self_attend_back(*back_args, kv_own, starts, SPAN, SPAN, query_state)
@@ -669,14 +678,11 @@
         normed_came = swap(other_block(grad_normed_one, 0).astype(jnp.bfloat16), "seq", 1)
         up_came, grad_normed_one = gate((up_came, grad_normed_one))
         up_rows = both(half_rows(up_rows, chip), up_came)
-        up_came, normed_came = gate((swap(half_rows(up_rows, chip // 2 + 1), "fsdp", 4), normed_came))
-        up_rows = over_chips(both(half_rows(up_rows, chip // 2), up_came), chip // 4, 8)
+        layer_out, normed_came = gate((layer_out, normed_came))
+        up_rows = over_chips(up_rows, chip // 2, 4)
         grad_normed_one = own_block(grad_normed_one, 0) + normed_came.astype(jnp.float32)
-        grad_cq, grad_wout = whole(small[:2])
-    else:
-        grad_cq, grad_wout = (whole(part) for part in small[:2])
+    else:
         grad_normed_one = summed_block(grad_normed_one, 0)
-    grad_ckv = columns(small[2], 2)
     n_one, root_one = normed(inputs)
     back_x, gain_one, bias_one = norm_back(grad_normed_one, n_one, root_one, gains[0])
     grad_tokens = (grad_one + back_x).astype(jnp.bfloat16)
@@ -684,11 +690,13 @@
         jnp.stack([gain_one, gain_two, gain_three, bias_one, bias_two, bias_three]), ("fsdp", "seq")
     )
     if by_steps:
-        norm_grads, up_rows = gate((norm_grads, up_rows))
+        norm_grads, up_rows, small = gate((norm_grads, up_rows, small))
+        grad_cq, grad_wout = whole(small[:2])
         quarters = own_rows(up_rows)
         grad_up, grad_cout = (jnp.concatenate(parts, axis=1) for parts in zip(*((q[:, :width], q[:, width:]) for q in quarters)))
     else:
-        grad_cout = whole(grad_cout)
+        grad_cout, grad_cq, grad_wout = whole(grad_cout), whole(small[0]), whole(small[1])
+    grad_ckv = columns(small[2], 2)
     grad_wqkv, grad_cout, grad_cq, grad_wout, grad_ckv, grad_up = gate(
         (grad_wqkv, grad_cout, grad_cq, grad_wout, grad_ckv, grad_up)
     )

time: 1030 us -> 1070 us (1.039)
  starting transfers between devices: 29.8 us -> 78.5 us
  Pallas kernels: 164 us -> 149 us
  waiting for transfers between devices: 300 us -> 287 us
  blocking collectives: 59.8 us -> 71.3 us
    ppermute x20 -> x23, starting transfers between devices: 22.9 us -> 71.6 us  [swap(): return lax.ppermute(value, axis, [(i, i ^ bit) for i in range(count)])]
    ppermute x20 -> x23, waiting for transfers between devices: 193 us -> 174 us  [swap(): return lax.ppermute(value, axis, [(i, i ^ bit) for i in range(count)])]
    psum x1, blocking collectives: 59.8 us -> 71.3 us  [shards(): lax.psum(jnp.stack([gain_one, gain_two, gain_three, bias_one, bias_two, b...]
    unnamed x144 -> x146, local copies, waits for them, and re-layouts: 21.6 us -> 20.7 us
    convert_element_type x6 -> x8, other arithmetic: 24.9 us -> 24.4 us  [both(): (first.astype(jnp.float32) + second.astype(jnp.float32)).astype(jnp.bfloa...]
  transfers between devices with their start and end apart: 30 -> 33, of which waited for: 11 -> 14; matrix products, arithmetic and copies ran while one was open for 42% -> 41% of each run, Pallas kernels for 16% -> 14%
where the time goes in v9:
time: 1070 us; the launch traced here: 1060 us
  waiting for transfers between devices  287 us (27%)
  matrix products  287 us (27%)
  Pallas kernels  149 us (14%)
  other arithmetic  115 us (11%)
  starting transfers between devices  78.5 us (7%)
  blocking collectives  71.3 us (7%)
  local copies, waits for them, and re-layouts  57.5 us (5%)
  between operations  15.8 us (1%)
    ppermute x23, waiting for transfers between devices, swap(): return lax.ppermute(value, axis, [(i, i ^ bit) for i in range(count)])  174 us
    all_gather x4, waiting for transfers between devices, shards(): row_block = lambda value: lax.all_gather(value, 'fsdp', axis=0, tiled=True)  111 us
    dot_general x9, matrix products, matmul(): return jnp.dot(left_side, right_side, preferred_element_type=jnp.float32)  108 us
    dot_general x7, matrix products, contract_cols(): lax.dot_general(left_side, right_side, (((1,), (1,)), ((), ())), preferre...  95.4 us
    dot_general x9, matrix products, contract_rows(): lax.dot_general(left_side, right_side, (((0,), (0,)), ((), ())), preferre...  83.1 us
    pallas_call x2, Pallas kernels, self_attend_back(): pl.pallas_call(functools.partial(attend_back_kernel, reach=reach, base=ba...  75.9 us
    ppermute x23, starting transfers between devices, swap(): return lax.ppermute(value, axis, [(i, i ^ bit) for i in range(count)])  71.6 us
    psum x1, blocking collectives, shards(): lax.psum(jnp.stack([gain_one, gain_two, gain_three, bias_one, bias_two, b...  71.3 us
  transfers between devices with their start and end apart: 33, of which 14 were waited for; matrix products, arithmetic and copies ran while one was open for 41% of the time, Pallas kernels for 14%

profile of v9, /device:TPU:0, one launch (start us, length us, event | category | flops | bytes accessed | tf_op | source)
XLA Modules:
  0.0 1061.2 jit_solution(5120744391021294032)
XLA Ops:
  30.3 45.8 %collective-permute-done = bf16[768,1536]{1,0:T(8,128)(2,1)} collective-permute-done((bf16[768,1536]{1,0:T(8,128)(2,1)S(1)}, bf16[768,1536]{1,0:T(8,128)(2,1)}, u32[]{:S(2)}, u32[]{:S(2)}) %collective-permute-start) | collective-permute-done | bytes 2359328 | tf_op jit(solution)/shard_map/ppermute | solution.py:381
  82.5 15.0 %all-gather.5.cloned.1.call-done = bf16[1536,2432]{1,0:T(8,128)(2,1)} async-done(((bf16[96,2432]{1,0:T(8,128)(2,1)}), bf16[1536,2432]{1,0:T(8,128)(2,1)}) %all-gather.5.cloned.1.call-update) | async-done | bytes 7471120 | tf_op jit(solution)/shard_map/all_gather | solution.py:530
  122.2 33.9 %self_attend.2.refs_0_ = f32[2,4,6,80,384]{4,3,2,1,0:T(8,128)} custom-call(s32[4,4]{1,0:T(4,128)} %pad_add_fusion.1.bounds, bf16[1536,768]{1,0:T(8,128)(2,1)} %convolution_convert_fusion.11.q_ref, bf16[1536,1536]{1,0:T(8,128)(2,1)} %convolution_convert_fusion.8.k_ref.v_ref, bf16[1536,1536]{1,0:T(8,128)(2,1)} %convolution_convert_fusion.8.k_ref.v_ref, ...), custom_call_target="tpu_custom_call" | custom-call | flops 150994944 | bytes 98304 | tf_op jit(solution)/shard_map/self_attend/pallas_call | solution.py:161
  174.6 12.1 %self_attend.3 = (bf16[1536,768]{1,0:T(8,128)(2,1)}, f32[2,4,8,384]{3,2,1,0:T(8,128)}) custom-call(s32[4,4]{1,0:T(4,128)} %pad_add_fusion.bounds, bf16[1536,768]{1,0:T(8,128)(2,1)} %convolution_convert_fusion.11.q_ref, bf16[1536,1536]{1,0:T(8,128)(2,1)} %convolution_convert_fusion.7.k_ref.v_ref, bf16[1536,1536]{1,0:T(8,128)(2,1)} %convolution_convert_fusion.7.k_ref.v_ref, ...), custom_call_target="tpu_custom_call" | custom-call | flops 150994944 | bytes 98304 | tf_op jit(solution)/shard_map/self_attend/pallas_call | solution.py:161
  191.1 14.4 %collective-permute-done.3 = bf16[768,768]{1,0:T(8,128)(2,1)} collective-permute-done((bf16[768,768]{1,0:T(8,128)(2,1)}, bf16[768,768]{1,0:T(8,128)(2,1)}, u32[]{:S(2)}, u32[]{:S(2)}) %collective-permute-start.3) | collective-permute-done | bytes 1179680 | tf_op jit(solution)/shard_map/ppermute | solution.py:381
  252.3 45.0 %all-gather.9.cloned.1.call-done = bf16[1536,6144]{1,0:T(8,128)(2,1)} async-done(((bf16[96,6144]{1,0:T(8,128)(2,1)}), bf16[1536,6144]{1,0:T(8,128)(2,1)}) %all-gather.9.cloned.1.call-update) | async-done | bytes 18874384 | tf_op jit(solution)/shard_map/all_gather | solution.py:530
  297.3 27.4 %fusion.3 = (f32[768,6144]{1,0:T(8,128)}, bf16[768,6144]{1,0:T(8,128)(2,1)S(1)}) fusion(bf16[1536,6144]{1,0:T(8,128)(2,1)} %all-gather.9.cloned.1.call-done, f32[768,1536]{1,0:T(8,128)} %copy-done.8, f32[1536]{0:T(1024)S(1)} %copy-done.49, f32[1536]{0:T(1024)S(1)} %get-tuple-element.138, f32[768]{0:T(1024)S(1)} %add_rsqrt_fusion.3, ...), kind=kOutput, calls=%fused_computation.5 | convolution fusion | flops 14548598784 | bytes 51922944 | tf_op jit(solution)/shard_map/dot_general | solution.py:22
  328.3 18.3 %convolution_convert_fusion = bf16[6144,1536]{1,0:T(8,128)(2,1)} fusion(bf16[768,6144]{1,0:T(8,128)(2,1)S(1)} %get-tuple-element.160, bf16[768,1536]{1,0:T(8,128)(2,1)S(1)} %copy-done.20), kind=kOutput, calls=%fused_computation.1 | convolution fusion | flops 14504951808 | bytes 30670848 | tf_op jit(solution)/shard_map/dot_general | solution.py:26
  346.6 51.1 %all-gather.11.cloned.1.call-done = bf16[6144,1536]{1,0:T(8,128)(2,1)} async-done(((bf16[384,1536]{1,0:T(8,128)(2,1)}), bf16[6144,1536]{1,0:T(8,128)(2,1)}) %all-gather.11.cloned.1.call-update) | async-done | bytes 18874384 | tf_op jit(solution)/shard_map/all_gather | solution.py:530
  397.8 26.9 %multiply_convert_fusion = bf16[768,6144]{1,0:T(8,128)(2,1)} fusion(f32[768,6144]{1,0:T(8,128)} %get-tuple-element.73, bf16[768,1536]{1,0:T(8,128)(2,1)S(1)} %copy-done.20, bf16[6144,1536]{1,0:T(8,128)(2,1)} %all-gather.11.cloned.1.call-done), kind=kOutput, calls=%fused_computation.6 | convolution fusion | flops 14504951808 | bytes 49545216 | tf_op jit(solution)/shard_map/dot_general | solution.py:32
  424.7 15.3 %convolution_convert_fusion.2 = bf16[1536,3072]{1,0:T(8,128)(2,1)} fusion(bf16[768,6144]{1,0:T(8,128)(2,1)} %multiply_convert_fusion, s32[]{:T(128)S(6)} %select_n.291, f32[768,1536]{1,0:T(8,128)} %copy-done.8, f32[1536]{0:T(1024)S(1)} %copy-done.49, f32[1536]{0:T(1024)S(1)} %get-tuple-element.138, f32[768]{0:T(1024)S(1)} %add_rsqrt_fusion.3, ...), kind=kOutput, calls=%fused_computation.15 | convolution fusion | flops 7258374144 | bytes 18892804 | tf_op jit(solution)/shard_map/dot_general | solution.py:26
  440.0 13.1 %convolution_convert_fusion.1 = bf16[1536,3072]{1,0:T(8,128)(2,1)} fusion(bf16[768,6144]{1,0:T(8,128)(2,1)S(1)} %copy-done.55, s32[]{:T(128)S(6)} %select_n.292, f32[768,1536]{1,0:T(8,128)} %copy-done.8, f32[1536]{0:T(1024)S(1)} %copy-done.49, f32[1536]{0:T(1024)S(1)} %get-tuple-element.138, f32[768]{0:T(1024)S(1)} %add_rsqrt_fusion.3, ...), kind=kOutput, calls=%fused_computation.14 | convolution fusion | flops 7258374144 | bytes 18898948 | tf_op jit(solution)/shard_map/dot_general | solution.py:26
  453.4 24.4 %multiply_reduce_fusion = (f32[1536]{0:T(1024)}, f32[768]{0:T(1024)S(1)}, f32[768]{0:T(1024)S(1)}, f32[1536]{0:T(1024)}, f32[768,1536]{1,0:T(8,128)}) fusion(f32[768,1536]{1,0:T(8,128)} %copy-done.8, f32[768]{0:T(1024)S(1)} %add_rsqrt_fusion.3, f32[768]{0:T(1024)S(1)} %broadcast_multiply_fusion.9, f32[1536]{0:T(1024)S(1)} %get-tuple-element.138, ...), kind=kOutput, calls=%fused_computation.62 | convolution fusion | flops 14506125312 | bytes 37779456 | tf_op jit(solution)/shard_map/dot_general | solution.py:32
  510.5 17.6 %cross_attend_back.1 = (bf16[768,1536]{1,0:T(8,128)(2,1)}, f32[128,1536]{1,0:T(8,128)}, f32[128,1536]{1,0:T(8,128)}) custom-call(bf16[768,1536]{1,0:T(8,128)(2,1)} %fusion.67.q_ref, bf16[768,1536]{1,0:T(8,128)(2,1)} %fusion.70.g_ref, bf16[128,1536]{1,0:T(8,128)(2,1)} %get-tuple-element.182.k_ref, bf16[128,1536]{1,0:T(8,128)(2,1)} %get-tuple-element.181.v_ref, ...), custom_call_target="tpu_custom_call" | custom-call | flops 3019898880 | bytes 7077888 | tf_op jit(solution)/shard_map/cross_attend_back/pallas_call | solution.py:349
  534.6 24.8 %collective-permute-done.8 = bf16[128,2,768]{2,0,1:T(8,128)(2,1)S(1)} collective-permute-done((bf16[128,2,768]{2,0,1:T(8,128)(2,1)S(1)}, bf16[128,2,768]{2,0,1:T(8,128)(2,1)S(1)}, u32[]{:S(2)}, u32[]{:S(2)}) %collective-permute-start.8) | collective-permute-done | bytes 393248 | tf_op jit(solution)/shard_map/ppermute | solution.py:381
  627.2 16.6 %self_attend_back.2 = (f32[2,4,6,64,384]{4,3,2,1,0:T(8,128)}, bf16[1536,768]{1,0:T(8,128)(2,1)}, bf16[1536,768]{1,0:T(8,128)(2,1)}) custom-call(s32[4,4]{1,0:T(4,128)} %pad_add_fusion.bounds, bf16[1536,768]{1,0:T(8,128)(2,1)} %convolution_convert_fusion.11.q_ref, bf16[1536,768]{1,0:T(8,128)(2,1)} %pad_maximum_fusion.6.g_ref, ...), custom_call_target="tpu_custom_call" | custom-call | flops 150994944 | bytes 98304 | tf_op jit(solution)/shard_map/self_attend_back/pallas_call | solution.py:261
  648.9 52.6 %collective-permute-done.12 = bf16[1536,384]{1,0:T(8,128)(2,1)} collective-permute-done((bf16[1536,384]{1,0:T(8,128)(2,1)}, bf16[1536,384]{1,0:T(8,128)(2,1)}, u32[]{:S(2)}, u32[]{:S(2)}) %collective-permute-start.12) | collective-permute-done | bytes 1179680 | tf_op jit(solution)/shard_map/ppermute | solution.py:381
  712.4 35.1 %collective-permute-start.17 = (bf16[4,192,1920]{2,1,0:T(8,128)(2,1)}, bf16[4,192,1920]{2,1,0:T(8,128)(2,1)}, u32[]{:S(2)}, u32[]{:S(2)}) collective-permute-start(bf16[4,192,1920]{2,1,0:T(8,128)(2,1)} %dynamic-slice_bitcast_fusion), channel_id=1, source_target_pairs={{0,4},{2,6},{4,0},{6,2},{8,12},{10,14},{12,8},{14,10},{16,20},{18,... | collective-permute-start | bytes 8847368 | tf_op jit(solution)/shard_map/ppermute | solution.py:381
  747.4 59.3 %self_attend_back.3 = (bf16[1536,768]{1,0:T(8,128)(2,1)}, bf16[1536,768]{1,0:T(8,128)(2,1)}, bf16[1536,768]{1,0:T(8,128)(2,1)}) custom-call(s32[4,4]{1,0:T(4,128)} %pad_add_fusion.1.bounds, bf16[1536,768]{1,0:T(8,128)(2,1)} %convolution_convert_fusion.11.q_ref, bf16[1536,768]{1,0:T(8,128)(2,1)} %pad_maximum_fusion.6.g_ref, ...), custom_call_target="tpu_custom_call" | custom-call | flops 150994944 | bytes 98304 | tf_op jit(solution)/shard_map/self_attend_back/pallas_call | solution.py:261
  818.3 19.2 %convolution_convert_fusion.3 = bf16[1536,2304]{1,0:T(8,128)(2,1)} fusion(bf16[1536,768]{1,0:T(8,128)(2,1)} %copy-done.12, bf16[1536,768]{1,0:T(8,128)(2,1)} %copy-done.13, bf16[1536,768]{1,0:T(8,128)(2,1)} %get-tuple-element.101, f32[1536]{0:T(1024)} %copy-done.46, f32[1536]{0:T(1024)S(1)} %copy-done.37, f32[1536]{0:T(1024)} %copy-done.54, ...), kind=kOutput, calls=%fused_computation.16 | convolution fusion | flops 10917642240 | bytes 18898944 | tf_op jit(solution)/shard_map/dot_general | solution.py:26
  837.5 16.0 %fusion.16 = f32[1536,1536]{1,0:T(8,128)S(1)} fusion(bf16[1536,2304]{1,0:T(8,128)(2,1)} %pad_maximum_fusion.1, bf16[1536,2432]{1,0:T(8,128)(2,1)} %all-gather.5.cloned.1.call-done), kind=kOutput, calls=%fused_computation.36 | convolution fusion | flops 10871635968 | bytes 23592960 | tf_op jit(solution)/shard_map/dot_general | solution.py:32
  876.9 22.2 %add_convert_fusion.5 = bf16[768,1536]{1,0:T(8,128)(2,1)} fusion(f32[768,1536]{1,0:T(8,128)} %copy-done.8, bf16[768,6144]{1,0:T(8,128)(2,1)} %copy-done.58, bf16[6144,1536]{1,0:T(8,128)(2,1)} %all-gather.11.cloned.1.call-done), kind=kOutput, calls=%fused_computation.75 | convolution fusion | flops 14497873920 | bytes 35389440 | tf_op jit(solution)/shard_map/dot_general | solution.py:22
  919.5 71.3 %psum.7 = f32[6,1536]{1,0:T(8,128)} all-reduce(f32[6,1536]{1,0:T(8,128)S(1)} %stack.114), channel_id=1, replica_groups=mesh['fsdp'=16,'seq'=2] {'fsdp','seq'}, use_global_device_ids=true, to_apply=%region_26.27 | all-reduce | flops 9216 | bytes 73728 | tf_op jit(solution)/shard_map/psum | solution.py:689
  1020.7 13.3 %collective-permute-done.22 = bf16[2,96,1920]{2,1,0:T(8,128)(2,1)S(1)} collective-permute-done((bf16[2,96,1920]{2,1,0:T(8,128)(2,1)S(1)}, bf16[2,96,1920]{2,1,0:T(8,128)(2,1)S(1)}, u32[]{:S(2)}, u32[]{:S(2)}) %collective-permute-start.22) | collective-permute-done | bytes 737312 | tf_op jit(solution)/shard_map/ppermute | solution.py:381
  (364 shorter events, 354.6 us)
Async XLA Ops:
  7.2 90.3 %all-gather.5.cloned.1.call-start = ((), (), s32[]{:S(2)}) async-start(), calls=%async_computation.3 | async-start | bytes 7938048 | tf_op jit(solution)/shard_map/all_gather | solution.py:530
  11.6 197.4 %all-gather.7.cloned.1.call-start = ((), (), s32[]{:S(2)}) async-start(), calls=%async_computation.4 | async-start | bytes 20054016 | tf_op jit(solution)/shard_map/all_gather | solution.py:530
  16.4 281.0 %all-gather.9.cloned.1.call-start = ((), (), s32[]{:S(2)}) async-start(), calls=%async_computation.5 | async-start | bytes 20054016 | tf_op jit(solution)/shard_map/all_gather | solution.py:530
  17.1 380.6 %all-gather.11.cloned.1.call-start = ((), (), s32[]{:S(2)}) async-start(), calls=%async_computation.6 | async-start | bytes 20054016 | tf_op jit(solution)/shard_map/all_gather | solution.py:530
  17.7 692.9 %reduce-scatter.4.cloned.1.call-start = ((), (), s32[]{:S(2)}) async-start(), calls=%async_computation.7 | async-start | bytes 20054016 | tf_op jit(solution)/shard_map/reduce_scatter | solution.py:446
  21.5 54.6 %collective-permute-start = (bf16[768,1536]{1,0:T(8,128)(2,1)S(1)}, bf16[768,1536]{1,0:T(8,128)(2,1)}, u32[]{:S(2)}, u32[]{:S(2)}) collective-permute-start(bf16[768,1536]{1,0:T(8,128)(2,1)S(1)} %copy-done.1), channel_id=1, source_target_pairs={{0,1},{1,0},{2,3},{3,2},{4,5},{5,4},{6,7},{7,6},{8,9},{9,8},{10,11... | collective-permute-start | bytes 7077896 | tf_op jit(solution)/shard_map/ppermute | solution.py:381
  30.3 125.8 %collective-permute-start.2 = (bf16[768,1536]{1,0:T(8,128)(2,1)}, bf16[768,1536]{1,0:T(8,128)(2,1)}, u32[]{:S(2)}, u32[]{:S(2)}) collective-permute-start(bf16[768,1536]{1,0:T(8,128)(2,1)} %collective-permute-done.1), channel_id=1, source_target_pairs={{0,1},{1,0},{2,3},{3,2},{4,5},{5,4},{6,7},{7,6},{8,9},{9,8},{10,11... | collective-permute-start | bytes 7077896 | tf_op jit(solution)/shard_map/ppermute | solution.py:381
  346.6 530.2 %reduce-scatter.6.cloned.1.call-start = ((), (), s32[]{:S(2)}) async-start(), calls=%async_computation.8 | async-start | bytes 15040512 | tf_op jit(solution)/shard_map/reduce_scatter | solution.py:645
  453.1 30.1 %collective-permute-start.5 = (bf16[1536,3072]{1,0:T(8,128)(2,1)}, bf16[1536,3072]{1,0:T(8,128)(2,1)}, u32[]{:S(2)}, u32[]{:S(2)}) collective-permute-start(bf16[1536,3072]{1,0:T(8,128)(2,1)} %convolution_convert_fusion.1), channel_id=1, source_target_pairs={{0,2},{2,0},{4,6},{6,4},{8,10},{10,8},{12,14},{14,12},{16,18},{18,... | collective-permute-start | bytes 28311560 | tf_op jit(solution)/shard_map/ppermute | solution.py:381
  497.5 30.7 %collective-permute-start.6 = (bf16[1536,384]{1,0:T(8,128)(2,1)}, bf16[1536,384]{1,0:T(8,128)(2,1)}, u32[]{:S(2)}, u32[]{:S(2)}) collective-permute-start(bf16[1536,384]{1,0:T(8,128)(2,1)} %get-tuple-element.164), channel_id=1, source_target_pairs={{0,1},{1,0},{2,3},{3,2},{4,5},{5,4},{6,7},{7,6},{8,9},{9,8},{10,11... | collective-permute-start | bytes 3538952 | tf_op jit(solution)/shard_map/ppermute | solution.py:381
  499.0 79.5 %collective-permute-start.7 = (bf16[1536,384]{1,0:T(8,128)(2,1)}, bf16[1536,384]{1,0:T(8,128)(2,1)}, u32[]{:S(2)}, u32[]{:S(2)}) collective-permute-start(bf16[1536,384]{1,0:T(8,128)(2,1)} %get-tuple-element.163), channel_id=1, source_target_pairs={{0,1},{1,0},{2,3},{3,2},{4,5},{5,4},{6,7},{7,6},{8,9},{9,8},{10,11... | collective-permute-start | bytes 3538952 | tf_op jit(solution)/shard_map/ppermute | solution.py:381
  502.9 102.2 %collective-permute-start.9 = (bf16[1536,768]{1,0:T(8,128)(2,1)}, bf16[1536,768]{1,0:T(8,128)(2,1)S(1)}, u32[]{:S(2)}, u32[]{:S(2)}) collective-permute-start(bf16[1536,768]{1,0:T(8,128)(2,1)} %convolution_convert_fusion.9), channel_id=1, source_target_pairs={{0,2},{2,0},{4,6},{6,4},{8,10},{10,8},{12,14},{14,12},{16,18},{18,... | collective-permute-start | bytes 7077896 | tf_op jit(solution)/shard_map/ppermute | solution.py:381
  529.5 29.8 %collective-permute-start.8 = (bf16[128,2,768]{2,0,1:T(8,128)(2,1)S(1)}, bf16[128,2,768]{2,0,1:T(8,128)(2,1)S(1)}, u32[]{:S(2)}, u32[]{:S(2)}) collective-permute-start(bf16[128,2,768]{2,0,1:T(8,128)(2,1)S(1)} %fusion.88), channel_id=1, source_target_pairs={{0,1},{1,0},{2,3},{3,2},{4,5},{5,4},{6,7},{7,6},{8,9},{9,8},{10,11... | collective-permute-start | bytes 1179656 | tf_op jit(solution)/shard_map/ppermute | solution.py:381
  614.3 422.8 %reduce-scatter.8.cloned.1.call-start = ((), (), s32[]{:S(2)}) async-start(), calls=%async_computation.9 | async-start | bytes 7520256 | tf_op jit(solution)/shard_map/reduce_scatter | solution.py:446
  615.7 87.6 %collective-permute-start.11 = (bf16[1536,768]{1,0:T(8,128)(2,1)}, bf16[1536,768]{1,0:T(8,128)(2,1)}, u32[]{:S(2)}, u32[]{:S(2)}) collective-permute-start(bf16[1536,768]{1,0:T(8,128)(2,1)} %slice.189), channel_id=1, source_target_pairs={{0,1},{1,0},{2,3},{3,2},{4,5},{5,4},{6,7},{7,6},{8,9},{9,8},{10,11... | collective-permute-start | bytes 7077896 | tf_op jit(solution)/shard_map/ppermute | solution.py:381
  621.5 280.0 %collective-permute-start.18 = (bf16[128,1536]{1,0:T(8,128)(2,1)S(1)}, bf16[128,1536]{1,0:T(8,128)(2,1)S(1)}, u32[]{:S(2)}, u32[]{:S(2)}) collective-permute-start(bf16[128,1536]{1,0:T(8,128)(2,1)S(1)} %fusion.77), channel_id=1, source_target_pairs={{0,1},{1,0},{2,3},{3,2},{4,5},{5,4},{6,7},{7,6},{8,9},{9,8},{10,11... | collective-permute-start | bytes 1179656 | tf_op jit(solution)/shard_map/ppermute | solution.py:381
  621.9 79.7 %collective-permute-start.12 = (bf16[1536,384]{1,0:T(8,128)(2,1)}, bf16[1536,384]{1,0:T(8,128)(2,1)}, u32[]{:S(2)}, u32[]{:S(2)}) collective-permute-start(bf16[1536,384]{1,0:T(8,128)(2,1)} %add_convert_fusion.10), channel_id=1, source_target_pairs={{0,1},{1,0},{2,3},{3,2},{4,5},{5,4},{6,7},{7,6},{8,9},{9,8},{10,11... | collective-permute-start | bytes 3538952 | tf_op jit(solution)/shard_map/ppermute | solution.py:381
  643.8 163.0 %collective-permute-start.15 = (bf16[1536,768]{1,0:T(8,128)(2,1)}, bf16[1536,768]{1,0:T(8,128)(2,1)}, u32[]{:S(2)}, u32[]{:S(2)}) collective-permute-start(bf16[1536,768]{1,0:T(8,128)(2,1)} %get-tuple-element.105), channel_id=1, source_target_pairs={{2,0},{4,2},{6,4},{8,6},{10,8},{12,10},{14,12},{16,14},{18,16},{20... | collective-permute-start | bytes 7077896 | tf_op jit(solution)/shard_map/ppermute | solution.py:387
  647.6 162.4 %collective-permute-start.14 = (bf16[1536,768]{1,0:T(8,128)(2,1)}, bf16[1536,768]{1,0:T(8,128)(2,1)}, u32[]{:S(2)}, u32[]{:S(2)}) collective-permute-start(bf16[1536,768]{1,0:T(8,128)(2,1)} %get-tuple-element.103), channel_id=1, source_target_pairs={{2,0},{4,2},{6,4},{8,6},{10,8},{12,10},{14,12},{16,14},{18,16},{20... | collective-permute-start | bytes 7077896 | tf_op jit(solution)/shard_map/ppermute | solution.py:387
  710.6 102.7 %collective-permute-start.13 = (bf16[384,1536]{1,0:T(8,128)(2,1)}, bf16[384,1536]{1,0:T(8,128)(2,1)}, u32[]{:S(2)}, u32[]{:S(2)}) collective-permute-start(bf16[384,1536]{1,0:T(8,128)(2,1)} %reduce-scatter.4.cloned.1.call-done), channel_id=1, source_target_pairs={{0,1},{1,0},{2,3},{3,2},{4,5},{5,4},{6,7},{7,6},{8,9},{9,8},{10,11... | collective-permute-start | bytes 3538952 | tf_op jit(solution)/shard_map/ppermute | solution.py:381
  712.4 146.2 %collective-permute-start.17 = (bf16[4,192,1920]{2,1,0:T(8,128)(2,1)}, bf16[4,192,1920]{2,1,0:T(8,128)(2,1)}, u32[]{:S(2)}, u32[]{:S(2)}) collective-permute-start(bf16[4,192,1920]{2,1,0:T(8,128)(2,1)} %dynamic-slice_bitcast_fusion), channel_id=1, source_target_pairs={{0,4},{2,6},{4,0},{6,2},{8,12},{10,14},{12,8},{14,10},{16,20},{18,... | collective-permute-start | bytes 8847368 | tf_op jit(solution)/shard_map/ppermute | solution.py:381
  855.5 50.0 %collective-permute-start.16 = (bf16[768,1536]{1,0:T(8,128)(2,1)}, bf16[768,1536]{1,0:T(8,128)(2,1)}, u32[]{:S(2)}, u32[]{:S(2)}) collective-permute-start(bf16[768,1536]{1,0:T(8,128)(2,1)} %dynamic-slice_convert_fusion), channel_id=1, source_target_pairs={{0,1},{1,0},{2,3},{3,2},{4,5},{5,4},{6,7},{7,6},{8,9},{9,8},{10,11... | collective-permute-start | bytes 7077896 | tf_op jit(solution)/shard_map/ppermute | solution.py:381
  864.8 42.5 %collective-permute-start.19 = (bf16[2,192,1920]{2,1,0:T(8,128)(2,1)}, bf16[2,192,1920]{2,1,0:T(8,128)(2,1)}, u32[]{:S(2)}, u32[]{:S(2)}) collective-permute-start(bf16[2,192,1920]{2,1,0:T(8,128)(2,1)} %dynamic-slice_bitcast_fusion.1), channel_id=1, source_target_pairs={{0,8},{2,10},{4,12},{6,14},{8,0},{10,2},{12,4},{14,6},{16,24},{18,... | collective-permute-start | bytes 4423688 | tf_op jit(solution)/shard_map/ppermute | solution.py:381
  910.6 80.9 %collective-permute-start.20 = (bf16[1,192,1920]{2,1,0:T(8,128)(2,1)S(1)}, bf16[1,192,1920]{2,1,0:T(8,128)(2,1)}, u32[]{:S(2)}, u32[]{:S(2)}) collective-permute-start(bf16[1,192,1920]{2,1,0:T(8,128)(2,1)S(1)} %constant_dynamic-slice_fusion.1), channel_id=1, source_target_pairs={{0,16},{2,18},{4,20},{6,22},{8,24},{10,26},{12,28},{14,30},{16,0},... | collective-permute-start | bytes 2211848 | tf_op jit(solution)/shard_map/ppermute | solution.py:381
  (80 other events, 1632.9 us)
Sparse Core Ops, SparseCore 0:
  11.7 85.7 all-gather.4
  99.6 97.0 all-gather.6
  198.4 98.9 all-gather.8
  298.8 98.9 all-gather.10
  401.7 194.7 reduce-scatter.3
  614.4 205.7 reduce-scatter.5
  877.0 112.9 reduce-scatter.7

commit v10 on v7

--- a/solution.py
+++ b/solution.py
@@ -554,7 +554,7 @@
     kv_own = matmul(normed_one, w_kv).astype(jnp.bfloat16)
     queries = matmul(normed_one, w_q).astype(jnp.bfloat16)
     if by_steps:
-        before = passed_along(tokens, "fsdp", 1)
+        before = passed_along(gate((tokens, first))[0], "fsdp", 1)
         before_other = swap(before, "seq", 1)
     else:
         kv_before = passed_along(kv_own[group_rows - SPAN :], "fsdp", 1)
@@ -603,19 +603,28 @@
     grad_two_low = grad_two.astype(jnp.bfloat16)
     if by_steps:
         up_beside, grad_two_low = gate((seq_away(up_kept, up_came), grad_two_low))
-        up_beside = swap(up_beside, "seq", 1)
     grad_result = contract_cols(grad_two_low, full_cout).astype(jnp.bfloat16)
     grad_query_c, grad_text_k, grad_text_v = cross_attend_back(cross_query, grad_result, cross_k, cross_v, slots_wide)
-    grad_text_kv = summed_block(jnp.stack([grad_text_k, grad_text_v], axis=1), 2)
+    grad_text_kv = jnp.stack([grad_text_k, grad_text_v], axis=1)
+    if by_steps:
+        text_came = swap(other_block(grad_text_kv, 2).astype(jnp.bfloat16), "seq", 1)
+    else:
+        grad_text_kv = summed_block(grad_text_kv, 2)
+    back_h1, gain_two, bias_two = norm_back(contract_cols(grad_query_c, full_cq), n_two, root_two, gains[1])
+    grad_one = grad_two + back_h1
+
+    grad_one_low = grad_one.astype(jnp.bfloat16)
+    if by_steps:
+        text_came, grad_one_low = gate((text_came, grad_one_low))
+        grad_text_kv = own_block(grad_text_kv, 2) + text_came.astype(jnp.float32)
     grad_text_kv = grad_text_kv.astype(jnp.bfloat16).reshape(text_count, 2 * head_cols)
     grad_text = contract_cols(grad_text_kv, w_ckv)
-    back_h1, gain_two, bias_two = norm_back(contract_cols(grad_query_c, full_cq), n_two, root_two, gains[1])
-    grad_one = grad_two + back_h1
-
-    grad_one_low = grad_one.astype(jnp.bfloat16)
     grad_attended = contract_cols(grad_one_low, full_out).astype(jnp.bfloat16)
     grad_attended, grad_query_c, grad_two_low = gate((grad_attended, grad_query_c, grad_two_low))
-    grad_heads = paired(exchanged(grad_attended, 1, 0))
+    if by_steps:
+        heads_came = swap(other_block(grad_attended, 1), "seq", 1)
+    else:
+        grad_heads = paired(exchanged(grad_attended, 1, 0))
     small = [
         contract_rows(left, right).astype(jnp.bfloat16)
         for left, right in (
@@ -626,7 +635,10 @@
         )
     ]
     if by_steps:
-        small = lax.psum_scatter(gate((jnp.stack(small), grad_down, grad_heads))[0], "fsdp", scatter_dimension=1, tiled=True)
+        small, up_beside, heads_came = gate((jnp.stack(small), up_beside, heads_came))
+        small = lax.psum_scatter(small, "fsdp", scatter_dimension=1, tiled=True)
+        up_beside = swap(up_beside, "seq", 1)
+        grad_heads = in_order(own_block(grad_attended, 1), heads_came, 0)
     else:
         small = [scattered(part) for part in small]
     back_args = (queries, grad_heads, heads_out, log_totals)
@@ -649,8 +661,12 @@
         part = jnp.concatenate([part[:late], part[late:] + more]) if late else part + more
         owned.append(part.astype(jnp.bfloat16))
     grad_proj = jnp.concatenate(owned, axis=1)
-    grad_normed_one, grad_proj = gate((contract_cols(grad_proj, w_qkv), grad_proj))
-    grad_normed_one = summed_block(grad_normed_one, 0)
+    if by_steps:
+        away = contract_cols(other_block(grad_proj, 0), w_qkv).astype(jnp.bfloat16)
+        away, grad_proj = gate((away, grad_proj))
+        grad_normed_one = swap(away, "seq", 1).astype(jnp.float32) + contract_cols(own_block(grad_proj, 0), w_qkv)
+    else:
+        grad_normed_one = summed_block(contract_cols(grad_proj, w_qkv), 0)
     grad_wqkv = contract_rows(normed_one, grad_proj).astype(jnp.bfloat16)
     n_one, root_one = normed(inputs)
     back_x, gain_one, bias_one = norm_back(grad_normed_one, n_one, root_one, gains[0])

time: 1030 us -> 1020 us (level)
  Pallas kernels: 148 us -> 165 us
  other arithmetic: 110 us -> 96.4 us
  starting transfers between devices: 27.7 us -> 38.5 us
    ppermute x20, waiting for transfers between devices: 256 us -> 244 us  [swap(): return lax.ppermute(value, axis, [(i, i ^ bit) for i in range(count)])]
    ppermute x20, starting transfers between devices: 21.1 us -> 32.5 us  [swap(): return lax.ppermute(value, axis, [(i, i ^ bit) for i in range(count)])]
    pallas_call x2, Pallas kernels: 75 us -> 85.9 us  [self_attend_back(): pl.pallas_call(functools.partial(attend_back_kernel, reach=reach, base=ba...]
    dot_general x7 -> x8, matrix products: 98.7 us -> 95.5 us  [contract_cols(): lax.dot_general(left_side, right_side, (((1,), (1,)), ((), ())), preferre...]
  transfers between devices with their start and end apart: 30 -> 30, of which waited for: 14 -> 13; matrix products, arithmetic and copies ran while one was open for 42% -> 40% of each run, Pallas kernels for 15% -> 16%
where the time goes in v10:
time: 1020 us; the launch traced here: 1010 us
  waiting for transfers between devices  368 us (36%)
  matrix products  281 us (28%)
  Pallas kernels  165 us (16%)
  other arithmetic  96.4 us (9%)
  local copies, waits for them, and re-layouts  44.2 us (4%)
  starting transfers between devices  38.5 us (4%)
  between operations  15.7 us (2%)
    ppermute x20, waiting for transfers between devices, swap(): return lax.ppermute(value, axis, [(i, i ^ bit) for i in range(count)])  244 us
    all_gather x4, waiting for transfers between devices, shards(): row_block = lambda value: lax.all_gather(value, 'fsdp', axis=0, tiled=True)  113 us
    dot_general x9, matrix products, matmul(): return jnp.dot(left_side, right_side, preferred_element_type=jnp.float32)  110 us
    dot_general x8, matrix products, contract_cols(): lax.dot_general(left_side, right_side, (((1,), (1,)), ((), ())), preferre...  95.5 us
    pallas_call x2, Pallas kernels, self_attend_back(): pl.pallas_call(functools.partial(attend_back_kernel, reach=reach, base=ba...  85.9 us
    dot_general x8, matrix products, contract_rows(): lax.dot_general(left_side, right_side, (((0,), (0,)), ((), ())), preferre...  75.3 us
    pallas_call x2, Pallas kernels, self_attend(): pl.pallas_call(functools.partial(attend_kernel, reach=reach, base=base, p...  51.4 us
    ppermute x20, starting transfers between devices, swap(): return lax.ppermute(value, axis, [(i, i ^ bit) for i in range(count)])  32.5 us
  transfers between devices with their start and end apart: 30, of which 13 were waited for; matrix products, arithmetic and copies ran while one was open for 40% of the time, Pallas kernels for 16%

profile of v10, /device:TPU:0, one launch (start us, length us, event | category | flops | bytes accessed | tf_op | source)
XLA Modules:
  0.0 1008.8 jit_solution(7441123653748842246)
XLA Ops:
  27.2 44.9 %collective-permute-done = bf16[768,1536]{1,0:T(8,128)(2,1)} collective-permute-done((bf16[768,1536]{1,0:T(8,128)(2,1)S(1)}, bf16[768,1536]{1,0:T(8,128)(2,1)}, u32[]{:S(2)}, u32[]{:S(2)}) %collective-permute-start) | collective-permute-done | bytes 2359328 | tf_op jit(solution)/shard_map/ppermute | solution.py:381
  105.3 11.3 %convolution_convert_fusion.9.k_ref.v_ref = bf16[1536,1536]{1,0:T(8,128)(2,1)} fusion(bf16[1536,2432]{1,0:T(8,128)(2,1)S(1)} %bitcast.160, f32[1536]{0:T(1024)S(1)} %get-tuple-element.170, f32[1536]{0:T(1024)S(1)} %get-tuple-element.171, f32[1536]{0:T(1024)S(1)} %add_rsqrt_fusion.1, f32[1536]{0:T(1024)S(1)} %broadcast_multiply_fusion.1, ...), kind=kOutput, calls=%fused_computation.39 | convolution fusion | flops 7271350272 | bytes 14188544 | tf_op jit(solution)/shard_map/dot_general | solution.py:22
  116.7 39.2 %self_attend.2.refs_0_ = f32[2,4,6,80,384]{4,3,2,1,0:T(8,128)} custom-call(s32[4,4]{1,0:T(4,128)} %pad_add_fusion.1.bounds, bf16[1536,768]{1,0:T(8,128)(2,1)} %convolution_convert_fusion.10.q_ref, bf16[1536,1536]{1,0:T(8,128)(2,1)} %convolution_convert_fusion.9.k_ref.v_ref, bf16[1536,1536]{1,0:T(8,128)(2,1)} %convolution_convert_fusion.9.k_ref.v_ref, ...), custom_call_target="tpu_custom_call" | custom-call | flops 150994944 | bytes 98304 | tf_op jit(solution)/shard_map/self_attend/pallas_call | solution.py:161
  160.3 11.4 %convolution_convert_fusion.8.k_ref.v_ref = bf16[1536,1536]{1,0:T(8,128)(2,1)} fusion(f32[1536]{0:T(1024)S(1)} %add_rsqrt_fusion, f32[1536]{0:T(1024)S(1)} %broadcast_multiply_fusion, f32[1536]{0:T(1024)S(1)} %get-tuple-element.170, f32[1536]{0:T(1024)S(1)} %get-tuple-element.171, bf16[1536,2432]{1,0:T(8,128)(2,1)S(1)} %bitcast.162, ...), kind=kOutput, calls=%fused_computation.38 | convolution fusion | flops 7271350272 | bytes 14188544 | tf_op jit(solution)/shard_map/dot_general | solution.py:22
  171.7 12.2 %self_attend.3 = (bf16[1536,768]{1,0:T(8,128)(2,1)}, f32[2,4,8,384]{3,2,1,0:T(8,128)}) custom-call(s32[4,4]{1,0:T(4,128)} %pad_add_fusion.bounds, bf16[1536,768]{1,0:T(8,128)(2,1)} %convolution_convert_fusion.10.q_ref, bf16[1536,1536]{1,0:T(8,128)(2,1)} %convolution_convert_fusion.8.k_ref.v_ref, bf16[1536,1536]{1,0:T(8,128)(2,1)} %convolution_convert_fusion.8.k_ref.v_ref, ...), custom_call_target="tpu_custom_call" | custom-call | flops 150994944 | bytes 98304 | tf_op jit(solution)/shard_map/self_attend/pallas_call | solution.py:161
  187.4 15.4 %collective-permute-done.3 = bf16[768,768]{1,0:T(8,128)(2,1)} collective-permute-done((bf16[768,768]{1,0:T(8,128)(2,1)}, bf16[768,768]{1,0:T(8,128)(2,1)}, u32[]{:S(2)}, u32[]{:S(2)}) %collective-permute-start.3) | collective-permute-done | bytes 1179680 | tf_op jit(solution)/shard_map/ppermute | solution.py:381
  249.6 54.7 %all-gather.9.cloned.1.call-done = bf16[1536,6144]{1,0:T(8,128)(2,1)} async-done(((bf16[96,6144]{1,0:T(8,128)(2,1)}), bf16[1536,6144]{1,0:T(8,128)(2,1)}) %all-gather.9.cloned.1.call-update) | async-done | bytes 18874384 | tf_op jit(solution)/shard_map/all_gather | solution.py:530
  304.3 27.4 %fusion.3 = (f32[768,6144]{1,0:T(8,128)}, bf16[768,6144]{1,0:T(8,128)(2,1)S(1)}) fusion(bf16[1536,6144]{1,0:T(8,128)(2,1)} %all-gather.9.cloned.1.call-done, f32[768,1536]{1,0:T(8,128)} %copy-done.9, f32[1536]{0:T(1024)S(1)} %copy-done.51, f32[1536]{0:T(1024)S(1)} %get-tuple-element.166, f32[768]{0:T(1024)S(1)} %add_rsqrt_fusion.3, ...), kind=kOutput, calls=%fused_computation.5 | convolution fusion | flops 14548598784 | bytes 51922944 | tf_op jit(solution)/shard_map/dot_general | solution.py:22
  335.3 18.0 %convolution_convert_fusion = bf16[6144,1536]{1,0:T(8,128)(2,1)} fusion(bf16[768,6144]{1,0:T(8,128)(2,1)S(1)} %get-tuple-element.185, bf16[768,1536]{1,0:T(8,128)(2,1)S(1)} %copy-done.18), kind=kOutput, calls=%fused_computation.1 | convolution fusion | flops 14504951808 | bytes 30670848 | tf_op jit(solution)/shard_map/dot_general | solution.py:26
  353.4 51.3 %all-gather.11.cloned.1.call-done = bf16[6144,1536]{1,0:T(8,128)(2,1)} async-done(((bf16[384,1536]{1,0:T(8,128)(2,1)}), bf16[6144,1536]{1,0:T(8,128)(2,1)}) %all-gather.11.cloned.1.call-update) | async-done | bytes 18874384 | tf_op jit(solution)/shard_map/all_gather | solution.py:530
  404.7 27.0 %multiply_convert_fusion = bf16[768,6144]{1,0:T(8,128)(2,1)} fusion(f32[768,6144]{1,0:T(8,128)} %get-tuple-element.64, bf16[768,1536]{1,0:T(8,128)(2,1)S(1)} %copy-done.18, bf16[6144,1536]{1,0:T(8,128)(2,1)} %all-gather.11.cloned.1.call-done), kind=kOutput, calls=%fused_computation.7 | convolution fusion | flops 14504951808 | bytes 49545216 | tf_op jit(solution)/shard_map/dot_general | solution.py:32
  431.7 15.4 %convolution_convert_fusion.2 = bf16[1536,3072]{1,0:T(8,128)(2,1)} fusion(bf16[768,6144]{1,0:T(8,128)(2,1)} %multiply_convert_fusion, s32[]{:T(128)S(6)} %select_n.272, f32[768,1536]{1,0:T(8,128)} %copy-done.9, f32[1536]{0:T(1024)S(1)} %copy-done.51, f32[1536]{0:T(1024)S(1)} %get-tuple-element.166, f32[768]{0:T(1024)S(1)} %add_rsqrt_fusion.3, ...), kind=kOutput, calls=%fused_computation.17 | convolution fusion | flops 7258374144 | bytes 18892804 | tf_op jit(solution)/shard_map/dot_general | solution.py:26
  447.1 13.0 %convolution_convert_fusion.1 = bf16[1536,3072]{1,0:T(8,128)(2,1)} fusion(bf16[768,6144]{1,0:T(8,128)(2,1)S(1)} %copy-done.60, s32[]{:T(128)S(6)} %select_n.273, f32[768,1536]{1,0:T(8,128)} %copy-done.9, f32[1536]{0:T(1024)S(1)} %copy-done.51, f32[1536]{0:T(1024)S(1)} %get-tuple-element.166, f32[768]{0:T(1024)S(1)} %add_rsqrt_fusion.3, ...), kind=kOutput, calls=%fused_computation.16 | convolution fusion | flops 7258374144 | bytes 18898948 | tf_op jit(solution)/shard_map/dot_general | solution.py:26
  460.4 24.4 %multiply_reduce_fusion = (bf16[1536]{0:T(1024)(128)(2,1)}, f32[768]{0:T(1024)S(1)}, f32[768]{0:T(1024)S(1)}, bf16[1536]{0:T(1024)(128)(2,1)}, f32[768,1536]{1,0:T(8,128)}) fusion(f32[768,1536]{1,0:T(8,128)} %copy-done.9, f32[768]{0:T(1024)S(1)} %add_rsqrt_fusion.3, f32[768]{0:T(1024)S(1)} %broadcast_multiply_fusion.9, f32[1536]{0:T(1024)S(1)} %get-tuple-element.166, ...), kind=kOutput, calls=%fused_computation.69 | convolution fusion | flops 14506125312 | bytes 37773312 | tf_op jit(solution)/shard_map/dot_general | solution.py:32
  506.8 17.6 %cross_attend_back.1 = (bf16[768,1536]{1,0:T(8,128)(2,1)}, f32[128,1536]{1,0:T(8,128)}, f32[128,1536]{1,0:T(8,128)}) custom-call(bf16[768,1536]{1,0:T(8,128)(2,1)} %fusion.78.q_ref, bf16[768,1536]{1,0:T(8,128)(2,1)} %fusion.81.g_ref, bf16[128,1536]{1,0:T(8,128)(2,1)} %get-tuple-element.204.k_ref, bf16[128,1536]{1,0:T(8,128)(2,1)} %get-tuple-element.203.v_ref, ...), custom_call_target="tpu_custom_call" | custom-call | flops 3019898880 | bytes 7077888 | tf_op jit(solution)/shard_map/cross_attend_back/pallas_call | solution.py:349
  581.1 14.9 %self_attend_back.2 = (f32[2,4,6,64,384]{4,3,2,1,0:T(8,128)}, bf16[1536,768]{1,0:T(8,128)(2,1)}, bf16[1536,768]{1,0:T(8,128)(2,1)}) custom-call(s32[4,4]{1,0:T(4,128)} %pad_add_fusion.bounds, bf16[1536,768]{1,0:T(8,128)(2,1)} %convolution_convert_fusion.10.q_ref, bf16[1536,768]{1,0:T(8,128)(2,1)} %pad_maximum_fusion.5.g_ref, ...), custom_call_target="tpu_custom_call" | custom-call | flops 150994944 | bytes 98304 | tf_op jit(solution)/shard_map/self_attend_back/pallas_call | solution.py:261
  607.7 74.1 %collective-permute-done.8 = bf16[1536,1536]{1,0:T(8,128)(2,1)} collective-permute-done((bf16[1536,1536]{1,0:T(8,128)(2,1)}, bf16[1536,1536]{1,0:T(8,128)(2,1)}, u32[]{:S(2)}, u32[]{:S(2)}) %collective-permute-start.8) | collective-permute-done | bytes 4718624 | tf_op jit(solution)/shard_map/ppermute | solution.py:381
  694.4 70.9 %self_attend_back.3 = (bf16[1536,768]{1,0:T(8,128)(2,1)}, bf16[1536,768]{1,0:T(8,128)(2,1)}, bf16[1536,768]{1,0:T(8,128)(2,1)}) custom-call(s32[4,4]{1,0:T(4,128)} %pad_add_fusion.1.bounds, bf16[1536,768]{1,0:T(8,128)(2,1)} %convolution_convert_fusion.10.q_ref, bf16[1536,768]{1,0:T(8,128)(2,1)} %pad_maximum_fusion.5.g_ref, ...), custom_call_target="tpu_custom_call" | custom-call | flops 150994944 | bytes 98304 | tf_op jit(solution)/shard_map/self_attend_back/pallas_call | solution.py:261
  781.9 14.2 %convolution_convert_fusion.3 = bf16[1536,2304]{1,0:T(8,128)(2,1)} fusion(bf16[1536,2304]{1,0:T(8,128)(2,1)S(1)} %pad_maximum_fusion.1, f32[1536]{0:T(1024)S(1)} %copy-done.48, f32[1536]{0:T(1024)S(1)} %copy-done.35, f32[1536]{0:T(1024)S(1)} %copy-done.53, f32[1536]{0:T(1024)S(1)} %copy-done.39, bf16[768,1536]{1,0:T(8,128)(2,1)S(1)} %copy-done.8, ...), kind=kOutput, calls=%fused_computation.18 | convolution fusion | flops 10896408576 | bytes 18898944 | tf_op jit(solution)/shard_map/dot_general | solution.py:26
  796.1 36.9 %collective-permute-done.12 = bf16[768,1536]{1,0:T(8,128)(2,1)S(1)} collective-permute-done((bf16[768,1536]{1,0:T(8,128)(2,1)S(1)}, bf16[768,1536]{1,0:T(8,128)(2,1)S(1)}, u32[]{:S(2)}, u32[]{:S(2)}) %collective-permute-start.12) | collective-permute-done | bytes 2359328 | tf_op jit(solution)/shard_map/ppermute | solution.py:381
  833.0 11.1 %fusion.36 = (bf16[1536]{0:T(1024)(128)(2,1)S(1)}, f32[768]{0:T(1024)}, f32[768]{0:T(1024)}, bf16[1536]{0:T(1024)(128)(2,1)S(1)}, f32[768,1536]{1,0:T(8,128)}) fusion(bf16[768,1536]{1,0:T(8,128)(2,1)S(1)} %copy-done.2, f32[768]{0:T(1024)S(1)} %add_rsqrt_fusion.2, f32[768]{0:T(1024)S(1)} %broadcast_multiply_fusion.3, f32[1536]{0:T(1024)S(1)} %copy-done.35, ...), kind=kOutput, calls=%fused_computation.63 | convolution fusion | flops 5449969152 | bytes 20082692 | tf_op jit(solution)/shard_map/dot_general | solution.py:32
  870.9 23.5 %add_convert_fusion.5 = bf16[768,1536]{1,0:T(8,128)(2,1)} fusion(f32[768,1536]{1,0:T(8,128)} %copy-done.9, bf16[768,6144]{1,0:T(8,128)(2,1)} %copy-done.62, bf16[6144,1536]{1,0:T(8,128)(2,1)} %all-gather.11.cloned.1.call-done), kind=kOutput, calls=%fused_computation.80 | convolution fusion | flops 14497873920 | bytes 35389440 | tf_op jit(solution)/shard_map/dot_general | solution.py:22
  905.8 48.3 %collective-permute-done.18 = bf16[1,192,1536]{2,1,0:T(8,128)(2,1)} collective-permute-done((bf16[1,192,1536]{2,1,0:T(8,128)(2,1)}, bf16[1,192,1536]{2,1,0:T(8,128)(2,1)}, u32[]{:S(2)}, u32[]{:S(2)}) %collective-permute-start.18) | collective-permute-done | bytes 589856 | tf_op jit(solution)/shard_map/ppermute | solution.py:381
  961.7 11.6 %collective-permute-done.20 = bf16[2,96,1536]{2,1,0:T(8,128)(2,1)S(1)} collective-permute-done((bf16[2,96,1536]{2,1,0:T(8,128)(2,1)S(1)}, bf16[2,96,1536]{2,1,0:T(8,128)(2,1)S(1)}, u32[]{:S(2)}, u32[]{:S(2)}) %collective-permute-start.20) | collective-permute-done | bytes 589856 | tf_op jit(solution)/shard_map/ppermute | solution.py:381
  (360 shorter events, 304.2 us)
Async XLA Ops:
  7.2 76.4 %all-gather.5.cloned.1.call-start = ((), (), s32[]{:S(2)}) async-start(), calls=%async_computation.3 | async-start | bytes 7938048 | tf_op jit(solution)/shard_map/all_gather | solution.py:530
  11.6 194.7 %all-gather.7.cloned.1.call-start = ((), (), s32[]{:S(2)}) async-start(), calls=%async_computation.4 | async-start | bytes 20054016 | tf_op jit(solution)/shard_map/all_gather | solution.py:530
  16.4 287.9 %all-gather.9.cloned.1.call-start = ((), (), s32[]{:S(2)}) async-start(), calls=%async_computation.5 | async-start | bytes 20054016 | tf_op jit(solution)/shard_map/all_gather | solution.py:530
  17.1 387.6 %all-gather.11.cloned.1.call-start = ((), (), s32[]{:S(2)}) async-start(), calls=%async_computation.6 | async-start | bytes 20054016 | tf_op jit(solution)/shard_map/all_gather | solution.py:530
  17.7 674.8 %reduce-scatter.4.cloned.1.call-start = ((), (), s32[]{:S(2)}) async-start(), calls=%async_computation.7 | async-start | bytes 20054016 | tf_op jit(solution)/shard_map/reduce_scatter | solution.py:446
  17.8 54.4 %collective-permute-start = (bf16[768,1536]{1,0:T(8,128)(2,1)S(1)}, bf16[768,1536]{1,0:T(8,128)(2,1)}, u32[]{:S(2)}, u32[]{:S(2)}) collective-permute-start(bf16[768,1536]{1,0:T(8,128)(2,1)S(1)} %copy-done.1), channel_id=1, source_target_pairs={{0,1},{1,0},{2,3},{3,2},{4,5},{5,4},{6,7},{7,6},{8,9},{9,8},{10,11... | collective-permute-start | bytes 7077896 | tf_op jit(solution)/shard_map/ppermute | solution.py:381
  83.6 20.2 %collective-permute-start.1 = (bf16[768,1536]{1,0:T(8,128)(2,1)S(1)}, bf16[768,1536]{1,0:T(8,128)(2,1)S(1)}, u32[]{:S(2)}, u32[]{:S(2)}) collective-permute-start(bf16[768,1536]{1,0:T(8,128)(2,1)S(1)} %copy-done.1), channel_id=1, source_target_pairs={{0,2},{2,4},{4,6},{6,8},{8,10},{10,12},{12,14},{14,16},{16,18},{18... | collective-permute-start | bytes 7077896 | tf_op jit(solution)/shard_map/ppermute | solution.py:387
  103.7 52.2 %collective-permute-start.2 = (bf16[768,1536]{1,0:T(8,128)(2,1)S(1)}, bf16[768,1536]{1,0:T(8,128)(2,1)S(1)}, u32[]{:S(2)}, u32[]{:S(2)}) collective-permute-start(bf16[768,1536]{1,0:T(8,128)(2,1)S(1)} %collective-permute-done.1), channel_id=1, source_target_pairs={{0,1},{1,0},{2,3},{3,2},{4,5},{5,4},{6,7},{7,6},{8,9},{9,8},{10,11... | collective-permute-start | bytes 7077896 | tf_op jit(solution)/shard_map/ppermute | solution.py:381
  210.2 17.6 %collective-permute-start.4 = (bf16[128,2,768]{2,0,1:T(8,128)(2,1)S(1)}, bf16[128,2,768]{2,0,1:T(8,128)(2,1)S(1)}, u32[]{:S(2)}, u32[]{:S(2)}) collective-permute-start(bf16[128,2,768]{2,0,1:T(8,128)(2,1)S(1)} %copy.92), channel_id=1, source_target_pairs={{0,1},{1,0},{2,3},{3,2},{4,5},{5,4},{6,7},{7,6},{8,9},{9,8},{10,11... | collective-permute-start | bytes 1179656 | tf_op jit(solution)/shard_map/ppermute | solution.py:381
  353.3 503.8 %reduce-scatter.6.cloned.1.call-start = ((), (), s32[]{:S(2)}) async-start(), calls=%async_computation.8 | async-start | bytes 20054016 | tf_op jit(solution)/shard_map/reduce_scatter | solution.py:639
  460.1 31.3 %collective-permute-start.5 = (bf16[1536,3072]{1,0:T(8,128)(2,1)}, bf16[1536,3072]{1,0:T(8,128)(2,1)}, u32[]{:S(2)}, u32[]{:S(2)}) collective-permute-start(bf16[1536,3072]{1,0:T(8,128)(2,1)} %convolution_convert_fusion.1), channel_id=1, source_target_pairs={{0,2},{2,0},{4,6},{6,4},{8,10},{10,8},{12,14},{14,12},{16,18},{18,... | collective-permute-start | bytes 28311560 | tf_op jit(solution)/shard_map/ppermute | solution.py:381
  548.4 28.1 %collective-permute-start.7 = (bf16[768,768]{1,0:T(8,128)(2,1)}, bf16[768,768]{1,0:T(8,128)(2,1)}, u32[]{:S(2)}, u32[]{:S(2)}) collective-permute-start(bf16[768,768]{1,0:T(8,128)(2,1)} %constant_dynamic-slice_fusion.1), channel_id=1, source_target_pairs={{0,1},{1,0},{2,3},{3,2},{4,5},{5,4},{6,7},{7,6},{8,9},{9,8},{10,11... | collective-permute-start | bytes 3538952 | tf_op jit(solution)/shard_map/ppermute | solution.py:381
  576.5 402.5 %reduce-scatter.8.cloned.1.call-start = ((), (), s32[]{:S(2)}) async-start(), calls=%async_computation.9 | async-start | bytes 7938048 | tf_op jit(solution)/shard_map/reduce_scatter | solution.py:446
  576.6 105.1 %collective-permute-start.8 = (bf16[1536,1536]{1,0:T(8,128)(2,1)}, bf16[1536,1536]{1,0:T(8,128)(2,1)}, u32[]{:S(2)}, u32[]{:S(2)}) collective-permute-start(bf16[1536,1536]{1,0:T(8,128)(2,1)} %add_convert_fusion.2), channel_id=1, source_target_pairs={{0,1},{1,0},{2,3},{3,2},{4,5},{5,4},{6,7},{7,6},{8,9},{9,8},{10,11... | collective-permute-start | bytes 14155784 | tf_op jit(solution)/shard_map/ppermute | solution.py:381
  596.0 169.3 %collective-permute-start.11 = (bf16[1536,768]{1,0:T(8,128)(2,1)}, bf16[1536,768]{1,0:T(8,128)(2,1)}, u32[]{:S(2)}, u32[]{:S(2)}) collective-permute-start(bf16[1536,768]{1,0:T(8,128)(2,1)} %get-tuple-element.90), channel_id=1, source_target_pairs={{2,0},{4,2},{6,4},{8,6},{10,8},{12,10},{14,12},{16,14},{18,16},{20... | collective-permute-start | bytes 7077896 | tf_op jit(solution)/shard_map/ppermute | solution.py:387
  600.7 167.8 %collective-permute-start.10 = (bf16[1536,768]{1,0:T(8,128)(2,1)}, bf16[1536,768]{1,0:T(8,128)(2,1)}, u32[]{:S(2)}, u32[]{:S(2)}) collective-permute-start(bf16[1536,768]{1,0:T(8,128)(2,1)} %get-tuple-element.88), channel_id=1, source_target_pairs={{2,0},{4,2},{6,4},{8,6},{10,8},{12,10},{14,12},{16,14},{18,16},{20... | collective-permute-start | bytes 7077896 | tf_op jit(solution)/shard_map/ppermute | solution.py:387
  606.0 288.5 %collective-permute-start.13 = (bf16[128,1536]{1,0:T(8,128)(2,1)S(1)}, bf16[128,1536]{1,0:T(8,128)(2,1)}, u32[]{:S(2)}, u32[]{:S(2)}) collective-permute-start(bf16[128,1536]{1,0:T(8,128)(2,1)S(1)} %fusion.92), channel_id=1, source_target_pairs={{0,1},{1,0},{2,3},{3,2},{4,5},{5,4},{6,7},{7,6},{8,9},{9,8},{10,11... | collective-permute-start | bytes 1179656 | tf_op jit(solution)/shard_map/ppermute | solution.py:381
  692.5 78.5 %collective-permute-start.9 = (bf16[384,1536]{1,0:T(8,128)(2,1)}, bf16[384,1536]{1,0:T(8,128)(2,1)S(1)}, u32[]{:S(2)}, u32[]{:S(2)}) collective-permute-start(bf16[384,1536]{1,0:T(8,128)(2,1)} %reduce-scatter.4.cloned.1.call-done), channel_id=1, source_target_pairs={{0,1},{1,0},{2,3},{3,2},{4,5},{5,4},{6,7},{7,6},{8,9},{9,8},{10,11... | collective-permute-start | bytes 3538952 | tf_op jit(solution)/shard_map/ppermute | solution.py:381
  692.8 164.3 %collective-permute-start.14 = (bf16[4,192,1536]{2,1,0:T(8,128)(2,1)}, bf16[4,192,1536]{2,1,0:T(8,128)(2,1)}, u32[]{:S(2)}, u32[]{:S(2)}) collective-permute-start(bf16[4,192,1536]{2,1,0:T(8,128)(2,1)} %dynamic-slice_bitcast_fusion), channel_id=1, source_target_pairs={{0,4},{2,6},{4,0},{6,2},{8,12},{10,14},{12,8},{14,10},{16,20},{18,... | collective-permute-start | bytes 7077896 | tf_op jit(solution)/shard_map/ppermute | solution.py:381
  779.8 53.1 %collective-permute-start.12 = (bf16[768,1536]{1,0:T(8,128)(2,1)S(1)}, bf16[768,1536]{1,0:T(8,128)(2,1)S(1)}, u32[]{:S(2)}, u32[]{:S(2)}) collective-permute-start(bf16[768,1536]{1,0:T(8,128)(2,1)S(1)} %fusion.84), channel_id=1, source_target_pairs={{0,1},{1,0},{2,3},{3,2},{4,5},{5,4},{6,7},{7,6},{8,9},{9,8},{10,11... | collective-permute-start | bytes 7077896 | tf_op jit(solution)/shard_map/ppermute | solution.py:381
  860.3 36.4 %collective-permute-start.17 = (bf16[2,192,1536]{2,1,0:T(8,128)(2,1)S(1)}, bf16[2,192,1536]{2,1,0:T(8,128)(2,1)S(1)}, u32[]{:S(2)}, u32[]{:S(2)}) collective-permute-start(bf16[2,192,1536]{2,1,0:T(8,128)(2,1)S(1)} %dynamic-slice_bitcast_fusion.1), channel_id=1, source_target_pairs={{0,8},{2,10},{4,12},{6,14},{8,0},{10,2},{12,4},{14,6},{16,24},{18,... | collective-permute-start | bytes 3538952 | tf_op jit(solution)/shard_map/ppermute | solution.py:381
  898.8 55.3 %collective-permute-start.18 = (bf16[1,192,1536]{2,1,0:T(8,128)(2,1)}, bf16[1,192,1536]{2,1,0:T(8,128)(2,1)}, u32[]{:S(2)}, u32[]{:S(2)}) collective-permute-start(bf16[1,192,1536]{2,1,0:T(8,128)(2,1)} %constant_dynamic-slice_fusion), channel_id=1, source_target_pairs={{0,16},{2,18},{4,20},{6,22},{8,24},{10,26},{12,28},{14,30},{16,0},... | collective-permute-start | bytes 1769480 | tf_op jit(solution)/shard_map/ppermute | solution.py:381
  903.6 55.5 %collective-permute-start.15 = (bf16[3,96,1536]{2,1,0:T(8,128)(2,1)}, bf16[3,96,1536]{2,1,0:T(8,128)(2,1)}, u32[]{:S(2)}, u32[]{:S(2)}) collective-permute-start(bf16[3,96,1536]{2,1,0:T(8,128)(2,1)} %slice.149), channel_id=1, source_target_pairs={{0,1},{1,0},{2,3},{3,2},{4,5},{5,4},{6,7},{7,6},{8,9},{9,8},{10,11... | collective-permute-start | bytes 2654216 | tf_op jit(solution)/shard_map/ppermute | solution.py:381
  905.0 50.6 %collective-permute-start.16 = (bf16[96,2,768]{2,1,0:T(2,128)(2,1)S(1)}, bf16[96,2,768]{2,1,0:T(2,128)(2,1)S(1)}, u32[]{:S(2)}, u32[]{:S(2)}) collective-permute-start(bf16[96,2,768]{2,1,0:T(2,128)(2,1)S(1)} %reshape_squeeze.3), channel_id=1, source_target_pairs={{0,1},{1,0},{2,3},{3,2},{4,5},{5,4},{6,7},{7,6},{8,9},{9,8},{10,11... | collective-permute-start | bytes 884744 | tf_op jit(solution)/shard_map/ppermute | solution.py:381
  (84 other events, 1503.8 us)
Sparse Core Ops, SparseCore 0:
  11.7 71.7 all-gather.4
  85.7 114.9 all-gather.6
  202.3 101.9 all-gather.8
  305.7 98.9 all-gather.10
  408.7 194.8 reduce-scatter.3
  607.6 249.5 reduce-scatter.5
  861.2 117.8 reduce-scatter.7

commit v11 on v10

--- a/solution.py
+++ b/solution.py
@@ -554,7 +554,7 @@
     kv_own = matmul(normed_one, w_kv).astype(jnp.bfloat16)
     queries = matmul(normed_one, w_q).astype(jnp.bfloat16)
     if by_steps:
-        before = passed_along(gate((tokens, first))[0], "fsdp", 1)
+        before = passed_along(tokens, "fsdp", 1)
         before_other = swap(before, "seq", 1)
     else:
         kv_before = passed_along(kv_own[group_rows - SPAN :], "fsdp", 1)
@@ -683,8 +683,8 @@
     else:
         grad_cout, grad_cq, grad_wout = (whole(part) for part in small[:3])
     grad_ckv = columns(small[3], 2)
-    last, grad_cout, grad_cq, grad_wout, grad_ckv, grad_up = gate(
-        (last, grad_cout, grad_cq, grad_wout, grad_ckv, grad_up)
+    last, grad_cout, grad_cq, grad_wout, grad_ckv, grad_up, grad_tokens = gate(
+        (last, grad_cout, grad_cq, grad_wout, grad_ckv, grad_up, grad_tokens)
     )
     norm_grads = whole(last[:, -PAIR:]).T
     return (

time: 1020 us -> 1010 us (level)
  waiting for transfers between devices: 368 us -> 382 us
  starting transfers between devices: 38.5 us -> 27.9 us
    reduce_scatter x1, waiting for transfers between devices: 4.78 us -> 23.4 us  [shards(): small = lax.psum_scatter(small, 'fsdp', scatter_dimension=1, tiled=True)]
    ppermute x20, starting transfers between devices: 32.5 us -> 21.3 us  [swap(): return lax.ppermute(value, axis, [(i, i ^ bit) for i in range(count)])]
    all_gather x4, waiting for transfers between devices: 113 us -> 102 us  [shards(): row_block = lambda value: lax.all_gather(value, 'fsdp', axis=0, tiled=True)]
  transfers between devices with their start and end apart: 30 -> 30, of which waited for: 13 -> 14; matrix products, arithmetic and copies ran while one was open for 40% -> 39% of each run, Pallas kernels for 16% -> 16%
where the time goes in v11:
time: 1010 us
  waiting for transfers between devices  382 us (38%)
  matrix products  281 us (28%)
  Pallas kernels  164 us (16%)
  other arithmetic  95.3 us (9%)
  local copies, waits for them, and re-layouts  40.6 us (4%)
  starting transfers between devices  27.9 us (3%)
  between operations  15.8 us (2%)
    ppermute x20, waiting for transfers between devices, swap(): return lax.ppermute(value, axis, [(i, i ^ bit) for i in range(count)])  249 us
    dot_general x9, matrix products, matmul(): return jnp.dot(left_side, right_side, preferred_element_type=jnp.float32)  109 us
    all_gather x4, waiting for transfers between devices, shards(): row_block = lambda value: lax.all_gather(value, 'fsdp', axis=0, tiled=True)  102 us
    dot_general x8, matrix products, contract_cols(): lax.dot_general(left_side, right_side, (((1,), (1,)), ((), ())), preferre...  96.8 us
    pallas_call x2, Pallas kernels, self_attend_back(): pl.pallas_call(functools.partial(attend_back_kernel, reach=reach, base=ba...  85.3 us
    dot_general x8, matrix products, contract_rows(): lax.dot_general(left_side, right_side, (((0,), (0,)), ((), ())), preferre...  75.2 us
    pallas_call x2, Pallas kernels, self_attend(): pl.pallas_call(functools.partial(attend_kernel, reach=reach, base=base, p...  51.1 us
    reduce_scatter x1, waiting for transfers between devices, shards(): small = lax.psum_scatter(small, 'fsdp', scatter_dimension=1, tiled=True)  23.4 us
  transfers between devices with their start and end apart: 30, of which 14 were waited for; matrix products, arithmetic and copies ran while one was open for 39% of the time, Pallas kernels for 16%

profile of v11, /device:TPU:0, one launch (start us, length us, event | category | flops | bytes accessed | tf_op | source)
XLA Modules:
  0.0 1006.9 jit_solution(14974470490227031638)
XLA Ops:
  30.3 45.8 %collective-permute-done = bf16[768,1536]{1,0:T(8,128)(2,1)} collective-permute-done((bf16[768,1536]{1,0:T(8,128)(2,1)S(1)}, bf16[768,1536]{1,0:T(8,128)(2,1)}, u32[]{:S(2)}, u32[]{:S(2)}) %collective-permute-start) | collective-permute-done | bytes 2359328 | tf_op jit(solution)/shard_map/ppermute | solution.py:381
  82.7 14.8 %all-gather.5.cloned.1.call-done = bf16[1536,2432]{1,0:T(8,128)(2,1)} async-done(((bf16[96,2432]{1,0:T(8,128)(2,1)}), bf16[1536,2432]{1,0:T(8,128)(2,1)}) %all-gather.5.cloned.1.call-update) | async-done | bytes 7471120 | tf_op jit(solution)/shard_map/all_gather | solution.py:530
  122.3 38.8 %self_attend.2.refs_0_ = f32[2,4,6,80,384]{4,3,2,1,0:T(8,128)} custom-call(s32[4,4]{1,0:T(4,128)} %pad_add_fusion.1.bounds, bf16[1536,768]{1,0:T(8,128)(2,1)} %convolution_convert_fusion.10.q_ref, bf16[1536,1536]{1,0:T(8,128)(2,1)} %convolution_convert_fusion.9.k_ref.v_ref, bf16[1536,1536]{1,0:T(8,128)(2,1)} %convolution_convert_fusion.9.k_ref.v_ref, ...), custom_call_target="tpu_custom_call" | custom-call | flops 150994944 | bytes 98304 | tf_op jit(solution)/shard_map/self_attend/pallas_call | solution.py:161
  179.5 12.3 %self_attend.3 = (bf16[1536,768]{1,0:T(8,128)(2,1)}, f32[2,4,8,384]{3,2,1,0:T(8,128)}) custom-call(s32[4,4]{1,0:T(4,128)} %pad_add_fusion.bounds, bf16[1536,768]{1,0:T(8,128)(2,1)} %convolution_convert_fusion.10.q_ref, bf16[1536,1536]{1,0:T(8,128)(2,1)} %convolution_convert_fusion.8.k_ref.v_ref, bf16[1536,1536]{1,0:T(8,128)(2,1)} %convolution_convert_fusion.8.k_ref.v_ref, ...), custom_call_target="tpu_custom_call" | custom-call | flops 150994944 | bytes 98304 | tf_op jit(solution)/shard_map/self_attend/pallas_call | solution.py:161
  196.3 17.6 %collective-permute-done.3 = bf16[768,768]{1,0:T(8,128)(2,1)} collective-permute-done((bf16[768,768]{1,0:T(8,128)(2,1)}, bf16[768,768]{1,0:T(8,128)(2,1)}, u32[]{:S(2)}, u32[]{:S(2)}) %collective-permute-start.3) | collective-permute-done | bytes 1179680 | tf_op jit(solution)/shard_map/ppermute | solution.py:381
  261.2 36.1 %all-gather.9.cloned.1.call-done = bf16[1536,6144]{1,0:T(8,128)(2,1)} async-done(((bf16[96,6144]{1,0:T(8,128)(2,1)}), bf16[1536,6144]{1,0:T(8,128)(2,1)}) %all-gather.9.cloned.1.call-update) | async-done | bytes 18874384 | tf_op jit(solution)/shard_map/all_gather | solution.py:530
  297.3 27.6 %fusion.3 = (f32[768,6144]{1,0:T(8,128)}, bf16[768,6144]{1,0:T(8,128)(2,1)S(1)}) fusion(bf16[1536,6144]{1,0:T(8,128)(2,1)} %all-gather.9.cloned.1.call-done, f32[768,1536]{1,0:T(8,128)} %copy-done.9, f32[1536]{0:T(1024)S(1)} %copy-done.51, f32[1536]{0:T(1024)S(1)} %get-tuple-element.166, f32[768]{0:T(1024)S(1)} %add_rsqrt_fusion.3, ...), kind=kOutput, calls=%fused_computation.5 | convolution fusion | flops 14548598784 | bytes 51922944 | tf_op jit(solution)/shard_map/dot_general | solution.py:22
  328.5 18.0 %convolution_convert_fusion = bf16[6144,1536]{1,0:T(8,128)(2,1)} fusion(bf16[768,6144]{1,0:T(8,128)(2,1)S(1)} %get-tuple-element.185, bf16[768,1536]{1,0:T(8,128)(2,1)S(1)} %copy-done.18), kind=kOutput, calls=%fused_computation.1 | convolution fusion | flops 14504951808 | bytes 30670848 | tf_op jit(solution)/shard_map/dot_general | solution.py:26
  346.5 51.2 %all-gather.11.cloned.1.call-done = bf16[6144,1536]{1,0:T(8,128)(2,1)} async-done(((bf16[384,1536]{1,0:T(8,128)(2,1)}), bf16[6144,1536]{1,0:T(8,128)(2,1)}) %all-gather.11.cloned.1.call-update) | async-done | bytes 18874384 | tf_op jit(solution)/shard_map/all_gather | solution.py:530
  397.8 27.6 %multiply_convert_fusion = bf16[768,6144]{1,0:T(8,128)(2,1)} fusion(f32[768,6144]{1,0:T(8,128)} %get-tuple-element.63, bf16[768,1536]{1,0:T(8,128)(2,1)S(1)} %copy-done.18, bf16[6144,1536]{1,0:T(8,128)(2,1)} %all-gather.11.cloned.1.call-done), kind=kOutput, calls=%fused_computation.7 | convolution fusion | flops 14504951808 | bytes 49545216 | tf_op jit(solution)/shard_map/dot_general | solution.py:32
  425.4 15.4 %convolution_convert_fusion.2 = bf16[1536,3072]{1,0:T(8,128)(2,1)} fusion(bf16[768,6144]{1,0:T(8,128)(2,1)} %multiply_convert_fusion, s32[]{:T(128)S(6)} %select_n.272, f32[768,1536]{1,0:T(8,128)} %copy-done.9, f32[1536]{0:T(1024)S(1)} %copy-done.51, f32[1536]{0:T(1024)S(1)} %get-tuple-element.166, f32[768]{0:T(1024)S(1)} %add_rsqrt_fusion.3, ...), kind=kOutput, calls=%fused_computation.17 | convolution fusion | flops 7258374144 | bytes 18892804 | tf_op jit(solution)/shard_map/dot_general | solution.py:26
  440.8 12.9 %convolution_convert_fusion.1 = bf16[1536,3072]{1,0:T(8,128)(2,1)} fusion(bf16[768,6144]{1,0:T(8,128)(2,1)S(1)} %copy-done.60, s32[]{:T(128)S(6)} %select_n.273, f32[768,1536]{1,0:T(8,128)} %copy-done.9, f32[1536]{0:T(1024)S(1)} %copy-done.51, f32[1536]{0:T(1024)S(1)} %get-tuple-element.166, f32[768]{0:T(1024)S(1)} %add_rsqrt_fusion.3, ...), kind=kOutput, calls=%fused_computation.16 | convolution fusion | flops 7258374144 | bytes 18898948 | tf_op jit(solution)/shard_map/dot_general | solution.py:26
  454.1 24.4 %multiply_reduce_fusion = (bf16[1536]{0:T(1024)(128)(2,1)}, f32[768]{0:T(1024)S(1)}, f32[768]{0:T(1024)S(1)}, bf16[1536]{0:T(1024)(128)(2,1)}, f32[768,1536]{1,0:T(8,128)}) fusion(f32[768,1536]{1,0:T(8,128)} %copy-done.9, f32[768]{0:T(1024)S(1)} %add_rsqrt_fusion.3, f32[768]{0:T(1024)S(1)} %broadcast_multiply_fusion.9, f32[1536]{0:T(1024)S(1)} %get-tuple-element.166, ...), kind=kOutput, calls=%fused_computation.69 | convolution fusion | flops 14506125312 | bytes 37773312 | tf_op jit(solution)/shard_map/dot_general | solution.py:32
  500.4 17.6 %cross_attend_back.1 = (bf16[768,1536]{1,0:T(8,128)(2,1)}, f32[128,1536]{1,0:T(8,128)}, f32[128,1536]{1,0:T(8,128)}) custom-call(bf16[768,1536]{1,0:T(8,128)(2,1)} %fusion.78.q_ref, bf16[768,1536]{1,0:T(8,128)(2,1)} %fusion.81.g_ref, bf16[128,1536]{1,0:T(8,128)(2,1)} %get-tuple-element.204.k_ref, bf16[128,1536]{1,0:T(8,128)(2,1)} %get-tuple-element.203.v_ref, ...), custom_call_target="tpu_custom_call" | custom-call | flops 3019898880 | bytes 7077888 | tf_op jit(solution)/shard_map/cross_attend_back/pallas_call | solution.py:349
  574.8 14.6 %self_attend_back.2 = (f32[2,4,6,64,384]{4,3,2,1,0:T(8,128)}, bf16[1536,768]{1,0:T(8,128)(2,1)}, bf16[1536,768]{1,0:T(8,128)(2,1)}) custom-call(s32[4,4]{1,0:T(4,128)} %pad_add_fusion.bounds, bf16[1536,768]{1,0:T(8,128)(2,1)} %convolution_convert_fusion.10.q_ref, bf16[1536,768]{1,0:T(8,128)(2,1)} %pad_maximum_fusion.5.g_ref, ...), custom_call_target="tpu_custom_call" | custom-call | flops 150994944 | bytes 98304 | tf_op jit(solution)/shard_map/self_attend_back/pallas_call | solution.py:261
  600.8 74.3 %collective-permute-done.8 = bf16[1536,1536]{1,0:T(8,128)(2,1)} collective-permute-done((bf16[1536,1536]{1,0:T(8,128)(2,1)}, bf16[1536,1536]{1,0:T(8,128)(2,1)}, u32[]{:S(2)}, u32[]{:S(2)}) %collective-permute-start.8) | collective-permute-done | bytes 4718624 | tf_op jit(solution)/shard_map/ppermute | solution.py:381
  687.9 70.8 %self_attend_back.3 = (bf16[1536,768]{1,0:T(8,128)(2,1)}, bf16[1536,768]{1,0:T(8,128)(2,1)}, bf16[1536,768]{1,0:T(8,128)(2,1)}) custom-call(s32[4,4]{1,0:T(4,128)} %pad_add_fusion.1.bounds, bf16[1536,768]{1,0:T(8,128)(2,1)} %convolution_convert_fusion.10.q_ref, bf16[1536,768]{1,0:T(8,128)(2,1)} %pad_maximum_fusion.5.g_ref, ...), custom_call_target="tpu_custom_call" | custom-call | flops 150994944 | bytes 98304 | tf_op jit(solution)/shard_map/self_attend_back/pallas_call | solution.py:261
  774.8 14.2 %convolution_convert_fusion.3 = bf16[1536,2304]{1,0:T(8,128)(2,1)} fusion(bf16[1536,2304]{1,0:T(8,128)(2,1)S(1)} %pad_maximum_fusion.1, f32[1536]{0:T(1024)S(1)} %copy-done.48, f32[1536]{0:T(1024)S(1)} %copy-done.35, f32[1536]{0:T(1024)S(1)} %copy-done.53, f32[1536]{0:T(1024)S(1)} %copy-done.39, bf16[768,1536]{1,0:T(8,128)(2,1)S(1)} %copy-done.8, ...), kind=kOutput, calls=%fused_computation.18 | convolution fusion | flops 10896408576 | bytes 18898944 | tf_op jit(solution)/shard_map/dot_general | solution.py:26
  789.0 33.3 %collective-permute-done.13 = bf16[768,1536]{1,0:T(8,128)(2,1)S(1)} collective-permute-done((bf16[768,1536]{1,0:T(8,128)(2,1)S(1)}, bf16[768,1536]{1,0:T(8,128)(2,1)S(1)}, u32[]{:S(2)}, u32[]{:S(2)}) %collective-permute-start.13) | collective-permute-done | bytes 2359328 | tf_op jit(solution)/shard_map/ppermute | solution.py:381
  822.4 11.8 %fusion.32 = (f32[768]{0:T(1024)}, bf16[1536]{0:T(1024)(128)(2,1)S(1)}, f32[768]{0:T(1024)}, bf16[1536]{0:T(1024)(128)(2,1)S(1)}, f32[768,1536]{1,0:T(8,128)}) fusion(bf16[768,1536]{1,0:T(8,128)(2,1)S(1)} %copy-done.2, f32[1536]{0:T(1024)S(1)} %copy-done.35, f32[768]{0:T(1024)S(1)} %add_rsqrt_fusion.2, f32[768]{0:T(1024)S(1)} %broadcast_multiply_fusion.4, ...), kind=kOutput, calls=%fused_computation.59 | convolution fusion | flops 5449969152 | bytes 20082692 | tf_op jit(solution)/shard_map/dot_general | solution.py:32
  842.5 23.4 %reduce-scatter.6.cloned.1.call-done = bf16[4,96,1536]{2,1,0:T(8,128)(2,1)} async-done(((bf16[4,1536,1536]{2,1,0:T(8,128)(2,1)}), bf16[4,96,1536]{2,1,0:T(8,128)(2,1)}) %reduce-scatter.6.cloned.1.call-update) | async-done | bytes 1179664 | tf_op jit(solution)/shard_map/reduce_scatter | solution.py:639
  869.4 22.8 %add_convert_fusion.5 = bf16[768,1536]{1,0:T(8,128)(2,1)} fusion(f32[768,1536]{1,0:T(8,128)} %copy-done.9, bf16[768,6144]{1,0:T(8,128)(2,1)} %copy-done.62, bf16[6144,1536]{1,0:T(8,128)(2,1)} %all-gather.11.cloned.1.call-done), kind=kOutput, calls=%fused_computation.80 | convolution fusion | flops 14497873920 | bytes 35389440 | tf_op jit(solution)/shard_map/dot_general | solution.py:22
  905.2 48.9 %collective-permute-done.17 = bf16[1,192,1536]{2,1,0:T(8,128)(2,1)} collective-permute-done((bf16[1,192,1536]{2,1,0:T(8,128)(2,1)}, bf16[1,192,1536]{2,1,0:T(8,128)(2,1)}, u32[]{:S(2)}, u32[]{:S(2)}) %collective-permute-start.17) | collective-permute-done | bytes 589856 | tf_op jit(solution)/shard_map/ppermute | solution.py:381
  960.5 12.8 %collective-permute-done.19 = bf16[2,96,1536]{2,1,0:T(8,128)(2,1)S(1)} collective-permute-done((bf16[2,96,1536]{2,1,0:T(8,128)(2,1)S(1)}, bf16[2,96,1536]{2,1,0:T(8,128)(2,1)S(1)}, u32[]{:S(2)}, u32[]{:S(2)}) %collective-permute-start.19) | collective-permute-done | bytes 589856 | tf_op jit(solution)/shard_map/ppermute | solution.py:381
  (370 shorter events, 304.0 us)
Async XLA Ops:
  7.2 90.3 %all-gather.5.cloned.1.call-start = ((), (), s32[]{:S(2)}) async-start(), calls=%async_computation.3 | async-start | bytes 7938048 | tf_op jit(solution)/shard_map/all_gather | solution.py:530
  11.6 205.9 %all-gather.7.cloned.1.call-start = ((), (), s32[]{:S(2)}) async-start(), calls=%async_computation.4 | async-start | bytes 20054016 | tf_op jit(solution)/shard_map/all_gather | solution.py:530
  16.4 281.0 %all-gather.9.cloned.1.call-start = ((), (), s32[]{:S(2)}) async-start(), calls=%async_computation.5 | async-start | bytes 20054016 | tf_op jit(solution)/shard_map/all_gather | solution.py:530
  17.1 380.6 %all-gather.11.cloned.1.call-start = ((), (), s32[]{:S(2)}) async-start(), calls=%async_computation.6 | async-start | bytes 20054016 | tf_op jit(solution)/shard_map/all_gather | solution.py:530
  17.7 668.1 %reduce-scatter.4.cloned.1.call-start = ((), (), s32[]{:S(2)}) async-start(), calls=%async_computation.7 | async-start | bytes 20054016 | tf_op jit(solution)/shard_map/reduce_scatter | solution.py:446
  21.5 54.6 %collective-permute-start = (bf16[768,1536]{1,0:T(8,128)(2,1)S(1)}, bf16[768,1536]{1,0:T(8,128)(2,1)}, u32[]{:S(2)}, u32[]{:S(2)}) collective-permute-start(bf16[768,1536]{1,0:T(8,128)(2,1)S(1)} %copy-done.1), channel_id=1, source_target_pairs={{0,1},{1,0},{2,3},{3,2},{4,5},{5,4},{6,7},{7,6},{8,9},{9,8},{10,11... | collective-permute-start | bytes 7077896 | tf_op jit(solution)/shard_map/ppermute | solution.py:381
  30.3 130.9 %collective-permute-start.2 = (bf16[768,1536]{1,0:T(8,128)(2,1)}, bf16[768,1536]{1,0:T(8,128)(2,1)}, u32[]{:S(2)}, u32[]{:S(2)}) collective-permute-start(bf16[768,1536]{1,0:T(8,128)(2,1)} %collective-permute-done.1), channel_id=1, source_target_pairs={{0,1},{1,0},{2,3},{3,2},{4,5},{5,4},{6,7},{7,6},{8,9},{9,8},{10,11... | collective-permute-start | bytes 7077896 | tf_op jit(solution)/shard_map/ppermute | solution.py:381
  194.1 19.7 %collective-permute-start.3 = (bf16[768,768]{1,0:T(8,128)(2,1)}, bf16[768,768]{1,0:T(8,128)(2,1)}, u32[]{:S(2)}, u32[]{:S(2)}) collective-permute-start(bf16[768,768]{1,0:T(8,128)(2,1)} %constant_dynamic-slice_fusion.3), channel_id=1, source_target_pairs={{0,1},{1,0},{2,3},{3,2},{4,5},{5,4},{6,7},{7,6},{8,9},{9,8},{10,11... | collective-permute-start | bytes 3538952 | tf_op jit(solution)/shard_map/ppermute | solution.py:381
  221.6 18.0 %collective-permute-start.4 = (bf16[128,2,768]{2,0,1:T(8,128)(2,1)S(1)}, bf16[128,2,768]{2,0,1:T(8,128)(2,1)S(1)}, u32[]{:S(2)}, u32[]{:S(2)}) collective-permute-start(bf16[128,2,768]{2,0,1:T(8,128)(2,1)S(1)} %copy.92), channel_id=1, source_target_pairs={{0,1},{1,0},{2,3},{3,2},{4,5},{5,4},{6,7},{7,6},{8,9},{9,8},{10,11... | collective-permute-start | bytes 1179656 | tf_op jit(solution)/shard_map/ppermute | solution.py:381
  346.5 519.5 %reduce-scatter.6.cloned.1.call-start = ((), (), s32[]{:S(2)}) async-start(), calls=%async_computation.8 | async-start | bytes 20054016 | tf_op jit(solution)/shard_map/reduce_scatter | solution.py:639
  453.8 31.3 %collective-permute-start.5 = (bf16[1536,3072]{1,0:T(8,128)(2,1)}, bf16[1536,3072]{1,0:T(8,128)(2,1)}, u32[]{:S(2)}, u32[]{:S(2)}) collective-permute-start(bf16[1536,3072]{1,0:T(8,128)(2,1)} %convolution_convert_fusion.1), channel_id=1, source_target_pairs={{0,2},{2,0},{4,6},{6,4},{8,10},{10,8},{12,14},{14,12},{16,18},{18,... | collective-permute-start | bytes 28311560 | tf_op jit(solution)/shard_map/ppermute | solution.py:381
  541.7 28.2 %collective-permute-start.7 = (bf16[768,768]{1,0:T(8,128)(2,1)}, bf16[768,768]{1,0:T(8,128)(2,1)}, u32[]{:S(2)}, u32[]{:S(2)}) collective-permute-start(bf16[768,768]{1,0:T(8,128)(2,1)} %constant_dynamic-slice_fusion.1), channel_id=1, source_target_pairs={{0,1},{1,0},{2,3},{3,2},{4,5},{5,4},{6,7},{7,6},{8,9},{9,8},{10,11... | collective-permute-start | bytes 3538952 | tf_op jit(solution)/shard_map/ppermute | solution.py:381
  569.9 411.3 %reduce-scatter.8.cloned.1.call-start = ((), (), s32[]{:S(2)}) async-start(), calls=%async_computation.9 | async-start | bytes 7938048 | tf_op jit(solution)/shard_map/reduce_scatter | solution.py:446
  569.9 105.1 %collective-permute-start.8 = (bf16[1536,1536]{1,0:T(8,128)(2,1)}, bf16[1536,1536]{1,0:T(8,128)(2,1)}, u32[]{:S(2)}, u32[]{:S(2)}) collective-permute-start(bf16[1536,1536]{1,0:T(8,128)(2,1)} %add_convert_fusion.1), channel_id=1, source_target_pairs={{0,1},{1,0},{2,3},{3,2},{4,5},{5,4},{6,7},{7,6},{8,9},{9,8},{10,11... | collective-permute-start | bytes 14155784 | tf_op jit(solution)/shard_map/ppermute | solution.py:381
  589.4 169.3 %collective-permute-start.12 = (bf16[1536,768]{1,0:T(8,128)(2,1)}, bf16[1536,768]{1,0:T(8,128)(2,1)}, u32[]{:S(2)}, u32[]{:S(2)}) collective-permute-start(bf16[1536,768]{1,0:T(8,128)(2,1)} %get-tuple-element.90), channel_id=1, source_target_pairs={{2,0},{4,2},{6,4},{8,6},{10,8},{12,10},{14,12},{16,14},{18,16},{20... | collective-permute-start | bytes 7077896 | tf_op jit(solution)/shard_map/ppermute | solution.py:387
  594.0 167.8 %collective-permute-start.11 = (bf16[1536,768]{1,0:T(8,128)(2,1)}, bf16[1536,768]{1,0:T(8,128)(2,1)}, u32[]{:S(2)}, u32[]{:S(2)}) collective-permute-start(bf16[1536,768]{1,0:T(8,128)(2,1)} %get-tuple-element.88), channel_id=1, source_target_pairs={{2,0},{4,2},{6,4},{8,6},{10,8},{12,10},{14,12},{16,14},{18,16},{20... | collective-permute-start | bytes 7077896 | tf_op jit(solution)/shard_map/ppermute | solution.py:387
  599.4 292.8 %collective-permute-start.20 = (bf16[128,1536]{1,0:T(8,128)(2,1)S(1)}, bf16[128,1536]{1,0:T(8,128)(2,1)}, u32[]{:S(2)}, u32[]{:S(2)}) collective-permute-start(bf16[128,1536]{1,0:T(8,128)(2,1)S(1)} %fusion.92), channel_id=1, source_target_pairs={{0,1},{1,0},{2,3},{3,2},{4,5},{5,4},{6,7},{7,6},{8,9},{9,8},{10,11... | collective-permute-start | bytes 1179656 | tf_op jit(solution)/shard_map/ppermute | solution.py:381
  685.8 180.1 %collective-permute-start.9 = (bf16[4,192,1536]{2,1,0:T(8,128)(2,1)}, bf16[4,192,1536]{2,1,0:T(8,128)(2,1)}, u32[]{:S(2)}, u32[]{:S(2)}) collective-permute-start(bf16[4,192,1536]{2,1,0:T(8,128)(2,1)} %dynamic-slice_bitcast_fusion), channel_id=1, source_target_pairs={{0,4},{2,6},{4,0},{6,2},{8,12},{10,14},{12,8},{14,10},{16,20},{18,... | collective-permute-start | bytes 7077896 | tf_op jit(solution)/shard_map/ppermute | solution.py:381
  687.4 76.9 %collective-permute-start.10 = (bf16[384,1536]{1,0:T(8,128)(2,1)}, bf16[384,1536]{1,0:T(8,128)(2,1)S(1)}, u32[]{:S(2)}, u32[]{:S(2)}) collective-permute-start(bf16[384,1536]{1,0:T(8,128)(2,1)} %reduce-scatter.4.cloned.1.call-done), channel_id=1, source_target_pairs={{0,1},{1,0},{2,3},{3,2},{4,5},{5,4},{6,7},{7,6},{8,9},{9,8},{10,11... | collective-permute-start | bytes 3538952 | tf_op jit(solution)/shard_map/ppermute | solution.py:381
  773.2 49.2 %collective-permute-start.13 = (bf16[768,1536]{1,0:T(8,128)(2,1)S(1)}, bf16[768,1536]{1,0:T(8,128)(2,1)S(1)}, u32[]{:S(2)}, u32[]{:S(2)}) collective-permute-start(bf16[768,1536]{1,0:T(8,128)(2,1)S(1)} %fusion.84), channel_id=1, source_target_pairs={{0,1},{1,0},{2,3},{3,2},{4,5},{5,4},{6,7},{7,6},{8,9},{9,8},{10,11... | collective-permute-start | bytes 7077896 | tf_op jit(solution)/shard_map/ppermute | solution.py:381
  869.1 27.8 %collective-permute-start.16 = (bf16[2,192,1536]{2,1,0:T(8,128)(2,1)S(1)}, bf16[2,192,1536]{2,1,0:T(8,128)(2,1)S(1)}, u32[]{:S(2)}, u32[]{:S(2)}) collective-permute-start(bf16[2,192,1536]{2,1,0:T(8,128)(2,1)S(1)} %dynamic-slice_bitcast_fusion.1), channel_id=1, source_target_pairs={{0,8},{2,10},{4,12},{6,14},{8,0},{10,2},{12,4},{14,6},{16,24},{18,... | collective-permute-start | bytes 3538952 | tf_op jit(solution)/shard_map/ppermute | solution.py:381
  898.2 55.8 %collective-permute-start.17 = (bf16[1,192,1536]{2,1,0:T(8,128)(2,1)}, bf16[1,192,1536]{2,1,0:T(8,128)(2,1)}, u32[]{:S(2)}, u32[]{:S(2)}) collective-permute-start(bf16[1,192,1536]{2,1,0:T(8,128)(2,1)} %constant_dynamic-slice_fusion), channel_id=1, source_target_pairs={{0,16},{2,18},{4,20},{6,22},{8,24},{10,26},{12,28},{14,30},{16,0},... | collective-permute-start | bytes 1769480 | tf_op jit(solution)/shard_map/ppermute | solution.py:381
  902.9 56.0 %collective-permute-start.14 = (bf16[3,96,1536]{2,1,0:T(8,128)(2,1)S(1)}, bf16[3,96,1536]{2,1,0:T(8,128)(2,1)S(1)}, u32[]{:S(2)}, u32[]{:S(2)}) collective-permute-start(bf16[3,96,1536]{2,1,0:T(8,128)(2,1)S(1)} %slice.149), channel_id=1, source_target_pairs={{0,1},{1,0},{2,3},{3,2},{4,5},{5,4},{6,7},{7,6},{8,9},{9,8},{10,11... | collective-permute-start | bytes 2654216 | tf_op jit(solution)/shard_map/ppermute | solution.py:381
  904.5 51.0 %collective-permute-start.15 = (bf16[96,2,768]{2,1,0:T(2,128)(2,1)S(1)}, bf16[96,2,768]{2,1,0:T(2,128)(2,1)S(1)}, u32[]{:S(2)}, u32[]{:S(2)}) collective-permute-start(bf16[96,2,768]{2,1,0:T(2,128)(2,1)S(1)} %reshape_squeeze.3), channel_id=1, source_target_pairs={{0,1},{1,0},{2,3},{3,2},{4,5},{5,4},{6,7},{7,6},{8,9},{9,8},{10,11... | collective-permute-start | bytes 884744 | tf_op jit(solution)/shard_map/ppermute | solution.py:381
  (88 other events, 1681.6 us)
Sparse Core Ops, SparseCore 0:
  11.7 85.7 all-gather.4
  99.6 97.0 all-gather.6
  198.4 98.9 all-gather.8
  298.8 98.9 all-gather.10
  401.7 194.8 reduce-scatter.3
  600.6 265.2 reduce-scatter.5
  869.9 111.1 reduce-scatter.7

commit v12 on v11

--- a/solution.py
+++ b/solution.py
@@ -530,8 +530,8 @@
     row_block = lambda value: lax.all_gather(value, "fsdp", axis=0, tiled=True)
 
     norms = jnp.pad(jnp.concatenate([norm_gain, norm_bias]).T, ((0, 0), (0, PAIR - 6)))
-    qkv_mine = own_block(qkv_weight.reshape(shard_rows, 3, width), 2).reshape(shard_rows, 3 * head_cols)
-    first = row_block(jnp.concatenate([qkv_mine, norms], axis=1))
+    qkv_mine = [own_block(qkv_weight[:, i * width : (i + 1) * width], 1) for i in range(3)]
+    first = row_block(jnp.concatenate([*qkv_mine, norms], axis=1))
     w_q, w_kv, w_qkv = first[:, :head_cols], first[:, head_cols : 3 * head_cols], first[:, : 3 * head_cols]
     norm_rows = first[:, 3 * head_cols : 3 * head_cols + 6].astype(jnp.float32).T
     gains, biases = norm_rows[:3], norm_rows[3:]

time: 1010 us -> 1010 us (level)
  waiting for transfers between devices: 382 us -> 400 us
  Pallas kernels: 164 us -> 148 us
    pallas_call x2, Pallas kernels: 85.3 us -> 74.5 us  [self_attend_back(): pl.pallas_call(functools.partial(attend_back_kernel, reach=reach, base=ba...]
    reduce_scatter x1, waiting for transfers between devices: 23.4 us -> 33.9 us  [shards(): small = lax.psum_scatter(small, 'fsdp', scatter_dimension=1, tiled=True)]
  transfers between devices with their start and end apart: 30 -> 30, of which waited for: 14 -> 14; matrix products, arithmetic and copies ran while one was open for 39% -> 39% of each run, Pallas kernels for 16% -> 15%
where the time goes in v12:
time: 1010 us
  waiting for transfers between devices  400 us (40%)
  matrix products  280 us (28%)
  Pallas kernels  148 us (15%)
  other arithmetic  95.4 us (9%)
  local copies, waits for them, and re-layouts  39.4 us (4%)
  starting transfers between devices  27.8 us (3%)
  between operations  15.8 us (2%)
    ppermute x20, waiting for transfers between devices, swap(): return lax.ppermute(value, axis, [(i, i ^ bit) for i in range(count)])  247 us
    all_gather x4, waiting for transfers between devices, shards(): row_block = lambda value: lax.all_gather(value, 'fsdp', axis=0, tiled=True)  111 us
    dot_general x9, matrix products, matmul(): return jnp.dot(left_side, right_side, preferred_element_type=jnp.float32)  109 us
    dot_general x8, matrix products, contract_cols(): lax.dot_general(left_side, right_side, (((1,), (1,)), ((), ())), preferre...  95.8 us
    dot_general x8, matrix products, contract_rows(): lax.dot_general(left_side, right_side, (((0,), (0,)), ((), ())), preferre...  75.2 us
    pallas_call x2, Pallas kernels, self_attend_back(): pl.pallas_call(functools.partial(attend_back_kernel, reach=reach, base=ba...  74.5 us
    pallas_call x2, Pallas kernels, self_attend(): pl.pallas_call(functools.partial(attend_kernel, reach=reach, base=base, p...  45.7 us
    reduce_scatter x1, waiting for transfers between devices, shards(): small = lax.psum_scatter(small, 'fsdp', scatter_dimension=1, tiled=True)  33.9 us
  transfers between devices with their start and end apart: 30, of which 14 were waited for; matrix products, arithmetic and copies ran while one was open for 39% of the time, Pallas kernels for 15%

profile of v12, /device:TPU:0, one launch (start us, length us, event | category | flops | bytes accessed | tf_op | source)
XLA Modules:
  0.0 1005.9 jit_solution(8844694622857063315)
XLA Ops:
  28.9 45.8 %collective-permute-done = bf16[768,1536]{1,0:T(8,128)(2,1)} collective-permute-done((bf16[768,1536]{1,0:T(8,128)(2,1)S(1)}, bf16[768,1536]{1,0:T(8,128)(2,1)}, u32[]{:S(2)}, u32[]{:S(2)}) %collective-permute-start) | collective-permute-done | bytes 2359328 | tf_op jit(solution)/shard_map/ppermute | solution.py:381
  81.3 15.3 %all-gather.5.cloned.1.call-done = bf16[1536,2432]{1,0:T(8,128)(2,1)} async-done(((bf16[96,2432]{1,0:T(8,128)(2,1)}), bf16[1536,2432]{1,0:T(8,128)(2,1)}) %all-gather.5.cloned.1.call-update) | async-done | bytes 7471120 | tf_op jit(solution)/shard_map/all_gather | solution.py:530
  121.4 33.6 %self_attend.2.refs_0_ = f32[2,4,6,80,384]{4,3,2,1,0:T(8,128)} custom-call(s32[4,4]{1,0:T(4,128)} %pad_add_fusion.1.bounds, bf16[1536,768]{1,0:T(8,128)(2,1)} %convolution_convert_fusion.10.q_ref, bf16[1536,1536]{1,0:T(8,128)(2,1)} %convolution_convert_fusion.9.k_ref.v_ref, bf16[1536,1536]{1,0:T(8,128)(2,1)} %convolution_convert_fusion.9.k_ref.v_ref, ...), custom_call_target="tpu_custom_call" | custom-call | flops 150994944 | bytes 98304 | tf_op jit(solution)/shard_map/self_attend/pallas_call | solution.py:161
  162.1 11.4 %convolution_convert_fusion.8.k_ref.v_ref = bf16[1536,1536]{1,0:T(8,128)(2,1)} fusion(f32[1536]{0:T(1024)S(1)} %add_rsqrt_fusion, f32[1536]{0:T(1024)S(1)} %broadcast_multiply_fusion, f32[1536]{0:T(1024)S(1)} %get-tuple-element.170, f32[1536]{0:T(1024)S(1)} %get-tuple-element.171, bf16[1536,2432]{1,0:T(8,128)(2,1)S(1)} %bitcast.162, ...), kind=kOutput, calls=%fused_computation.38 | convolution fusion | flops 7271350272 | bytes 14188544 | tf_op jit(solution)/shard_map/dot_general | solution.py:22
  173.5 12.2 %self_attend.3 = (bf16[1536,768]{1,0:T(8,128)(2,1)}, f32[2,4,8,384]{3,2,1,0:T(8,128)}) custom-call(s32[4,4]{1,0:T(4,128)} %pad_add_fusion.bounds, bf16[1536,768]{1,0:T(8,128)(2,1)} %convolution_convert_fusion.10.q_ref, bf16[1536,1536]{1,0:T(8,128)(2,1)} %convolution_convert_fusion.8.k_ref.v_ref, bf16[1536,1536]{1,0:T(8,128)(2,1)} %convolution_convert_fusion.8.k_ref.v_ref, ...), custom_call_target="tpu_custom_call" | custom-call | flops 150994944 | bytes 98304 | tf_op jit(solution)/shard_map/self_attend/pallas_call | solution.py:161
  190.2 14.4 %collective-permute-done.3 = bf16[768,768]{1,0:T(8,128)(2,1)} collective-permute-done((bf16[768,768]{1,0:T(8,128)(2,1)}, bf16[768,768]{1,0:T(8,128)(2,1)}, u32[]{:S(2)}, u32[]{:S(2)}) %collective-permute-start.3) | collective-permute-done | bytes 1179680 | tf_op jit(solution)/shard_map/ppermute | solution.py:381
  251.4 44.6 %all-gather.9.cloned.1.call-done = bf16[1536,6144]{1,0:T(8,128)(2,1)} async-done(((bf16[96,6144]{1,0:T(8,128)(2,1)}), bf16[1536,6144]{1,0:T(8,128)(2,1)}) %all-gather.9.cloned.1.call-update) | async-done | bytes 18874384 | tf_op jit(solution)/shard_map/all_gather | solution.py:530
  296.0 27.4 %fusion.3 = (f32[768,6144]{1,0:T(8,128)}, bf16[768,6144]{1,0:T(8,128)(2,1)S(1)}) fusion(bf16[1536,6144]{1,0:T(8,128)(2,1)} %all-gather.9.cloned.1.call-done, f32[768,1536]{1,0:T(8,128)} %copy-done.9, f32[1536]{0:T(1024)S(1)} %copy-done.51, f32[1536]{0:T(1024)S(1)} %get-tuple-element.166, f32[768]{0:T(1024)S(1)} %add_rsqrt_fusion.3, ...), kind=kOutput, calls=%fused_computation.5 | convolution fusion | flops 14548598784 | bytes 51922944 | tf_op jit(solution)/shard_map/dot_general | solution.py:22
  327.0 18.0 %convolution_convert_fusion = bf16[6144,1536]{1,0:T(8,128)(2,1)} fusion(bf16[768,6144]{1,0:T(8,128)(2,1)S(1)} %get-tuple-element.185, bf16[768,1536]{1,0:T(8,128)(2,1)S(1)} %copy-done.18), kind=kOutput, calls=%fused_computation.1 | convolution fusion | flops 14504951808 | bytes 30670848 | tf_op jit(solution)/shard_map/dot_general | solution.py:26
  345.1 51.4 %all-gather.11.cloned.1.call-done = bf16[6144,1536]{1,0:T(8,128)(2,1)} async-done(((bf16[384,1536]{1,0:T(8,128)(2,1)}), bf16[6144,1536]{1,0:T(8,128)(2,1)}) %all-gather.11.cloned.1.call-update) | async-done | bytes 18874384 | tf_op jit(solution)/shard_map/all_gather | solution.py:530
  396.5 27.4 %multiply_convert_fusion = bf16[768,6144]{1,0:T(8,128)(2,1)} fusion(f32[768,6144]{1,0:T(8,128)} %get-tuple-element.63, bf16[768,1536]{1,0:T(8,128)(2,1)S(1)} %copy-done.18, bf16[6144,1536]{1,0:T(8,128)(2,1)} %all-gather.11.cloned.1.call-done), kind=kOutput, calls=%fused_computation.7 | convolution fusion | flops 14504951808 | bytes 49545216 | tf_op jit(solution)/shard_map/dot_general | solution.py:32
  423.8 15.4 %convolution_convert_fusion.2 = bf16[1536,3072]{1,0:T(8,128)(2,1)} fusion(bf16[768,6144]{1,0:T(8,128)(2,1)} %multiply_convert_fusion, s32[]{:T(128)S(6)} %select_n.274, f32[768,1536]{1,0:T(8,128)} %copy-done.9, f32[1536]{0:T(1024)S(1)} %copy-done.51, f32[1536]{0:T(1024)S(1)} %get-tuple-element.166, f32[768]{0:T(1024)S(1)} %add_rsqrt_fusion.3, ...), kind=kOutput, calls=%fused_computation.17 | convolution fusion | flops 7258374144 | bytes 18892804 | tf_op jit(solution)/shard_map/dot_general | solution.py:26
  439.2 13.0 %convolution_convert_fusion.1 = bf16[1536,3072]{1,0:T(8,128)(2,1)} fusion(bf16[768,6144]{1,0:T(8,128)(2,1)S(1)} %copy-done.60, s32[]{:T(128)S(6)} %select_n.275, f32[768,1536]{1,0:T(8,128)} %copy-done.9, f32[1536]{0:T(1024)S(1)} %copy-done.51, f32[1536]{0:T(1024)S(1)} %get-tuple-element.166, f32[768]{0:T(1024)S(1)} %add_rsqrt_fusion.3, ...), kind=kOutput, calls=%fused_computation.16 | convolution fusion | flops 7258374144 | bytes 18898948 | tf_op jit(solution)/shard_map/dot_general | solution.py:26
  452.5 24.4 %multiply_reduce_fusion = (bf16[1536]{0:T(1024)(128)(2,1)}, f32[768]{0:T(1024)S(1)}, f32[768]{0:T(1024)S(1)}, bf16[1536]{0:T(1024)(128)(2,1)}, f32[768,1536]{1,0:T(8,128)}) fusion(f32[768,1536]{1,0:T(8,128)} %copy-done.9, f32[768]{0:T(1024)S(1)} %add_rsqrt_fusion.3, f32[768]{0:T(1024)S(1)} %broadcast_multiply_fusion.9, f32[1536]{0:T(1024)S(1)} %get-tuple-element.166, ...), kind=kOutput, calls=%fused_computation.69 | convolution fusion | flops 14506125312 | bytes 37773312 | tf_op jit(solution)/shard_map/dot_general | solution.py:32
  498.9 17.6 %cross_attend_back.1 = (bf16[768,1536]{1,0:T(8,128)(2,1)}, f32[128,1536]{1,0:T(8,128)}, f32[128,1536]{1,0:T(8,128)}) custom-call(bf16[768,1536]{1,0:T(8,128)(2,1)} %fusion.78.q_ref, bf16[768,1536]{1,0:T(8,128)(2,1)} %fusion.81.g_ref, bf16[128,1536]{1,0:T(8,128)(2,1)} %get-tuple-element.207.k_ref, bf16[128,1536]{1,0:T(8,128)(2,1)} %get-tuple-element.206.v_ref, ...), custom_call_target="tpu_custom_call" | custom-call | flops 3019898880 | bytes 7077888 | tf_op jit(solution)/shard_map/cross_attend_back/pallas_call | solution.py:349
  573.2 14.8 %self_attend_back.2 = (f32[2,4,6,64,384]{4,3,2,1,0:T(8,128)}, bf16[1536,768]{1,0:T(8,128)(2,1)}, bf16[1536,768]{1,0:T(8,128)(2,1)}) custom-call(s32[4,4]{1,0:T(4,128)} %pad_add_fusion.bounds, bf16[1536,768]{1,0:T(8,128)(2,1)} %convolution_convert_fusion.10.q_ref, bf16[1536,768]{1,0:T(8,128)(2,1)} %pad_maximum_fusion.5.g_ref, ...), custom_call_target="tpu_custom_call" | custom-call | flops 150994944 | bytes 98304 | tf_op jit(solution)/shard_map/self_attend_back/pallas_call | solution.py:261
  599.5 74.1 %collective-permute-done.8 = bf16[1536,1536]{1,0:T(8,128)(2,1)} collective-permute-done((bf16[1536,1536]{1,0:T(8,128)(2,1)}, bf16[1536,1536]{1,0:T(8,128)(2,1)}, u32[]{:S(2)}, u32[]{:S(2)}) %collective-permute-start.8) | collective-permute-done | bytes 4718624 | tf_op jit(solution)/shard_map/ppermute | solution.py:381
  686.4 59.7 %self_attend_back.3 = (bf16[1536,768]{1,0:T(8,128)(2,1)}, bf16[1536,768]{1,0:T(8,128)(2,1)}, bf16[1536,768]{1,0:T(8,128)(2,1)}) custom-call(s32[4,4]{1,0:T(4,128)} %pad_add_fusion.1.bounds, bf16[1536,768]{1,0:T(8,128)(2,1)} %convolution_convert_fusion.10.q_ref, bf16[1536,768]{1,0:T(8,128)(2,1)} %pad_maximum_fusion.5.g_ref, ...), custom_call_target="tpu_custom_call" | custom-call | flops 150994944 | bytes 98304 | tf_op jit(solution)/shard_map/self_attend_back/pallas_call | solution.py:261
  762.2 14.2 %convolution_convert_fusion.3 = bf16[1536,2304]{1,0:T(8,128)(2,1)} fusion(bf16[1536,2304]{1,0:T(8,128)(2,1)S(1)} %pad_maximum_fusion.1, f32[1536]{0:T(1024)S(1)} %copy-done.48, f32[1536]{0:T(1024)S(1)} %copy-done.35, f32[1536]{0:T(1024)S(1)} %copy-done.53, f32[1536]{0:T(1024)S(1)} %copy-done.39, bf16[768,1536]{1,0:T(8,128)(2,1)S(1)} %copy-done.8, ...), kind=kOutput, calls=%fused_computation.18 | convolution fusion | flops 10896408576 | bytes 18898944 | tf_op jit(solution)/shard_map/dot_general | solution.py:26
  776.4 35.3 %collective-permute-done.13 = bf16[768,1536]{1,0:T(8,128)(2,1)S(1)} collective-permute-done((bf16[768,1536]{1,0:T(8,128)(2,1)S(1)}, bf16[768,1536]{1,0:T(8,128)(2,1)S(1)}, u32[]{:S(2)}, u32[]{:S(2)}) %collective-permute-start.13) | collective-permute-done | bytes 2359328 | tf_op jit(solution)/shard_map/ppermute | solution.py:381
  831.1 33.9 %reduce-scatter.6.cloned.1.call-done = bf16[4,96,1536]{2,1,0:T(8,128)(2,1)} async-done(((bf16[4,1536,1536]{2,1,0:T(8,128)(2,1)}), bf16[4,96,1536]{2,1,0:T(8,128)(2,1)}) %reduce-scatter.6.cloned.1.call-update) | async-done | bytes 1179664 | tf_op jit(solution)/shard_map/reduce_scatter | solution.py:639
  868.4 22.8 %add_convert_fusion.5 = bf16[768,1536]{1,0:T(8,128)(2,1)} fusion(f32[768,1536]{1,0:T(8,128)} %copy-done.9, bf16[768,6144]{1,0:T(8,128)(2,1)} %copy-done.62, bf16[6144,1536]{1,0:T(8,128)(2,1)} %all-gather.11.cloned.1.call-done), kind=kOutput, calls=%fused_computation.80 | convolution fusion | flops 14497873920 | bytes 35389440 | tf_op jit(solution)/shard_map/dot_general | solution.py:22
  904.2 48.9 %collective-permute-done.17 = bf16[1,192,1536]{2,1,0:T(8,128)(2,1)} collective-permute-done((bf16[1,192,1536]{2,1,0:T(8,128)(2,1)}, bf16[1,192,1536]{2,1,0:T(8,128)(2,1)}, u32[]{:S(2)}, u32[]{:S(2)}) %collective-permute-start.17) | collective-permute-done | bytes 589856 | tf_op jit(solution)/shard_map/ppermute | solution.py:381
  959.5 12.7 %collective-permute-done.19 = bf16[2,96,1536]{2,1,0:T(8,128)(2,1)S(1)} collective-permute-done((bf16[2,96,1536]{2,1,0:T(8,128)(2,1)S(1)}, bf16[2,96,1536]{2,1,0:T(8,128)(2,1)S(1)}, u32[]{:S(2)}, u32[]{:S(2)}) %collective-permute-start.19) | collective-permute-done | bytes 589856 | tf_op jit(solution)/shard_map/ppermute | solution.py:381
  (371 shorter events, 302.0 us)
Async XLA Ops:
  7.2 89.5 %all-gather.5.cloned.1.call-start = ((), (), s32[]{:S(2)}) async-start(), calls=%async_computation.3 | async-start | bytes 7938048 | tf_op jit(solution)/shard_map/all_gather | solution.py:530
  10.2 197.8 %all-gather.7.cloned.1.call-start = ((), (), s32[]{:S(2)}) async-start(), calls=%async_computation.4 | async-start | bytes 20054016 | tf_op jit(solution)/shard_map/all_gather | solution.py:530
  15.0 281.0 %all-gather.9.cloned.1.call-start = ((), (), s32[]{:S(2)}) async-start(), calls=%async_computation.5 | async-start | bytes 20054016 | tf_op jit(solution)/shard_map/all_gather | solution.py:530
  15.8 380.7 %all-gather.11.cloned.1.call-start = ((), (), s32[]{:S(2)}) async-start(), calls=%async_computation.6 | async-start | bytes 20054016 | tf_op jit(solution)/shard_map/all_gather | solution.py:530
  16.4 668.2 %reduce-scatter.4.cloned.1.call-start = ((), (), s32[]{:S(2)}) async-start(), calls=%async_computation.7 | async-start | bytes 20054016 | tf_op jit(solution)/shard_map/reduce_scatter | solution.py:446
  20.1 54.6 %collective-permute-start = (bf16[768,1536]{1,0:T(8,128)(2,1)S(1)}, bf16[768,1536]{1,0:T(8,128)(2,1)}, u32[]{:S(2)}, u32[]{:S(2)}) collective-permute-start(bf16[768,1536]{1,0:T(8,128)(2,1)S(1)} %copy-done.1), channel_id=1, source_target_pairs={{0,1},{1,0},{2,3},{3,2},{4,5},{5,4},{6,7},{7,6},{8,9},{9,8},{10,11... | collective-permute-start | bytes 7077896 | tf_op jit(solution)/shard_map/ppermute | solution.py:381
  28.9 126.1 %collective-permute-start.2 = (bf16[768,1536]{1,0:T(8,128)(2,1)}, bf16[768,1536]{1,0:T(8,128)(2,1)}, u32[]{:S(2)}, u32[]{:S(2)}) collective-permute-start(bf16[768,1536]{1,0:T(8,128)(2,1)} %collective-permute-done.1), channel_id=1, source_target_pairs={{0,1},{1,0},{2,3},{3,2},{4,5},{5,4},{6,7},{7,6},{8,9},{9,8},{10,11... | collective-permute-start | bytes 7077896 | tf_op jit(solution)/shard_map/ppermute | solution.py:381
  188.0 16.5 %collective-permute-start.3 = (bf16[768,768]{1,0:T(8,128)(2,1)}, bf16[768,768]{1,0:T(8,128)(2,1)}, u32[]{:S(2)}, u32[]{:S(2)}) collective-permute-start(bf16[768,768]{1,0:T(8,128)(2,1)} %constant_dynamic-slice_fusion.3), channel_id=1, source_target_pairs={{0,1},{1,0},{2,3},{3,2},{4,5},{5,4},{6,7},{7,6},{8,9},{9,8},{10,11... | collective-permute-start | bytes 3538952 | tf_op jit(solution)/shard_map/ppermute | solution.py:381
  212.0 17.9 %collective-permute-start.4 = (bf16[128,2,768]{2,0,1:T(8,128)(2,1)S(1)}, bf16[128,2,768]{2,0,1:T(8,128)(2,1)S(1)}, u32[]{:S(2)}, u32[]{:S(2)}) collective-permute-start(bf16[128,2,768]{2,0,1:T(8,128)(2,1)S(1)} %copy.90), channel_id=1, source_target_pairs={{0,1},{1,0},{2,3},{3,2},{4,5},{5,4},{6,7},{7,6},{8,9},{9,8},{10,11... | collective-permute-start | bytes 1179656 | tf_op jit(solution)/shard_map/ppermute | solution.py:381
  345.1 519.9 %reduce-scatter.6.cloned.1.call-start = ((), (), s32[]{:S(2)}) async-start(), calls=%async_computation.8 | async-start | bytes 20054016 | tf_op jit(solution)/shard_map/reduce_scatter | solution.py:639
  452.2 31.3 %collective-permute-start.5 = (bf16[1536,3072]{1,0:T(8,128)(2,1)}, bf16[1536,3072]{1,0:T(8,128)(2,1)}, u32[]{:S(2)}, u32[]{:S(2)}) collective-permute-start(bf16[1536,3072]{1,0:T(8,128)(2,1)} %convolution_convert_fusion.1), channel_id=1, source_target_pairs={{0,2},{2,0},{4,6},{6,4},{8,10},{10,8},{12,14},{14,12},{16,18},{18,... | collective-permute-start | bytes 28311560 | tf_op jit(solution)/shard_map/ppermute | solution.py:381
  540.2 28.1 %collective-permute-start.7 = (bf16[768,768]{1,0:T(8,128)(2,1)}, bf16[768,768]{1,0:T(8,128)(2,1)}, u32[]{:S(2)}, u32[]{:S(2)}) collective-permute-start(bf16[768,768]{1,0:T(8,128)(2,1)} %constant_dynamic-slice_fusion.1), channel_id=1, source_target_pairs={{0,1},{1,0},{2,3},{3,2},{4,5},{5,4},{6,7},{7,6},{8,9},{9,8},{10,11... | collective-permute-start | bytes 3538952 | tf_op jit(solution)/shard_map/ppermute | solution.py:381
  568.4 411.8 %reduce-scatter.8.cloned.1.call-start = ((), (), s32[]{:S(2)}) async-start(), calls=%async_computation.9 | async-start | bytes 7938048 | tf_op jit(solution)/shard_map/reduce_scatter | solution.py:446
  568.4 105.1 %collective-permute-start.8 = (bf16[1536,1536]{1,0:T(8,128)(2,1)}, bf16[1536,1536]{1,0:T(8,128)(2,1)}, u32[]{:S(2)}, u32[]{:S(2)}) collective-permute-start(bf16[1536,1536]{1,0:T(8,128)(2,1)} %add_convert_fusion.1), channel_id=1, source_target_pairs={{0,1},{1,0},{2,3},{3,2},{4,5},{5,4},{6,7},{7,6},{8,9},{9,8},{10,11... | collective-permute-start | bytes 14155784 | tf_op jit(solution)/shard_map/ppermute | solution.py:381
  588.0 158.1 %collective-permute-start.12 = (bf16[1536,768]{1,0:T(8,128)(2,1)}, bf16[1536,768]{1,0:T(8,128)(2,1)}, u32[]{:S(2)}, u32[]{:S(2)}) collective-permute-start(bf16[1536,768]{1,0:T(8,128)(2,1)} %get-tuple-element.90), channel_id=1, source_target_pairs={{2,0},{4,2},{6,4},{8,6},{10,8},{12,10},{14,12},{16,14},{18,16},{20... | collective-permute-start | bytes 7077896 | tf_op jit(solution)/shard_map/ppermute | solution.py:387
  592.6 156.6 %collective-permute-start.11 = (bf16[1536,768]{1,0:T(8,128)(2,1)}, bf16[1536,768]{1,0:T(8,128)(2,1)}, u32[]{:S(2)}, u32[]{:S(2)}) collective-permute-start(bf16[1536,768]{1,0:T(8,128)(2,1)} %get-tuple-element.88), channel_id=1, source_target_pairs={{2,0},{4,2},{6,4},{8,6},{10,8},{12,10},{14,12},{16,14},{18,16},{20... | collective-permute-start | bytes 7077896 | tf_op jit(solution)/shard_map/ppermute | solution.py:387
  598.0 293.2 %collective-permute-start.20 = (bf16[128,1536]{1,0:T(8,128)(2,1)S(1)}, bf16[128,1536]{1,0:T(8,128)(2,1)}, u32[]{:S(2)}, u32[]{:S(2)}) collective-permute-start(bf16[128,1536]{1,0:T(8,128)(2,1)S(1)} %fusion.92), channel_id=1, source_target_pairs={{0,1},{1,0},{2,3},{3,2},{4,5},{5,4},{6,7},{7,6},{8,9},{9,8},{10,11... | collective-permute-start | bytes 1179656 | tf_op jit(solution)/shard_map/ppermute | solution.py:381
  684.5 180.5 %collective-permute-start.9 = (bf16[4,192,1536]{2,1,0:T(8,128)(2,1)}, bf16[4,192,1536]{2,1,0:T(8,128)(2,1)}, u32[]{:S(2)}, u32[]{:S(2)}) collective-permute-start(bf16[4,192,1536]{2,1,0:T(8,128)(2,1)} %dynamic-slice_bitcast_fusion), channel_id=1, source_target_pairs={{0,4},{2,6},{4,0},{6,2},{8,12},{10,14},{12,8},{14,10},{16,20},{18,... | collective-permute-start | bytes 7077896 | tf_op jit(solution)/shard_map/ppermute | solution.py:381
  685.9 65.9 %collective-permute-start.10 = (bf16[384,1536]{1,0:T(8,128)(2,1)}, bf16[384,1536]{1,0:T(8,128)(2,1)S(1)}, u32[]{:S(2)}, u32[]{:S(2)}) collective-permute-start(bf16[384,1536]{1,0:T(8,128)(2,1)} %reduce-scatter.4.cloned.1.call-done), channel_id=1, source_target_pairs={{0,1},{1,0},{2,3},{3,2},{4,5},{5,4},{6,7},{7,6},{8,9},{9,8},{10,11... | collective-permute-start | bytes 3538952 | tf_op jit(solution)/shard_map/ppermute | solution.py:381
  760.6 51.1 %collective-permute-start.13 = (bf16[768,1536]{1,0:T(8,128)(2,1)S(1)}, bf16[768,1536]{1,0:T(8,128)(2,1)S(1)}, u32[]{:S(2)}, u32[]{:S(2)}) collective-permute-start(bf16[768,1536]{1,0:T(8,128)(2,1)S(1)} %fusion.84), channel_id=1, source_target_pairs={{0,1},{1,0},{2,3},{3,2},{4,5},{5,4},{6,7},{7,6},{8,9},{9,8},{10,11... | collective-permute-start | bytes 7077896 | tf_op jit(solution)/shard_map/ppermute | solution.py:381
  868.2 27.8 %collective-permute-start.16 = (bf16[2,192,1536]{2,1,0:T(8,128)(2,1)S(1)}, bf16[2,192,1536]{2,1,0:T(8,128)(2,1)S(1)}, u32[]{:S(2)}, u32[]{:S(2)}) collective-permute-start(bf16[2,192,1536]{2,1,0:T(8,128)(2,1)S(1)} %dynamic-slice_bitcast_fusion.1), channel_id=1, source_target_pairs={{0,8},{2,10},{4,12},{6,14},{8,0},{10,2},{12,4},{14,6},{16,24},{18,... | collective-permute-start | bytes 3538952 | tf_op jit(solution)/shard_map/ppermute | solution.py:381
  897.3 55.8 %collective-permute-start.17 = (bf16[1,192,1536]{2,1,0:T(8,128)(2,1)}, bf16[1,192,1536]{2,1,0:T(8,128)(2,1)}, u32[]{:S(2)}, u32[]{:S(2)}) collective-permute-start(bf16[1,192,1536]{2,1,0:T(8,128)(2,1)} %constant_dynamic-slice_fusion), channel_id=1, source_target_pairs={{0,16},{2,18},{4,20},{6,22},{8,24},{10,26},{12,28},{14,30},{16,0},... | collective-permute-start | bytes 1769480 | tf_op jit(solution)/shard_map/ppermute | solution.py:381
  902.0 56.1 %collective-permute-start.14 = (bf16[3,96,1536]{2,1,0:T(8,128)(2,1)S(1)}, bf16[3,96,1536]{2,1,0:T(8,128)(2,1)S(1)}, u32[]{:S(2)}, u32[]{:S(2)}) collective-permute-start(bf16[3,96,1536]{2,1,0:T(8,128)(2,1)S(1)} %slice.161), channel_id=1, source_target_pairs={{0,1},{1,0},{2,3},{3,2},{4,5},{5,4},{6,7},{7,6},{8,9},{9,8},{10,11... | collective-permute-start | bytes 2654216 | tf_op jit(solution)/shard_map/ppermute | solution.py:381
  903.6 51.0 %collective-permute-start.15 = (bf16[96,2,768]{2,1,0:T(2,128)(2,1)S(1)}, bf16[96,2,768]{2,1,0:T(2,128)(2,1)S(1)}, u32[]{:S(2)}, u32[]{:S(2)}) collective-permute-start(bf16[96,2,768]{2,1,0:T(2,128)(2,1)S(1)} %reshape_squeeze.3), channel_id=1, source_target_pairs={{0,1},{1,0},{2,3},{3,2},{4,5},{5,4},{6,7},{7,6},{8,9},{9,8},{10,11... | collective-permute-start | bytes 884744 | tf_op jit(solution)/shard_map/ppermute | solution.py:381
  (88 other events, 1667.4 us)
Sparse Core Ops, SparseCore 0:
  10.9 85.7 all-gather.4
  98.8 96.5 all-gather.6
  197.1 98.9 all-gather.8
  297.5 98.9 all-gather.10
  400.4 194.8 reduce-scatter.3
  599.3 265.6 reduce-scatter.5
  869.0 111.1 reduce-scatter.7
